TPU v7x, 128 devices: a whole 4x4x4 slice. The times are simulated.
128 devices in a mesh: row: 16 (over y, z), col: 8 (over x, core).
Axes of the slice: x: 4, y: 4, z: 4, core: 2. Of those that a mesh axis runs over, the one named last changes fastest.
Arguments:
- spectrum: float32 [2, 8192, 4096], P(None, 'row', 'col'), may hold values from -6 to 6
- pupil: float32 [2, 512, 512], replicated, may hold values from -4.2 to 4.2
- amplitudes: float32 [16, 8, 1, 512, 512], P('row', 'col'), may hold values from 0.1 to 3
- offsets: int32 [16, 8, 1, 2], P('row', 'col'), may hold values from 0 to 511, as said below
- counts: int32 [16, 8], P('row', 'col'), may hold values from 1 to 1, as said below
Outputs:
- recovered: float32 [2, 8192, 4096], P(None, 'row', 'col')
Inputs may be any that keep to these rules, and one draw needn't show every extreme that they name: `offsets`: offsets are corners inside the tile: the row below 512, the column below 512. `counts`: some device has all 1 slots live.
All inputs are finite; a program needn't handle non-finite values.
Results may differ from a plain program's by a relative error of at most 0.012.
Values sent between devices are 32-bit elements; how exact they have to be, the bound alone decides.
No kernel may reach another device: no remote copies, remote signals or barrier semaphores. Data moves between devices by JAX's collectives and lax.ppermute only.
A program may use at most 128 MiB of HBM per device.

v0:
```python
import math

import jax
import jax.numpy as jnp
from jax import lax
from jax.sharding import PartitionSpec as P

SWEEPS = 2


step_size = 0.5
floor_value = 0.05


def shifted(value, axis, steps):
    count = lax.axis_size(axis)
    leading, last = (max(0, -steps), min(count, count - steps))
    return lax.ppermute(value, axis, [(source, source + steps) for source in range(leading, last)])


def dft_tables(width):
    index = jnp.arange(width, dtype=jnp.int32)
    phase = index[:, None] * index[None, :] % width
    angle = phase.astype(jnp.float32) * (2.0 * math.pi / width)
    scale = 1.0 / math.sqrt(width)
    return (
        (jnp.cos(angle) * scale).astype(jnp.bfloat16),
        (jnp.sin(angle) * scale).astype(jnp.bfloat16),
    )


def transform(real, imag, cosine, sine, sign):
    real = real.astype(jnp.bfloat16)
    imag = imag.astype(jnp.bfloat16)

    def right(a, b):
        return jnp.einsum("swk,kj->swj", a, b, preferred_element_type=jnp.float32)

    def left(b, a):
        return jnp.einsum("ik,skj->sij", b, a, preferred_element_type=jnp.float32)

    first_real = (right(real, cosine) - sign * right(imag, sine)).astype(jnp.bfloat16)
    first_imag = (right(imag, cosine) + sign * right(real, sine)).astype(jnp.bfloat16)
    out_real = left(cosine, first_real) - sign * left(sine, first_imag)
    out_imag = left(cosine, first_imag) + sign * left(sine, first_real)
    return (out_real, out_imag)


def slot_gradient(windows, pupil, amps, live, cosine, sine):
    pupil_real = pupil[0][None]
    pupil_imag = pupil[1][None]
    window_real = windows[:, 0]
    window_imag = windows[:, 1]
    field_real = window_real * pupil_real - window_imag * pupil_imag
    field_imag = window_real * pupil_imag + window_imag * pupil_real
    wave_real, wave_imag = transform(field_real, field_imag, cosine, sine, 1.0)
    magnitude = jnp.sqrt(wave_real * wave_real + wave_imag * wave_imag)
    keep = 1.0 - amps / jnp.maximum(magnitude, floor_value)
    back_real, back_imag = transform(wave_real * keep, wave_imag * keep, cosine, sine, -1.0)
    mask = live[:, None, None]
    grad_real = (back_real * pupil_real + back_imag * pupil_imag) * mask
    grad_imag = (back_imag * pupil_real - back_real * pupil_imag) * mask
    return jnp.stack([grad_real, grad_imag], axis=1)


def extend(tile):
    below = shifted(tile, "row", -1)
    tall = jnp.concatenate([tile, below], axis=1)
    right = shifted(tall, "col", -1)
    return jnp.concatenate([tall, right], axis=2)


def fold_back(region, rows, cols, width):
    right = shifted(region[:, :, cols:], "col", 1)
    left_part = jnp.concatenate([region[:, :, :width] + right, region[:, :, width:cols]], axis=2)
    bottom = shifted(left_part[:, rows:, :], "row", 1)
    return jnp.concatenate([left_part[:, :width, :] + bottom, left_part[:, width:rows, :]], axis=1)


def add_piece(region, piece, place):
    zero = jnp.zeros((), jnp.int32)
    start = (zero, place[0], place[1])
    current = lax.dynamic_slice(region, start, piece.shape)
    return lax.dynamic_update_slice(region, current + piece, start)


def on_device(spectrum, pupil, amplitudes, offsets, counts):
    width = pupil.shape[1]
    rows = spectrum.shape[1]
    cols = spectrum.shape[2]
    amps = amplitudes[0, 0]
    places = offsets[0, 0]
    live_count = counts[0, 0]
    cosine, sine = dft_tables(width)
    zero = jnp.zeros((), jnp.int32)
    for sweep in range(SWEEPS):
        region = extend(spectrum)
        empty = jnp.zeros_like(region)

        def one_slot(slot, gathered):
            place = places[slot]
            window = lax.dynamic_slice(region, (zero, place[0], place[1]), (2, width, width))
            piece = slot_gradient(
                window[None], pupil, amps, jnp.ones((1,), jnp.float32), cosine, sine
            )
            return add_piece(gathered, piece[0], place)

        gathered = lax.fori_loop(zero, live_count, one_slot, empty)
        gradient = fold_back(gathered, rows, cols, width)
        spectrum = spectrum - step_size * gradient
    return spectrum


def solution(mesh):
    in_specs = (
        P(None, "row", "col"),
        P(),
        P("row", "col", None, None, None),
        P("row", "col", None, None),
        P("row", "col"),
    )
    out_specs = P(None, "row", "col")
    return jax.shard_map(
        on_device, mesh=mesh, in_specs=in_specs, out_specs=out_specs, check_vma=False
    )
```

profile of v0, /device:TPU:28, one launch (start us, length us, event | category | flops | bytes accessed | tf_op | source)
XLA Modules:
  0.0 634.2 jit_solution(18013991846376937791)
XLA Ops:
  0.0 6.1 collective-permute-start
  9.2 42.1 %collective-permute-done = f32[2,512,512]{2,1,0:T(8,128)S(1)} collective-permute-done((f32[2,512,512]{2,1,0:T(8,128)}, f32[2,512,512]{2,1,0:T(8,128)S(1)}, u32[]{:S(2)}, u32[]{:S(2)}) %collective-permute-start) | collective-permute-done | bytes 2097184 | tf_op jit(solution)/shard_map/ppermute | solution.py:18
  60.7 40.4 %collective-permute-done.1 = f32[2,1024,512]{2,1,0:T(8,128)} collective-permute-done((f32[2,1024,512]{2,1,0:T(8,128)}, f32[2,1024,512]{2,1,0:T(8,128)}, u32[]{:S(2)}, u32[]{:S(2)}) %collective-permute-start.1) | collective-permute-done | bytes 4194336 | tf_op jit(solution)/shard_map/ppermute | solution.py:18
  104.6 5.4 fusion.70
  110.0 4.9 fusion.72
  114.9 5.0 fusion.28
  119.9 5.0 fusion.27
  125.0 5.0 fusion.71
  130.0 5.0 fusion.69
  135.0 5.4 convolution_add_fusion.2
  140.4 5.3 fusion.36
  145.7 5.0 fusion.67
  150.7 5.0 fusion.68
  155.7 5.5 fusion.23
  161.2 4.0 fusion.73
  165.2 5.2 fusion.58
  170.4 5.1 fusion.24
  175.4 5.2 fusion.57
  180.6 5.2 fusion.74
  185.8 4.3 broadcast.118.clone
  190.2 22.7 %while.28 = (s32[]{:T(128)}, f32[2,1024,1024]{2,1,0:T(8,128)}, s32[]{:T(128)}, s32[]{:T(128)}, s32[]{:T(128)}, /*index=5*/f32[512,512]{0,1:T(8,128)S(1)}, f32[51...) while((s32[]{:T(128)}, f32[2,1024,1024]{2,1,0:T(8,128)}, ...), condition=%wide.region_1.2_spmd, body=%wide.region_0.1_spmd.sunk | while | flops 3670018 | bytes 18874496 | solution.py:108
  197.2 15.0 %dynamic_update_slice.16 = f32[2,1024,1024]{2,1,0:T(8,128)} dynamic-update-slice(f32[2,1024,1024]{2,1,0:T(8,128)} %get-tuple-element.698, f32[2,512,512]{2,1,0:T(8,128)} %fusion.275, s32[]{:T(128)} %constant.87.clone.1..sunk, s32[]{:T(128)} %get-tuple-element.712, s32[]{:T(128)} %get-tuple-element.713) | dynamic-update-slice | bytes 4194308 | tf_op jit(solution)/shard_map/while/body/dynamic_update_slice | solution.py:84
  215.7 3.9 collective-permute-start.2
  219.5 46.4 %collective-permute-done.2 = f32[2,1024,512]{2,1,0:T(8,128)S(1)} collective-permute-done((f32[2,1024,512]{2,1,0:T(8,128)S(1)}, f32[2,1024,512]{2,1,0:T(8,128)S(1)}, u32[]{:S(2)}, u32[]{:S(2)}) %collective-permute-start.2) | collective-permute-done | bytes 4194336 | tf_op jit(solution)/shard_map/ppermute | solution.py:18
  269.4 48.8 %collective-permute-done.3 = f32[2,512,512]{2,1,0:T(8,128)S(1)} collective-permute-done((f32[2,512,512]{2,1,0:T(8,128)S(1)}, f32[2,512,512]{2,1,0:T(8,128)S(1)}, u32[]{:S(2)}, u32[]{:S(2)}) %collective-permute-start.3) | collective-permute-done | bytes 2097184 | tf_op jit(solution)/shard_map/ppermute | solution.py:18
  322.7 44.0 %collective-permute-done.4 = f32[2,512,512]{2,1,0:T(8,128)S(1)} collective-permute-done((f32[2,512,512]{2,1,0:T(8,128)S(1)}, f32[2,512,512]{2,1,0:T(8,128)S(1)}, u32[]{:S(2)}, u32[]{:S(2)}) %collective-permute-start.4) | collective-permute-done | bytes 2097184 | tf_op jit(solution)/shard_map/ppermute | solution.py:18
  371.2 46.3 %collective-permute-done.5 = f32[2,1024,512]{2,1,0:T(8,128)} collective-permute-done((f32[2,1024,512]{2,1,0:T(8,128)}, f32[2,1024,512]{2,1,0:T(8,128)}, u32[]{:S(2)}, u32[]{:S(2)}) %collective-permute-start.5) | collective-permute-done | bytes 4194336 | tf_op jit(solution)/shard_map/ppermute | solution.py:18
  421.6 4.9 fusion.62
  426.5 4.9 fusion.64
  431.3 5.0 fusion.30
  436.4 5.0 fusion.29
  441.4 5.0 fusion.63
  446.4 5.0 fusion.61
  451.4 5.6 convolution_add_fusion
  457.1 5.3 fusion.34
  462.4 5.0 fusion.59
  467.4 5.0 fusion.60
  472.4 5.2 fusion.25
  477.7 4.0 fusion.75
  481.7 5.2 fusion.66
  486.8 5.1 fusion.26
  491.9 5.2 fusion.65
  497.1 5.2 fusion.76
  502.3 4.3 broadcast.118
  506.6 22.7 %while.29 = (s32[]{:T(128)}, f32[2,1024,1024]{2,1,0:T(8,128)}, s32[]{:T(128)}, s32[]{:T(128)}, s32[]{:T(128)}, /*index=5*/f32[512,512]{0,1:T(8,128)S(1)}, f32[51...) while((s32[]{:T(128)}, f32[2,1024,1024]{2,1,0:T(8,128)}, ...), condition=%wide.region_3.4_spmd, body=%wide.region_2.3_spmd.sunk | while | flops 3670018 | bytes 18874496 | solution.py:108
  513.7 15.0 %dynamic_update_slice.17 = f32[2,1024,1024]{2,1,0:T(8,128)} dynamic-update-slice(f32[2,1024,1024]{2,1,0:T(8,128)} %get-tuple-element.734, f32[2,512,512]{2,1,0:T(8,128)} %fusion.277, s32[]{:T(128)} %constant.87.clone.1..sunk.1, s32[]{:T(128)} %get-tuple-element.748, s32[]{:T(128)} %get-tuple-element.749) | dynamic-update-slice | bytes 4194308 | tf_op jit(solution)/shard_map/while/body/dynamic_update_slice | solution.py:84
  534.6 47.9 %collective-permute-done.6 = f32[2,1024,512]{2,1,0:T(8,128)S(1)} collective-permute-done((f32[2,1024,512]{2,1,0:T(8,128)S(1)}, f32[2,1024,512]{2,1,0:T(8,128)S(1)}, u32[]{:S(2)}, u32[]{:S(2)}) %collective-permute-start.6) | collective-permute-done | bytes 4194336 | tf_op jit(solution)/shard_map/ppermute | solution.py:18
  585.8 46.1 %collective-permute-done.7 = f32[2,512,512]{2,1,0:T(8,128)S(1)} collective-permute-done((f32[2,512,512]{2,1,0:T(8,128)S(1)}, f32[2,512,512]{2,1,0:T(8,128)S(1)}, u32[]{:S(2)}, u32[]{:S(2)}) %collective-permute-start.7) | collective-permute-done | bytes 2097184 | tf_op jit(solution)/shard_map/ppermute | solution.py:18
  (49 shorter events, 54.5 us)
Async XLA Ops:
  0.0 51.3 %collective-permute-start = (f32[2,512,512]{2,1,0:T(8,128)}, f32[2,512,512]{2,1,0:T(8,128)S(1)}, u32[]{:S(2)}, u32[]{:S(2)}) collective-permute-start(f32[2,512,512]{2,1,0:T(8,128)} %param.9), channel_id=1, source_target_pairs={{8,0},{16,8},{24,16},{32,24},{40,32},{48,40},{56,48},{64,56},{72,6... | collective-permute-start | bytes 6291464 | tf_op jit(solution)/shard_map/ppermute | solution.py:18
  9.2 45.6 %copy-start.10 = (s32[1,1,1,2]{3,2,1,0:T(1,128)S(1)}, s32[1,1,1,2]{3,2,1,0:T(1,128)}, u32[]{:S(2)}) copy-start(s32[1,1,1,2]{3,2,1,0:T(1,128)} %param.12) | copy-start | bytes 28
  9.2 48.9 %copy-start.7 = (f32[1,1,1,512,512]{4,3,2,1,0:T(8,128)S(1)}, f32[1,1,1,512,512]{4,3,2,1,0:T(8,128)}, u32[]{:S(2)}) copy-start(f32[1,1,1,512,512]{4,3,2,1,0:T(8,128)} %param.11) | copy-start | bytes 3145732
  52.9 48.2 %collective-permute-start.1 = (f32[2,1024,512]{2,1,0:T(8,128)}, f32[2,1024,512]{2,1,0:T(8,128)}, u32[]{:S(2)}, u32[]{:S(2)}) collective-permute-start(f32[2,1024,512]{2,1,0:T(8,128)} %constant_dynamic-update-slice_fusion), channel_id=1, source_target_pairs={{1,0},{2,1},{3,2},{4,3},{5,4},{6,5},{7,6},{9,8},{10,9},{11,10},{12... | collective-permute-start | bytes 12582920 | tf_op jit(solution)/shard_map/ppermute | solution.py:18
  60.7 43.3 %copy-start = (f32[2,512,512]{2,1,0:T(8,128)S(1)}, f32[2,512,512]{2,1,0:T(8,128)}, u32[]{:S(2)}) copy-start(f32[2,512,512]{2,1,0:T(8,128)} %param.10) | copy-start | bytes 6291460
  135.0 5.4 copy-start.8
  212.8 53.1 %copy-start.2 = (f32[2,1024,1024]{2,1,0:T(8,128)S(1)}, f32[2,1024,1024]{2,1,0:T(8,128)}, u32[]{:S(2)}) copy-start(f32[2,1024,1024]{2,1,0:T(8,128)} %get-tuple-element.477) | copy-start | bytes 25165828
  215.7 50.3 %collective-permute-start.2 = (f32[2,1024,512]{2,1,0:T(8,128)S(1)}, f32[2,1024,512]{2,1,0:T(8,128)S(1)}, u32[]{:S(2)}, u32[]{:S(2)}) collective-permute-start(f32[2,1024,512]{2,1,0:T(8,128)S(1)} %slice.111), channel_id=1, source_target_pairs={{0,1},{1,2},{2,3},{3,4},{4,5},{5,6},{6,7},{8,9},{9,10},{10,11},{11... | collective-permute-start | bytes 12582920 | tf_op jit(solution)/shard_map/ppermute | solution.py:18
  267.0 51.3 %copy-start.5 = (f32[2,512,512]{2,1,0:T(8,128)S(1)}, f32[2,512,512]{2,1,0:T(8,128)}, u32[]{:S(2)}) copy-start(f32[2,512,512]{2,1,0:T(8,128)} %param.9) | copy-start | bytes 6291460
  267.2 51.1 %collective-permute-start.3 = (f32[2,512,512]{2,1,0:T(8,128)S(1)}, f32[2,512,512]{2,1,0:T(8,128)S(1)}, u32[]{:S(2)}, u32[]{:S(2)}) collective-permute-start(f32[2,512,512]{2,1,0:T(8,128)S(1)} %slice.123), channel_id=1, source_target_pairs={{0,8},{8,16},{16,24},{24,32},{32,40},{40,48},{48,56},{56,64},{64,7... | collective-permute-start | bytes 6291464 | tf_op jit(solution)/shard_map/ppermute | solution.py:18
  319.0 50.3 %copy-start.3 = (f32[2,512,512]{2,1,0:T(8,128)}, f32[2,512,512]{2,1,0:T(8,128)S(1)}, u32[]{:S(2)}) copy-start(f32[2,512,512]{2,1,0:T(8,128)S(1)} %fusion.18) | copy-start | bytes 6291460
  319.0 47.6 %collective-permute-start.4 = (f32[2,512,512]{2,1,0:T(8,128)S(1)}, f32[2,512,512]{2,1,0:T(8,128)S(1)}, u32[]{:S(2)}, u32[]{:S(2)}) collective-permute-start(f32[2,512,512]{2,1,0:T(8,128)S(1)} %fusion.18), channel_id=1, source_target_pairs={{8,0},{16,8},{24,16},{32,24},{40,32},{48,40},{56,48},{64,56},{72,6... | collective-permute-start | bytes 6291464 | tf_op jit(solution)/shard_map/ppermute | solution.py:18
  366.6 2.7 copy-start.6
  369.3 48.2 %collective-permute-start.5 = (f32[2,1024,512]{2,1,0:T(8,128)}, f32[2,1024,512]{2,1,0:T(8,128)}, u32[]{:S(2)}, u32[]{:S(2)}) collective-permute-start(f32[2,1024,512]{2,1,0:T(8,128)} %pad_maximum_fusion), channel_id=1, source_target_pairs={{1,0},{2,1},{3,2},{4,3},{5,4},{6,5},{7,6},{9,8},{10,9},{11,10},{12... | collective-permute-start | bytes 12582920 | tf_op jit(solution)/shard_map/ppermute | solution.py:18
  451.4 5.6 copy-start.9
  529.4 53.1 %copy-start.1 = (f32[2,1024,1024]{2,1,0:T(8,128)S(1)}, f32[2,1024,1024]{2,1,0:T(8,128)}, u32[]{:S(2)}) copy-start(f32[2,1024,1024]{2,1,0:T(8,128)} %get-tuple-element.478) | copy-start | bytes 25165828
  532.2 50.3 %collective-permute-start.6 = (f32[2,1024,512]{2,1,0:T(8,128)S(1)}, f32[2,1024,512]{2,1,0:T(8,128)S(1)}, u32[]{:S(2)}, u32[]{:S(2)}) collective-permute-start(f32[2,1024,512]{2,1,0:T(8,128)S(1)} %slice.117), channel_id=1, source_target_pairs={{0,1},{1,2},{2,3},{3,4},{4,5},{5,6},{6,7},{8,9},{9,10},{10,11},{11... | collective-permute-start | bytes 12582920 | tf_op jit(solution)/shard_map/ppermute | solution.py:18
  583.5 48.4 %copy-start.4 = (f32[2,512,512]{2,1,0:T(8,128)S(1)}, f32[2,512,512]{2,1,0:T(8,128)}, u32[]{:S(2)}) copy-start(f32[2,512,512]{2,1,0:T(8,128)} %copy-done.3) | copy-start | bytes 6291460
  583.7 48.2 %collective-permute-start.7 = (f32[2,512,512]{2,1,0:T(8,128)S(1)}, f32[2,512,512]{2,1,0:T(8,128)S(1)}, u32[]{:S(2)}, u32[]{:S(2)}) collective-permute-start(f32[2,512,512]{2,1,0:T(8,128)S(1)} %slice.127), channel_id=1, source_target_pairs={{0,8},{8,16},{16,24},{24,32},{32,40},{40,48},{48,56},{56,64},{64,7... | collective-permute-start | bytes 6291464 | tf_op jit(solution)/shard_map/ppermute | solution.py:18
where the time goes:
time: 641 us; the launch traced here: 634 us
  waiting for transfers between devices  362 us (56%)
  matrix products  162 us (25%)
  local copies, waits for them, and re-layouts  51.2 us (8%)
  other arithmetic  27.8 us (4%)
  starting transfers between devices  24.1 us (4%)
    ppermute x8, waiting for transfers between devices, shifted(): lax.ppermute(value, axis, [(source, source + steps) for source in range(l...  362 us
    dot_general x16, matrix products, right(): return jnp.einsum('swk,kj->swj', a, b, preferred_element_type=jnp.float32)  81 us
    dot_general x16, matrix products, left(): return jnp.einsum('ik,skj->sij', b, a, preferred_element_type=jnp.float32)  80.7 us
    dynamic_update_slice x2, local copies, waits for them, and re-layouts, add_piece(): return lax.dynamic_update_slice(region, current + piece, start)  30 us
    ppermute x8, starting transfers between devices, shifted(): lax.ppermute(value, axis, [(source, source + steps) for source in range(l...  24.1 us
  transfers between devices with their start and end apart: 8, of which 8 were waited for; matrix products, arithmetic and copies ran while one was open for 1% of the time, Pallas kernels for 0%

commit v1 on v0

v1 whole, which is shorter than its diff:
```python
import functools
import math

import jax
import jax.numpy as jnp
from jax import lax
from jax.experimental import pallas as pl
from jax.experimental.pallas import tpu as pltpu
from jax.sharding import PartitionSpec as P

STEP = 0.5
FLOOR = 0.05
VMEM = pl.BlockSpec(memory_space=pltpu.VMEM)
SMEM = pl.BlockSpec(memory_space=pltpu.SMEM)
LIMIT = 48 * 1024 * 1024
CHUNKS = (128, 128, 128, 128)

OY, OX, OYA, OXA, OYB, OXB, OYL, OYR, EDGE_Y, EDGE_X, LIVE = range(11)


def shifted(value, axis, steps):
    count = lax.axis_size(axis)
    leading, last = (max(0, -steps), min(count, count - steps))
    return lax.ppermute(value, axis, [(source, source + steps) for source in range(leading, last)])


def dft_tables(width):
    index = jnp.arange(width, dtype=jnp.int32)
    phase = index[:, None] * index[None, :] % width
    angle = phase.astype(jnp.float32) * (2.0 * math.pi / width)
    scale = 1.0 / math.sqrt(width)
    return (
        (jnp.cos(angle) * scale).astype(jnp.bfloat16),
        (jnp.sin(angle) * scale).astype(jnp.bfloat16),
    )


def call(kernel, outs, arrays, scalars, scratch=()):
    return pl.pallas_call(
        kernel,
        out_shape=outs,
        in_specs=[SMEM] + [VMEM] * len(arrays),
        out_specs=jax.tree.map(lambda _: VMEM, outs),
        scratch_shapes=list(scratch),
        compiler_params=pltpu.CompilerParams(vmem_limit_bytes=LIMIT),
    )(scalars, *arrays)


def rows_of(shape, first):
    return lax.broadcasted_iota(jnp.int32, shape, 0) + first


def cols_of(shape):
    return lax.broadcasted_iota(jnp.int32, shape, 1)


def prepare_kernel(sc, cos_ref, sin_ref, pupil_ref, bx, bxt, by, byt, pupil_out):
    w = cos_ref.shape[0]
    cosine = cos_ref[...].astype(jnp.float32)
    sine = sin_ref[...].astype(jnp.float32)
    for shift, plain, flipped in ((sc[OX], bx, bxt), (sc[OY], by, byt)):
        for axis, out, sign in ((0, plain, 1.0), (1, flipped, -1.0)):
            c = pltpu.roll(cosine, shift, axis).astype(jnp.bfloat16)
            s = (pltpu.roll(sine, shift, axis) * sign).astype(jnp.bfloat16)
            out[:w, :w] = c
            out[w:, w:] = c
            out[:w, w:] = s
            out[w:, :w] = -s
    for part in range(2):
        pupil_out[part] = pltpu.roll(pltpu.roll(pupil_ref[part], sc[OY], 0), sc[OX], 1)


def gradient(sc, window, pupil, amp, bx, bxt, by, byt, outs, firsts, left, stacked, extra):
    w = amp.shape[0]
    for first, size in firsts:
        rows = pl.ds(first, size)
        wr, wi = window(first, size)
        pr, pi = pupil[0, rows, :], pupil[1, rows, :]
        left[rows, :w] = (wr * pr - wi * pi).astype(jnp.bfloat16)
        left[rows, w:] = (wr * pi + wi * pr).astype(jnp.bfloat16)

    def dot(a, b):
        return jnp.dot(a, b, preferred_element_type=jnp.float32)

    stacked[:w, :] = dot(left[...], bx[:, :w]).astype(jnp.bfloat16)
    stacked[w:, :] = dot(left[...], bx[:, w:]).astype(jnp.bfloat16)
    live = (sc[LIVE] > 0).astype(jnp.float32)
    block = 128
    for first in range(0, w, block):
        rows = pl.ds(first, block)
        wave_r = dot(byt[rows, :], stacked[...])
        wave_i = dot(byt[pl.ds(w + first, block), :], stacked[...])
        power = jnp.maximum(wave_r * wave_r + wave_i * wave_i, FLOOR * FLOOR)
        keep = (1.0 - amp[rows, :] * lax.rsqrt(power)) * live
        left[rows, :w] = (wave_r * keep).astype(jnp.bfloat16)
        left[rows, w:] = (wave_i * keep).astype(jnp.bfloat16)
    stacked[:w, :] = dot(left[...], bxt[:, :w]).astype(jnp.bfloat16)
    stacked[w:, :] = dot(left[...], bxt[:, w:]).astype(jnp.bfloat16)
    for index, (first, size) in enumerate(firsts):
        rows = pl.ds(first, size)
        back_r = dot(by[rows, :], stacked[...])
        back_i = dot(by[pl.ds(w + first, size), :], stacked[...])
        pr, pi = pupil[0, rows, :], pupil[1, rows, :]
        grad_r = back_r * pr + back_i * pi
        grad_i = back_i * pr - back_r * pi
        if extra is not None:
            grad_r = grad_r + extra[index][0]
            grad_i = grad_i + extra[index][1]
        outs[index][0] = grad_r
        outs[index][1] = grad_i


def first_kernel(n, firsts, sc, tile, *refs):
    below, right = refs[:n], refs[n : 2 * n]
    pupil, amp, bx, bxt, by, byt = refs[2 * n : 2 * n + 6]
    outs, (kept, left, stacked) = refs[2 * n + 6 : 3 * n + 6], refs[3 * n + 6 :]

    def window(first, size):
        index = [f for f, _ in firsts].index(first)
        shape = (size, tile.shape[2])
        low = rows_of(shape, first) < sc[OY]
        far = cols_of(shape) < sc[OX]
        parts = []
        for part in range(2):
            near = jnp.where(low, below[index][part], tile[part, pl.ds(first, size), :])
            value = jnp.where(far, right[index][part], near)
            kept[part, pl.ds(first, size), :] = value
            parts.append(value)
        return parts

    gradient(sc, window, pupil, amp, bx, bxt, by, byt, outs, firsts, left, stacked, None)


def second_kernel(n, firsts, sc, kept, *refs):
    own, from_left, from_right, grads = (refs[k * n : (k + 1) * n] for k in range(4))
    pupil, amp, bx, bxt, by, byt = refs[4 * n : 4 * n + 6]
    outs, (left, stacked) = refs[4 * n + 6 : 5 * n + 6], refs[5 * n + 6 :]

    def window(first, size):
        index = [f for f, _ in firsts].index(first)
        shape = (size, kept.shape[2])
        rows, cols = rows_of(shape, first), cols_of(shape)
        far = cols < sc[OX]
        inside = (rows >= sc[EDGE_Y]) & (cols >= sc[EDGE_X])
        parts = []
        for part in range(2):
            near = jnp.where(far, from_right[index][part], from_left[index][part])
            value = kept[part, pl.ds(first, size), :] - STEP * (own[index][part] + near)
            parts.append(jnp.where(inside, value, 0.0))
        return parts

    gradient(sc, window, pupil, amp, bx, bxt, by, byt, outs, firsts, left, stacked, grads)


def compose_kernel(first, sc, tile, below, out):
    shape = tile.shape[1:]
    low = rows_of(shape, first) < sc[OYL]
    for part in range(2):
        out[part] = jnp.where(low, below[part], tile[part])


def between_kernel(first, sc, mine, above, below, to_left, to_right, own):
    shape = mine.shape[1:]
    i, j = rows_of(shape, first), cols_of(shape)
    low, low_a, low_b = i < sc[OY], i < sc[OYA], i < sc[OYB]
    far, far_a, far_b = j < sc[OX], j < sc[OXA], j < sc[OXB]
    low_l, low_r = i < sc[OYL], i < sc[OYR]
    zero = jnp.zeros(shape, jnp.float32)

    def seen(low_x):
        same = low == low_x
        return same, ~low_x & low_a, low_x & ~low_b

    left_m = [a & ~b for a, b in zip(seen(low_l), (far, far_a, far_b))]
    right_m = [a & b for a, b in zip(seen(low_r), (far, far_a, far_b))]
    _, own_a, own_b = seen(low)
    own_a, own_b = own_a & (far == far_a), own_b & (far == far_b)
    for part in range(2):
        values = (mine[part], above[part], below[part])
        for out, masks in ((to_left, left_m), (to_right, right_m)):
            terms = [jnp.where(m, v, zero) for m, v in zip(masks, values)]
            out[part] = terms[0] + terms[1] + terms[2]
        own[part] = values[0] + jnp.where(own_a, values[1], zero) + jnp.where(own_b, values[2], zero)


def final_kernel(first, sc, tile, mine, above, to_right, base):
    shape = mine.shape[1:]
    i, j = rows_of(shape, first), cols_of(shape)
    stay, come = i >= sc[OY], i < sc[OYA]
    far, far_a = j < sc[OX], j < sc[OXA]
    zero = jnp.zeros(shape, jnp.float32)
    for part in range(2):
        own = jnp.where(stay, mine[part], zero)
        other = jnp.where(come, above[part], zero)
        to_right[part] = jnp.where(far, own, zero) + jnp.where(far_a, other, zero)
        kept = jnp.where(far, zero, own) + jnp.where(far_a, zero, other)
        base[part] = tile[part] - STEP * kept


def on_device(spectrum, pupil, amplitudes, offsets, counts):
    w = pupil.shape[1]
    amp = amplitudes[0, 0, 0]
    f32 = jnp.float32
    spans, first = [], 0
    for size in CHUNKS:
        spans.append((first, size))
        first += size
    n = len(spans)
    piece = [jax.ShapeDtypeStruct((2, size, w), f32) for _, size in spans]
    whole = jax.ShapeDtypeStruct((2, w, w), f32)

    tiles = [spectrum[:, first : first + size] for first, size in spans]
    below = [shifted(t, "row", -1) for t in tiles]
    place = offsets[0, 0]
    from_left = shifted(place, "col", 1)
    from_right = shifted(place, "col", -1)
    from_above = shifted(place, "row", 1)
    from_below = shifted(place, "row", -1)
    last_row = lax.axis_index("row") == lax.axis_size("row") - 1
    last_col = lax.axis_index("col") == lax.axis_size("col") - 1
    sc = jnp.stack(
        [
            place[0, 0],
            place[0, 1],
            from_above[0, 0],
            from_above[0, 1],
            from_below[0, 0],
            from_below[0, 1],
            from_left[0, 0],
            from_right[0, 0],
            jnp.where(last_row, place[0, 0], 0),
            jnp.where(last_col, place[0, 1], 0),
            counts[0, 0],
        ]
    ).astype(jnp.int32)
    cosine, sine = dft_tables(w)
    table = jax.ShapeDtypeStruct((2 * w, 2 * w), jnp.bfloat16)
    *tables, rolled = call(
        prepare_kernel, [table, table, table, table, whole], (cosine, sine, pupil), sc
    )

    composed = [
        call(functools.partial(compose_kernel, spans[k][0]), piece[k], (tiles[k], below[k]), sc)
        for k in range(n)
    ]
    right = [shifted(c, "col", -1) for c in composed]
    scratch = [pltpu.VMEM((w, 2 * w), jnp.bfloat16), pltpu.VMEM((2 * w, w), jnp.bfloat16)]
    *grads, kept = call(
        functools.partial(first_kernel, n, spans),
        piece + [whole],
        (spectrum, *below, *right, rolled, amp, *tables),
        sc,
        scratch,
    )

    above = [shifted(g, "row", 1) for g in grads]
    under = [shifted(g, "row", -1) for g in grads]
    mixed = [
        call(
            functools.partial(between_kernel, spans[k][0]),
            [piece[k]] * 3,
            (grads[k], above[k], under[k]),
            sc,
        )
        for k in range(n)
    ]
    got_right = [shifted(m[0], "col", -1) for m in mixed]
    got_left = [shifted(m[1], "col", 1) for m in mixed]
    sums = call(
        functools.partial(second_kernel, n, spans),
        piece,
        (kept, *[m[2] for m in mixed], *got_left, *got_right, *grads, rolled, amp, *tables),
        sc,
        scratch,
    )

    above = [shifted(s, "row", 1) for s in sums]
    done = [
        call(
            functools.partial(final_kernel, spans[k][0]),
            [piece[k]] * 2,
            (tiles[k], sums[k], above[k]),
            sc,
        )
        for k in range(n)
    ]
    got = [shifted(d[0], "col", 1) for d in done]
    return jnp.concatenate([d[1] - STEP * g for d, g in zip(done, got)], axis=1)


def solution(mesh):
    in_specs = (
        P(None, "row", "col"),
        P(),
        P("row", "col", None, None, None),
        P("row", "col", None, None),
        P("row", "col"),
    )
    out_specs = P(None, "row", "col")
    return jax.shard_map(
        on_device, mesh=mesh, in_specs=in_specs, out_specs=out_specs, check_vma=False
    )
```

time: 641 us -> 268 us (0.42)
  waiting for transfers between devices: 362 us -> 104 us
  matrix products: 162 us -> 0 us
  starting transfers between devices: 24.1 us -> 100 us
  Pallas kernels: 0 us -> 42.6 us
  local copies, waits for them, and re-layouts: 51.2 us -> 11.7 us
  other arithmetic: 27.8 us -> 6.26 us
    ppermute x8 -> x36, waiting for transfers between devices: 362 us -> 104 us  [shifted(): lax.ppermute(value, axis, [(source, source + steps) for source in range(l...]
    dot_general x32 -> x0, matrix products: 162 us -> none  [the longest x16 81 us: right(): return jnp.einsum('swk,kj->swj', a, b, preferred_element_type=jnp.float32)]
    ppermute x8 -> x36, starting transfers between devices: 24.1 us -> 100 us  [shifted(): lax.ppermute(value, axis, [(source, source + steps) for source in range(l...]
    pallas_call x0 -> x15, Pallas kernels: none -> 42.6 us  [call(): pl.pallas_call(kernel, out_shape=outs, in_specs=[SMEM] + [VMEM] * len(arr...]
    dynamic_update_slice x2 -> x0, local copies, waits for them, and re-layouts: 30 us -> none  [add_piece(): return lax.dynamic_update_slice(region, current + piece, start)]
    add x4 -> x0, other arithmetic: 9.54 us -> none  [the longest x2 7.51 us: add_piece(): return lax.dynamic_update_slice(region, current + piece, start)]
  transfers between devices with their start and end apart: 8 -> 36, of which waited for: 8 -> 18; matrix products, arithmetic and copies ran while one was open for 1% -> 4% of each run, Pallas kernels for 0% -> 7%
where the time goes in v1:
time: 268 us; the launch traced here: 267 us
  waiting for transfers between devices  104 us (39%)
  starting transfers between devices  100 us (37%)
  Pallas kernels  42.6 us (16%)
  local copies, waits for them, and re-layouts  11.7 us (4%)
  other arithmetic  6.26 us (2%)
    ppermute x36, waiting for transfers between devices, shifted(): lax.ppermute(value, axis, [(source, source + steps) for source in range(l...  104 us
    ppermute x36, starting transfers between devices, shifted(): lax.ppermute(value, axis, [(source, source + steps) for source in range(l...  100 us
    pallas_call x15, Pallas kernels, call(): pl.pallas_call(kernel, out_shape=outs, in_specs=[SMEM] + [VMEM] * len(arr...  42.6 us
  transfers between devices with their start and end apart: 36, of which 18 were waited for; matrix products, arithmetic and copies ran while one was open for 4% of the time, Pallas kernels for 7%

profile of v1, /device:TPU:28, one launch (start us, length us, event | category | flops | bytes accessed | tf_op | source)
XLA Modules:
  0.0 266.8 jit_solution(4155907433249226907)
XLA Ops:
  1.8 6.1 %collective-permute-start.6 = (f32[2,128,512]{2,1,0:T(8,128)S(1)}, f32[2,128,512]{2,1,0:T(8,128)S(1)}, u32[]{:S(2)}, u32[]{:S(2)}) collective-permute-start(f32[2,128,512]{2,1,0:T(8,128)S(1)} %get-tuple-element.73.tile), channel_id=1, source_target_pairs={{8,0},{16,8},{24,16},{32,24},{40,32},{48,40},{56,48},{64,56},{72,6... | collective-permute-start | bytes 1572872 | tf_op jit(solution)/shard_map/ppermute | solution.py:24
  8.0 2.3 collective-permute-start.5
  10.3 2.0 collective-permute-start.4
  12.3 2.0 collective-permute-start.7
  14.3 5.8 %collective-permute-start.1 = (s32[1,2]{1,0:T(1,128)S(1)}, s32[1,2]{1,0:T(1,128)S(1)}, u32[]{:S(2)}, u32[]{:S(2)}) collective-permute-start(s32[1,2]{1,0:T(1,128)S(1)} %bitcast.20), channel_id=1, source_target_pairs={{8,0},{16,8},{24,16},{32,24},{40,32},{48,40},{56,48},{64,56},{72,6... | collective-permute-start | bytes 32 | tf_op jit(solution)/shard_map/ppermute | solution.py:24
  22.6 30.2 %collective-permute-done.1 = s32[1,2]{1,0:T(1,128)S(1)} collective-permute-done((s32[1,2]{1,0:T(1,128)S(1)}, s32[1,2]{1,0:T(1,128)S(1)}, u32[]{:S(2)}, u32[]{:S(2)}) %collective-permute-start.1) | collective-permute-done | bytes 40 | tf_op jit(solution)/shard_map/ppermute | solution.py:24
  52.9 2.3 collective-permute-start
  55.8 5.1 %collective-permute-done = s32[1,2]{1,0:T(1,128)S(1)} collective-permute-done((s32[1,2]{1,0:T(1,128)S(1)}, s32[1,2]{1,0:T(1,128)S(1)}, u32[]{:S(2)}, u32[]{:S(2)}) %collective-permute-start) | collective-permute-done | bytes 40 | tf_op jit(solution)/shard_map/ppermute | solution.py:24
  63.5 2.3 collective-permute-done.2
  69.0 3.8 %stack.11.sc = s32[11]{0:T(128)S(1)} concatenate(s32[1]{0:T(128)} %bitcast.1, s32[1]{0:T(128)} %bitcast.2, s32[1]{0:T(128)} %bitcast.3, s32[1]{0:T(128)} %bitcast.4, s32[1]{0:T(128)} %bitcast.5, s32[1]{0:T(128)} %bitcast.6, s32[1]{0:T(128)S(1)} %bitcast.25, s32[1]{0:T(128)S(1)} %bitcast.26, s32[1]{0:T(128)} %bitcast.10, s32[1]{0:T(128)} %bitcast.12, s32[1]{0:T(128)} %bitcast.17), dimensions={0} | concatenate | bytes 88 | tf_op jit(solution)/shard_map/stack | solution.py:221
  73.4 3.6 %collective-permute-start.10 = (f32[2,128,512]{2,1,0:T(8,128)S(1)}, f32[2,128,512]{2,1,0:T(8,128)S(1)}, u32[]{:S(2)}, u32[]{:S(2)}) collective-permute-start(f32[2,128,512]{2,1,0:T(8,128)S(1)} %shard_map.57), channel_id=1, source_target_pairs={{1,0},{2,1},{3,2},{4,3},{5,4},{6,5},{7,6},{9,8},{10,9},{11,10},{12... | collective-permute-start | bytes 1572872 | tf_op jit(solution)/shard_map/ppermute | solution.py:24
  77.6 1.9 collective-permute-start.9
  80.6 2.5 collective-permute-start.8
  84.3 1.9 collective-permute-start.11
  86.2 4.4 %multiply_convert_fusion = (bf16[512,512]{1,0:T(8,128)(2,1)S(1)}, bf16[512,512]{1,0:T(8,128)(2,1)S(1)}) fusion(), kind=kLoop, calls=%fused_computation.7 | loop fusion | flops 4718592 | bytes 1048576 | tf_op jit(solution)/shard_map/convert_element_type | solution.py:34
  90.6 7.4 %shard_map.59 = (bf16[1024,1024]{1,0:T(8,128)(2,1)S(1)}, bf16[1024,1024]{1,0:T(8,128)(2,1)S(1)}, bf16[1024,1024]{1,0:T(8,128)(2,1)}, bf16[1024,1024]{1,0:T(8,128)(2,1)}, f32[2,512,512]{2,1,0:T(8,128)}) custom-call(s32[11]{0:T(128)S(1)} %stack.11.sc, bf16[512,512]{1,0:T(8,128)(2,1)S(1)} %get-tuple-element.84.cos_ref, ...), custom_call_target="tpu_custom_call" | custom-call | tf_op jit(solution)/shard_map/pallas_call | solution.py:39
  101.7 11.8 %shard_map.60 = (f32[2,128,512]{2,1,0:T(8,128)S(1)}, f32[2,128,512]{2,1,0:T(8,128)S(1)}, f32[2,128,512]{2,1,0:T(8,128)S(1)}, f32[2,128,512]{2,1,0:T(8,128)S(1)}, f32[2,512,512]{2,1,0:T(8,128)}) custom-call(s32[11]{0:T(128)S(1)} %stack.11.sc, f32[2,512,512]{2,1,0:T(8,128)} %tile.1, f32[2,128,512]{2,1,0:T(8,128)} %collective-permute-done.4.below.refs_0_, ...), custom_call_target="tpu_custom_call" | custom-call | tf_op jit(solution)/shard_map/pallas_call | solution.py:39
  113.5 3.9 %collective-permute-start.13 = (f32[2,128,512]{2,1,0:T(8,128)S(1)}, f32[2,128,512]{2,1,0:T(8,128)S(1)}, u32[]{:S(2)}, u32[]{:S(2)}) collective-permute-start(f32[2,128,512]{2,1,0:T(8,128)S(1)} %get-tuple-element.45.mine.refs_12_), channel_id=1, source_target_pairs={{8,0},{16,8},{24,16},{32,24},{40,32},{48,40},{56,48},{64,56},{72,6... | collective-permute-start | bytes 1572872 | tf_op jit(solution)/shard_map/ppermute | solution.py:24
  117.4 1.9 collective-permute-start.12
  119.4 6.0 %collective-permute-start.15 = (f32[2,128,512]{2,1,0:T(8,128)S(1)}, f32[2,128,512]{2,1,0:T(8,128)S(1)}, u32[]{:S(2)}, u32[]{:S(2)}) collective-permute-start(f32[2,128,512]{2,1,0:T(8,128)S(1)} %get-tuple-element.47.mine.refs_13_), channel_id=1, source_target_pairs={{8,0},{16,8},{24,16},{32,24},{40,32},{48,40},{56,48},{64,56},{72,6... | collective-permute-start | bytes 1572872 | tf_op jit(solution)/shard_map/ppermute | solution.py:24
  125.4 2.1 collective-permute-start.14
  127.5 6.0 %collective-permute-start.17 = (f32[2,128,512]{2,1,0:T(8,128)S(1)}, f32[2,128,512]{2,1,0:T(8,128)S(1)}, u32[]{:S(2)}, u32[]{:S(2)}) collective-permute-start(f32[2,128,512]{2,1,0:T(8,128)S(1)} %get-tuple-element.49.mine.refs_14_), channel_id=1, source_target_pairs={{8,0},{16,8},{24,16},{32,24},{40,32},{48,40},{56,48},{64,56},{72,6... | collective-permute-start | bytes 1572872 | tf_op jit(solution)/shard_map/ppermute | solution.py:24
  133.6 1.9 collective-permute-start.16
  136.2 5.3 %collective-permute-start.19 = (f32[2,128,512]{2,1,0:T(8,128)S(1)}, f32[2,128,512]{2,1,0:T(8,128)S(1)}, u32[]{:S(2)}, u32[]{:S(2)}) collective-permute-start(f32[2,128,512]{2,1,0:T(8,128)S(1)} %get-tuple-element.51.mine.refs_15_), channel_id=1, source_target_pairs={{8,0},{16,8},{24,16},{32,24},{40,32},{48,40},{56,48},{64,56},{72,6... | collective-permute-start | bytes 1572872 | tf_op jit(solution)/shard_map/ppermute | solution.py:24
  142.8 1.9 collective-permute-start.18
  144.7 2.7 %collective-permute-done.14.above = f32[2,128,512]{2,1,0:T(8,128)S(1)} collective-permute-done((f32[2,128,512]{2,1,0:T(8,128)S(1)}, f32[2,128,512]{2,1,0:T(8,128)S(1)}, u32[]{:S(2)}, u32[]{:S(2)}) %collective-permute-start.14) | collective-permute-done | bytes 524320 | tf_op jit(solution)/shard_map/ppermute | solution.py:24
  152.5 2.7 %collective-permute-start.24 = (f32[2,128,512]{2,1,0:T(8,128)S(1)}, f32[2,128,512]{2,1,0:T(8,128)S(1)}, u32[]{:S(2)}, u32[]{:S(2)}) collective-permute-start(f32[2,128,512]{2,1,0:T(8,128)S(1)} %get-tuple-element.57), channel_id=1, source_target_pairs={{1,0},{2,1},{3,2},{4,3},{5,4},{6,5},{7,6},{9,8},{10,9},{11,10},{12... | collective-permute-start | bytes 1572872 | tf_op jit(solution)/shard_map/ppermute | solution.py:24
  155.2 3.5 %collective-permute-done.16.above = f32[2,128,512]{2,1,0:T(8,128)S(1)} collective-permute-done((f32[2,128,512]{2,1,0:T(8,128)S(1)}, f32[2,128,512]{2,1,0:T(8,128)S(1)}, u32[]{:S(2)}, u32[]{:S(2)}) %collective-permute-start.16) | collective-permute-done | bytes 524320 | tf_op jit(solution)/shard_map/ppermute | solution.py:24
  163.8 2.0 collective-permute-start.25
  165.7 4.1 %collective-permute-done.18.above = f32[2,128,512]{2,1,0:T(8,128)S(1)} collective-permute-done((f32[2,128,512]{2,1,0:T(8,128)S(1)}, f32[2,128,512]{2,1,0:T(8,128)S(1)}, u32[]{:S(2)}, u32[]{:S(2)}) %collective-permute-start.18) | collective-permute-done | bytes 524320 | tf_op jit(solution)/shard_map/ppermute | solution.py:24
  173.0 3.6 %collective-permute-start.26 = (f32[2,128,512]{2,1,0:T(8,128)S(1)}, f32[2,128,512]{2,1,0:T(8,128)S(1)}, u32[]{:S(2)}, u32[]{:S(2)}) collective-permute-start(f32[2,128,512]{2,1,0:T(8,128)S(1)} %get-tuple-element.59), channel_id=1, source_target_pairs={{1,0},{2,1},{3,2},{4,3},{5,4},{6,5},{7,6},{9,8},{10,9},{11,10},{12... | collective-permute-start | bytes 1572872 | tf_op jit(solution)/shard_map/ppermute | solution.py:24
  176.7 1.9 collective-permute-start.23
  178.6 3.6 %collective-permute-start.27 = (f32[2,128,512]{2,1,0:T(8,128)S(1)}, f32[2,128,512]{2,1,0:T(8,128)S(1)}, u32[]{:S(2)}, u32[]{:S(2)}) collective-permute-start(f32[2,128,512]{2,1,0:T(8,128)S(1)} %get-tuple-element.60), channel_id=1, source_target_pairs={{1,0},{2,1},{3,2},{4,3},{5,4},{6,5},{7,6},{9,8},{10,9},{11,10},{12... | collective-permute-start | bytes 1572872 | tf_op jit(solution)/shard_map/ppermute | solution.py:24
  183.4 3.8 %collective-permute-done.23.refs_7_ = f32[2,128,512]{2,1,0:T(8,128)S(1)} collective-permute-done((f32[2,128,512]{2,1,0:T(8,128)S(1)}, f32[2,128,512]{2,1,0:T(8,128)S(1)}, u32[]{:S(2)}, u32[]{:S(2)}) %collective-permute-start.23) | collective-permute-done | bytes 524320 | tf_op jit(solution)/shard_map/ppermute | solution.py:24
  189.8 11.9 %shard_map.65 = (f32[2,128,512]{2,1,0:T(8,128)S(1)}, f32[2,128,512]{2,1,0:T(8,128)S(1)}, f32[2,128,512]{2,1,0:T(8,128)S(1)}, f32[2,128,512]{2,1,0:T(8,128)S(1)}) custom-call(s32[11]{0:T(128)S(1)} %stack.11.sc, f32[2,512,512]{2,1,0:T(8,128)} %get-tuple-element.44.kept, f32[2,128,512]{2,1,0:T(8,128)S(1)} %get-tuple-element.46.refs_0_, ...), custom_call_target="tpu_custom_call" | custom-call | tf_op jit(solution)/shard_map/pallas_call | solution.py:39
  201.7 1.9 collective-permute-start.28
  203.6 1.9 collective-permute-start.30
  205.5 1.9 collective-permute-start.32
  207.5 1.9 collective-permute-start.34
  209.4 10.9 %collective-permute-done.28.above = f32[2,128,512]{2,1,0:T(8,128)S(1)} collective-permute-done((f32[2,128,512]{2,1,0:T(8,128)S(1)}, f32[2,128,512]{2,1,0:T(8,128)S(1)}, u32[]{:S(2)}, u32[]{:S(2)}) %collective-permute-start.28) | collective-permute-done | bytes 524320 | tf_op jit(solution)/shard_map/ppermute | solution.py:24
  221.0 2.4 collective-permute-start.29
  223.5 8.0 %collective-permute-done.30.above = f32[2,128,512]{2,1,0:T(8,128)S(1)} collective-permute-done((f32[2,128,512]{2,1,0:T(8,128)S(1)}, f32[2,128,512]{2,1,0:T(8,128)S(1)}, u32[]{:S(2)}, u32[]{:S(2)}) %collective-permute-start.30) | collective-permute-done | bytes 524320 | tf_op jit(solution)/shard_map/ppermute | solution.py:24
  232.3 2.4 collective-permute-start.31
  234.7 8.0 %collective-permute-done.32.above = f32[2,128,512]{2,1,0:T(8,128)S(1)} collective-permute-done((f32[2,128,512]{2,1,0:T(8,128)S(1)}, f32[2,128,512]{2,1,0:T(8,128)S(1)}, u32[]{:S(2)}, u32[]{:S(2)}) %collective-permute-start.32) | collective-permute-done | bytes 524320 | tf_op jit(solution)/shard_map/ppermute | solution.py:24
  243.5 2.4 collective-permute-start.33
  245.9 8.0 %collective-permute-done.34.above = f32[2,128,512]{2,1,0:T(8,128)S(1)} collective-permute-done((f32[2,128,512]{2,1,0:T(8,128)S(1)}, f32[2,128,512]{2,1,0:T(8,128)S(1)}, u32[]{:S(2)}, u32[]{:S(2)}) %collective-permute-start.34) | collective-permute-done | bytes 524320 | tf_op jit(solution)/shard_map/ppermute | solution.py:24
  254.8 2.0 collective-permute-start.35
  257.1 8.1 %collective-permute-done.35 = f32[2,128,512]{2,1,0:T(8,128)S(1)} collective-permute-done((f32[2,128,512]{2,1,0:T(8,128)S(1)}, f32[2,128,512]{2,1,0:T(8,128)S(1)}, u32[]{:S(2)}, u32[]{:S(2)}) %collective-permute-start.35) | collective-permute-done | bytes 524320 | tf_op jit(solution)/shard_map/ppermute | solution.py:24
  (76 shorter events, 39.4 us)
Async XLA Ops:
  0.0 14.3 %copy-start.12 = (s32[1,1,1,2]{3,2,1,0:T(1,128)S(1)}, s32[1,1,1,2]{3,2,1,0:T(1,128)}, u32[]{:S(2)}) copy-start(s32[1,1,1,2]{3,2,1,0:T(1,128)} %param.8) | copy-start | bytes 28
  1.8 71.0 %collective-permute-start.6 = (f32[2,128,512]{2,1,0:T(8,128)S(1)}, f32[2,128,512]{2,1,0:T(8,128)S(1)}, u32[]{:S(2)}, u32[]{:S(2)}) collective-permute-start(f32[2,128,512]{2,1,0:T(8,128)S(1)} %get-tuple-element.73.tile), channel_id=1, source_target_pairs={{8,0},{16,8},{24,16},{32,24},{40,32},{48,40},{56,48},{64,56},{72,6... | collective-permute-start | bytes 1572872 | tf_op jit(solution)/shard_map/ppermute | solution.py:24
  8.0 69.0 %collective-permute-start.5 = (f32[2,128,512]{2,1,0:T(8,128)S(1)}, f32[2,128,512]{2,1,0:T(8,128)S(1)}, u32[]{:S(2)}, u32[]{:S(2)}) collective-permute-start(f32[2,128,512]{2,1,0:T(8,128)S(1)} %get-tuple-element.74.tile), channel_id=1, source_target_pairs={{8,0},{16,8},{24,16},{32,24},{40,32},{48,40},{56,48},{64,56},{72,6... | collective-permute-start | bytes 1572872 | tf_op jit(solution)/shard_map/ppermute | solution.py:24
  10.3 69.2 %collective-permute-start.4 = (f32[2,128,512]{2,1,0:T(8,128)S(1)}, f32[2,128,512]{2,1,0:T(8,128)}, u32[]{:S(2)}, u32[]{:S(2)}) collective-permute-start(f32[2,128,512]{2,1,0:T(8,128)S(1)} %get-tuple-element.75.tile), channel_id=1, source_target_pairs={{8,0},{16,8},{24,16},{32,24},{40,32},{48,40},{56,48},{64,56},{72,6... | collective-permute-start | bytes 1572872 | tf_op jit(solution)/shard_map/ppermute | solution.py:24
  12.3 70.9 %collective-permute-start.7 = (f32[2,128,512]{2,1,0:T(8,128)S(1)}, f32[2,128,512]{2,1,0:T(8,128)}, u32[]{:S(2)}, u32[]{:S(2)}) collective-permute-start(f32[2,128,512]{2,1,0:T(8,128)S(1)} %get-tuple-element.76.tile), channel_id=1, source_target_pairs={{8,0},{16,8},{24,16},{32,24},{40,32},{48,40},{56,48},{64,56},{72,6... | collective-permute-start | bytes 1572872 | tf_op jit(solution)/shard_map/ppermute | solution.py:24
  14.3 38.5 %collective-permute-start.1 = (s32[1,2]{1,0:T(1,128)S(1)}, s32[1,2]{1,0:T(1,128)S(1)}, u32[]{:S(2)}, u32[]{:S(2)}) collective-permute-start(s32[1,2]{1,0:T(1,128)S(1)} %bitcast.20), channel_id=1, source_target_pairs={{8,0},{16,8},{24,16},{32,24},{40,32},{48,40},{56,48},{64,56},{72,6... | collective-permute-start | bytes 32 | tf_op jit(solution)/shard_map/ppermute | solution.py:24
  52.9 8.1 %collective-permute-start = (s32[1,2]{1,0:T(1,128)S(1)}, s32[1,2]{1,0:T(1,128)S(1)}, u32[]{:S(2)}, u32[]{:S(2)}) collective-permute-start(s32[1,2]{1,0:T(1,128)S(1)} %bitcast.22), channel_id=1, source_target_pairs={{0,8},{8,16},{16,24},{24,32},{32,40},{40,48},{48,56},{56,64},{64,7... | collective-permute-start | bytes 32 | tf_op jit(solution)/shard_map/ppermute | solution.py:24
  60.9 4.8 %collective-permute-start.2 = (s32[1,2]{1,0:T(1,128)S(1)}, s32[1,2]{1,0:T(1,128)S(1)}, u32[]{:S(2)}, u32[]{:S(2)}) collective-permute-start(s32[1,2]{1,0:T(1,128)S(1)} %bitcast.23), channel_id=1, source_target_pairs={{0,1},{1,2},{2,3},{3,4},{4,5},{5,6},{6,7},{8,9},{9,10},{10,11},{11... | collective-permute-start | bytes 32 | tf_op jit(solution)/shard_map/ppermute | solution.py:24
  65.8 3.2 %collective-permute-start.3 = (s32[1,2]{1,0:T(1,128)S(1)}, s32[1,2]{1,0:T(1,128)S(1)}, u32[]{:S(2)}, u32[]{:S(2)}) collective-permute-start(s32[1,2]{1,0:T(1,128)S(1)} %bitcast.24), channel_id=1, source_target_pairs={{1,0},{2,1},{3,2},{4,3},{5,4},{6,5},{7,6},{9,8},{10,9},{11,10},{12... | collective-permute-start | bytes 32 | tf_op jit(solution)/shard_map/ppermute | solution.py:24
  73.4 27.4 %collective-permute-start.10 = (f32[2,128,512]{2,1,0:T(8,128)S(1)}, f32[2,128,512]{2,1,0:T(8,128)S(1)}, u32[]{:S(2)}, u32[]{:S(2)}) collective-permute-start(f32[2,128,512]{2,1,0:T(8,128)S(1)} %shard_map.57), channel_id=1, source_target_pairs={{1,0},{2,1},{3,2},{4,3},{5,4},{6,5},{7,6},{9,8},{10,9},{11,10},{12... | collective-permute-start | bytes 1572872 | tf_op jit(solution)/shard_map/ppermute | solution.py:24
  77.6 23.2 %collective-permute-start.9 = (f32[2,128,512]{2,1,0:T(8,128)S(1)}, f32[2,128,512]{2,1,0:T(8,128)S(1)}, u32[]{:S(2)}, u32[]{:S(2)}) collective-permute-start(f32[2,128,512]{2,1,0:T(8,128)S(1)} %shard_map.56), channel_id=1, source_target_pairs={{1,0},{2,1},{3,2},{4,3},{5,4},{6,5},{7,6},{9,8},{10,9},{11,10},{12... | collective-permute-start | bytes 1572872 | tf_op jit(solution)/shard_map/ppermute | solution.py:24
  80.6 20.2 %collective-permute-start.8 = (f32[2,128,512]{2,1,0:T(8,128)S(1)}, f32[2,128,512]{2,1,0:T(8,128)S(1)}, u32[]{:S(2)}, u32[]{:S(2)}) collective-permute-start(f32[2,128,512]{2,1,0:T(8,128)S(1)} %shard_map.55), channel_id=1, source_target_pairs={{1,0},{2,1},{3,2},{4,3},{5,4},{6,5},{7,6},{9,8},{10,9},{11,10},{12... | collective-permute-start | bytes 1572872 | tf_op jit(solution)/shard_map/ppermute | solution.py:24
  84.3 16.5 %collective-permute-start.11 = (f32[2,128,512]{2,1,0:T(8,128)S(1)}, f32[2,128,512]{2,1,0:T(8,128)S(1)}, u32[]{:S(2)}, u32[]{:S(2)}) collective-permute-start(f32[2,128,512]{2,1,0:T(8,128)S(1)} %shard_map.58), channel_id=1, source_target_pairs={{1,0},{2,1},{3,2},{4,3},{5,4},{6,5},{7,6},{9,8},{10,9},{11,10},{12... | collective-permute-start | bytes 1572872 | tf_op jit(solution)/shard_map/ppermute | solution.py:24
  98.1 1.4 copy-start
  99.4 1.4 copy-start.1
  100.8 0.8 copy-start.11
  113.5 48.4 %copy-start.2 = (f32[2,128,512]{2,1,0:T(8,128)}, f32[2,128,512]{2,1,0:T(8,128)S(1)}, u32[]{:S(2)}) copy-start(f32[2,128,512]{2,1,0:T(8,128)S(1)} %get-tuple-element.45.mine.refs_12_) | copy-start | bytes 1572868
  113.5 48.4 %copy-start.3 = (f32[2,128,512]{2,1,0:T(8,128)}, f32[2,128,512]{2,1,0:T(8,128)S(1)}, u32[]{:S(2)}) copy-start(f32[2,128,512]{2,1,0:T(8,128)S(1)} %get-tuple-element.47.mine.refs_13_) | copy-start | bytes 1572868
  113.5 48.4 %copy-start.4 = (f32[2,128,512]{2,1,0:T(8,128)}, f32[2,128,512]{2,1,0:T(8,128)S(1)}, u32[]{:S(2)}) copy-start(f32[2,128,512]{2,1,0:T(8,128)S(1)} %get-tuple-element.49.mine.refs_14_) | copy-start | bytes 1572868
  113.5 58.2 %copy-start.5 = (f32[2,128,512]{2,1,0:T(8,128)}, f32[2,128,512]{2,1,0:T(8,128)S(1)}, u32[]{:S(2)}) copy-start(f32[2,128,512]{2,1,0:T(8,128)S(1)} %get-tuple-element.51.mine.refs_15_) | copy-start | bytes 1572868
  113.5 20.0 %collective-permute-start.13 = (f32[2,128,512]{2,1,0:T(8,128)S(1)}, f32[2,128,512]{2,1,0:T(8,128)S(1)}, u32[]{:S(2)}, u32[]{:S(2)}) collective-permute-start(f32[2,128,512]{2,1,0:T(8,128)S(1)} %get-tuple-element.45.mine.refs_12_), channel_id=1, source_target_pairs={{8,0},{16,8},{24,16},{32,24},{40,32},{48,40},{56,48},{64,56},{72,6... | collective-permute-start | bytes 1572872 | tf_op jit(solution)/shard_map/ppermute | solution.py:24
  117.4 18.8 %collective-permute-start.12 = (f32[2,128,512]{2,1,0:T(8,128)S(1)}, f32[2,128,512]{2,1,0:T(8,128)S(1)}, u32[]{:S(2)}, u32[]{:S(2)}) collective-permute-start(f32[2,128,512]{2,1,0:T(8,128)S(1)} %get-tuple-element.45.mine.refs_12_), channel_id=1, source_target_pairs={{0,8},{8,16},{16,24},{24,32},{32,40},{40,48},{48,56},{56,64},{64,7... | collective-permute-start | bytes 1572872 | tf_op jit(solution)/shard_map/ppermute | solution.py:24
  119.4 23.4 %collective-permute-start.15 = (f32[2,128,512]{2,1,0:T(8,128)S(1)}, f32[2,128,512]{2,1,0:T(8,128)S(1)}, u32[]{:S(2)}, u32[]{:S(2)}) collective-permute-start(f32[2,128,512]{2,1,0:T(8,128)S(1)} %get-tuple-element.47.mine.refs_13_), channel_id=1, source_target_pairs={{8,0},{16,8},{24,16},{32,24},{40,32},{48,40},{56,48},{64,56},{72,6... | collective-permute-start | bytes 1572872 | tf_op jit(solution)/shard_map/ppermute | solution.py:24
  125.4 22.1 %collective-permute-start.14 = (f32[2,128,512]{2,1,0:T(8,128)S(1)}, f32[2,128,512]{2,1,0:T(8,128)S(1)}, u32[]{:S(2)}, u32[]{:S(2)}) collective-permute-start(f32[2,128,512]{2,1,0:T(8,128)S(1)} %get-tuple-element.47.mine.refs_13_), channel_id=1, source_target_pairs={{0,8},{8,16},{16,24},{24,32},{32,40},{40,48},{48,56},{56,64},{64,7... | collective-permute-start | bytes 1572872 | tf_op jit(solution)/shard_map/ppermute | solution.py:24
  127.5 25.0 %collective-permute-start.17 = (f32[2,128,512]{2,1,0:T(8,128)S(1)}, f32[2,128,512]{2,1,0:T(8,128)S(1)}, u32[]{:S(2)}, u32[]{:S(2)}) collective-permute-start(f32[2,128,512]{2,1,0:T(8,128)S(1)} %get-tuple-element.49.mine.refs_14_), channel_id=1, source_target_pairs={{8,0},{16,8},{24,16},{32,24},{40,32},{48,40},{56,48},{64,56},{72,6... | collective-permute-start | bytes 1572872 | tf_op jit(solution)/shard_map/ppermute | solution.py:24
  133.6 25.1 %collective-permute-start.16 = (f32[2,128,512]{2,1,0:T(8,128)S(1)}, f32[2,128,512]{2,1,0:T(8,128)S(1)}, u32[]{:S(2)}, u32[]{:S(2)}) collective-permute-start(f32[2,128,512]{2,1,0:T(8,128)S(1)} %get-tuple-element.49.mine.refs_14_), channel_id=1, source_target_pairs={{0,8},{8,16},{16,24},{24,32},{32,40},{40,48},{48,56},{56,64},{64,7... | collective-permute-start | bytes 1572872 | tf_op jit(solution)/shard_map/ppermute | solution.py:24
  136.2 27.5 %collective-permute-start.19 = (f32[2,128,512]{2,1,0:T(8,128)S(1)}, f32[2,128,512]{2,1,0:T(8,128)S(1)}, u32[]{:S(2)}, u32[]{:S(2)}) collective-permute-start(f32[2,128,512]{2,1,0:T(8,128)S(1)} %get-tuple-element.51.mine.refs_15_), channel_id=1, source_target_pairs={{8,0},{16,8},{24,16},{32,24},{40,32},{48,40},{56,48},{64,56},{72,6... | collective-permute-start | bytes 1572872 | tf_op jit(solution)/shard_map/ppermute | solution.py:24
  142.8 27.0 %collective-permute-start.18 = (f32[2,128,512]{2,1,0:T(8,128)S(1)}, f32[2,128,512]{2,1,0:T(8,128)S(1)}, u32[]{:S(2)}, u32[]{:S(2)}) collective-permute-start(f32[2,128,512]{2,1,0:T(8,128)S(1)} %get-tuple-element.51.mine.refs_15_), channel_id=1, source_target_pairs={{0,8},{8,16},{16,24},{24,32},{32,40},{40,48},{48,56},{56,64},{64,7... | collective-permute-start | bytes 1572872 | tf_op jit(solution)/shard_map/ppermute | solution.py:24
  147.5 25.5 %collective-permute-start.20 = (f32[2,128,512]{2,1,0:T(8,128)S(1)}, f32[2,128,512]{2,1,0:T(8,128)S(1)}, u32[]{:S(2)}, u32[]{:S(2)}) collective-permute-start(f32[2,128,512]{2,1,0:T(8,128)S(1)} %get-tuple-element.53), channel_id=1, source_target_pairs={{0,1},{1,2},{2,3},{3,4},{4,5},{5,6},{6,7},{8,9},{9,10},{10,11},{11... | collective-permute-start | bytes 1572872 | tf_op jit(solution)/shard_map/ppermute | solution.py:24
  152.5 24.2 %collective-permute-start.24 = (f32[2,128,512]{2,1,0:T(8,128)S(1)}, f32[2,128,512]{2,1,0:T(8,128)S(1)}, u32[]{:S(2)}, u32[]{:S(2)}) collective-permute-start(f32[2,128,512]{2,1,0:T(8,128)S(1)} %get-tuple-element.57), channel_id=1, source_target_pairs={{1,0},{2,1},{3,2},{4,3},{5,4},{6,5},{7,6},{9,8},{10,9},{11,10},{12... | collective-permute-start | bytes 1572872 | tf_op jit(solution)/shard_map/ppermute | solution.py:24
  158.7 19.9 %collective-permute-start.21 = (f32[2,128,512]{2,1,0:T(8,128)S(1)}, f32[2,128,512]{2,1,0:T(8,128)S(1)}, u32[]{:S(2)}, u32[]{:S(2)}) collective-permute-start(f32[2,128,512]{2,1,0:T(8,128)S(1)} %get-tuple-element.54), channel_id=1, source_target_pairs={{0,1},{1,2},{2,3},{3,4},{4,5},{5,6},{6,7},{8,9},{9,10},{10,11},{11... | collective-permute-start | bytes 1572872 | tf_op jit(solution)/shard_map/ppermute | solution.py:24
  163.8 18.5 %collective-permute-start.25 = (f32[2,128,512]{2,1,0:T(8,128)S(1)}, f32[2,128,512]{2,1,0:T(8,128)S(1)}, u32[]{:S(2)}, u32[]{:S(2)}) collective-permute-start(f32[2,128,512]{2,1,0:T(8,128)S(1)} %get-tuple-element.58), channel_id=1, source_target_pairs={{1,0},{2,1},{3,2},{4,3},{5,4},{6,5},{7,6},{9,8},{10,9},{11,10},{12... | collective-permute-start | bytes 1572872 | tf_op jit(solution)/shard_map/ppermute | solution.py:24
  169.8 12.5 %collective-permute-start.22 = (f32[2,128,512]{2,1,0:T(8,128)S(1)}, f32[2,128,512]{2,1,0:T(8,128)S(1)}, u32[]{:S(2)}, u32[]{:S(2)}) collective-permute-start(f32[2,128,512]{2,1,0:T(8,128)S(1)} %get-tuple-element.55), channel_id=1, source_target_pairs={{0,1},{1,2},{2,3},{3,4},{4,5},{5,6},{6,7},{8,9},{9,10},{10,11},{11... | collective-permute-start | bytes 1572872 | tf_op jit(solution)/shard_map/ppermute | solution.py:24
  173.0 10.3 %collective-permute-start.26 = (f32[2,128,512]{2,1,0:T(8,128)S(1)}, f32[2,128,512]{2,1,0:T(8,128)S(1)}, u32[]{:S(2)}, u32[]{:S(2)}) collective-permute-start(f32[2,128,512]{2,1,0:T(8,128)S(1)} %get-tuple-element.59), channel_id=1, source_target_pairs={{1,0},{2,1},{3,2},{4,3},{5,4},{6,5},{7,6},{9,8},{10,9},{11,10},{12... | collective-permute-start | bytes 1572872 | tf_op jit(solution)/shard_map/ppermute | solution.py:24
  176.7 12.3 %copy-start.6 = (f32[2,128,512]{2,1,0:T(8,128)}, f32[2,128,512]{2,1,0:T(8,128)S(1)}, u32[]{:S(2)}) copy-start(f32[2,128,512]{2,1,0:T(8,128)S(1)} %collective-permute-done.24.refs_8_) | copy-start | bytes 1572868
  176.7 10.5 %collective-permute-start.23 = (f32[2,128,512]{2,1,0:T(8,128)S(1)}, f32[2,128,512]{2,1,0:T(8,128)S(1)}, u32[]{:S(2)}, u32[]{:S(2)}) collective-permute-start(f32[2,128,512]{2,1,0:T(8,128)S(1)} %get-tuple-element.56), channel_id=1, source_target_pairs={{0,1},{1,2},{2,3},{3,4},{4,5},{5,6},{6,7},{8,9},{9,10},{10,11},{11... | collective-permute-start | bytes 1572872 | tf_op jit(solution)/shard_map/ppermute | solution.py:24
  178.6 10.3 %collective-permute-start.27 = (f32[2,128,512]{2,1,0:T(8,128)S(1)}, f32[2,128,512]{2,1,0:T(8,128)S(1)}, u32[]{:S(2)}, u32[]{:S(2)}) collective-permute-start(f32[2,128,512]{2,1,0:T(8,128)S(1)} %get-tuple-element.60), channel_id=1, source_target_pairs={{1,0},{2,1},{3,2},{4,3},{5,4},{6,5},{7,6},{9,8},{10,9},{11,10},{12... | collective-permute-start | bytes 1572872 | tf_op jit(solution)/shard_map/ppermute | solution.py:24
  182.3 6.7 %copy-start.7 = (f32[2,128,512]{2,1,0:T(8,128)}, f32[2,128,512]{2,1,0:T(8,128)S(1)}, u32[]{:S(2)}) copy-start(f32[2,128,512]{2,1,0:T(8,128)S(1)} %collective-permute-done.25.refs_9_) | copy-start | bytes 1572868
  183.4 5.6 %copy-start.8 = (f32[2,128,512]{2,1,0:T(8,128)}, f32[2,128,512]{2,1,0:T(8,128)S(1)}, u32[]{:S(2)}) copy-start(f32[2,128,512]{2,1,0:T(8,128)S(1)} %collective-permute-done.26.refs_10_) | copy-start | bytes 1572868
  187.2 1.8 copy-start.9
  201.7 18.6 %collective-permute-start.28 = (f32[2,128,512]{2,1,0:T(8,128)S(1)}, f32[2,128,512]{2,1,0:T(8,128)S(1)}, u32[]{:S(2)}, u32[]{:S(2)}) collective-permute-start(f32[2,128,512]{2,1,0:T(8,128)S(1)} %get-tuple-element.61.mine), channel_id=1, source_target_pairs={{0,8},{8,16},{16,24},{24,32},{32,40},{40,48},{48,56},{56,64},{64,7... | collective-permute-start | bytes 1572872 | tf_op jit(solution)/shard_map/ppermute | solution.py:24
  203.6 27.9 %collective-permute-start.30 = (f32[2,128,512]{2,1,0:T(8,128)S(1)}, f32[2,128,512]{2,1,0:T(8,128)S(1)}, u32[]{:S(2)}, u32[]{:S(2)}) collective-permute-start(f32[2,128,512]{2,1,0:T(8,128)S(1)} %get-tuple-element.64.mine), channel_id=1, source_target_pairs={{0,8},{8,16},{16,24},{24,32},{32,40},{40,48},{48,56},{56,64},{64,7... | collective-permute-start | bytes 1572872 | tf_op jit(solution)/shard_map/ppermute | solution.py:24
  205.5 37.2 %collective-permute-start.32 = (f32[2,128,512]{2,1,0:T(8,128)S(1)}, f32[2,128,512]{2,1,0:T(8,128)S(1)}, u32[]{:S(2)}, u32[]{:S(2)}) collective-permute-start(f32[2,128,512]{2,1,0:T(8,128)S(1)} %get-tuple-element.67.mine), channel_id=1, source_target_pairs={{0,8},{8,16},{16,24},{24,32},{32,40},{40,48},{48,56},{56,64},{64,7... | collective-permute-start | bytes 1572872 | tf_op jit(solution)/shard_map/ppermute | solution.py:24
  207.5 46.5 %collective-permute-start.34 = (f32[2,128,512]{2,1,0:T(8,128)S(1)}, f32[2,128,512]{2,1,0:T(8,128)S(1)}, u32[]{:S(2)}, u32[]{:S(2)}) collective-permute-start(f32[2,128,512]{2,1,0:T(8,128)S(1)} %get-tuple-element.70.mine), channel_id=1, source_target_pairs={{0,8},{8,16},{16,24},{24,32},{32,40},{40,48},{48,56},{56,64},{64,7... | collective-permute-start | bytes 1572872 | tf_op jit(solution)/shard_map/ppermute | solution.py:24
  221.0 35.7 %collective-permute-start.29 = (f32[2,128,512]{2,1,0:T(8,128)S(1)}, f32[2,128,512]{2,1,0:T(8,128)S(1)}, u32[]{:S(2)}, u32[]{:S(2)}) collective-permute-start(f32[2,128,512]{2,1,0:T(8,128)S(1)} %get-tuple-element.63), channel_id=1, source_target_pairs={{0,1},{1,2},{2,3},{3,4},{4,5},{5,6},{6,7},{8,9},{9,10},{10,11},{11... | collective-permute-start | bytes 1572872 | tf_op jit(solution)/shard_map/ppermute | solution.py:24
  232.3 24.6 %collective-permute-start.31 = (f32[2,128,512]{2,1,0:T(8,128)S(1)}, f32[2,128,512]{2,1,0:T(8,128)S(1)}, u32[]{:S(2)}, u32[]{:S(2)}) collective-permute-start(f32[2,128,512]{2,1,0:T(8,128)S(1)} %get-tuple-element.66), channel_id=1, source_target_pairs={{0,1},{1,2},{2,3},{3,4},{4,5},{5,6},{6,7},{8,9},{9,10},{10,11},{11... | collective-permute-start | bytes 1572872 | tf_op jit(solution)/shard_map/ppermute | solution.py:24
  243.5 13.5 %collective-permute-start.33 = (f32[2,128,512]{2,1,0:T(8,128)S(1)}, f32[2,128,512]{2,1,0:T(8,128)S(1)}, u32[]{:S(2)}, u32[]{:S(2)}) collective-permute-start(f32[2,128,512]{2,1,0:T(8,128)S(1)} %get-tuple-element.69), channel_id=1, source_target_pairs={{0,1},{1,2},{2,3},{3,4},{4,5},{5,6},{6,7},{8,9},{9,10},{10,11},{11... | collective-permute-start | bytes 1572872 | tf_op jit(solution)/shard_map/ppermute | solution.py:24
  254.8 10.5 %collective-permute-start.35 = (f32[2,128,512]{2,1,0:T(8,128)S(1)}, f32[2,128,512]{2,1,0:T(8,128)S(1)}, u32[]{:S(2)}, u32[]{:S(2)}) collective-permute-start(f32[2,128,512]{2,1,0:T(8,128)S(1)} %get-tuple-element.72), channel_id=1, source_target_pairs={{0,1},{1,2},{2,3},{3,4},{4,5},{5,6},{6,7},{8,9},{9,10},{10,11},{11... | collective-permute-start | bytes 1572872 | tf_op jit(solution)/shard_map/ppermute | solution.py:24
  (1 other events, 0.8 us)

commit v2 on v0

v2 whole, which is shorter than its diff:
```python
import functools
import math

import jax
import jax.numpy as jnp
from jax import lax
from jax.experimental import pallas as pl
from jax.experimental.pallas import tpu as pltpu
from jax.sharding import PartitionSpec as P

STEP = 0.5
FLOOR = 0.05
VMEM = pl.BlockSpec(memory_space=pltpu.VMEM)
ANY = pl.BlockSpec(memory_space=pl.ANY)
SMEM = pl.BlockSpec(memory_space=pltpu.SMEM)
LIMIT = 12 * 1024 * 1024
F32 = jnp.float32
BF16 = jnp.bfloat16

EXTRA = 8
HEAD = 224


def shifted(value, axis, steps):
    count = lax.axis_size(axis)
    leading, last = (max(0, -steps), min(count, count - steps))
    return lax.ppermute(value, axis, [(source, source + steps) for source in range(leading, last)])


def dft_tables(width):
    index = jnp.arange(width, dtype=jnp.int32)
    phase = index[:, None] * index[None, :] % width
    angle = phase.astype(jnp.float32) * (2.0 * math.pi / width)
    scale = 1.0 / math.sqrt(width)
    return (
        (jnp.cos(angle) * scale).astype(jnp.bfloat16),
        (jnp.sin(angle) * scale).astype(jnp.bfloat16),
    )


def call(kernel, outs, arrays, scratch=(), scalars=(), after=()):
    skip = len(after)

    def body(*refs):
        kernel(*refs[skip:])

    return pl.pallas_call(
        body,
        out_shape=outs,
        in_specs=[ANY] * skip + [SMEM] * len(scalars) + [VMEM] * len(arrays),
        out_specs=jax.tree.map(lambda _: VMEM, outs),
        scratch_shapes=list(scratch),
        compiler_params=pltpu.CompilerParams(vmem_limit_bytes=LIMIT),
    )(*after, *scalars, *arrays)


def indices(shape, first):
    return (
        lax.broadcasted_iota(jnp.int32, shape, 0) + first,
        lax.broadcasted_iota(jnp.int32, shape, 1),
    )


def low(i, place):
    return i + 1 < place[0, :1, :].astype(jnp.int32)


def far(j, place):
    return j + 1 < place[1, :1, :].astype(jnp.int32)


def absent(place):
    return place[0, :1, :] == 0.0


def prepare_kernel(offset, cos_ref, sin_ref, pupil_ref, bx, bxt, by, byt_head, byt_tail, pupil_out):
    w = cos_ref.shape[0]
    h = HEAD
    cosine = cos_ref[...].astype(F32)
    sine = sin_ref[...].astype(F32)
    oy, ox = offset[0, 0], offset[0, 1]

    def rolled(value, shift, axis):
        return pltpu.roll(value, shift, axis)

    c, s = rolled(cosine, ox, 0).astype(BF16), rolled(sine, ox, 0).astype(BF16)
    bx[:w, :w], bx[:w, w:], bx[w:, :w], bx[w:, w:] = c, s, -s, c
    c, s = rolled(cosine, ox, 1).astype(BF16), rolled(sine, ox, 1).astype(BF16)
    bxt[:w, :w], bxt[:w, w:], bxt[w:, :w], bxt[w:, w:] = c, -s, s, c
    c, s = rolled(cosine, oy, 0).astype(BF16), rolled(sine, oy, 0).astype(BF16)
    by[:w, :w], by[:w, w:], by[w:, :w], by[w:, w:] = c, s, -s, c
    c, s = rolled(cosine, oy, 1).astype(BF16), rolled(sine, oy, 1).astype(BF16)
    for out, part in ((byt_head, slice(0, h)), (byt_tail, slice(h, w))):
        n = part.stop - part.start
        out[:w, :n], out[:w, n:] = c[:, part], -s[:, part]
        out[w:, :n], out[w:, n:] = s[:, part], c[:, part]
    for part in range(2):
        pupil_out[part] = rolled(rolled(pupil_ref[part], oy, 0), ox, 1)


def dot(a, b):
    return jnp.dot(a, b, preferred_element_type=F32)


def right_product(first, window, pupil, bx, left, half):
    w = bx.shape[0] // 2
    h = half.shape[0] // 2
    wr, wi = window
    rows = pl.ds(first, h)
    pr, pi = pupil[0, rows, :], pupil[1, rows, :]
    left[:, :w] = (wr * pr - wi * pi).astype(BF16)
    left[:, w:] = (wr * pi + wi * pr).astype(BF16)
    half[:h, :] = dot(left[...], bx[:, :w]).astype(BF16)
    half[h:, :] = dot(left[...], bx[:, w:]).astype(BF16)


def finish(acc, byt_tail, half, amp, live, bxt, left, stacked):
    w = amp.shape[0]
    block = 128
    alive = (live[0, 0] > 0).astype(F32)
    for first in range(0, w, block):
        rows = pl.ds(first, block)
        wave_r = acc[rows, :] + dot(byt_tail[rows, :], half[...])
        shifted_rows = pl.ds(w + first, block)
        wave_i = acc[shifted_rows, :] + dot(byt_tail[shifted_rows, :], half[...])
        power = jnp.maximum(wave_r * wave_r + wave_i * wave_i, FLOOR * FLOOR)
        keep = (1.0 - amp[rows, :] * lax.rsqrt(power)) * alive
        left[rows, :w] = (wave_r * keep).astype(BF16)
        left[rows, w:] = (wave_i * keep).astype(BF16)
    stacked[:w, :] = dot(left[...], bxt[:, :w]).astype(BF16)
    stacked[w:, :] = dot(left[...], bxt[:, w:]).astype(BF16)


def back(first, by, stacked, pupil, out, extra):
    w = stacked.shape[1]
    size = out.shape[1]
    rows = pl.ds(first, size)
    back_r = dot(by[rows, :], stacked[...])
    back_i = dot(by[pl.ds(w + first, size), :], stacked[...])
    pr, pi = pupil[0, rows, :], pupil[1, rows, :]
    grad_r = back_r * pr + back_i * pi
    grad_i = back_i * pr - back_r * pi
    if extra is not None:
        grad_r = grad_r + extra[0]
        grad_i = grad_i + extra[1]
    out[0] = grad_r
    out[1] = grad_i


def gathered(first, head, place, tile, one, both):
    h = both.shape[1]
    i, j = indices(both.shape[1:], first)
    a, b = low(i, place), far(j, place)
    if not head:
        a, b = b, a
    return [jnp.where(b, both[p], jnp.where(a, one[p, :h, :], tile[p, :h, :])) for p in range(2)]


def updated(first, head, place, edge_row, edge_col, kept, own, minus, plus):
    i, j = indices(kept.shape[1:], first)
    a, b = low(i, place), far(j, place)
    outside = (a & absent(edge_row)) | (b & absent(edge_col))
    second = b if head else a
    parts = []
    for p in range(2):
        near = jnp.where(second, plus[p], minus[p])
        parts.append(jnp.where(outside, 0.0, kept[p] - STEP * (own[p] + near)))
    return parts


def open_first(first, place, tile, one, both, pupil, bx, byt, kept, acc, left, half):
    window = gathered(first, True, place, tile, one, both)
    kept[0], kept[1] = window
    right_product(first, window, pupil, bx, left, half)
    acc[...] = dot(byt[...], half[...])


def close_first(
    first, live, place, tile, one, both, acc, pupil, amp, bx, byt, bxt, by, kept, stacked, out, left, half
):
    window = gathered(first, False, place, tile, one, both)
    kept[0], kept[1] = window
    right_product(first, window, pupil, bx, left.at[: half.shape[0] // 2], half)
    finish(acc, byt, half, amp, live, bxt, left, stacked)
    back(0, by, stacked, pupil, out, None)


def open_second(
    first, place, edge_row, edge_col, kept, own, minus, plus, pupil, bx, byt, acc, left, half
):
    window = updated(first, True, place, edge_row, edge_col, kept, own, minus, plus)
    right_product(first, window, pupil, bx, left, half)
    acc[...] = dot(byt[...], half[...])


def close_second(
    first, live, place, edge_row, edge_col, kept, own, minus, plus, acc, pupil, amp, bx, byt, bxt, by,
    extra, stacked, out, left, half
):
    window = updated(first, False, place, edge_row, edge_col, kept, own, minus, plus)
    right_product(first, window, pupil, bx, left.at[: half.shape[0] // 2], half)
    finish(acc, byt, half, amp, live, bxt, left, stacked)
    back(0, by, stacked, pupil, out, extra)


def rest_first(first, by, stacked, pupil, out):
    back(first, by, stacked, pupil, out, None)


def rest_second(first, by, stacked, pupil, extra, out):
    back(first, by, stacked, pupil, out, extra)


def compose_kernel(first, head, target, tile, one, out, place):
    h = out.shape[1]
    i, j = indices(out.shape[1:], first)
    mask = low(i, target) if head else far(j, target)
    for p in range(2):
        out[p] = jnp.where(mask, one[p, :h, :], tile[p, :h, :])
        place[p] = one[p, h:, :]


def between_kernel(
    first, head, me, minus, plus, target_minus, target_plus, mine, got_minus, got_plus, to_minus, to_plus, own
):
    i, j = indices(mine.shape[1:], first)
    ways = (functools.partial(low, i), functools.partial(far, j))
    if not head:
        ways = ways[::-1]
    f, f_minus, f_plus = (ways[0](x) for x in (me, minus, plus))
    s, s_minus, s_plus = (ways[1](x) for x in (me, minus, plus))

    def seen(goal):
        return f == goal, ~goal & f_minus, goal & ~f_plus

    minus_m = [a & ~b for a, b in zip(seen(ways[0](target_minus)), (s, s_minus, s_plus))]
    plus_m = [a & b for a, b in zip(seen(ways[0](target_plus)), (s, s_minus, s_plus))]
    _, own_minus, own_plus = seen(f)
    own_minus, own_plus = own_minus & (s == s_minus), own_plus & (s == s_plus)
    for p in range(2):
        values = (mine[p], got_minus[p], got_plus[p])
        for out, masks in ((to_minus, minus_m), (to_plus, plus_m)):
            terms = [jnp.where(m, v, 0.0) for m, v in zip(masks, values)]
            out[p] = terms[0] + terms[1] + terms[2]
        own[p] = values[0] + jnp.where(own_minus, values[1], 0.0) + jnp.where(own_plus, values[2], 0.0)


def final_kernel(first, head, me, minus, tile, mine, got, to_plus, base):
    h = mine.shape[1]
    i, j = indices(mine.shape[1:], first)
    ways = (functools.partial(low, i), functools.partial(far, j))
    if not head:
        ways = ways[::-1]
    f, f_minus = ways[0](me), ways[0](minus)
    s, s_minus = ways[1](me), ways[1](minus)
    for p in range(2):
        own = jnp.where(f, 0.0, mine[p])
        other = jnp.where(f_minus, got[p], 0.0)
        to_plus[p] = jnp.where(s, own, 0.0) + jnp.where(s_minus, other, 0.0)
        kept = jnp.where(s, 0.0, own) + jnp.where(s_minus, 0.0, other)
        base[p] = tile[p, :h, :] - STEP * kept


def store_kernel(first, base, got, *rest):
    out, value, sem = rest[-3:]
    for p in range(2):
        value[p] = base[p] - STEP * got[p]
    copy = pltpu.make_async_copy(value, out.at[:, pl.ds(first, value.shape[1]), :], sem)
    copy.start()
    copy.wait()


def store(first, base, got, whole, previous=None):
    _, h, w = base.shape
    held = () if previous is None else (previous,)
    return pl.pallas_call(
        functools.partial(store_kernel, first),
        out_shape=whole,
        in_specs=[VMEM, VMEM] + [ANY] * len(held),
        out_specs=ANY,
        scratch_shapes=[pltpu.VMEM((2, h, w), F32), pltpu.SemaphoreType.DMA],
        input_output_aliases={2: 0} if held else {},
        compiler_params=pltpu.CompilerParams(vmem_limit_bytes=LIMIT),
    )(base, got, *held)


def on_device(spectrum, pupil, amplitudes, offsets, counts):
    w = pupil.shape[1]
    h = HEAD
    amp = amplitudes[0, 0, 0]
    offset = offsets[0, 0]
    piece = jax.ShapeDtypeStruct((2, h, w), F32)
    rest = jax.ShapeDtypeStruct((2, w - h, w), F32)
    whole = jax.ShapeDtypeStruct((2, w, w), F32)
    spot = jax.ShapeDtypeStruct((2, EXTRA, w), F32)
    me = jnp.broadcast_to((offset[0] + 1).astype(F32)[:, None, None], (2, EXTRA, w))
    head = jnp.concatenate([spectrum[:, :h], me], axis=1)
    tail = jnp.concatenate([spectrum[:, h:], me], axis=1)

    head_below = shifted(head, "row", -1)
    tail_right = shifted(tail, "col", -1)
    above = shifted(me, "row", 1)
    left_of = shifted(me, "col", 1)

    cosine, sine = dft_tables(w)
    table = jax.ShapeDtypeStruct((2 * w, 2 * w), BF16)
    narrow = [jax.ShapeDtypeStruct((2 * w, 2 * n), BF16) for n in (h, w - h)]
    bx, bxt, by, byt_head, byt_tail, rolled = call(
        prepare_kernel, [table, table, table, *narrow, whole], (cosine, sine, pupil), scalars=(offset,)
    )

    tail_made, right_of = call(
        functools.partial(compose_kernel, h, False), [rest, spot], (above, tail, tail_right)
    )
    tail_both = shifted(tail_made, "row", -1)
    head_made, under = call(
        functools.partial(compose_kernel, 0, True),
        [piece, spot],
        (left_of, head, head_below),
        after=(tail_made,),
    )
    head_both = shifted(head_made, "col", -1)

    total = jax.ShapeDtypeStruct((2 * w, w), F32)
    stack = jax.ShapeDtypeStruct((2 * w, w), BF16)
    half, half_tail = (pltpu.VMEM((2 * n, w), BF16) for n in (h, w - h))
    left_half, left_whole = pltpu.VMEM((h, 2 * w), BF16), pltpu.VMEM((w, 2 * w), BF16)
    head_kept, acc = call(
        functools.partial(open_first, 0),
        [piece, total],
        (me, head, head_below, head_both, rolled, bx, byt_head),
        (left_half, half),
    )
    tail_kept, stacked, head_grad = call(
        functools.partial(close_first, h),
        [rest, stack, piece],
        (me, tail, tail_right, tail_both, acc, rolled, amp, bx, byt_tail, bxt, by),
        (left_whole, half_tail),
        scalars=(counts,),
    )

    got_above, got_under = shifted(head_grad, "row", 1), shifted(head_grad, "row", -1)
    tail_grad = call(functools.partial(rest_first, h), rest, (by, stacked, rolled))
    got_left, got_right = shifted(tail_grad, "col", 1), shifted(tail_grad, "col", -1)
    to_up, to_down, tail_own = call(
        functools.partial(between_kernel, h, False),
        [rest] * 3,
        (me, left_of, right_of, above, under, tail_grad, got_left, got_right),
    )
    tail_sums = (tail_own, shifted(to_down, "row", 1), shifted(to_up, "row", -1))
    to_left, to_right, head_own = call(
        functools.partial(between_kernel, 0, True),
        [piece] * 3,
        (me, above, under, left_of, right_of, head_grad, got_above, got_under),
        after=(to_up,),
    )
    head_sums = (head_own, shifted(to_right, "col", 1), shifted(to_left, "col", -1))

    acc = call(
        functools.partial(open_second, 0),
        total,
        (me, under, right_of, head_kept, *head_sums, rolled, bx, byt_head),
        (left_half, half),
    )
    stacked, head_total = call(
        functools.partial(close_second, h),
        [stack, piece],
        (me, under, right_of, tail_kept, *tail_sums, acc, rolled, amp, bx, byt_tail, bxt, by, head_grad),
        (left_whole, half_tail),
        scalars=(counts,),
    )

    head_above = shifted(head_total, "row", 1)
    tail_total = call(functools.partial(rest_second, h), rest, (by, stacked, rolled, tail_grad))
    tail_left = shifted(tail_total, "col", 1)
    tail_down, tail_base = call(
        functools.partial(final_kernel, h, False), [rest] * 2, (me, left_of, tail, tail_total, tail_left)
    )
    tail_got = shifted(tail_down, "row", 1)
    head_right, head_base = call(
        functools.partial(final_kernel, 0, True),
        [piece] * 2,
        (me, above, head, head_total, head_above),
        after=(tail_down,),
    )
    head_got = shifted(head_right, "col", 1)
    partial = store(0, head_base, head_got, whole)
    return store(h, tail_base, tail_got, whole, partial)


def solution(mesh):
    in_specs = (
        P(None, "row", "col"),
        P(),
        P("row", "col", None, None, None),
        P("row", "col", None, None),
        P("row", "col"),
    )
    out_specs = P(None, "row", "col")
    return jax.shard_map(
        on_device, mesh=mesh, in_specs=in_specs, out_specs=out_specs, check_vma=False
    )
```

time: 641 us -> 185 us (0.29)
  waiting for transfers between devices: 362 us -> 93.9 us
  matrix products: 162 us -> 0 us
  local copies, waits for them, and re-layouts: 51.2 us -> 1.29 us
  starting transfers between devices: 24.1 us -> 56.4 us
  Pallas kernels: 0 us -> 25.5 us
  other arithmetic: 27.8 us -> 5.2 us
    ppermute x8 -> x18, waiting for transfers between devices: 362 us -> 93.9 us  [shifted(): lax.ppermute(value, axis, [(source, source + steps) for source in range(l...]
    dot_general x32 -> x0, matrix products: 162 us -> none  [the longest x16 81 us: right(): return jnp.einsum('swk,kj->swj', a, b, preferred_element_type=jnp.float32)]
    ppermute x8 -> x18, starting transfers between devices: 24.1 us -> 56.4 us  [shifted(): lax.ppermute(value, axis, [(source, source + steps) for source in range(l...]
    dynamic_update_slice x2 -> x0, local copies, waits for them, and re-layouts: 30 us -> none  [add_piece(): return lax.dynamic_update_slice(region, current + piece, start)]
    pallas_call x0 -> x15, Pallas kernels: none -> 25.5 us  [the longest x13 23.3 us: call(): pl.pallas_call(body, out_shape=outs, in_specs=[ANY] * skip + [SMEM] * len...]
    add x4 -> x0, other arithmetic: 9.54 us -> none  [the longest x2 7.51 us: add_piece(): return lax.dynamic_update_slice(region, current + piece, start)]
    another operation x2 -> x0, local copies, waits for them, and re-layouts: 8.67 us -> none
  transfers between devices with their start and end apart: 8 -> 18, of which waited for: 8 -> 15; matrix products, arithmetic and copies ran while one was open for 1% -> 2% of each run, Pallas kernels for 0% -> 8%
where the time goes in v2:
time: 185 us; the launch traced here: 183 us
  waiting for transfers between devices  93.9 us (51%)
  starting transfers between devices  56.4 us (30%)
  Pallas kernels  25.5 us (14%)
  other arithmetic  5.2 us (3%)
    ppermute x18, waiting for transfers between devices, shifted(): lax.ppermute(value, axis, [(source, source + steps) for source in range(l...  93.9 us
    ppermute x18, starting transfers between devices, shifted(): lax.ppermute(value, axis, [(source, source + steps) for source in range(l...  56.4 us
    pallas_call x13, Pallas kernels, call(): pl.pallas_call(body, out_shape=outs, in_specs=[ANY] * skip + [SMEM] * len...  23.3 us
    convert_element_type x1, other arithmetic, dft_tables(): (jnp.sin(angle) * scale).astype(jnp.bfloat16)  4.39 us
  transfers between devices with their start and end apart: 18, of which 15 were waited for; matrix products, arithmetic and copies ran while one was open for 2% of the time, Pallas kernels for 8%

profile of v2, /device:TPU:28, one launch (start us, length us, event | category | flops | bytes accessed | tf_op | source)
XLA Modules:
  0.0 183.4 jit_solution(13234130297248618449)
XLA Ops:
  0.0 0.7 convert_bitcast_fusion
  0.7 1.2 slice-done
  2.0 2.1 %collective-permute-start.2 = (f32[2,296,512]{2,1,0:T(8,128)S(1)}, f32[2,296,512]{2,1,0:T(8,128)S(1)}, u32[]{:S(2)}, u32[]{:S(2)}) collective-permute-start(f32[2,296,512]{2,1,0:T(8,128)S(1)} %pad_maximum_fusion.refs_1_.refs_2_), channel_id=1, source_target_pairs={{1,0},{2,1},{3,2},{4,3},{5,4},{6,5},{7,6},{9,8},{10,9},{11,10},{12... | collective-permute-start | bytes 3637256 | tf_op jit(solution)/shard_map/ppermute | solution.py:27
  4.2 6.1 %collective-permute-start.3 = (f32[2,232,512]{2,1,0:T(8,128)S(1)}, f32[2,232,512]{2,1,0:T(8,128)S(1)}, u32[]{:S(2)}, u32[]{:S(2)}) collective-permute-start(f32[2,232,512]{2,1,0:T(8,128)S(1)} %pad_maximum_fusion.1.refs_2_.refs_1_.refs_3_), channel_id=1, source_target_pairs={{8,0},{16,8},{24,16},{32,24},{40,32},{48,40},{56,48},{64,56},{72,6... | collective-permute-start | bytes 2850824 | tf_op jit(solution)/shard_map/ppermute | solution.py:27
  10.3 1.9 %collective-permute-start.1 = (f32[2,8,512]{2,1,0:T(8,128)S(1)}, f32[2,8,512]{2,1,0:T(8,128)S(1)}, u32[]{:S(2)}, u32[]{:S(2)}) collective-permute-start(f32[2,8,512]{2,1,0:T(8,128)S(1)} %broadcast_in_dim.2.refs_0_.refs_1_), channel_id=1, source_target_pairs={{0,8},{8,16},{16,24},{24,32},{32,40},{40,48},{48,56},{56,64},{64,7... | collective-permute-start | bytes 98312 | tf_op jit(solution)/shard_map/ppermute | solution.py:27
  12.2 6.0 %collective-permute-done.1.refs_0_.refs_3_.refs_2_ = f32[2,8,512]{2,1,0:T(8,128)S(1)} collective-permute-done((f32[2,8,512]{2,1,0:T(8,128)S(1)}, f32[2,8,512]{2,1,0:T(8,128)S(1)}, u32[]{:S(2)}, u32[]{:S(2)}) %collective-permute-start.1) | collective-permute-done | bytes 32800 | tf_op jit(solution)/shard_map/ppermute | solution.py:27
  18.4 6.0 %collective-permute-start.4 = (f32[2,288,512]{2,1,0:T(8,128)S(1)}, f32[2,288,512]{2,1,0:T(8,128)S(1)}, u32[]{:S(2)}, u32[]{:S(2)}) collective-permute-start(f32[2,288,512]{2,1,0:T(8,128)S(1)} %get-tuple-element.33.refs_0_), channel_id=1, source_target_pairs={{8,0},{16,8},{24,16},{32,24},{40,32},{48,40},{56,48},{64,56},{72,6... | collective-permute-start | bytes 3538952 | tf_op jit(solution)/shard_map/ppermute | solution.py:27
  24.4 3.7 %collective-permute-start = (f32[2,8,512]{2,1,0:T(8,128)S(1)}, f32[2,8,512]{2,1,0:T(8,128)S(1)}, u32[]{:S(2)}, u32[]{:S(2)}) collective-permute-start(f32[2,8,512]{2,1,0:T(8,128)S(1)} %broadcast_in_dim.2.refs_0_.refs_1_), channel_id=1, source_target_pairs={{0,1},{1,2},{2,3},{3,4},{4,5},{5,6},{6,7},{8,9},{9,10},{10,11},{11... | collective-permute-start | bytes 98312 | tf_op jit(solution)/shard_map/ppermute | solution.py:27
  28.1 1.8 collective-permute-done.refs_1_.refs_4_
  29.8 1.8 collective-permute-done.3.refs_3_.refs_2_
  31.8 2.1 %collective-permute-start.5 = (f32[2,224,512]{2,1,0:T(8,128)S(1)}, f32[2,224,512]{2,1,0:T(8,128)S(1)}, u32[]{:S(2)}, u32[]{:S(2)}) collective-permute-start(f32[2,224,512]{2,1,0:T(8,128)S(1)} %get-tuple-element.36), channel_id=1, source_target_pairs={{1,0},{2,1},{3,2},{4,3},{5,4},{6,5},{7,6},{9,8},{10,9},{11,10},{12... | collective-permute-start | bytes 2752520 | tf_op jit(solution)/shard_map/ppermute | solution.py:27
  34.5 4.4 %multiply_convert_fusion = (bf16[512,512]{1,0:T(8,128)(2,1)S(1)}, bf16[512,512]{1,0:T(8,128)(2,1)S(1)}) fusion(), kind=kLoop, calls=%fused_computation.7 | loop fusion | flops 4718592 | bytes 1048576 | tf_op jit(solution)/shard_map/convert_element_type | solution.py:37
  38.9 5.9 %shard_map.55 = (bf16[1024,1024]{1,0:T(8,128)(2,1)S(1)}, bf16[1024,1024]{1,0:T(8,128)(2,1)S(1)}, bf16[1024,1024]{1,0:T(8,128)(2,1)S(1)}, bf16[1024,448]{1,0:T(8,...) custom-call(s32[1,2]{1,0:T(1,128)S(1)} %bitcast.6, ...), custom_call_target="tpu_custom_call" | custom-call | tf_op jit(solution)/shard_map/pallas_call | solution.py:47
  44.8 1.5 shard_map.58
  46.3 10.2 %collective-permute-done.4.refs_4_ = f32[2,288,512]{2,1,0:T(8,128)S(1)} collective-permute-done((f32[2,288,512]{2,1,0:T(8,128)S(1)}, f32[2,288,512]{2,1,0:T(8,128)S(1)}, u32[]{:S(2)}, u32[]{:S(2)}) %collective-permute-start.4) | collective-permute-done | bytes 1179680 | tf_op jit(solution)/shard_map/ppermute | solution.py:27
  56.5 3.7 %shard_map.59 = (f32[2,288,512]{2,1,0:T(8,128)S(1)}, bf16[1024,512]{1,0:T(8,128)(2,1)S(1)}, f32[2,224,512]{2,1,0:T(8,128)S(1)}) custom-call(s32[1,1]{1,0:T(1,128)S(6)} %copy.8.refs_0_, f32[2,8,512]{2,1,0:T(8,128)S(1)} %broadcast_in_dim.2.refs_0_.refs_1_, f32[2,296,512]{2,1,0:T(8,128)S(1)} %pad_maximum_fusion.refs_1_.refs_2_, ...), custom_call_target="tpu_custom_call" | custom-call | tf_op jit(solution)/shard_map/pallas_call | solution.py:47
  60.2 0.9 shard_map.60.refs_5_.refs_3_
  61.1 1.9 %collective-permute-start.7 = (f32[2,288,512]{2,1,0:T(8,128)S(1)}, f32[2,288,512]{2,1,0:T(8,128)S(1)}, u32[]{:S(2)}, u32[]{:S(2)}) collective-permute-start(f32[2,288,512]{2,1,0:T(8,128)S(1)} %shard_map.60.refs_5_.refs_3_), channel_id=1, source_target_pairs={{1,0},{2,1},{3,2},{4,3},{5,4},{6,5},{7,6},{9,8},{10,9},{11,10},{12... | collective-permute-start | bytes 3538952 | tf_op jit(solution)/shard_map/ppermute | solution.py:27
  63.0 2.4 %collective-permute-start.6 = (f32[2,288,512]{2,1,0:T(8,128)S(1)}, f32[2,288,512]{2,1,0:T(8,128)S(1)}, u32[]{:S(2)}, u32[]{:S(2)}) collective-permute-start(f32[2,288,512]{2,1,0:T(8,128)S(1)} %shard_map.60.refs_5_.refs_3_), channel_id=1, source_target_pairs={{0,1},{1,2},{2,3},{3,4},{4,5},{5,6},{6,7},{8,9},{9,10},{10,11},{11... | collective-permute-start | bytes 3538952 | tf_op jit(solution)/shard_map/ppermute | solution.py:27
  65.4 6.5 %collective-permute-start.11 = (f32[2,224,512]{2,1,0:T(8,128)S(1)}, f32[2,224,512]{2,1,0:T(8,128)S(1)}, u32[]{:S(2)}, u32[]{:S(2)}) collective-permute-start(f32[2,224,512]{2,1,0:T(8,128)S(1)} %get-tuple-element.49.refs_6_.refs_15_), channel_id=1, source_target_pairs={{8,0},{16,8},{24,16},{32,24},{40,32},{48,40},{56,48},{64,56},{72,6... | collective-permute-start | bytes 2752520 | tf_op jit(solution)/shard_map/ppermute | solution.py:27
  71.9 2.1 %collective-permute-start.10 = (f32[2,224,512]{2,1,0:T(8,128)S(1)}, f32[2,224,512]{2,1,0:T(8,128)S(1)}, u32[]{:S(2)}, u32[]{:S(2)}) collective-permute-start(f32[2,224,512]{2,1,0:T(8,128)S(1)} %get-tuple-element.49.refs_6_.refs_15_), channel_id=1, source_target_pairs={{0,8},{8,16},{16,24},{24,32},{32,40},{40,48},{48,56},{56,64},{64,7... | collective-permute-start | bytes 2752520 | tf_op jit(solution)/shard_map/ppermute | solution.py:27
  74.0 2.7 %collective-permute-done.7.refs_7_ = f32[2,288,512]{2,1,0:T(8,128)S(1)} collective-permute-done((f32[2,288,512]{2,1,0:T(8,128)S(1)}, f32[2,288,512]{2,1,0:T(8,128)S(1)}, u32[]{:S(2)}, u32[]{:S(2)}) %collective-permute-start.7) | collective-permute-done | bytes 1179680 | tf_op jit(solution)/shard_map/ppermute | solution.py:27
  76.7 3.8 %collective-permute-done.6.refs_6_ = f32[2,288,512]{2,1,0:T(8,128)S(1)} collective-permute-done((f32[2,288,512]{2,1,0:T(8,128)S(1)}, f32[2,288,512]{2,1,0:T(8,128)S(1)}, u32[]{:S(2)}, u32[]{:S(2)}) %collective-permute-start.6) | collective-permute-done | bytes 1179680 | tf_op jit(solution)/shard_map/ppermute | solution.py:27
  80.5 2.0 %shard_map.61 = (f32[2,288,512]{2,1,0:T(8,128)S(1)}, f32[2,288,512]{2,1,0:T(8,128)S(1)}, f32[2,288,512]{2,1,0:T(8,128)S(1)}) custom-call(f32[2,8,512]{2,1,0:T(8,128)S(1)} %broadcast_in_dim.2.refs_0_.refs_1_, f32[2,8,512]{2,1,0:T(8,128)S(1)} %collective-permute-done.refs_1_.refs_4_, f32[2,8,512]{2,1,0:T(8,128)S(1)} %get-tuple-element.35.refs_2_.refs_5_.refs_3_, ...), custom_call_target="tpu_custom_call" | custom-call | tf_op jit(solution)/shard_map/pallas_call | solution.py:47
  82.6 2.3 %collective-permute-start.8 = (f32[2,288,512]{2,1,0:T(8,128)S(1)}, f32[2,288,512]{2,1,0:T(8,128)S(1)}, u32[]{:S(2)}, u32[]{:S(2)}) collective-permute-start(f32[2,288,512]{2,1,0:T(8,128)S(1)} %get-tuple-element.46), channel_id=1, source_target_pairs={{0,8},{8,16},{16,24},{24,32},{32,40},{40,48},{48,56},{56,64},{64,7... | collective-permute-start | bytes 3538952 | tf_op jit(solution)/shard_map/ppermute | solution.py:27
  84.9 6.1 %collective-permute-start.9 = (f32[2,288,512]{2,1,0:T(8,128)S(1)}, f32[2,288,512]{2,1,0:T(8,128)S(1)}, u32[]{:S(2)}, u32[]{:S(2)}) collective-permute-start(f32[2,288,512]{2,1,0:T(8,128)S(1)} %get-tuple-element.47.refs_0_), channel_id=1, source_target_pairs={{8,0},{16,8},{24,16},{32,24},{40,32},{48,40},{56,48},{64,56},{72,6... | collective-permute-start | bytes 3538952 | tf_op jit(solution)/shard_map/ppermute | solution.py:27
  91.0 1.6 collective-permute-done.11.refs_8_
  92.6 6.5 %collective-permute-done.10.refs_7_ = f32[2,224,512]{2,1,0:T(8,128)S(1)} collective-permute-done((f32[2,224,512]{2,1,0:T(8,128)S(1)}, f32[2,224,512]{2,1,0:T(8,128)S(1)}, u32[]{:S(2)}, u32[]{:S(2)}) %collective-permute-start.10) | collective-permute-done | bytes 917536 | tf_op jit(solution)/shard_map/ppermute | solution.py:27
  99.2 2.0 %shard_map.62 = (f32[2,224,512]{2,1,0:T(8,128)S(1)}, f32[2,224,512]{2,1,0:T(8,128)S(1)}, f32[2,224,512]{2,1,0:T(8,128)S(1)}) custom-call(f32[2,288,512]{2,1,0:T(8,128)S(1)} %get-tuple-element.47.refs_0_, f32[2,8,512]{2,1,0:T(8,128)S(1)} %broadcast_in_dim.2.refs_0_.refs_1_, f32[2,8,512]{2,1,0:T(8,128)S(1)} %collective-permute-done.1.refs_0_.refs_3_.refs_2_, ...), custom_call_target="tpu_custom_call" | custom-call | tf_op jit(solution)/shard_map/pallas_call | solution.py:47
  101.1 1.9 %collective-permute-start.12 = (f32[2,224,512]{2,1,0:T(8,128)S(1)}, f32[2,224,512]{2,1,0:T(8,128)S(1)}, u32[]{:S(2)}, u32[]{:S(2)}) collective-permute-start(f32[2,224,512]{2,1,0:T(8,128)S(1)} %get-tuple-element.51), channel_id=1, source_target_pairs={{0,1},{1,2},{2,3},{3,4},{4,5},{5,6},{6,7},{8,9},{9,10},{10,11},{11... | collective-permute-start | bytes 2752520 | tf_op jit(solution)/shard_map/ppermute | solution.py:27
  103.0 3.6 %collective-permute-start.13 = (f32[2,224,512]{2,1,0:T(8,128)S(1)}, f32[2,224,512]{2,1,0:T(8,128)S(1)}, u32[]{:S(2)}, u32[]{:S(2)}) collective-permute-start(f32[2,224,512]{2,1,0:T(8,128)S(1)} %get-tuple-element.52), channel_id=1, source_target_pairs={{1,0},{2,1},{3,2},{4,3},{5,4},{6,5},{7,6},{9,8},{10,9},{11,10},{12... | collective-permute-start | bytes 2752520 | tf_op jit(solution)/shard_map/ppermute | solution.py:27
  106.7 9.1 %collective-permute-done.12.refs_5_ = f32[2,224,512]{2,1,0:T(8,128)S(1)} collective-permute-done((f32[2,224,512]{2,1,0:T(8,128)S(1)}, f32[2,224,512]{2,1,0:T(8,128)S(1)}, u32[]{:S(2)}, u32[]{:S(2)}) %collective-permute-start.12) | collective-permute-done | bytes 917536 | tf_op jit(solution)/shard_map/ppermute | solution.py:27
  115.8 1.8 collective-permute-done.13.refs_6_
  117.6 1.5 shard_map.63.refs_8_
  119.1 5.1 %collective-permute-done.8.refs_6_ = f32[2,288,512]{2,1,0:T(8,128)S(1)} collective-permute-done((f32[2,288,512]{2,1,0:T(8,128)S(1)}, f32[2,288,512]{2,1,0:T(8,128)S(1)}, u32[]{:S(2)}, u32[]{:S(2)}) %collective-permute-start.8) | collective-permute-done | bytes 1179680 | tf_op jit(solution)/shard_map/ppermute | solution.py:27
  124.1 3.7 %shard_map.64 = (bf16[1024,512]{1,0:T(8,128)(2,1)S(1)}, f32[2,224,512]{2,1,0:T(8,128)S(1)}) custom-call(s32[1,1]{1,0:T(1,128)S(6)} %copy.8.refs_0_, f32[2,8,512]{2,1,0:T(8,128)S(1)} %broadcast_in_dim.2.refs_0_.refs_1_, f32[2,8,512]{2,1,0:T(8,128)S(1)} %get-tuple-element.34.refs_4_.refs_3_.refs_1_.refs_2_, ...), custom_call_target="tpu_custom_call" | custom-call | tf_op jit(solution)/shard_map/pallas_call | solution.py:47
  127.8 0.9 shard_map.65.refs_3_
  128.8 1.9 %collective-permute-start.14 = (f32[2,288,512]{2,1,0:T(8,128)S(1)}, f32[2,288,512]{2,1,0:T(8,128)S(1)}, u32[]{:S(2)}, u32[]{:S(2)}) collective-permute-start(f32[2,288,512]{2,1,0:T(8,128)S(1)} %shard_map.65.refs_3_), channel_id=1, source_target_pairs={{0,1},{1,2},{2,3},{3,4},{4,5},{5,6},{6,7},{8,9},{9,10},{10,11},{11... | collective-permute-start | bytes 3538952 | tf_op jit(solution)/shard_map/ppermute | solution.py:27
  130.7 1.9 %collective-permute-start.16 = (f32[2,224,512]{2,1,0:T(8,128)S(1)}, f32[2,224,512]{2,1,0:T(8,128)S(1)}, u32[]{:S(2)}, u32[]{:S(2)}) collective-permute-start(f32[2,224,512]{2,1,0:T(8,128)S(1)} %get-tuple-element.56.refs_4_), channel_id=1, source_target_pairs={{0,8},{8,16},{16,24},{24,32},{32,40},{40,48},{48,56},{56,64},{64,7... | collective-permute-start | bytes 2752520 | tf_op jit(solution)/shard_map/ppermute | solution.py:27
  132.6 13.7 %collective-permute-done.14.refs_4_ = f32[2,288,512]{2,1,0:T(8,128)S(1)} collective-permute-done((f32[2,288,512]{2,1,0:T(8,128)S(1)}, f32[2,288,512]{2,1,0:T(8,128)S(1)}, u32[]{:S(2)}, u32[]{:S(2)}) %collective-permute-start.14) | collective-permute-done | bytes 1179680 | tf_op jit(solution)/shard_map/ppermute | solution.py:27
  146.3 0.7 shard_map.66
  147.0 1.9 %collective-permute-start.15 = (f32[2,288,512]{2,1,0:T(8,128)S(1)}, f32[2,288,512]{2,1,0:T(8,128)S(1)}, u32[]{:S(2)}, u32[]{:S(2)}) collective-permute-start(f32[2,288,512]{2,1,0:T(8,128)S(1)} %get-tuple-element.55.refs_0_), channel_id=1, source_target_pairs={{0,8},{8,16},{16,24},{24,32},{32,40},{40,48},{48,56},{56,64},{64,7... | collective-permute-start | bytes 3538952 | tf_op jit(solution)/shard_map/ppermute | solution.py:27
  148.9 9.0 %collective-permute-done.16.refs_5_ = f32[2,224,512]{2,1,0:T(8,128)S(1)} collective-permute-done((f32[2,224,512]{2,1,0:T(8,128)S(1)}, f32[2,224,512]{2,1,0:T(8,128)S(1)}, u32[]{:S(2)}, u32[]{:S(2)}) %collective-permute-start.16) | collective-permute-done | bytes 917536 | tf_op jit(solution)/shard_map/ppermute | solution.py:27
  158.3 1.9 %collective-permute-start.17 = (f32[2,224,512]{2,1,0:T(8,128)S(1)}, f32[2,224,512]{2,1,0:T(8,128)S(1)}, u32[]{:S(2)}, u32[]{:S(2)}) collective-permute-start(f32[2,224,512]{2,1,0:T(8,128)S(1)} %get-tuple-element.58), channel_id=1, source_target_pairs={{0,1},{1,2},{2,3},{3,4},{4,5},{5,6},{6,7},{8,9},{9,10},{10,11},{11... | collective-permute-start | bytes 2752520 | tf_op jit(solution)/shard_map/ppermute | solution.py:27
  160.2 12.8 %collective-permute-done.17.got = f32[2,224,512]{2,1,0:T(8,128)S(1)} collective-permute-done((f32[2,224,512]{2,1,0:T(8,128)S(1)}, f32[2,224,512]{2,1,0:T(8,128)S(1)}, u32[]{:S(2)}, u32[]{:S(2)}) %collective-permute-start.17) | collective-permute-done | bytes 917536 | tf_op jit(solution)/shard_map/ppermute | solution.py:27
  173.0 1.0 shard_map.68.rest_0_
  174.1 8.1 %collective-permute-done.15.got = f32[2,288,512]{2,1,0:T(8,128)S(1)} collective-permute-done((f32[2,288,512]{2,1,0:T(8,128)S(1)}, f32[2,288,512]{2,1,0:T(8,128)S(1)}, u32[]{:S(2)}, u32[]{:S(2)}) %collective-permute-start.15) | collective-permute-done | bytes 1179680 | tf_op jit(solution)/shard_map/ppermute | solution.py:27
  182.1 1.1 shard_map.69
  (18 shorter events, 0.9 us)
Async XLA Ops:
  0.7 1.3 slice-start
  2.0 2.1 %slice-start.1 = ((f32[2,512,512]{2,1,0:T(8,128)}), f32[2,224,512]{2,1,0:T(8,128)S(1)}, s32[]{:S(2)}) async-start(f32[2,512,512]{2,1,0:T(8,128)} %param.5), calls=%async_computation.1 | async-start | bytes 1835008 | tf_op jit(solution)/shard_map/slice | solution.py:297
  2.0 16.2 %collective-permute-start.2 = (f32[2,296,512]{2,1,0:T(8,128)S(1)}, f32[2,296,512]{2,1,0:T(8,128)S(1)}, u32[]{:S(2)}, u32[]{:S(2)}) collective-permute-start(f32[2,296,512]{2,1,0:T(8,128)S(1)} %pad_maximum_fusion.refs_1_.refs_2_), channel_id=1, source_target_pairs={{1,0},{2,1},{3,2},{4,3},{5,4},{6,5},{7,6},{9,8},{10,9},{11,10},{12... | collective-permute-start | bytes 3637256 | tf_op jit(solution)/shard_map/ppermute | solution.py:27
  4.2 27.5 %collective-permute-start.3 = (f32[2,232,512]{2,1,0:T(8,128)S(1)}, f32[2,232,512]{2,1,0:T(8,128)S(1)}, u32[]{:S(2)}, u32[]{:S(2)}) collective-permute-start(f32[2,232,512]{2,1,0:T(8,128)S(1)} %pad_maximum_fusion.1.refs_2_.refs_1_.refs_3_), channel_id=1, source_target_pairs={{8,0},{16,8},{24,16},{32,24},{40,32},{48,40},{56,48},{64,56},{72,6... | collective-permute-start | bytes 2850824 | tf_op jit(solution)/shard_map/ppermute | solution.py:27
  10.3 7.9 %collective-permute-start.1 = (f32[2,8,512]{2,1,0:T(8,128)S(1)}, f32[2,8,512]{2,1,0:T(8,128)S(1)}, u32[]{:S(2)}, u32[]{:S(2)}) collective-permute-start(f32[2,8,512]{2,1,0:T(8,128)S(1)} %broadcast_in_dim.2.refs_0_.refs_1_), channel_id=1, source_target_pairs={{0,8},{8,16},{16,24},{24,32},{32,40},{40,48},{48,56},{56,64},{64,7... | collective-permute-start | bytes 98312 | tf_op jit(solution)/shard_map/ppermute | solution.py:27
  18.4 20.5 %copy-start.2 = (s32[1,1,1,2]{3,2,1,0:T(1,128)S(1)}, s32[1,1,1,2]{3,2,1,0:T(1,128)}, u32[]{:S(2)}) copy-start(s32[1,1,1,2]{3,2,1,0:T(1,128)} %param.8) | copy-start | bytes 28
  18.4 38.2 %collective-permute-start.4 = (f32[2,288,512]{2,1,0:T(8,128)S(1)}, f32[2,288,512]{2,1,0:T(8,128)S(1)}, u32[]{:S(2)}, u32[]{:S(2)}) collective-permute-start(f32[2,288,512]{2,1,0:T(8,128)S(1)} %get-tuple-element.33.refs_0_), channel_id=1, source_target_pairs={{8,0},{16,8},{24,16},{32,24},{40,32},{48,40},{56,48},{64,56},{72,6... | collective-permute-start | bytes 3538952 | tf_op jit(solution)/shard_map/ppermute | solution.py:27
  24.4 5.4 %collective-permute-start = (f32[2,8,512]{2,1,0:T(8,128)S(1)}, f32[2,8,512]{2,1,0:T(8,128)S(1)}, u32[]{:S(2)}, u32[]{:S(2)}) collective-permute-start(f32[2,8,512]{2,1,0:T(8,128)S(1)} %broadcast_in_dim.2.refs_0_.refs_1_), channel_id=1, source_target_pairs={{0,1},{1,2},{2,3},{3,4},{4,5},{5,6},{6,7},{8,9},{9,10},{10,11},{11... | collective-permute-start | bytes 98312 | tf_op jit(solution)/shard_map/ppermute | solution.py:27
  31.7 7.2 %copy-start.1 = (f32[2,512,512]{2,1,0:T(8,128)S(1)}, f32[2,512,512]{2,1,0:T(8,128)}, u32[]{:S(2)}) copy-start(f32[2,512,512]{2,1,0:T(8,128)} %refs_3_.1) | copy-start | bytes 6291460
  31.8 13.0 %collective-permute-start.5 = (f32[2,224,512]{2,1,0:T(8,128)S(1)}, f32[2,224,512]{2,1,0:T(8,128)S(1)}, u32[]{:S(2)}, u32[]{:S(2)}) collective-permute-start(f32[2,224,512]{2,1,0:T(8,128)S(1)} %get-tuple-element.36), channel_id=1, source_target_pairs={{1,0},{2,1},{3,2},{4,3},{5,4},{6,5},{7,6},{9,8},{10,9},{11,10},{12... | collective-permute-start | bytes 2752520 | tf_op jit(solution)/shard_map/ppermute | solution.py:27
  44.8 11.7 %copy-start = (f32[1,1,1,512,512]{4,3,2,1,0:T(8,128)S(1)}, f32[1,1,1,512,512]{4,3,2,1,0:T(8,128)}, u32[]{:S(2)}) copy-start(f32[1,1,1,512,512]{4,3,2,1,0:T(8,128)} %param.7) | copy-start | bytes 3145732
  61.1 15.6 %collective-permute-start.7 = (f32[2,288,512]{2,1,0:T(8,128)S(1)}, f32[2,288,512]{2,1,0:T(8,128)S(1)}, u32[]{:S(2)}, u32[]{:S(2)}) collective-permute-start(f32[2,288,512]{2,1,0:T(8,128)S(1)} %shard_map.60.refs_5_.refs_3_), channel_id=1, source_target_pairs={{1,0},{2,1},{3,2},{4,3},{5,4},{6,5},{7,6},{9,8},{10,9},{11,10},{12... | collective-permute-start | bytes 3538952 | tf_op jit(solution)/shard_map/ppermute | solution.py:27
  63.0 17.5 %collective-permute-start.6 = (f32[2,288,512]{2,1,0:T(8,128)S(1)}, f32[2,288,512]{2,1,0:T(8,128)S(1)}, u32[]{:S(2)}, u32[]{:S(2)}) collective-permute-start(f32[2,288,512]{2,1,0:T(8,128)S(1)} %shard_map.60.refs_5_.refs_3_), channel_id=1, source_target_pairs={{0,1},{1,2},{2,3},{3,4},{4,5},{5,6},{6,7},{8,9},{9,10},{10,11},{11... | collective-permute-start | bytes 3538952 | tf_op jit(solution)/shard_map/ppermute | solution.py:27
  65.4 27.2 %collective-permute-start.11 = (f32[2,224,512]{2,1,0:T(8,128)S(1)}, f32[2,224,512]{2,1,0:T(8,128)S(1)}, u32[]{:S(2)}, u32[]{:S(2)}) collective-permute-start(f32[2,224,512]{2,1,0:T(8,128)S(1)} %get-tuple-element.49.refs_6_.refs_15_), channel_id=1, source_target_pairs={{8,0},{16,8},{24,16},{32,24},{40,32},{48,40},{56,48},{64,56},{72,6... | collective-permute-start | bytes 2752520 | tf_op jit(solution)/shard_map/ppermute | solution.py:27
  71.9 27.2 %collective-permute-start.10 = (f32[2,224,512]{2,1,0:T(8,128)S(1)}, f32[2,224,512]{2,1,0:T(8,128)S(1)}, u32[]{:S(2)}, u32[]{:S(2)}) collective-permute-start(f32[2,224,512]{2,1,0:T(8,128)S(1)} %get-tuple-element.49.refs_6_.refs_15_), channel_id=1, source_target_pairs={{0,8},{8,16},{16,24},{24,32},{32,40},{40,48},{48,56},{56,64},{64,7... | collective-permute-start | bytes 2752520 | tf_op jit(solution)/shard_map/ppermute | solution.py:27
  82.6 41.6 %collective-permute-start.8 = (f32[2,288,512]{2,1,0:T(8,128)S(1)}, f32[2,288,512]{2,1,0:T(8,128)S(1)}, u32[]{:S(2)}, u32[]{:S(2)}) collective-permute-start(f32[2,288,512]{2,1,0:T(8,128)S(1)} %get-tuple-element.46), channel_id=1, source_target_pairs={{0,8},{8,16},{16,24},{24,32},{32,40},{40,48},{48,56},{56,64},{64,7... | collective-permute-start | bytes 3538952 | tf_op jit(solution)/shard_map/ppermute | solution.py:27
  84.9 39.3 %collective-permute-start.9 = (f32[2,288,512]{2,1,0:T(8,128)S(1)}, f32[2,288,512]{2,1,0:T(8,128)S(1)}, u32[]{:S(2)}, u32[]{:S(2)}) collective-permute-start(f32[2,288,512]{2,1,0:T(8,128)S(1)} %get-tuple-element.47.refs_0_), channel_id=1, source_target_pairs={{8,0},{16,8},{24,16},{32,24},{40,32},{48,40},{56,48},{64,56},{72,6... | collective-permute-start | bytes 3538952 | tf_op jit(solution)/shard_map/ppermute | solution.py:27
  101.1 14.7 %collective-permute-start.12 = (f32[2,224,512]{2,1,0:T(8,128)S(1)}, f32[2,224,512]{2,1,0:T(8,128)S(1)}, u32[]{:S(2)}, u32[]{:S(2)}) collective-permute-start(f32[2,224,512]{2,1,0:T(8,128)S(1)} %get-tuple-element.51), channel_id=1, source_target_pairs={{0,1},{1,2},{2,3},{3,4},{4,5},{5,6},{6,7},{8,9},{9,10},{10,11},{11... | collective-permute-start | bytes 2752520 | tf_op jit(solution)/shard_map/ppermute | solution.py:27
  103.0 14.5 %collective-permute-start.13 = (f32[2,224,512]{2,1,0:T(8,128)S(1)}, f32[2,224,512]{2,1,0:T(8,128)S(1)}, u32[]{:S(2)}, u32[]{:S(2)}) collective-permute-start(f32[2,224,512]{2,1,0:T(8,128)S(1)} %get-tuple-element.52), channel_id=1, source_target_pairs={{1,0},{2,1},{3,2},{4,3},{5,4},{6,5},{7,6},{9,8},{10,9},{11,10},{12... | collective-permute-start | bytes 2752520 | tf_op jit(solution)/shard_map/ppermute | solution.py:27
  128.8 17.5 %collective-permute-start.14 = (f32[2,288,512]{2,1,0:T(8,128)S(1)}, f32[2,288,512]{2,1,0:T(8,128)S(1)}, u32[]{:S(2)}, u32[]{:S(2)}) collective-permute-start(f32[2,288,512]{2,1,0:T(8,128)S(1)} %shard_map.65.refs_3_), channel_id=1, source_target_pairs={{0,1},{1,2},{2,3},{3,4},{4,5},{5,6},{6,7},{8,9},{9,10},{10,11},{11... | collective-permute-start | bytes 3538952 | tf_op jit(solution)/shard_map/ppermute | solution.py:27
  130.7 27.2 %collective-permute-start.16 = (f32[2,224,512]{2,1,0:T(8,128)S(1)}, f32[2,224,512]{2,1,0:T(8,128)S(1)}, u32[]{:S(2)}, u32[]{:S(2)}) collective-permute-start(f32[2,224,512]{2,1,0:T(8,128)S(1)} %get-tuple-element.56.refs_4_), channel_id=1, source_target_pairs={{0,8},{8,16},{16,24},{24,32},{32,40},{40,48},{48,56},{56,64},{64,7... | collective-permute-start | bytes 2752520 | tf_op jit(solution)/shard_map/ppermute | solution.py:27
  147.0 35.1 %collective-permute-start.15 = (f32[2,288,512]{2,1,0:T(8,128)S(1)}, f32[2,288,512]{2,1,0:T(8,128)S(1)}, u32[]{:S(2)}, u32[]{:S(2)}) collective-permute-start(f32[2,288,512]{2,1,0:T(8,128)S(1)} %get-tuple-element.55.refs_0_), channel_id=1, source_target_pairs={{0,8},{8,16},{16,24},{24,32},{32,40},{40,48},{48,56},{56,64},{64,7... | collective-permute-start | bytes 3538952 | tf_op jit(solution)/shard_map/ppermute | solution.py:27
  158.3 14.7 %collective-permute-start.17 = (f32[2,224,512]{2,1,0:T(8,128)S(1)}, f32[2,224,512]{2,1,0:T(8,128)S(1)}, u32[]{:S(2)}, u32[]{:S(2)}) collective-permute-start(f32[2,224,512]{2,1,0:T(8,128)S(1)} %get-tuple-element.58), channel_id=1, source_target_pairs={{0,1},{1,2},{2,3},{3,4},{4,5},{5,6},{6,7},{8,9},{9,10},{10,11},{11... | collective-permute-start | bytes 2752520 | tf_op jit(solution)/shard_map/ppermute | solution.py:27

commit v3 on v2

v3 whole, which is shorter than its diff:
```python
import functools
import math

import jax
import jax.numpy as jnp
from jax import lax
from jax.experimental import pallas as pl
from jax.experimental.pallas import tpu as pltpu
from jax.sharding import PartitionSpec as P

STEP = 0.5
FLOOR = 0.05
VMEM = pl.BlockSpec(memory_space=pltpu.VMEM)
ANY = pl.BlockSpec(memory_space=pl.ANY)
SMEM = pl.BlockSpec(memory_space=pltpu.SMEM)
LIMIT = 12 * 1024 * 1024
F32 = jnp.float32
BF16 = jnp.bfloat16

EXTRA = 8
HEAD = 240
HEAD_PIECES = 1
TAIL_PIECES = 2


def shifted(value, axis, steps):
    count = lax.axis_size(axis)
    leading, last = (max(0, -steps), min(count, count - steps))
    return lax.ppermute(value, axis, [(source, source + steps) for source in range(leading, last)])


def dft_tables(width):
    index = jnp.arange(width, dtype=jnp.int32)
    phase = index[:, None] * index[None, :] % width
    angle = phase.astype(jnp.float32) * (2.0 * math.pi / width)
    scale = 1.0 / math.sqrt(width)
    return (
        (jnp.cos(angle) * scale).astype(jnp.bfloat16),
        (jnp.sin(angle) * scale).astype(jnp.bfloat16),
    )


def call(kernel, outs, arrays, scratch=(), scalars=(), after=()):
    flat, tree = jax.tree.flatten(tuple(arrays))
    out_flat, out_tree = jax.tree.flatten(tuple(outs))
    skip, count = len(after), len(scalars)

    def body(*refs):
        refs = refs[skip:]
        numbers, refs = refs[:count], refs[count:]
        given = jax.tree.unflatten(tree, refs[: len(flat)])
        made = jax.tree.unflatten(out_tree, refs[len(flat) : len(flat) + len(out_flat)])
        kernel(*numbers, *given, *made, *refs[len(flat) + len(out_flat) :])

    results = pl.pallas_call(
        body,
        out_shape=out_flat,
        in_specs=[ANY] * skip + [SMEM] * count + [VMEM] * len(flat),
        out_specs=[VMEM] * len(out_flat),
        scratch_shapes=list(scratch),
        compiler_params=pltpu.CompilerParams(vmem_limit_bytes=LIMIT),
    )(*after, *scalars, *flat)
    return jax.tree.unflatten(out_tree, results)


def split(first, width):
    height, count = (HEAD, HEAD_PIECES) if first == 0 else (width - HEAD, TAIL_PIECES)
    size = height // count
    return [(k, first + k * size, slice(k * size, (k + 1) * size)) for k in range(count)]


def part(half, plane, k, rows):
    if isinstance(half, list):
        return half[k][plane, : rows.stop - rows.start, :]
    return half[plane, rows, :]


def put(half, plane, k, rows, value):
    if isinstance(half, list):
        half[k][plane, : rows.stop - rows.start, :] = value
    else:
        half[plane, rows, :] = value


def indices(rows, width, first):
    shape = (rows.stop - rows.start, width)
    return (
        lax.broadcasted_iota(jnp.int32, shape, 0) + first,
        lax.broadcasted_iota(jnp.int32, shape, 1),
    )


def low(i, place):
    return i + 1 < place[0, :1, :].astype(jnp.int32)


def far(j, place):
    return j + 1 < place[1, :1, :].astype(jnp.int32)


def ways_of(head, rows, width, first):
    i, j = indices(rows, width, first)
    pair = (functools.partial(low, i), functools.partial(far, j))
    return pair if head else pair[::-1]


def absent(place):
    return place[0, :1, :] == 0.0


def prepare_kernel(offset, cos_ref, sin_ref, pupil_ref, bx, bxt, by, byt_head, byt_tail, pupil_out):
    w = cos_ref.shape[0]
    h = HEAD
    cosine = cos_ref[...].astype(F32)
    sine = sin_ref[...].astype(F32)
    oy, ox = offset[0, 0], offset[0, 1]

    def rolled(value, shift, axis):
        return pltpu.roll(value, shift, axis)

    c, s = rolled(cosine, ox, 0).astype(BF16), rolled(sine, ox, 0).astype(BF16)
    bx[:w, :w], bx[:w, w:], bx[w:, :w], bx[w:, w:] = c, s, -s, c
    c, s = rolled(cosine, ox, 1).astype(BF16), rolled(sine, ox, 1).astype(BF16)
    bxt[:w, :w], bxt[:w, w:], bxt[w:, :w], bxt[w:, w:] = c, -s, s, c
    c, s = rolled(cosine, oy, 0).astype(BF16), rolled(sine, oy, 0).astype(BF16)
    by[:w, :w], by[:w, w:], by[w:, :w], by[w:, w:] = c, s, -s, c
    c, s = rolled(cosine, oy, 1).astype(BF16), rolled(sine, oy, 1).astype(BF16)
    for out, cols in ((byt_head, slice(0, h)), (byt_tail, slice(h, w))):
        n = cols.stop - cols.start
        out[:w, :n], out[:w, n:] = c[:, cols], -s[:, cols]
        out[w:, :n], out[w:, n:] = s[:, cols], c[:, cols]
    for plane in range(2):
        pupil_out[plane] = rolled(rolled(pupil_ref[plane], oy, 0), ox, 1)


def dot(a, b):
    return jnp.dot(a, b, preferred_element_type=F32)


def right_product(first, window, pupil, bx, left, half):
    w = bx.shape[0] // 2
    h = half.shape[0] // 2
    for k, row, rows in split(first, w):
        wr, wi = window(k, row, rows)
        across = slice(row, row + rows.stop - rows.start)
        pr, pi = pupil[0, across, :], pupil[1, across, :]
        left[rows, :w] = (wr * pr - wi * pi).astype(BF16)
        left[rows, w:] = (wr * pi + wi * pr).astype(BF16)
    half[:h, :] = dot(left[:h, :], bx[:, :w]).astype(BF16)
    half[h:, :] = dot(left[:h, :], bx[:, w:]).astype(BF16)


def finish(acc, byt_tail, half, amp, live, bxt, left, stacked):
    w = amp.shape[0]
    block = 128
    alive = (live[0, 0] > 0).astype(F32)
    for first in range(0, w, block):
        rows = slice(first, first + block)
        lower = slice(w + first, w + first + block)
        wave_r = acc[rows, :] + dot(byt_tail[rows, :], half[...])
        wave_i = acc[lower, :] + dot(byt_tail[lower, :], half[...])
        power = jnp.maximum(wave_r * wave_r + wave_i * wave_i, FLOOR * FLOOR)
        keep = (1.0 - amp[rows, :] * lax.rsqrt(power)) * alive
        left[rows, :w] = (wave_r * keep).astype(BF16)
        left[rows, w:] = (wave_i * keep).astype(BF16)
    stacked[:w, :] = dot(left[...], bxt[:, :w]).astype(BF16)
    stacked[w:, :] = dot(left[...], bxt[:, w:]).astype(BF16)


def back(first, by, stacked, pupil, out, extra):
    w = stacked.shape[1]
    for k, row, rows in split(first, w):
        size = rows.stop - rows.start
        back_r = dot(by[row : row + size, :], stacked[...])
        back_i = dot(by[w + row : w + row + size, :], stacked[...])
        pr, pi = pupil[0, row : row + size, :], pupil[1, row : row + size, :]
        grad_r = back_r * pr + back_i * pi
        grad_i = back_i * pr - back_r * pi
        if extra is not None:
            grad_r = grad_r + part(extra, 0, k, rows)
            grad_i = grad_i + part(extra, 1, k, rows)
        put(out, 0, k, rows, grad_r)
        put(out, 1, k, rows, grad_i)


def gathered(head, place, tile, one, both, kept):
    def window(k, row, rows):
        first_way, second_way = ways_of(head, rows, kept.shape[2], row)
        a, b = first_way(place), second_way(place)
        values = []
        for plane in range(2):
            near = jnp.where(a, part(one, plane, k, rows), part(tile, plane, k, rows))
            value = jnp.where(b, part(both, plane, k, rows), near)
            kept[plane, rows, :] = value
            values.append(value)
        return values

    return window


def updated(head, place, edge_row, edge_col, kept, own, minus, plus):
    def window(k, row, rows):
        i, j = indices(rows, kept.shape[2], row)
        a, b = low(i, place), far(j, place)
        outside = (a & absent(edge_row)) | (b & absent(edge_col))
        second = b if head else a
        values = []
        for plane in range(2):
            near = jnp.where(second, part(plus, plane, k, rows), part(minus, plane, k, rows))
            value = kept[plane, rows, :] - STEP * (own[plane, rows, :] + near)
            values.append(jnp.where(outside, 0.0, value))
        return values

    return window


def open_first(first, place, tile, one, both, pupil, bx, byt, kept, acc, right_of, left, half):
    right_product(first, gathered(True, place, tile, one, both, kept), pupil, bx, left, half)
    acc[...] = dot(byt[...], half[...])
    right_of[...] = both[-1][:, both[-1].shape[1] - EXTRA :, :]


def close_first(
    first, live, place, tile, one, both, acc, pupil, amp, bx, byt, bxt, by, kept, under, stacked, out, left, half
):
    right_product(first, gathered(False, place, tile, one, both, kept), pupil, bx, left, half)
    finish(acc, byt, half, amp, live, bxt, left, stacked)
    back(0, by, stacked, pupil, out, None)
    under[...] = both[:, both.shape[1] - EXTRA :, :]


def open_second(
    first, place, edge_row, edge_col, kept, own, minus, plus, pupil, bx, byt, acc, left, half
):
    window = updated(True, place, edge_row, edge_col, kept, own, minus, plus)
    right_product(first, window, pupil, bx, left, half)
    acc[...] = dot(byt[...], half[...])


def close_second(
    first, live, place, edge_row, edge_col, kept, own, minus, plus, acc, pupil, amp, bx, byt, bxt, by,
    extra, stacked, out, left, half
):
    window = updated(False, place, edge_row, edge_col, kept, own, minus, plus)
    right_product(first, window, pupil, bx, left, half)
    finish(acc, byt, half, amp, live, bxt, left, stacked)
    back(0, by, stacked, pupil, out, extra)


def rest_first(first, by, stacked, pupil, out):
    back(first, by, stacked, pupil, out, None)


def rest_second(first, by, stacked, pupil, extra, out):
    back(first, by, stacked, pupil, out, extra)


def compose_kernel(first, head, me, target, tile, one, out):
    w = me.shape[2]
    for k, row, rows in split(first, w):
        mask = ways_of(head, rows, w, row)[0](target)
        for plane in range(2):
            value = jnp.where(mask, part(one, plane, k, rows), part(tile, plane, k, rows))
            put(out, plane, k, rows, value)
    end = out[-1] if head else out
    end[:, end.shape[1] - EXTRA :, :] = me[...]


def between_kernel(
    first, head, me, minus, plus, target_minus, target_plus, mine, got_minus, got_plus, to_minus, to_plus, own
):
    w = me.shape[2]
    for k, row, rows in split(first, w):
        ways = ways_of(head, rows, w, row)
        f, f_minus, f_plus = (ways[0](x) for x in (me, minus, plus))
        s, s_minus, s_plus = (ways[1](x) for x in (me, minus, plus))

        def seen(goal):
            return f == goal, ~goal & f_minus, goal & ~f_plus

        minus_m = [a & ~b for a, b in zip(seen(ways[0](target_minus)), (s, s_minus, s_plus))]
        plus_m = [a & b for a, b in zip(seen(ways[0](target_plus)), (s, s_minus, s_plus))]
        _, own_minus, own_plus = seen(f)
        own_minus, own_plus = own_minus & (s == s_minus), own_plus & (s == s_plus)
        for plane in range(2):
            values = [part(x, plane, k, rows) for x in (mine, got_minus, got_plus)]
            for out, masks in ((to_minus, minus_m), (to_plus, plus_m)):
                terms = [jnp.where(m, v, 0.0) for m, v in zip(masks, values)]
                put(out, plane, k, rows, terms[0] + terms[1] + terms[2])
            others = jnp.where(own_minus, values[1], 0.0) + jnp.where(own_plus, values[2], 0.0)
            put(own, plane, k, rows, values[0] + others)


def final_kernel(first, head, me, minus, tile, mine, got, to_plus, base):
    w = me.shape[2]
    for k, row, rows in split(first, w):
        ways = ways_of(head, rows, w, row)
        f, f_minus = ways[0](me), ways[0](minus)
        s, s_minus = ways[1](me), ways[1](minus)
        for plane in range(2):
            own = jnp.where(f, 0.0, part(mine, plane, k, rows))
            other = jnp.where(f_minus, part(got, plane, k, rows), 0.0)
            put(to_plus, plane, k, rows, jnp.where(s, own, 0.0) + jnp.where(s_minus, other, 0.0))
            kept = jnp.where(s, 0.0, own) + jnp.where(s_minus, 0.0, other)
            base[plane, rows, :] = part(tile, plane, k, rows) - STEP * kept


def store(first, base, got, whole, previous=None):
    _, h, w = base.shape
    held = () if previous is None else (previous,)
    got = got if isinstance(got, list) else [got]

    def kernel(base, *refs):
        pieces = refs[: len(got)]
        out, value, sems = refs[-3:]
        copies, row = [], 0
        for k, piece in enumerate(pieces):
            size = piece.shape[1]
            rows = slice(row, row + size)
            value[:, rows, :] = base[:, rows, :] - STEP * piece[...]
            copy = pltpu.make_async_copy(
                value.at[:, pl.ds(row, size), :], out.at[:, pl.ds(first + row, size), :], sems.at[k]
            )
            copy.start()
            copies.append(copy)
            row += size
        for copy in copies:
            copy.wait()

    return pl.pallas_call(
        kernel,
        out_shape=whole,
        in_specs=[VMEM] * (1 + len(got)) + [ANY] * len(held),
        out_specs=ANY,
        scratch_shapes=[pltpu.VMEM((2, h, w), F32), pltpu.SemaphoreType.DMA((len(got),))],
        input_output_aliases={1 + len(got): 0} if held else {},
        compiler_params=pltpu.CompilerParams(vmem_limit_bytes=LIMIT),
    )(base, *got, *held)


def on_device(spectrum, pupil, amplitudes, offsets, counts):
    w = pupil.shape[1]
    h = HEAD
    amp = amplitudes[0, 0, 0]
    offset = offsets[0, 0]

    def block(rows):
        return jax.ShapeDtypeStruct((2, rows, w), F32)

    head_half, tail_half, whole, spot = block(h), block(w - h), block(w), block(EXTRA)
    head_pieces, tail_pieces = (
        [block(rows.stop - rows.start) for _, _, rows in split(first, w)] for first in (0, h)
    )
    me = jnp.broadcast_to((offset[0] + 1).astype(F32)[:, None, None], (2, EXTRA, w))
    head = spectrum[:, :h]
    tail = [spectrum[:, h + rows.start : h + rows.stop] for _, _, rows in split(h, w)]

    def each(values, axis, steps):
        return [shifted(value, axis, steps) for value in values]

    head_below = shifted(head, "row", -1)
    tail_right = each(tail, "col", -1)
    above = shifted(me, "row", 1)
    left_of = shifted(me, "col", 1)

    cosine, sine = dft_tables(w)
    square = jax.ShapeDtypeStruct((2 * w, 2 * w), BF16)
    stack = jax.ShapeDtypeStruct((2 * w, w), BF16)
    narrow = [jax.ShapeDtypeStruct((2 * w, 2 * n), BF16) for n in (h, w - h)]
    bx, bxt, by, byt_head, byt_tail, rolled = call(
        prepare_kernel, [square] * 3 + narrow + [whole], (cosine, sine, pupil), scalars=(offset,)
    )

    (tail_made,) = call(
        functools.partial(compose_kernel, h, False), [block(w - h + EXTRA)], (me, above, tail, tail_right)
    )
    tail_both = shifted(tail_made, "row", -1)
    (head_made,) = call(
        functools.partial(compose_kernel, 0, True),
        [head_pieces[:-1] + [block(head_pieces[-1].shape[1] + EXTRA)]],
        (me, left_of, head, head_below),
        after=(tail_made,),
    )
    head_both = each(head_made, "col", -1)

    total = jax.ShapeDtypeStruct((2 * w, w), F32)
    products = [pltpu.VMEM((2 * n, w), BF16) for n in (h, w - h)]
    left_half, left_whole = pltpu.VMEM((h, 2 * w), BF16), pltpu.VMEM((w, 2 * w), BF16)
    head_kept, acc, right_of = call(
        functools.partial(open_first, 0),
        [head_half, total, spot],
        (me, head, head_below, head_both, rolled, bx, byt_head),
        (left_half, products[0]),
    )
    tail_kept, under, stacked, head_grad = call(
        functools.partial(close_first, h),
        [tail_half, spot, stack, head_half],
        (me, tail, tail_right, tail_both, acc, rolled, amp, bx, byt_tail, bxt, by),
        (left_whole, products[1]),
        scalars=(counts,),
    )

    got_above, got_under = shifted(head_grad, "row", 1), shifted(head_grad, "row", -1)
    (tail_grad,) = call(functools.partial(rest_first, h), [tail_pieces], (by, stacked, rolled))
    got_left, got_right = each(tail_grad, "col", 1), each(tail_grad, "col", -1)
    to_up, to_down, tail_own = call(
        functools.partial(between_kernel, h, False),
        [tail_half] * 3,
        (me, left_of, right_of, above, under, tail_grad, got_left, got_right),
    )
    tail_sums = (tail_own, shifted(to_down, "row", 1), shifted(to_up, "row", -1))
    to_left, to_right, head_own = call(
        functools.partial(between_kernel, 0, True),
        [head_pieces, head_pieces, head_half],
        (me, above, under, left_of, right_of, head_grad, got_above, got_under),
        after=(to_up,),
    )
    head_sums = (head_own, each(to_right, "col", 1), each(to_left, "col", -1))

    (acc,) = call(
        functools.partial(open_second, 0),
        [total],
        (me, under, right_of, head_kept, *head_sums, rolled, bx, byt_head),
        (left_half, products[0]),
    )
    stacked, head_total = call(
        functools.partial(close_second, h),
        [stack, head_half],
        (me, under, right_of, tail_kept, *tail_sums, acc, rolled, amp, bx, byt_tail, bxt, by, head_grad),
        (left_whole, products[1]),
        scalars=(counts,),
    )

    head_above = shifted(head_total, "row", 1)
    (tail_total,) = call(
        functools.partial(rest_second, h), [tail_pieces], (by, stacked, rolled, tail_grad)
    )
    tail_left = each(tail_total, "col", 1)
    tail_down, tail_base = call(
        functools.partial(final_kernel, h, False), [tail_half] * 2, (me, left_of, tail, tail_total, tail_left)
    )
    tail_got = shifted(tail_down, "row", 1)
    head_right, head_base = call(
        functools.partial(final_kernel, 0, True),
        [head_pieces, head_half],
        (me, above, head, head_total, head_above),
        after=(tail_down,),
    )
    head_got = each(head_right, "col", 1)
    partial = store(0, head_base, head_got, whole)
    return store(h, tail_base, tail_got, whole, partial)


def solution(mesh):
    in_specs = (
        P(None, "row", "col"),
        P(),
        P("row", "col", None, None, None),
        P("row", "col", None, None),
        P("row", "col"),
    )
    out_specs = P(None, "row", "col")
    return jax.shard_map(
        on_device, mesh=mesh, in_specs=in_specs, out_specs=out_specs, check_vma=False
    )
```

time: 185 us -> 175 us (0.946)
  waiting for transfers between devices: 93.9 us -> 77.4 us
  starting transfers between devices: 56.4 us -> 62.8 us
    ppermute x18 -> x22, waiting for transfers between devices: 93.9 us -> 77.4 us  [shifted(): lax.ppermute(value, axis, [(source, source + steps) for source in range(l...]
    ppermute x18 -> x22, starting transfers between devices: 56.4 us -> 62.8 us  [shifted(): lax.ppermute(value, axis, [(source, source + steps) for source in range(l...]
  transfers between devices with their start and end apart: 18 -> 22, of which waited for: 15 -> 16; matrix products, arithmetic and copies ran while one was open for 2% -> 3% of each run, Pallas kernels for 8% -> 9%
where the time goes in v3:
time: 175 us; the launch traced here: 174 us
  waiting for transfers between devices  77.4 us (44%)
  starting transfers between devices  62.8 us (36%)
  Pallas kernels  25.6 us (15%)
  other arithmetic  4.4 us (3%)
  local copies, waits for them, and re-layouts  2.66 us (2%)
    ppermute x22, waiting for transfers between devices, shifted(): lax.ppermute(value, axis, [(source, source + steps) for source in range(l...  77.4 us
    ppermute x22, starting transfers between devices, shifted(): lax.ppermute(value, axis, [(source, source + steps) for source in range(l...  62.8 us
    pallas_call x13, Pallas kernels, call(): pl.pallas_call(body, out_shape=out_flat, in_specs=[ANY] * skip + [SMEM] *...  23.4 us
    convert_element_type x1, other arithmetic, dft_tables(): (jnp.sin(angle) * scale).astype(jnp.bfloat16)  4.39 us
  transfers between devices with their start and end apart: 22, of which 16 were waited for; matrix products, arithmetic and copies ran while one was open for 3% of the time, Pallas kernels for 9%

profile of v3, /device:TPU:28, one launch (start us, length us, event | category | flops | bytes accessed | tf_op | source)
XLA Modules:
  0.0 173.9 jit_solution(10645929227944210717)
XLA Ops:
  0.0 1.3 slice.11.refs_3_.refs_1_
  1.3 6.1 %collective-permute-start.5 = (f32[2,240,512]{2,1,0:T(8,128)S(1)}, f32[2,240,512]{2,1,0:T(8,128)S(1)}, u32[]{:S(2)}, u32[]{:S(2)}) collective-permute-start(f32[2,240,512]{2,1,0:T(8,128)S(1)} %slice.11.refs_3_.refs_1_), channel_id=1, source_target_pairs={{8,0},{16,8},{24,16},{32,24},{40,32},{48,40},{56,48},{64,56},{72,6... | collective-permute-start | bytes 2949128 | tf_op jit(solution)/shard_map/ppermute | solution.py:29
  7.4 1.3 fusion.6
  8.7 1.9 %collective-permute-start.2 = (f32[2,136,512]{2,1,0:T(8,128)S(1)}, f32[2,136,512]{2,1,0:T(8,128)S(1)}, u32[]{:S(2)}, u32[]{:S(2)}) collective-permute-start(f32[2,136,512]{2,1,0:T(8,128)S(1)} %get-tuple-element.63.refs_3_), channel_id=1, source_target_pairs={{1,0},{2,1},{3,2},{4,3},{5,4},{6,5},{7,6},{9,8},{10,9},{11,10},{12... | collective-permute-start | bytes 1671176 | tf_op jit(solution)/shard_map/ppermute | solution.py:29
  10.7 2.5 %collective-permute-start.1 = (f32[2,136,512]{2,1,0:T(8,128)S(1)}, f32[2,136,512]{2,1,0:T(8,128)S(1)}, u32[]{:S(2)}, u32[]{:S(2)}) collective-permute-start(f32[2,136,512]{2,1,0:T(8,128)S(1)} %get-tuple-element.64.refs_2_), channel_id=1, source_target_pairs={{1,0},{2,1},{3,2},{4,3},{5,4},{6,5},{7,6},{9,8},{10,9},{11,10},{12... | collective-permute-start | bytes 1671176 | tf_op jit(solution)/shard_map/ppermute | solution.py:29
  13.3 1.9 %collective-permute-start.3 = (f32[2,8,512]{2,1,0:T(8,128)S(1)}, f32[2,8,512]{2,1,0:T(8,128)S(1)}, u32[]{:S(2)}, u32[]{:S(2)}) collective-permute-start(f32[2,8,512]{2,1,0:T(8,128)S(1)} %broadcast_in_dim.2.refs_0_.refs_1_), channel_id=1, source_target_pairs={{0,8},{8,16},{16,24},{24,32},{32,40},{40,48},{48,56},{56,64},{64,7... | collective-permute-start | bytes 98312 | tf_op jit(solution)/shard_map/ppermute | solution.py:29
  15.2 6.0 %collective-permute-done.3.refs_1_.refs_3_.refs_2_ = f32[2,8,512]{2,1,0:T(8,128)S(1)} collective-permute-done((f32[2,8,512]{2,1,0:T(8,128)S(1)}, f32[2,8,512]{2,1,0:T(8,128)S(1)}, u32[]{:S(2)}, u32[]{:S(2)}) %collective-permute-start.3) | collective-permute-done | bytes 32800 | tf_op jit(solution)/shard_map/ppermute | solution.py:29
  21.2 2.4 %collective-permute-done.1.refs_4_ = f32[2,136,512]{2,1,0:T(8,128)S(1)} collective-permute-done((f32[2,136,512]{2,1,0:T(8,128)S(1)}, f32[2,136,512]{2,1,0:T(8,128)S(1)}, u32[]{:S(2)}, u32[]{:S(2)}) %collective-permute-start.1) | collective-permute-done | bytes 557088 | tf_op jit(solution)/shard_map/ppermute | solution.py:29
  23.8 2.3 %collective-permute-start.4 = (f32[2,280,512]{2,1,0:T(8,128)S(1)}, f32[2,280,512]{2,1,0:T(8,128)S(1)}, u32[]{:S(2)}, u32[]{:S(2)}) collective-permute-start(f32[2,280,512]{2,1,0:T(8,128)S(1)} %shard_map.56.refs_0_), channel_id=1, source_target_pairs={{8,0},{16,8},{24,16},{32,24},{40,32},{48,40},{56,48},{64,56},{72,6... | collective-permute-start | bytes 3440648 | tf_op jit(solution)/shard_map/ppermute | solution.py:29
  26.1 3.4 %collective-permute-start = (f32[2,8,512]{2,1,0:T(8,128)S(1)}, f32[2,8,512]{2,1,0:T(8,128)S(1)}, u32[]{:S(2)}, u32[]{:S(2)}) collective-permute-start(f32[2,8,512]{2,1,0:T(8,128)S(1)} %broadcast_in_dim.2.refs_0_.refs_1_), channel_id=1, source_target_pairs={{0,1},{1,2},{2,3},{3,4},{4,5},{5,6},{6,7},{8,9},{9,10},{10,11},{11... | collective-permute-start | bytes 98312 | tf_op jit(solution)/shard_map/ppermute | solution.py:29
  29.5 2.0 %collective-permute-done.refs_2_.refs_1_.refs_4_ = f32[2,8,512]{2,1,0:T(8,128)S(1)} collective-permute-done((f32[2,8,512]{2,1,0:T(8,128)S(1)}, f32[2,8,512]{2,1,0:T(8,128)S(1)}, u32[]{:S(2)}, u32[]{:S(2)}) %collective-permute-start) | collective-permute-done | bytes 32800 | tf_op jit(solution)/shard_map/ppermute | solution.py:29
  31.6 2.1 %collective-permute-start.6 = (f32[2,248,512]{2,1,0:T(8,128)S(1)}, f32[2,248,512]{2,1,0:T(8,128)S(1)}, u32[]{:S(2)}, u32[]{:S(2)}) collective-permute-start(f32[2,248,512]{2,1,0:T(8,128)S(1)} %shard_map.57), channel_id=1, source_target_pairs={{1,0},{2,1},{3,2},{4,3},{5,4},{6,5},{7,6},{9,8},{10,9},{11,10},{12... | collective-permute-start | bytes 3047432 | tf_op jit(solution)/shard_map/ppermute | solution.py:29
  34.3 4.4 %multiply_convert_fusion = (bf16[512,512]{1,0:T(8,128)(2,1)S(1)}, bf16[512,512]{1,0:T(8,128)(2,1)S(1)}) fusion(), kind=kLoop, calls=%fused_computation.6 | loop fusion | flops 4718592 | bytes 1048576 | tf_op jit(solution)/shard_map/convert_element_type | solution.py:39
  38.7 5.9 %shard_map.55 = (bf16[1024,1024]{1,0:T(8,128)(2,1)S(1)}, bf16[1024,1024]{1,0:T(8,128)(2,1)S(1)}, bf16[1024,1024]{1,0:T(8,128)(2,1)S(1)}, bf16[1024,480]{1,0:T(8,...) custom-call(s32[1,2]{1,0:T(1,128)S(1)} %bitcast.6, ...), custom_call_target="tpu_custom_call" | custom-call | tf_op jit(solution)/shard_map/pallas_call | solution.py:55
  45.6 1.6 shard_map.58
  47.2 5.8 %collective-permute-done.4.refs_6_ = f32[2,280,512]{2,1,0:T(8,128)S(1)} collective-permute-done((f32[2,280,512]{2,1,0:T(8,128)S(1)}, f32[2,280,512]{2,1,0:T(8,128)S(1)}, u32[]{:S(2)}, u32[]{:S(2)}) %collective-permute-start.4) | collective-permute-done | bytes 1146912 | tf_op jit(solution)/shard_map/ppermute | solution.py:29
  53.0 3.7 %shard_map.59 = (f32[2,272,512]{2,1,0:T(8,128)S(1)}, f32[2,8,512]{2,1,0:T(8,128)S(1)}, bf16[1024,512]{1,0:T(8,128)(2,1)S(1)}, f32[2,240,512]{2,1,0:T(8,128)S(1)}) custom-call(s32[1,1]{1,0:T(1,128)S(6)} %copy.8.refs_0_, f32[2,8,512]{2,1,0:T(8,128)S(1)} %broadcast_in_dim.2.refs_0_.refs_1_, f32[2,136,512]{2,1,0:T(8,128)S(1)} %get-tuple-element.64.refs_2_, ...), custom_call_target="tpu_custom_call" | custom-call | tf_op jit(solution)/shard_map/pallas_call | solution.py:55
  57.6 2.6 %collective-permute-start.9 = (f32[2,136,512]{2,1,0:T(8,128)S(1)}, f32[2,136,512]{2,1,0:T(8,128)S(1)}, u32[]{:S(2)}, u32[]{:S(2)}) collective-permute-start(f32[2,136,512]{2,1,0:T(8,128)S(1)} %get-tuple-element.45.refs_5_.refs_3_), channel_id=1, source_target_pairs={{1,0},{2,1},{3,2},{4,3},{5,4},{6,5},{7,6},{9,8},{10,9},{11,10},{12... | collective-permute-start | bytes 1671176 | tf_op jit(solution)/shard_map/ppermute | solution.py:29
  60.2 5.9 %collective-permute-start.14 = (f32[2,240,512]{2,1,0:T(8,128)S(1)}, f32[2,240,512]{2,1,0:T(8,128)S(1)}, u32[]{:S(2)}, u32[]{:S(2)}) collective-permute-start(f32[2,240,512]{2,1,0:T(8,128)S(1)} %get-tuple-element.51.refs_6_.refs_15_), channel_id=1, source_target_pairs={{8,0},{16,8},{24,16},{32,24},{40,32},{48,40},{56,48},{64,56},{72,6... | collective-permute-start | bytes 2949128 | tf_op jit(solution)/shard_map/ppermute | solution.py:29
  66.1 1.9 %collective-permute-start.13 = (f32[2,240,512]{2,1,0:T(8,128)S(1)}, f32[2,240,512]{2,1,0:T(8,128)S(1)}, u32[]{:S(2)}, u32[]{:S(2)}) collective-permute-start(f32[2,240,512]{2,1,0:T(8,128)S(1)} %get-tuple-element.51.refs_6_.refs_15_), channel_id=1, source_target_pairs={{0,8},{8,16},{16,24},{24,32},{32,40},{40,48},{48,56},{56,64},{64,7... | collective-permute-start | bytes 2949128 | tf_op jit(solution)/shard_map/ppermute | solution.py:29
  68.0 2.0 %collective-permute-start.7 = (f32[2,136,512]{2,1,0:T(8,128)S(1)}, f32[2,136,512]{2,1,0:T(8,128)S(1)}, u32[]{:S(2)}, u32[]{:S(2)}) collective-permute-start(f32[2,136,512]{2,1,0:T(8,128)S(1)} %get-tuple-element.45.refs_5_.refs_3_), channel_id=1, source_target_pairs={{0,1},{1,2},{2,3},{3,4},{4,5},{5,6},{6,7},{8,9},{9,10},{10,11},{11... | collective-permute-start | bytes 1671176 | tf_op jit(solution)/shard_map/ppermute | solution.py:29
  70.0 3.6 %collective-permute-start.10 = (f32[2,136,512]{2,1,0:T(8,128)S(1)}, f32[2,136,512]{2,1,0:T(8,128)S(1)}, u32[]{:S(2)}, u32[]{:S(2)}) collective-permute-start(f32[2,136,512]{2,1,0:T(8,128)S(1)} %get-tuple-element.46.refs_6_.refs_4_), channel_id=1, source_target_pairs={{1,0},{2,1},{3,2},{4,3},{5,4},{6,5},{7,6},{9,8},{10,9},{11,10},{12... | collective-permute-start | bytes 1671176 | tf_op jit(solution)/shard_map/ppermute | solution.py:29
  73.6 2.1 %collective-permute-start.8 = (f32[2,136,512]{2,1,0:T(8,128)S(1)}, f32[2,136,512]{2,1,0:T(8,128)S(1)}, u32[]{:S(2)}, u32[]{:S(2)}) collective-permute-start(f32[2,136,512]{2,1,0:T(8,128)S(1)} %get-tuple-element.46.refs_6_.refs_4_), channel_id=1, source_target_pairs={{0,1},{1,2},{2,3},{3,4},{4,5},{5,6},{6,7},{8,9},{9,10},{10,11},{11... | collective-permute-start | bytes 1671176 | tf_op jit(solution)/shard_map/ppermute | solution.py:29
  75.7 3.2 %collective-permute-done.7.refs_7_ = f32[2,136,512]{2,1,0:T(8,128)S(1)} collective-permute-done((f32[2,136,512]{2,1,0:T(8,128)S(1)}, f32[2,136,512]{2,1,0:T(8,128)S(1)}, u32[]{:S(2)}, u32[]{:S(2)}) %collective-permute-start.7) | collective-permute-done | bytes 557088 | tf_op jit(solution)/shard_map/ppermute | solution.py:29
  78.9 1.8 %collective-permute-done.10.refs_10_ = f32[2,136,512]{2,1,0:T(8,128)S(1)} collective-permute-done((f32[2,136,512]{2,1,0:T(8,128)S(1)}, f32[2,136,512]{2,1,0:T(8,128)S(1)}, u32[]{:S(2)}, u32[]{:S(2)}) %collective-permute-start.10) | collective-permute-done | bytes 557088 | tf_op jit(solution)/shard_map/ppermute | solution.py:29
  80.6 4.2 %collective-permute-done.8.refs_8_ = f32[2,136,512]{2,1,0:T(8,128)S(1)} collective-permute-done((f32[2,136,512]{2,1,0:T(8,128)S(1)}, f32[2,136,512]{2,1,0:T(8,128)S(1)}, u32[]{:S(2)}, u32[]{:S(2)}) %collective-permute-start.8) | collective-permute-done | bytes 557088 | tf_op jit(solution)/shard_map/ppermute | solution.py:29
  84.9 1.9 %shard_map.61 = (f32[2,272,512]{2,1,0:T(8,128)S(1)}, f32[2,272,512]{2,1,0:T(8,128)S(1)}, f32[2,272,512]{2,1,0:T(8,128)S(1)}) custom-call(f32[2,8,512]{2,1,0:T(8,128)S(1)} %broadcast_in_dim.2.refs_0_.refs_1_, f32[2,8,512]{2,1,0:T(8,128)S(1)} %collective-permute-done.refs_2_.refs_1_.refs_4_, f32[2,8,512]{2,1,0:T(8,128)S(1)} %get-tuple-element.42.refs_2_.refs_5_.refs_3_, ...), custom_call_target="tpu_custom_call" | custom-call | tf_op jit(solution)/shard_map/pallas_call | solution.py:55
  86.8 1.9 %collective-permute-start.11 = (f32[2,272,512]{2,1,0:T(8,128)S(1)}, f32[2,272,512]{2,1,0:T(8,128)S(1)}, u32[]{:S(2)}, u32[]{:S(2)}) collective-permute-start(f32[2,272,512]{2,1,0:T(8,128)S(1)} %get-tuple-element.48), channel_id=1, source_target_pairs={{0,8},{8,16},{16,24},{24,32},{32,40},{40,48},{48,56},{56,64},{64,7... | collective-permute-start | bytes 3342344 | tf_op jit(solution)/shard_map/ppermute | solution.py:29
  88.7 6.0 %collective-permute-start.12 = (f32[2,272,512]{2,1,0:T(8,128)S(1)}, f32[2,272,512]{2,1,0:T(8,128)S(1)}, u32[]{:S(2)}, u32[]{:S(2)}) collective-permute-start(f32[2,272,512]{2,1,0:T(8,128)S(1)} %get-tuple-element.49.refs_0_), channel_id=1, source_target_pairs={{8,0},{16,8},{24,16},{32,24},{40,32},{48,40},{56,48},{64,56},{72,6... | collective-permute-start | bytes 3342344 | tf_op jit(solution)/shard_map/ppermute | solution.py:29
  94.7 2.1 %shard_map.62 = (f32[2,240,512]{2,1,0:T(8,128)S(1)}, f32[2,240,512]{2,1,0:T(8,128)S(1)}, f32[2,240,512]{2,1,0:T(8,128)S(1)}) custom-call(f32[2,272,512]{2,1,0:T(8,128)S(1)} %get-tuple-element.49.refs_0_, f32[2,8,512]{2,1,0:T(8,128)S(1)} %broadcast_in_dim.2.refs_0_.refs_1_, f32[2,8,512]{2,1,0:T(8,128)S(1)} %collective-permute-done.3.refs_1_.refs_3_.refs_2_, ...), custom_call_target="tpu_custom_call" | custom-call | tf_op jit(solution)/shard_map/pallas_call | solution.py:55
  96.9 1.9 %collective-permute-start.15 = (f32[2,240,512]{2,1,0:T(8,128)S(1)}, f32[2,240,512]{2,1,0:T(8,128)S(1)}, u32[]{:S(2)}, u32[]{:S(2)}) collective-permute-start(f32[2,240,512]{2,1,0:T(8,128)S(1)} %get-tuple-element.53), channel_id=1, source_target_pairs={{0,1},{1,2},{2,3},{3,4},{4,5},{5,6},{6,7},{8,9},{9,10},{10,11},{11... | collective-permute-start | bytes 2949128 | tf_op jit(solution)/shard_map/ppermute | solution.py:29
  98.8 3.6 %collective-permute-start.16 = (f32[2,240,512]{2,1,0:T(8,128)S(1)}, f32[2,240,512]{2,1,0:T(8,128)S(1)}, u32[]{:S(2)}, u32[]{:S(2)}) collective-permute-start(f32[2,240,512]{2,1,0:T(8,128)S(1)} %get-tuple-element.54), channel_id=1, source_target_pairs={{1,0},{2,1},{3,2},{4,3},{5,4},{6,5},{7,6},{9,8},{10,9},{11,10},{12... | collective-permute-start | bytes 2949128 | tf_op jit(solution)/shard_map/ppermute | solution.py:29
  102.4 9.8 %collective-permute-done.15.refs_5_ = f32[2,240,512]{2,1,0:T(8,128)S(1)} collective-permute-done((f32[2,240,512]{2,1,0:T(8,128)S(1)}, f32[2,240,512]{2,1,0:T(8,128)S(1)}, u32[]{:S(2)}, u32[]{:S(2)}) %collective-permute-start.15) | collective-permute-done | bytes 983072 | tf_op jit(solution)/shard_map/ppermute | solution.py:29
  112.3 1.8 %collective-permute-done.16.refs_6_ = f32[2,240,512]{2,1,0:T(8,128)S(1)} collective-permute-done((f32[2,240,512]{2,1,0:T(8,128)S(1)}, f32[2,240,512]{2,1,0:T(8,128)S(1)}, u32[]{:S(2)}, u32[]{:S(2)}) %collective-permute-start.16) | collective-permute-done | bytes 983072 | tf_op jit(solution)/shard_map/ppermute | solution.py:29
  114.0 1.5 shard_map.63.refs_8_
  115.6 2.2 %collective-permute-done.11.refs_6_ = f32[2,272,512]{2,1,0:T(8,128)S(1)} collective-permute-done((f32[2,272,512]{2,1,0:T(8,128)S(1)}, f32[2,272,512]{2,1,0:T(8,128)S(1)}, u32[]{:S(2)}, u32[]{:S(2)}) %collective-permute-start.11) | collective-permute-done | bytes 1114144 | tf_op jit(solution)/shard_map/ppermute | solution.py:29
  117.7 3.7 %shard_map.64 = (bf16[1024,512]{1,0:T(8,128)(2,1)S(1)}, f32[2,240,512]{2,1,0:T(8,128)S(1)}) custom-call(s32[1,1]{1,0:T(1,128)S(6)} %copy.8.refs_0_, f32[2,8,512]{2,1,0:T(8,128)S(1)} %broadcast_in_dim.2.refs_0_.refs_1_, f32[2,8,512]{2,1,0:T(8,128)S(1)} %get-tuple-element.41.refs_4_.refs_3_.refs_1_.refs_2_, ...), custom_call_target="tpu_custom_call" | custom-call | tf_op jit(solution)/shard_map/pallas_call | solution.py:55
  121.4 1.9 %collective-permute-start.20 = (f32[2,240,512]{2,1,0:T(8,128)S(1)}, f32[2,240,512]{2,1,0:T(8,128)S(1)}, u32[]{:S(2)}, u32[]{:S(2)}) collective-permute-start(f32[2,240,512]{2,1,0:T(8,128)S(1)} %get-tuple-element.60.refs_4_), channel_id=1, source_target_pairs={{0,8},{8,16},{16,24},{24,32},{32,40},{40,48},{48,56},{56,64},{64,7... | collective-permute-start | bytes 2949128 | tf_op jit(solution)/shard_map/ppermute | solution.py:29
  124.3 1.9 %collective-permute-start.17 = (f32[2,136,512]{2,1,0:T(8,128)S(1)}, f32[2,136,512]{2,1,0:T(8,128)S(1)}, u32[]{:S(2)}, u32[]{:S(2)}) collective-permute-start(f32[2,136,512]{2,1,0:T(8,128)S(1)} %get-tuple-element.56.refs_4_), channel_id=1, source_target_pairs={{0,1},{1,2},{2,3},{3,4},{4,5},{5,6},{6,7},{8,9},{9,10},{10,11},{11... | collective-permute-start | bytes 1671176 | tf_op jit(solution)/shard_map/ppermute | solution.py:29
  126.2 3.2 %collective-permute-start.18 = (f32[2,136,512]{2,1,0:T(8,128)S(1)}, f32[2,136,512]{2,1,0:T(8,128)S(1)}, u32[]{:S(2)}, u32[]{:S(2)}) collective-permute-start(f32[2,136,512]{2,1,0:T(8,128)S(1)} %get-tuple-element.57.refs_5_), channel_id=1, source_target_pairs={{0,1},{1,2},{2,3},{3,4},{4,5},{5,6},{6,7},{8,9},{9,10},{10,11},{11... | collective-permute-start | bytes 1671176 | tf_op jit(solution)/shard_map/ppermute | solution.py:29
  129.5 5.7 %collective-permute-done.17.refs_6_ = f32[2,136,512]{2,1,0:T(8,128)S(1)} collective-permute-done((f32[2,136,512]{2,1,0:T(8,128)S(1)}, f32[2,136,512]{2,1,0:T(8,128)S(1)}, u32[]{:S(2)}, u32[]{:S(2)}) %collective-permute-start.17) | collective-permute-done | bytes 557088 | tf_op jit(solution)/shard_map/ppermute | solution.py:29
  135.1 6.0 %collective-permute-done.18.refs_7_ = f32[2,136,512]{2,1,0:T(8,128)S(1)} collective-permute-done((f32[2,136,512]{2,1,0:T(8,128)S(1)}, f32[2,136,512]{2,1,0:T(8,128)S(1)}, u32[]{:S(2)}, u32[]{:S(2)}) %collective-permute-start.18) | collective-permute-done | bytes 557088 | tf_op jit(solution)/shard_map/ppermute | solution.py:29
  141.8 1.9 %collective-permute-start.19 = (f32[2,272,512]{2,1,0:T(8,128)S(1)}, f32[2,272,512]{2,1,0:T(8,128)S(1)}, u32[]{:S(2)}, u32[]{:S(2)}) collective-permute-start(f32[2,272,512]{2,1,0:T(8,128)S(1)} %get-tuple-element.59.refs_0_), channel_id=1, source_target_pairs={{0,8},{8,16},{16,24},{24,32},{32,40},{40,48},{48,56},{56,64},{64,7... | collective-permute-start | bytes 3342344 | tf_op jit(solution)/shard_map/ppermute | solution.py:29
  143.7 6.3 %collective-permute-done.20.refs_5_ = f32[2,240,512]{2,1,0:T(8,128)S(1)} collective-permute-done((f32[2,240,512]{2,1,0:T(8,128)S(1)}, f32[2,240,512]{2,1,0:T(8,128)S(1)}, u32[]{:S(2)}, u32[]{:S(2)}) %collective-permute-start.20) | collective-permute-done | bytes 983072 | tf_op jit(solution)/shard_map/ppermute | solution.py:29
  150.4 1.9 %collective-permute-start.21 = (f32[2,240,512]{2,1,0:T(8,128)S(1)}, f32[2,240,512]{2,1,0:T(8,128)S(1)}, u32[]{:S(2)}, u32[]{:S(2)}) collective-permute-start(f32[2,240,512]{2,1,0:T(8,128)S(1)} %get-tuple-element.62), channel_id=1, source_target_pairs={{0,1},{1,2},{2,3},{3,4},{4,5},{5,6},{6,7},{8,9},{9,10},{10,11},{11... | collective-permute-start | bytes 2949128 | tf_op jit(solution)/shard_map/ppermute | solution.py:29
  152.3 13.5 %collective-permute-done.21.refs_0_ = f32[2,240,512]{2,1,0:T(8,128)S(1)} collective-permute-done((f32[2,240,512]{2,1,0:T(8,128)S(1)}, f32[2,240,512]{2,1,0:T(8,128)S(1)}, u32[]{:S(2)}, u32[]{:S(2)}) %collective-permute-start.21) | collective-permute-done | bytes 983072 | tf_op jit(solution)/shard_map/ppermute | solution.py:29
  166.9 5.8 %collective-permute-done.19.refs_0_ = f32[2,272,512]{2,1,0:T(8,128)S(1)} collective-permute-done((f32[2,272,512]{2,1,0:T(8,128)S(1)}, f32[2,272,512]{2,1,0:T(8,128)S(1)}, u32[]{:S(2)}, u32[]{:S(2)}) %collective-permute-start.19) | collective-permute-done | bytes 1114144 | tf_op jit(solution)/shard_map/ppermute | solution.py:29
  172.7 1.1 shard_map.69
  (22 shorter events, 5.2 us)
Async XLA Ops:
  1.3 11.9 %copy-start.2 = (s32[1,1,1,2]{3,2,1,0:T(1,128)S(1)}, s32[1,1,1,2]{3,2,1,0:T(1,128)}, u32[]{:S(2)}) copy-start(s32[1,1,1,2]{3,2,1,0:T(1,128)} %param.8) | copy-start | bytes 28
  1.3 30.2 %collective-permute-start.5 = (f32[2,240,512]{2,1,0:T(8,128)S(1)}, f32[2,240,512]{2,1,0:T(8,128)S(1)}, u32[]{:S(2)}, u32[]{:S(2)}) collective-permute-start(f32[2,240,512]{2,1,0:T(8,128)S(1)} %slice.11.refs_3_.refs_1_), channel_id=1, source_target_pairs={{8,0},{16,8},{24,16},{32,24},{40,32},{48,40},{56,48},{64,56},{72,6... | collective-permute-start | bytes 2949128 | tf_op jit(solution)/shard_map/ppermute | solution.py:29
  8.7 12.5 %collective-permute-start.2 = (f32[2,136,512]{2,1,0:T(8,128)S(1)}, f32[2,136,512]{2,1,0:T(8,128)S(1)}, u32[]{:S(2)}, u32[]{:S(2)}) collective-permute-start(f32[2,136,512]{2,1,0:T(8,128)S(1)} %get-tuple-element.63.refs_3_), channel_id=1, source_target_pairs={{1,0},{2,1},{3,2},{4,3},{5,4},{6,5},{7,6},{9,8},{10,9},{11,10},{12... | collective-permute-start | bytes 1671176 | tf_op jit(solution)/shard_map/ppermute | solution.py:29
  10.7 13.0 %collective-permute-start.1 = (f32[2,136,512]{2,1,0:T(8,128)S(1)}, f32[2,136,512]{2,1,0:T(8,128)S(1)}, u32[]{:S(2)}, u32[]{:S(2)}) collective-permute-start(f32[2,136,512]{2,1,0:T(8,128)S(1)} %get-tuple-element.64.refs_2_), channel_id=1, source_target_pairs={{1,0},{2,1},{3,2},{4,3},{5,4},{6,5},{7,6},{9,8},{10,9},{11,10},{12... | collective-permute-start | bytes 1671176 | tf_op jit(solution)/shard_map/ppermute | solution.py:29
  13.3 7.9 %collective-permute-start.3 = (f32[2,8,512]{2,1,0:T(8,128)S(1)}, f32[2,8,512]{2,1,0:T(8,128)S(1)}, u32[]{:S(2)}, u32[]{:S(2)}) collective-permute-start(f32[2,8,512]{2,1,0:T(8,128)S(1)} %broadcast_in_dim.2.refs_0_.refs_1_), channel_id=1, source_target_pairs={{0,8},{8,16},{16,24},{24,32},{32,40},{40,48},{48,56},{56,64},{64,7... | collective-permute-start | bytes 98312 | tf_op jit(solution)/shard_map/ppermute | solution.py:29
  23.8 29.3 %collective-permute-start.4 = (f32[2,280,512]{2,1,0:T(8,128)S(1)}, f32[2,280,512]{2,1,0:T(8,128)S(1)}, u32[]{:S(2)}, u32[]{:S(2)}) collective-permute-start(f32[2,280,512]{2,1,0:T(8,128)S(1)} %shard_map.56.refs_0_), channel_id=1, source_target_pairs={{8,0},{16,8},{24,16},{32,24},{40,32},{48,40},{56,48},{64,56},{72,6... | collective-permute-start | bytes 3440648 | tf_op jit(solution)/shard_map/ppermute | solution.py:29
  26.1 5.4 %collective-permute-start = (f32[2,8,512]{2,1,0:T(8,128)S(1)}, f32[2,8,512]{2,1,0:T(8,128)S(1)}, u32[]{:S(2)}, u32[]{:S(2)}) collective-permute-start(f32[2,8,512]{2,1,0:T(8,128)S(1)} %broadcast_in_dim.2.refs_0_.refs_1_), channel_id=1, source_target_pairs={{0,1},{1,2},{2,3},{3,4},{4,5},{5,6},{6,7},{8,9},{9,10},{10,11},{11... | collective-permute-start | bytes 98312 | tf_op jit(solution)/shard_map/ppermute | solution.py:29
  31.5 7.2 %copy-start.1 = (f32[2,512,512]{2,1,0:T(8,128)S(1)}, f32[2,512,512]{2,1,0:T(8,128)}, u32[]{:S(2)}) copy-start(f32[2,512,512]{2,1,0:T(8,128)} %refs_3_.1) | copy-start | bytes 6291460
  31.6 14.0 %collective-permute-start.6 = (f32[2,248,512]{2,1,0:T(8,128)S(1)}, f32[2,248,512]{2,1,0:T(8,128)S(1)}, u32[]{:S(2)}, u32[]{:S(2)}) collective-permute-start(f32[2,248,512]{2,1,0:T(8,128)S(1)} %shard_map.57), channel_id=1, source_target_pairs={{1,0},{2,1},{3,2},{4,3},{5,4},{6,5},{7,6},{9,8},{10,9},{11,10},{12... | collective-permute-start | bytes 3047432 | tf_op jit(solution)/shard_map/ppermute | solution.py:29
  45.6 7.4 %copy-start = (f32[1,1,1,512,512]{4,3,2,1,0:T(8,128)S(1)}, f32[1,1,1,512,512]{4,3,2,1,0:T(8,128)}, u32[]{:S(2)}) copy-start(f32[1,1,1,512,512]{4,3,2,1,0:T(8,128)} %param.7) | copy-start | bytes 3145732
  57.6 16.0 %collective-permute-start.9 = (f32[2,136,512]{2,1,0:T(8,128)S(1)}, f32[2,136,512]{2,1,0:T(8,128)S(1)}, u32[]{:S(2)}, u32[]{:S(2)}) collective-permute-start(f32[2,136,512]{2,1,0:T(8,128)S(1)} %get-tuple-element.45.refs_5_.refs_3_), channel_id=1, source_target_pairs={{1,0},{2,1},{3,2},{4,3},{5,4},{6,5},{7,6},{9,8},{10,9},{11,10},{12... | collective-permute-start | bytes 1671176 | tf_op jit(solution)/shard_map/ppermute | solution.py:29
  60.2 34.5 %collective-permute-start.14 = (f32[2,240,512]{2,1,0:T(8,128)S(1)}, f32[2,240,512]{2,1,0:T(8,128)S(1)}, u32[]{:S(2)}, u32[]{:S(2)}) collective-permute-start(f32[2,240,512]{2,1,0:T(8,128)S(1)} %get-tuple-element.51.refs_6_.refs_15_), channel_id=1, source_target_pairs={{8,0},{16,8},{24,16},{32,24},{40,32},{48,40},{56,48},{64,56},{72,6... | collective-permute-start | bytes 2949128 | tf_op jit(solution)/shard_map/ppermute | solution.py:29
  66.1 28.6 %collective-permute-start.13 = (f32[2,240,512]{2,1,0:T(8,128)S(1)}, f32[2,240,512]{2,1,0:T(8,128)S(1)}, u32[]{:S(2)}, u32[]{:S(2)}) collective-permute-start(f32[2,240,512]{2,1,0:T(8,128)S(1)} %get-tuple-element.51.refs_6_.refs_15_), channel_id=1, source_target_pairs={{0,8},{8,16},{16,24},{24,32},{32,40},{40,48},{48,56},{56,64},{64,7... | collective-permute-start | bytes 2949128 | tf_op jit(solution)/shard_map/ppermute | solution.py:29
  68.0 10.9 %collective-permute-start.7 = (f32[2,136,512]{2,1,0:T(8,128)S(1)}, f32[2,136,512]{2,1,0:T(8,128)S(1)}, u32[]{:S(2)}, u32[]{:S(2)}) collective-permute-start(f32[2,136,512]{2,1,0:T(8,128)S(1)} %get-tuple-element.45.refs_5_.refs_3_), channel_id=1, source_target_pairs={{0,1},{1,2},{2,3},{3,4},{4,5},{5,6},{6,7},{8,9},{9,10},{10,11},{11... | collective-permute-start | bytes 1671176 | tf_op jit(solution)/shard_map/ppermute | solution.py:29
  70.0 10.6 %collective-permute-start.10 = (f32[2,136,512]{2,1,0:T(8,128)S(1)}, f32[2,136,512]{2,1,0:T(8,128)S(1)}, u32[]{:S(2)}, u32[]{:S(2)}) collective-permute-start(f32[2,136,512]{2,1,0:T(8,128)S(1)} %get-tuple-element.46.refs_6_.refs_4_), channel_id=1, source_target_pairs={{1,0},{2,1},{3,2},{4,3},{5,4},{6,5},{7,6},{9,8},{10,9},{11,10},{12... | collective-permute-start | bytes 1671176 | tf_op jit(solution)/shard_map/ppermute | solution.py:29
  73.6 11.2 %collective-permute-start.8 = (f32[2,136,512]{2,1,0:T(8,128)S(1)}, f32[2,136,512]{2,1,0:T(8,128)S(1)}, u32[]{:S(2)}, u32[]{:S(2)}) collective-permute-start(f32[2,136,512]{2,1,0:T(8,128)S(1)} %get-tuple-element.46.refs_6_.refs_4_), channel_id=1, source_target_pairs={{0,1},{1,2},{2,3},{3,4},{4,5},{5,6},{6,7},{8,9},{9,10},{10,11},{11... | collective-permute-start | bytes 1671176 | tf_op jit(solution)/shard_map/ppermute | solution.py:29
  86.8 31.0 %collective-permute-start.11 = (f32[2,272,512]{2,1,0:T(8,128)S(1)}, f32[2,272,512]{2,1,0:T(8,128)S(1)}, u32[]{:S(2)}, u32[]{:S(2)}) collective-permute-start(f32[2,272,512]{2,1,0:T(8,128)S(1)} %get-tuple-element.48), channel_id=1, source_target_pairs={{0,8},{8,16},{16,24},{24,32},{32,40},{40,48},{48,56},{56,64},{64,7... | collective-permute-start | bytes 3342344 | tf_op jit(solution)/shard_map/ppermute | solution.py:29
  88.7 29.0 %collective-permute-start.12 = (f32[2,272,512]{2,1,0:T(8,128)S(1)}, f32[2,272,512]{2,1,0:T(8,128)S(1)}, u32[]{:S(2)}, u32[]{:S(2)}) collective-permute-start(f32[2,272,512]{2,1,0:T(8,128)S(1)} %get-tuple-element.49.refs_0_), channel_id=1, source_target_pairs={{8,0},{16,8},{24,16},{32,24},{40,32},{48,40},{56,48},{64,56},{72,6... | collective-permute-start | bytes 3342344 | tf_op jit(solution)/shard_map/ppermute | solution.py:29
  96.9 15.4 %collective-permute-start.15 = (f32[2,240,512]{2,1,0:T(8,128)S(1)}, f32[2,240,512]{2,1,0:T(8,128)S(1)}, u32[]{:S(2)}, u32[]{:S(2)}) collective-permute-start(f32[2,240,512]{2,1,0:T(8,128)S(1)} %get-tuple-element.53), channel_id=1, source_target_pairs={{0,1},{1,2},{2,3},{3,4},{4,5},{5,6},{6,7},{8,9},{9,10},{10,11},{11... | collective-permute-start | bytes 2949128 | tf_op jit(solution)/shard_map/ppermute | solution.py:29
  98.8 15.2 %collective-permute-start.16 = (f32[2,240,512]{2,1,0:T(8,128)S(1)}, f32[2,240,512]{2,1,0:T(8,128)S(1)}, u32[]{:S(2)}, u32[]{:S(2)}) collective-permute-start(f32[2,240,512]{2,1,0:T(8,128)S(1)} %get-tuple-element.54), channel_id=1, source_target_pairs={{1,0},{2,1},{3,2},{4,3},{5,4},{6,5},{7,6},{9,8},{10,9},{11,10},{12... | collective-permute-start | bytes 2949128 | tf_op jit(solution)/shard_map/ppermute | solution.py:29
  121.4 28.5 %collective-permute-start.20 = (f32[2,240,512]{2,1,0:T(8,128)S(1)}, f32[2,240,512]{2,1,0:T(8,128)S(1)}, u32[]{:S(2)}, u32[]{:S(2)}) collective-permute-start(f32[2,240,512]{2,1,0:T(8,128)S(1)} %get-tuple-element.60.refs_4_), channel_id=1, source_target_pairs={{0,8},{8,16},{16,24},{24,32},{32,40},{40,48},{48,56},{56,64},{64,7... | collective-permute-start | bytes 2949128 | tf_op jit(solution)/shard_map/ppermute | solution.py:29
  124.3 10.9 %collective-permute-start.17 = (f32[2,136,512]{2,1,0:T(8,128)S(1)}, f32[2,136,512]{2,1,0:T(8,128)S(1)}, u32[]{:S(2)}, u32[]{:S(2)}) collective-permute-start(f32[2,136,512]{2,1,0:T(8,128)S(1)} %get-tuple-element.56.refs_4_), channel_id=1, source_target_pairs={{0,1},{1,2},{2,3},{3,4},{4,5},{5,6},{6,7},{8,9},{9,10},{10,11},{11... | collective-permute-start | bytes 1671176 | tf_op jit(solution)/shard_map/ppermute | solution.py:29
  126.2 14.9 %collective-permute-start.18 = (f32[2,136,512]{2,1,0:T(8,128)S(1)}, f32[2,136,512]{2,1,0:T(8,128)S(1)}, u32[]{:S(2)}, u32[]{:S(2)}) collective-permute-start(f32[2,136,512]{2,1,0:T(8,128)S(1)} %get-tuple-element.57.refs_5_), channel_id=1, source_target_pairs={{0,1},{1,2},{2,3},{3,4},{4,5},{5,6},{6,7},{8,9},{9,10},{10,11},{11... | collective-permute-start | bytes 1671176 | tf_op jit(solution)/shard_map/ppermute | solution.py:29
  141.8 30.9 %collective-permute-start.19 = (f32[2,272,512]{2,1,0:T(8,128)S(1)}, f32[2,272,512]{2,1,0:T(8,128)S(1)}, u32[]{:S(2)}, u32[]{:S(2)}) collective-permute-start(f32[2,272,512]{2,1,0:T(8,128)S(1)} %get-tuple-element.59.refs_0_), channel_id=1, source_target_pairs={{0,8},{8,16},{16,24},{24,32},{32,40},{40,48},{48,56},{56,64},{64,7... | collective-permute-start | bytes 3342344 | tf_op jit(solution)/shard_map/ppermute | solution.py:29
  150.4 15.4 %collective-permute-start.21 = (f32[2,240,512]{2,1,0:T(8,128)S(1)}, f32[2,240,512]{2,1,0:T(8,128)S(1)}, u32[]{:S(2)}, u32[]{:S(2)}) collective-permute-start(f32[2,240,512]{2,1,0:T(8,128)S(1)} %get-tuple-element.62), channel_id=1, source_target_pairs={{0,1},{1,2},{2,3},{3,4},{4,5},{5,6},{6,7},{8,9},{9,10},{10,11},{11... | collective-permute-start | bytes 2949128 | tf_op jit(solution)/shard_map/ppermute | solution.py:29

commit v4 on v3

--- a/solution.py
+++ b/solution.py
@@ -18,9 +18,8 @@
 BF16 = jnp.bfloat16
 
 EXTRA = 8
-HEAD = 240
-HEAD_PIECES = 1
-TAIL_PIECES = 2
+BLOCK = 128
+PAD = 8
 
 
 def shifted(value, axis, steps):
@@ -64,22 +63,25 @@
 
 
 def split(first, width):
-    height, count = (HEAD, HEAD_PIECES) if first == 0 else (width - HEAD, TAIL_PIECES)
-    size = height // count
-    return [(k, first + k * size, slice(k * size, (k + 1) * size)) for k in range(count)]
-
-
-def part(half, plane, k, rows):
-    if isinstance(half, list):
-        return half[k][plane, : rows.stop - rows.start, :]
-    return half[plane, rows, :]
-
-
-def put(half, plane, k, rows, value):
-    if isinstance(half, list):
-        half[k][plane, : rows.stop - rows.start, :] = value
-    else:
-        half[plane, rows, :] = value
+    return [(first + row, slice(row, row + BLOCK)) for row in range(0, width // 2, BLOCK)]
+
+
+def place_in(half, rows, width):
+    if not isinstance(half, list):
+        return half, rows
+    height = width // 2 // len(half)
+    index = rows.start // height
+    return half[index], slice(rows.start - index * height, rows.stop - index * height)
+
+
+def part(half, plane, rows, width):
+    array, inner = place_in(half, rows, width)
+    return array[plane, inner, :]
+
+
+def put(half, plane, rows, value):
+    array, inner = place_in(half, rows, value.shape[1])
+    array[plane, inner, :] = value
 
 
 def indices(rows, width, first):
@@ -110,7 +112,7 @@
 
 def prepare_kernel(offset, cos_ref, sin_ref, pupil_ref, bx, bxt, by, byt_head, byt_tail, pupil_out):
     w = cos_ref.shape[0]
-    h = HEAD
+    h = w // 2
     cosine = cos_ref[...].astype(F32)
     sine = sin_ref[...].astype(F32)
     oy, ox = offset[0, 0], offset[0, 1]
@@ -140,8 +142,8 @@
 def right_product(first, window, pupil, bx, left, half):
     w = bx.shape[0] // 2
     h = half.shape[0] // 2
-    for k, row, rows in split(first, w):
-        wr, wi = window(k, row, rows)
+    for row, rows in split(first, w):
+        wr, wi = window(row, rows)
         across = slice(row, row + rows.stop - rows.start)
         pr, pi = pupil[0, across, :], pupil[1, across, :]
         left[rows, :w] = (wr * pr - wi * pi).astype(BF16)
@@ -169,7 +171,7 @@
 
 def back(first, by, stacked, pupil, out, extra):
     w = stacked.shape[1]
-    for k, row, rows in split(first, w):
+    for row, rows in split(first, w):
         size = rows.stop - rows.start
         back_r = dot(by[row : row + size, :], stacked[...])
         back_i = dot(by[w + row : w + row + size, :], stacked[...])
@@ -177,20 +179,22 @@
         grad_r = back_r * pr + back_i * pi
         grad_i = back_i * pr - back_r * pi
         if extra is not None:
-            grad_r = grad_r + part(extra, 0, k, rows)
-            grad_i = grad_i + part(extra, 1, k, rows)
-        put(out, 0, k, rows, grad_r)
-        put(out, 1, k, rows, grad_i)
+            grad_r = grad_r + part(extra, 0, rows, w)
+            grad_i = grad_i + part(extra, 1, rows, w)
+        put(out, 0, rows, grad_r)
+        put(out, 1, rows, grad_i)
 
 
 def gathered(head, place, tile, one, both, kept):
-    def window(k, row, rows):
-        first_way, second_way = ways_of(head, rows, kept.shape[2], row)
+    w = kept.shape[2]
+
+    def window(row, rows):
+        first_way, second_way = ways_of(head, rows, w, row)
         a, b = first_way(place), second_way(place)
         values = []
         for plane in range(2):
-            near = jnp.where(a, part(one, plane, k, rows), part(tile, plane, k, rows))
-            value = jnp.where(b, part(both, plane, k, rows), near)
+            near = jnp.where(a, part(one, plane, rows, w), part(tile, plane, rows, w))
+            value = jnp.where(b, part(both, plane, rows, w), near)
             kept[plane, rows, :] = value
             values.append(value)
         return values
@@ -199,14 +203,16 @@
 
 
 def updated(head, place, edge_row, edge_col, kept, own, minus, plus):
-    def window(k, row, rows):
-        i, j = indices(rows, kept.shape[2], row)
+    w = kept.shape[2]
+
+    def window(row, rows):
+        i, j = indices(rows, w, row)
         a, b = low(i, place), far(j, place)
         outside = (a & absent(edge_row)) | (b & absent(edge_col))
         second = b if head else a
         values = []
         for plane in range(2):
-            near = jnp.where(second, part(plus, plane, k, rows), part(minus, plane, k, rows))
+            near = jnp.where(second, part(plus, plane, rows, w), part(minus, plane, rows, w))
             value = kept[plane, rows, :] - STEP * (own[plane, rows, :] + near)
             values.append(jnp.where(outside, 0.0, value))
         return values
@@ -257,11 +263,11 @@
 
 def compose_kernel(first, head, me, target, tile, one, out):
     w = me.shape[2]
-    for k, row, rows in split(first, w):
+    for row, rows in split(first, w):
         mask = ways_of(head, rows, w, row)[0](target)
         for plane in range(2):
-            value = jnp.where(mask, part(one, plane, k, rows), part(tile, plane, k, rows))
-            put(out, plane, k, rows, value)
+            value = jnp.where(mask, part(one, plane, rows, w), part(tile, plane, rows, w))
+            put(out, plane, rows, value)
     end = out[-1] if head else out
     end[:, end.shape[1] - EXTRA :, :] = me[...]
 
@@ -270,7 +276,7 @@
     first, head, me, minus, plus, target_minus, target_plus, mine, got_minus, got_plus, to_minus, to_plus, own
 ):
     w = me.shape[2]
-    for k, row, rows in split(first, w):
+    for row, rows in split(first, w):
         ways = ways_of(head, rows, w, row)
         f, f_minus, f_plus = (ways[0](x) for x in (me, minus, plus))
         s, s_minus, s_plus = (ways[1](x) for x in (me, minus, plus))
@@ -283,26 +289,26 @@
         _, own_minus, own_plus = seen(f)
         own_minus, own_plus = own_minus & (s == s_minus), own_plus & (s == s_plus)
         for plane in range(2):
-            values = [part(x, plane, k, rows) for x in (mine, got_minus, got_plus)]
+            values = [part(x, plane, rows, w) for x in (mine, got_minus, got_plus)]
             for out, masks in ((to_minus, minus_m), (to_plus, plus_m)):
                 terms = [jnp.where(m, v, 0.0) for m, v in zip(masks, values)]
-                put(out, plane, k, rows, terms[0] + terms[1] + terms[2])
+                put(out, plane, rows, terms[0] + terms[1] + terms[2])
             others = jnp.where(own_minus, values[1], 0.0) + jnp.where(own_plus, values[2], 0.0)
-            put(own, plane, k, rows, values[0] + others)
+            put(own, plane, rows, values[0] + others)
 
 
 def final_kernel(first, head, me, minus, tile, mine, got, to_plus, base):
     w = me.shape[2]
-    for k, row, rows in split(first, w):
+    for row, rows in split(first, w):
         ways = ways_of(head, rows, w, row)
         f, f_minus = ways[0](me), ways[0](minus)
         s, s_minus = ways[1](me), ways[1](minus)
         for plane in range(2):
-            own = jnp.where(f, 0.0, part(mine, plane, k, rows))
-            other = jnp.where(f_minus, part(got, plane, k, rows), 0.0)
-            put(to_plus, plane, k, rows, jnp.where(s, own, 0.0) + jnp.where(s_minus, other, 0.0))
+            own = jnp.where(f, 0.0, part(mine, plane, rows, w))
+            other = jnp.where(f_minus, part(got, plane, rows, w), 0.0)
+            put(to_plus, plane, rows, jnp.where(s, own, 0.0) + jnp.where(s_minus, other, 0.0))
             kept = jnp.where(s, 0.0, own) + jnp.where(s_minus, 0.0, other)
-            base[plane, rows, :] = part(tile, plane, k, rows) - STEP * kept
+            base[plane, rows, :] = part(tile, plane, rows, w) - STEP * kept
 
 
 def store(first, base, got, whole, previous=None):
@@ -315,9 +321,9 @@
         out, value, sems = refs[-3:]
         copies, row = [], 0
         for k, piece in enumerate(pieces):
-            size = piece.shape[1]
+            size = min(piece.shape[1], h - row)
             rows = slice(row, row + size)
-            value[:, rows, :] = base[:, rows, :] - STEP * piece[...]
+            value[:, rows, :] = base[:, rows, :] - STEP * piece[:, :size, :]
             copy = pltpu.make_async_copy(
                 value.at[:, pl.ds(row, size), :], out.at[:, pl.ds(first + row, size), :], sems.at[k]
             )
@@ -340,20 +346,18 @@
 
 def on_device(spectrum, pupil, amplitudes, offsets, counts):
     w = pupil.shape[1]
-    h = HEAD
+    h = w // 2
     amp = amplitudes[0, 0, 0]
     offset = offsets[0, 0]
 
     def block(rows):
         return jax.ShapeDtypeStruct((2, rows, w), F32)
 
-    head_half, tail_half, whole, spot = block(h), block(w - h), block(w), block(EXTRA)
-    head_pieces, tail_pieces = (
-        [block(rows.stop - rows.start) for _, _, rows in split(first, w)] for first in (0, h)
-    )
+    half, whole, spot = block(h), block(w), block(EXTRA)
+    pieces = [block(h // 2)] * 2
     me = jnp.broadcast_to((offset[0] + 1).astype(F32)[:, None, None], (2, EXTRA, w))
     head = spectrum[:, :h]
-    tail = [spectrum[:, h + rows.start : h + rows.stop] for _, _, rows in split(h, w)]
+    tail = [spectrum[:, h : h + h // 2], spectrum[:, h + h // 2 :]]
 
     def each(values, axis, steps):
         return [shifted(value, axis, steps) for value in values]
@@ -366,52 +370,51 @@
     cosine, sine = dft_tables(w)
     square = jax.ShapeDtypeStruct((2 * w, 2 * w), BF16)
     stack = jax.ShapeDtypeStruct((2 * w, w), BF16)
-    narrow = [jax.ShapeDtypeStruct((2 * w, 2 * n), BF16) for n in (h, w - h)]
     bx, bxt, by, byt_head, byt_tail, rolled = call(
-        prepare_kernel, [square] * 3 + narrow + [whole], (cosine, sine, pupil), scalars=(offset,)
+        prepare_kernel, [square] * 3 + [stack] * 2 + [whole], (cosine, sine, pupil), scalars=(offset,)
     )
 
     (tail_made,) = call(
-        functools.partial(compose_kernel, h, False), [block(w - h + EXTRA)], (me, above, tail, tail_right)
+        functools.partial(compose_kernel, h, False), [block(h + EXTRA)], (me, above, tail, tail_right)
     )
     tail_both = shifted(tail_made, "row", -1)
     (head_made,) = call(
         functools.partial(compose_kernel, 0, True),
-        [head_pieces[:-1] + [block(head_pieces[-1].shape[1] + EXTRA)]],
+        [[pieces[0], block(h // 2 + EXTRA)]],
         (me, left_of, head, head_below),
         after=(tail_made,),
     )
     head_both = each(head_made, "col", -1)
 
     total = jax.ShapeDtypeStruct((2 * w, w), F32)
-    products = [pltpu.VMEM((2 * n, w), BF16) for n in (h, w - h)]
+    products = pltpu.VMEM((w, w), BF16)
     left_half, left_whole = pltpu.VMEM((h, 2 * w), BF16), pltpu.VMEM((w, 2 * w), BF16)
     head_kept, acc, right_of = call(
         functools.partial(open_first, 0),
-        [head_half, total, spot],
+        [half, total, spot],
         (me, head, head_below, head_both, rolled, bx, byt_head),
-        (left_half, products[0]),
+        (left_half, products),
     )
     tail_kept, under, stacked, head_grad = call(
         functools.partial(close_first, h),
-        [tail_half, spot, stack, head_half],
+        [half, spot, stack, block(h + PAD)],
         (me, tail, tail_right, tail_both, acc, rolled, amp, bx, byt_tail, bxt, by),
-        (left_whole, products[1]),
+        (left_whole, products),
         scalars=(counts,),
     )
 
     got_above, got_under = shifted(head_grad, "row", 1), shifted(head_grad, "row", -1)
-    (tail_grad,) = call(functools.partial(rest_first, h), [tail_pieces], (by, stacked, rolled))
+    (tail_grad,) = call(functools.partial(rest_first, h), [[half]], (by, stacked, rolled))
     got_left, got_right = each(tail_grad, "col", 1), each(tail_grad, "col", -1)
     to_up, to_down, tail_own = call(
         functools.partial(between_kernel, h, False),
-        [tail_half] * 3,
+        [block(h + PAD)] * 2 + [half],
         (me, left_of, right_of, above, under, tail_grad, got_left, got_right),
     )
     tail_sums = (tail_own, shifted(to_down, "row", 1), shifted(to_up, "row", -1))
     to_left, to_right, head_own = call(
         functools.partial(between_kernel, 0, True),
-        [head_pieces, head_pieces, head_half],
+        [[half], [half], half],
         (me, above, under, left_of, right_of, head_grad, got_above, got_under),
         after=(to_up,),
     )
@@ -421,28 +424,28 @@
         functools.partial(open_second, 0),
         [total],
         (me, under, right_of, head_kept, *head_sums, rolled, bx, byt_head),
-        (left_half, products[0]),
+        (left_half, products),
     )
     stacked, head_total = call(
         functools.partial(close_second, h),
-        [stack, head_half],
+        [stack, half],
         (me, under, right_of, tail_kept, *tail_sums, acc, rolled, amp, bx, byt_tail, bxt, by, head_grad),
-        (left_whole, products[1]),
+        (left_whole, products),
         scalars=(counts,),
     )
 
     head_above = shifted(head_total, "row", 1)
     (tail_total,) = call(
-        functools.partial(rest_second, h), [tail_pieces], (by, stacked, rolled, tail_grad)
+        functools.partial(rest_second, h), [pieces], (by, stacked, rolled, tail_grad)
     )
     tail_left = each(tail_total, "col", 1)
     tail_down, tail_base = call(
-        functools.partial(final_kernel, h, False), [tail_half] * 2, (me, left_of, tail, tail_total, tail_left)
+        functools.partial(final_kernel, h, False), [half, half], (me, left_of, tail, tail_total, tail_left)
     )
     tail_got = shifted(tail_down, "row", 1)
     head_right, head_base = call(
         functools.partial(final_kernel, 0, True),
-        [head_pieces, head_half],
+        [pieces, half],
         (me, above, head, head_total, head_above),
         after=(tail_down,),
     )

time: 175 us -> 174 us (level)
  waiting for transfers between devices: 77.4 us -> 79.5 us
    ppermute x22, waiting for transfers between devices: 77.4 us -> 79.5 us  [shifted(): lax.ppermute(value, axis, [(source, source + steps) for source in range(l...]
where the time goes in v4:
time: 174 us; the launch traced here: 173 us
  waiting for transfers between devices  79.5 us (46%)
  starting transfers between devices  62.2 us (36%)
  Pallas kernels  24.4 us (14%)
  other arithmetic  4.4 us (3%)
    ppermute x22, waiting for transfers between devices, shifted(): lax.ppermute(value, axis, [(source, source + steps) for source in range(l...  79.5 us
    ppermute x22, starting transfers between devices, shifted(): lax.ppermute(value, axis, [(source, source + steps) for source in range(l...  62.2 us
    pallas_call x13, Pallas kernels, call(): pl.pallas_call(body, out_shape=out_flat, in_specs=[ANY] * skip + [SMEM] *...  22.3 us
    convert_element_type x1, other arithmetic, dft_tables(): (jnp.sin(angle) * scale).astype(jnp.bfloat16)  4.39 us
  transfers between devices with their start and end apart: 22, of which 16 were waited for; matrix products, arithmetic and copies ran while one was open for 3% of the time, Pallas kernels for 9%

profile of v4, /device:TPU:28, one launch (start us, length us, event | category | flops | bytes accessed | tf_op | source)
XLA Modules:
  0.0 173.3 jit_solution(14031027396012541717)
XLA Ops:
  0.0 1.4 slice.11.refs_3_.refs_1_
  1.4 6.1 %collective-permute-start.5 = (f32[2,256,512]{2,1,0:T(8,128)S(1)}, f32[2,256,512]{2,1,0:T(8,128)S(1)}, u32[]{:S(2)}, u32[]{:S(2)}) collective-permute-start(f32[2,256,512]{2,1,0:T(8,128)S(1)} %slice.11.refs_3_.refs_1_), channel_id=1, source_target_pairs={{8,0},{16,8},{24,16},{32,24},{40,32},{48,40},{56,48},{64,56},{72,6... | collective-permute-start | bytes 3145736 | tf_op jit(solution)/shard_map/ppermute | solution.py:28
  7.7 1.9 %collective-permute-start.2 = (f32[2,128,512]{2,1,0:T(8,128)S(1)}, f32[2,128,512]{2,1,0:T(8,128)S(1)}, u32[]{:S(2)}, u32[]{:S(2)}) collective-permute-start(f32[2,128,512]{2,1,0:T(8,128)S(1)} %get-tuple-element.65.refs_3_), channel_id=1, source_target_pairs={{1,0},{2,1},{3,2},{4,3},{5,4},{6,5},{7,6},{9,8},{10,9},{11,10},{12... | collective-permute-start | bytes 1572872 | tf_op jit(solution)/shard_map/ppermute | solution.py:28
  9.6 2.5 %collective-permute-start.1 = (f32[2,128,512]{2,1,0:T(8,128)S(1)}, f32[2,128,512]{2,1,0:T(8,128)S(1)}, u32[]{:S(2)}, u32[]{:S(2)}) collective-permute-start(f32[2,128,512]{2,1,0:T(8,128)S(1)} %get-tuple-element.66.refs_2_), channel_id=1, source_target_pairs={{1,0},{2,1},{3,2},{4,3},{5,4},{6,5},{7,6},{9,8},{10,9},{11,10},{12... | collective-permute-start | bytes 1572872 | tf_op jit(solution)/shard_map/ppermute | solution.py:28
  12.2 1.9 %collective-permute-start.3 = (f32[2,8,512]{2,1,0:T(8,128)S(1)}, f32[2,8,512]{2,1,0:T(8,128)S(1)}, u32[]{:S(2)}, u32[]{:S(2)}) collective-permute-start(f32[2,8,512]{2,1,0:T(8,128)S(1)} %broadcast_in_dim.2.refs_0_.refs_1_), channel_id=1, source_target_pairs={{0,8},{8,16},{16,24},{24,32},{32,40},{40,48},{48,56},{56,64},{64,7... | collective-permute-start | bytes 98312 | tf_op jit(solution)/shard_map/ppermute | solution.py:28
  14.2 6.0 %collective-permute-done.3.refs_1_.refs_3_.refs_2_ = f32[2,8,512]{2,1,0:T(8,128)S(1)} collective-permute-done((f32[2,8,512]{2,1,0:T(8,128)S(1)}, f32[2,8,512]{2,1,0:T(8,128)S(1)}, u32[]{:S(2)}, u32[]{:S(2)}) %collective-permute-start.3) | collective-permute-done | bytes 32800 | tf_op jit(solution)/shard_map/ppermute | solution.py:28
  20.2 1.7 %collective-permute-done.1.refs_4_ = f32[2,128,512]{2,1,0:T(8,128)S(1)} collective-permute-done((f32[2,128,512]{2,1,0:T(8,128)S(1)}, f32[2,128,512]{2,1,0:T(8,128)S(1)}, u32[]{:S(2)}, u32[]{:S(2)}) %collective-permute-start.1) | collective-permute-done | bytes 524320 | tf_op jit(solution)/shard_map/ppermute | solution.py:28
  22.0 2.4 %collective-permute-start.4 = (f32[2,264,512]{2,1,0:T(8,128)S(1)}, f32[2,264,512]{2,1,0:T(8,128)S(1)}, u32[]{:S(2)}, u32[]{:S(2)}) collective-permute-start(f32[2,264,512]{2,1,0:T(8,128)S(1)} %shard_map.56.refs_0_), channel_id=1, source_target_pairs={{8,0},{16,8},{24,16},{32,24},{40,32},{48,40},{56,48},{64,56},{72,6... | collective-permute-start | bytes 3244040 | tf_op jit(solution)/shard_map/ppermute | solution.py:28
  24.5 3.4 %collective-permute-start = (f32[2,8,512]{2,1,0:T(8,128)S(1)}, f32[2,8,512]{2,1,0:T(8,128)S(1)}, u32[]{:S(2)}, u32[]{:S(2)}) collective-permute-start(f32[2,8,512]{2,1,0:T(8,128)S(1)} %broadcast_in_dim.2.refs_0_.refs_1_), channel_id=1, source_target_pairs={{0,1},{1,2},{2,3},{3,4},{4,5},{5,6},{6,7},{8,9},{9,10},{10,11},{11... | collective-permute-start | bytes 98312 | tf_op jit(solution)/shard_map/ppermute | solution.py:28
  27.9 2.0 %collective-permute-done.refs_2_.refs_1_.refs_4_ = f32[2,8,512]{2,1,0:T(8,128)S(1)} collective-permute-done((f32[2,8,512]{2,1,0:T(8,128)S(1)}, f32[2,8,512]{2,1,0:T(8,128)S(1)}, u32[]{:S(2)}, u32[]{:S(2)}) %collective-permute-start) | collective-permute-done | bytes 32800 | tf_op jit(solution)/shard_map/ppermute | solution.py:28
  29.9 1.2 collective-permute-done.5.refs_4_.refs_2_
  31.2 1.9 %collective-permute-start.7 = (f32[2,136,512]{2,1,0:T(8,128)S(1)}, f32[2,136,512]{2,1,0:T(8,128)S(1)}, u32[]{:S(2)}, u32[]{:S(2)}) collective-permute-start(f32[2,136,512]{2,1,0:T(8,128)S(1)} %get-tuple-element.37), channel_id=1, source_target_pairs={{1,0},{2,1},{3,2},{4,3},{5,4},{6,5},{7,6},{9,8},{10,9},{11,10},{12... | collective-permute-start | bytes 1671176 | tf_op jit(solution)/shard_map/ppermute | solution.py:28
  33.2 2.5 %collective-permute-start.6 = (f32[2,128,512]{2,1,0:T(8,128)S(1)}, f32[2,128,512]{2,1,0:T(8,128)S(1)}, u32[]{:S(2)}, u32[]{:S(2)}) collective-permute-start(f32[2,128,512]{2,1,0:T(8,128)S(1)} %get-tuple-element.36), channel_id=1, source_target_pairs={{1,0},{2,1},{3,2},{4,3},{5,4},{6,5},{7,6},{9,8},{10,9},{11,10},{12... | collective-permute-start | bytes 1572872 | tf_op jit(solution)/shard_map/ppermute | solution.py:28
  36.4 4.4 %multiply_convert_fusion = (bf16[512,512]{1,0:T(8,128)(2,1)S(1)}, bf16[512,512]{1,0:T(8,128)(2,1)S(1)}) fusion(), kind=kLoop, calls=%fused_computation.6 | loop fusion | flops 4718592 | bytes 1048576 | tf_op jit(solution)/shard_map/convert_element_type | solution.py:38
  40.8 5.4 %shard_map.55 = (bf16[1024,1024]{1,0:T(8,128)(2,1)S(1)}, bf16[1024,1024]{1,0:T(8,128)(2,1)S(1)}, bf16[1024,1024]{1,0:T(8,128)(2,1)S(1)}, bf16[1024,512]{1,0:T(8,...) custom-call(s32[1,2]{1,0:T(1,128)S(1)} %bitcast.6, ...), custom_call_target="tpu_custom_call" | custom-call | tf_op jit(solution)/shard_map/pallas_call | solution.py:54
  46.2 1.5 shard_map.58
  47.7 5.4 %collective-permute-done.4.refs_6_ = f32[2,264,512]{2,1,0:T(8,128)S(1)} collective-permute-done((f32[2,264,512]{2,1,0:T(8,128)S(1)}, f32[2,264,512]{2,1,0:T(8,128)S(1)}, u32[]{:S(2)}, u32[]{:S(2)}) %collective-permute-start.4) | collective-permute-done | bytes 1081376 | tf_op jit(solution)/shard_map/ppermute | solution.py:28
  53.2 3.5 %shard_map.59 = (f32[2,256,512]{2,1,0:T(8,128)S(1)}, f32[2,8,512]{2,1,0:T(8,128)S(1)}, bf16[1024,512]{1,0:T(8,128)(2,1)S(1)}, f32[2,264,512]{2,1,0:T(8,128)S(1)}) custom-call(s32[1,1]{1,0:T(1,128)S(6)} %copy.8.refs_0_, f32[2,8,512]{2,1,0:T(8,128)S(1)} %broadcast_in_dim.2.refs_0_.refs_1_, f32[2,128,512]{2,1,0:T(8,128)S(1)} %get-tuple-element.66.refs_2_, ...), custom_call_target="tpu_custom_call" | custom-call | tf_op jit(solution)/shard_map/pallas_call | solution.py:54
  56.6 6.5 %collective-permute-start.13 = (f32[2,264,512]{2,1,0:T(8,128)S(1)}, f32[2,264,512]{2,1,0:T(8,128)S(1)}, u32[]{:S(2)}, u32[]{:S(2)}) collective-permute-start(f32[2,264,512]{2,1,0:T(8,128)S(1)} %get-tuple-element.52.refs_6_.refs_15_), channel_id=1, source_target_pairs={{8,0},{16,8},{24,16},{32,24},{40,32},{48,40},{56,48},{64,56},{72,6... | collective-permute-start | bytes 3244040 | tf_op jit(solution)/shard_map/ppermute | solution.py:28
  63.1 2.1 %collective-permute-start.12 = (f32[2,264,512]{2,1,0:T(8,128)S(1)}, f32[2,264,512]{2,1,0:T(8,128)S(1)}, u32[]{:S(2)}, u32[]{:S(2)}) collective-permute-start(f32[2,264,512]{2,1,0:T(8,128)S(1)} %get-tuple-element.52.refs_6_.refs_15_), channel_id=1, source_target_pairs={{0,8},{8,16},{16,24},{24,32},{32,40},{40,48},{48,56},{56,64},{64,7... | collective-permute-start | bytes 3244040 | tf_op jit(solution)/shard_map/ppermute | solution.py:28
  66.1 1.9 %collective-permute-start.9 = (f32[2,256,512]{2,1,0:T(8,128)S(1)}, f32[2,256,512]{2,1,0:T(8,128)S(1)}, u32[]{:S(2)}, u32[]{:S(2)}) collective-permute-start(f32[2,256,512]{2,1,0:T(8,128)S(1)} %shard_map.60.refs_5_.refs_3_), channel_id=1, source_target_pairs={{1,0},{2,1},{3,2},{4,3},{5,4},{6,5},{7,6},{9,8},{10,9},{11,10},{12... | collective-permute-start | bytes 3145736 | tf_op jit(solution)/shard_map/ppermute | solution.py:28
  68.0 2.4 %collective-permute-start.8 = (f32[2,256,512]{2,1,0:T(8,128)S(1)}, f32[2,256,512]{2,1,0:T(8,128)S(1)}, u32[]{:S(2)}, u32[]{:S(2)}) collective-permute-start(f32[2,256,512]{2,1,0:T(8,128)S(1)} %shard_map.60.refs_5_.refs_3_), channel_id=1, source_target_pairs={{0,1},{1,2},{2,3},{3,4},{4,5},{5,6},{6,7},{8,9},{9,10},{10,11},{11... | collective-permute-start | bytes 3145736 | tf_op jit(solution)/shard_map/ppermute | solution.py:28
  70.4 9.9 %collective-permute-done.9.refs_7_ = f32[2,256,512]{2,1,0:T(8,128)S(1)} collective-permute-done((f32[2,256,512]{2,1,0:T(8,128)S(1)}, f32[2,256,512]{2,1,0:T(8,128)S(1)}, u32[]{:S(2)}, u32[]{:S(2)}) %collective-permute-start.9) | collective-permute-done | bytes 1048608 | tf_op jit(solution)/shard_map/ppermute | solution.py:28
  80.3 3.8 %collective-permute-done.8.refs_6_ = f32[2,256,512]{2,1,0:T(8,128)S(1)} collective-permute-done((f32[2,256,512]{2,1,0:T(8,128)S(1)}, f32[2,256,512]{2,1,0:T(8,128)S(1)}, u32[]{:S(2)}, u32[]{:S(2)}) %collective-permute-start.8) | collective-permute-done | bytes 1048608 | tf_op jit(solution)/shard_map/ppermute | solution.py:28
  84.1 1.8 %shard_map.61 = (f32[2,264,512]{2,1,0:T(8,128)S(1)}, f32[2,264,512]{2,1,0:T(8,128)S(1)}, f32[2,256,512]{2,1,0:T(8,128)S(1)}) custom-call(f32[2,8,512]{2,1,0:T(8,128)S(1)} %broadcast_in_dim.2.refs_0_.refs_1_, f32[2,8,512]{2,1,0:T(8,128)S(1)} %collective-permute-done.refs_2_.refs_1_.refs_4_, f32[2,8,512]{2,1,0:T(8,128)S(1)} %get-tuple-element.45.refs_2_.refs_5_.refs_3_, ...), custom_call_target="tpu_custom_call" | custom-call | tf_op jit(solution)/shard_map/pallas_call | solution.py:54
  85.9 1.9 %collective-permute-start.10 = (f32[2,264,512]{2,1,0:T(8,128)S(1)}, f32[2,264,512]{2,1,0:T(8,128)S(1)}, u32[]{:S(2)}, u32[]{:S(2)}) collective-permute-start(f32[2,264,512]{2,1,0:T(8,128)S(1)} %get-tuple-element.49), channel_id=1, source_target_pairs={{0,8},{8,16},{16,24},{24,32},{32,40},{40,48},{48,56},{56,64},{64,7... | collective-permute-start | bytes 3244040 | tf_op jit(solution)/shard_map/ppermute | solution.py:28
  87.8 6.0 %collective-permute-start.11 = (f32[2,264,512]{2,1,0:T(8,128)S(1)}, f32[2,264,512]{2,1,0:T(8,128)S(1)}, u32[]{:S(2)}, u32[]{:S(2)}) collective-permute-start(f32[2,264,512]{2,1,0:T(8,128)S(1)} %get-tuple-element.50.refs_0_), channel_id=1, source_target_pairs={{8,0},{16,8},{24,16},{32,24},{40,32},{48,40},{56,48},{64,56},{72,6... | collective-permute-start | bytes 3244040 | tf_op jit(solution)/shard_map/ppermute | solution.py:28
  93.9 2.1 %shard_map.62 = (f32[2,256,512]{2,1,0:T(8,128)S(1)}, f32[2,256,512]{2,1,0:T(8,128)S(1)}, f32[2,256,512]{2,1,0:T(8,128)S(1)}) custom-call(f32[2,264,512]{2,1,0:T(8,128)S(1)} %get-tuple-element.50.refs_0_, f32[2,8,512]{2,1,0:T(8,128)S(1)} %broadcast_in_dim.2.refs_0_.refs_1_, f32[2,8,512]{2,1,0:T(8,128)S(1)} %collective-permute-done.3.refs_1_.refs_3_.refs_2_, ...), custom_call_target="tpu_custom_call" | custom-call | tf_op jit(solution)/shard_map/pallas_call | solution.py:54
  96.0 1.9 %collective-permute-start.14 = (f32[2,256,512]{2,1,0:T(8,128)S(1)}, f32[2,256,512]{2,1,0:T(8,128)S(1)}, u32[]{:S(2)}, u32[]{:S(2)}) collective-permute-start(f32[2,256,512]{2,1,0:T(8,128)S(1)} %get-tuple-element.54), channel_id=1, source_target_pairs={{0,1},{1,2},{2,3},{3,4},{4,5},{5,6},{6,7},{8,9},{9,10},{10,11},{11... | collective-permute-start | bytes 3145736 | tf_op jit(solution)/shard_map/ppermute | solution.py:28
  97.9 3.6 %collective-permute-start.15 = (f32[2,256,512]{2,1,0:T(8,128)S(1)}, f32[2,256,512]{2,1,0:T(8,128)S(1)}, u32[]{:S(2)}, u32[]{:S(2)}) collective-permute-start(f32[2,256,512]{2,1,0:T(8,128)S(1)} %get-tuple-element.55), channel_id=1, source_target_pairs={{1,0},{2,1},{3,2},{4,3},{5,4},{6,5},{7,6},{9,8},{10,9},{11,10},{12... | collective-permute-start | bytes 3145736 | tf_op jit(solution)/shard_map/ppermute | solution.py:28
  101.6 10.5 %collective-permute-done.14.refs_5_ = f32[2,256,512]{2,1,0:T(8,128)S(1)} collective-permute-done((f32[2,256,512]{2,1,0:T(8,128)S(1)}, f32[2,256,512]{2,1,0:T(8,128)S(1)}, u32[]{:S(2)}, u32[]{:S(2)}) %collective-permute-start.14) | collective-permute-done | bytes 1048608 | tf_op jit(solution)/shard_map/ppermute | solution.py:28
  112.1 1.8 %collective-permute-done.15.refs_6_ = f32[2,256,512]{2,1,0:T(8,128)S(1)} collective-permute-done((f32[2,256,512]{2,1,0:T(8,128)S(1)}, f32[2,256,512]{2,1,0:T(8,128)S(1)}, u32[]{:S(2)}, u32[]{:S(2)}) %collective-permute-start.15) | collective-permute-done | bytes 1048608 | tf_op jit(solution)/shard_map/ppermute | solution.py:28
  113.9 1.5 shard_map.63.refs_8_
  116.0 3.5 %shard_map.64 = (bf16[1024,512]{1,0:T(8,128)(2,1)S(1)}, f32[2,256,512]{2,1,0:T(8,128)S(1)}) custom-call(s32[1,1]{1,0:T(1,128)S(6)} %copy.8.refs_0_, f32[2,8,512]{2,1,0:T(8,128)S(1)} %broadcast_in_dim.2.refs_0_.refs_1_, f32[2,8,512]{2,1,0:T(8,128)S(1)} %get-tuple-element.44.refs_4_.refs_3_.refs_1_.refs_2_, ...), custom_call_target="tpu_custom_call" | custom-call | tf_op jit(solution)/shard_map/pallas_call | solution.py:54
  119.5 1.9 %collective-permute-start.19 = (f32[2,256,512]{2,1,0:T(8,128)S(1)}, f32[2,256,512]{2,1,0:T(8,128)S(1)}, u32[]{:S(2)}, u32[]{:S(2)}) collective-permute-start(f32[2,256,512]{2,1,0:T(8,128)S(1)} %get-tuple-element.61.refs_4_), channel_id=1, source_target_pairs={{0,8},{8,16},{16,24},{24,32},{32,40},{40,48},{48,56},{56,64},{64,7... | collective-permute-start | bytes 3145736 | tf_op jit(solution)/shard_map/ppermute | solution.py:28
  122.3 2.9 %collective-permute-start.16 = (f32[2,128,512]{2,1,0:T(8,128)S(1)}, f32[2,128,512]{2,1,0:T(8,128)S(1)}, u32[]{:S(2)}, u32[]{:S(2)}) collective-permute-start(f32[2,128,512]{2,1,0:T(8,128)S(1)} %get-tuple-element.57.refs_4_), channel_id=1, source_target_pairs={{0,1},{1,2},{2,3},{3,4},{4,5},{5,6},{6,7},{8,9},{9,10},{10,11},{11... | collective-permute-start | bytes 1572872 | tf_op jit(solution)/shard_map/ppermute | solution.py:28
  125.2 1.9 %collective-permute-start.17 = (f32[2,128,512]{2,1,0:T(8,128)S(1)}, f32[2,128,512]{2,1,0:T(8,128)S(1)}, u32[]{:S(2)}, u32[]{:S(2)}) collective-permute-start(f32[2,128,512]{2,1,0:T(8,128)S(1)} %get-tuple-element.58.refs_5_), channel_id=1, source_target_pairs={{0,1},{1,2},{2,3},{3,4},{4,5},{5,6},{6,7},{8,9},{9,10},{10,11},{11... | collective-permute-start | bytes 1572872 | tf_op jit(solution)/shard_map/ppermute | solution.py:28
  127.1 5.7 %collective-permute-done.16.refs_6_ = f32[2,128,512]{2,1,0:T(8,128)S(1)} collective-permute-done((f32[2,128,512]{2,1,0:T(8,128)S(1)}, f32[2,128,512]{2,1,0:T(8,128)S(1)}, u32[]{:S(2)}, u32[]{:S(2)}) %collective-permute-start.16) | collective-permute-done | bytes 524320 | tf_op jit(solution)/shard_map/ppermute | solution.py:28
  132.8 5.6 %collective-permute-done.17.refs_7_ = f32[2,128,512]{2,1,0:T(8,128)S(1)} collective-permute-done((f32[2,128,512]{2,1,0:T(8,128)S(1)}, f32[2,128,512]{2,1,0:T(8,128)S(1)}, u32[]{:S(2)}, u32[]{:S(2)}) %collective-permute-start.17) | collective-permute-done | bytes 524320 | tf_op jit(solution)/shard_map/ppermute | solution.py:28
  139.0 1.9 %collective-permute-start.18 = (f32[2,256,512]{2,1,0:T(8,128)S(1)}, f32[2,256,512]{2,1,0:T(8,128)S(1)}, u32[]{:S(2)}, u32[]{:S(2)}) collective-permute-start(f32[2,256,512]{2,1,0:T(8,128)S(1)} %get-tuple-element.60.refs_0_), channel_id=1, source_target_pairs={{0,8},{8,16},{16,24},{24,32},{32,40},{40,48},{48,56},{56,64},{64,7... | collective-permute-start | bytes 3145736 | tf_op jit(solution)/shard_map/ppermute | solution.py:28
  141.0 9.0 %collective-permute-done.19.refs_5_ = f32[2,256,512]{2,1,0:T(8,128)S(1)} collective-permute-done((f32[2,256,512]{2,1,0:T(8,128)S(1)}, f32[2,256,512]{2,1,0:T(8,128)S(1)}, u32[]{:S(2)}, u32[]{:S(2)}) %collective-permute-start.19) | collective-permute-done | bytes 1048608 | tf_op jit(solution)/shard_map/ppermute | solution.py:28
  150.4 1.9 %collective-permute-start.20 = (f32[2,128,512]{2,1,0:T(8,128)S(1)}, f32[2,128,512]{2,1,0:T(8,128)S(1)}, u32[]{:S(2)}, u32[]{:S(2)}) collective-permute-start(f32[2,128,512]{2,1,0:T(8,128)S(1)} %get-tuple-element.63), channel_id=1, source_target_pairs={{0,1},{1,2},{2,3},{3,4},{4,5},{5,6},{6,7},{8,9},{9,10},{10,11},{11... | collective-permute-start | bytes 1572872 | tf_op jit(solution)/shard_map/ppermute | solution.py:28
  152.3 2.4 %collective-permute-start.21 = (f32[2,128,512]{2,1,0:T(8,128)S(1)}, f32[2,128,512]{2,1,0:T(8,128)S(1)}, u32[]{:S(2)}, u32[]{:S(2)}) collective-permute-start(f32[2,128,512]{2,1,0:T(8,128)S(1)} %get-tuple-element.64), channel_id=1, source_target_pairs={{0,1},{1,2},{2,3},{3,4},{4,5},{5,6},{6,7},{8,9},{9,10},{10,11},{11... | collective-permute-start | bytes 1572872 | tf_op jit(solution)/shard_map/ppermute | solution.py:28
  154.7 6.2 %collective-permute-done.20.refs_0_ = f32[2,128,512]{2,1,0:T(8,128)S(1)} collective-permute-done((f32[2,128,512]{2,1,0:T(8,128)S(1)}, f32[2,128,512]{2,1,0:T(8,128)S(1)}, u32[]{:S(2)}, u32[]{:S(2)}) %collective-permute-start.20) | collective-permute-done | bytes 524320 | tf_op jit(solution)/shard_map/ppermute | solution.py:28
  160.9 5.6 %collective-permute-done.21.refs_1_ = f32[2,128,512]{2,1,0:T(8,128)S(1)} collective-permute-done((f32[2,128,512]{2,1,0:T(8,128)S(1)}, f32[2,128,512]{2,1,0:T(8,128)S(1)}, u32[]{:S(2)}, u32[]{:S(2)}) %collective-permute-start.21) | collective-permute-done | bytes 524320 | tf_op jit(solution)/shard_map/ppermute | solution.py:28
  166.5 1.0 shard_map.68.refs_1_
  167.6 4.4 %collective-permute-done.18.refs_0_ = f32[2,256,512]{2,1,0:T(8,128)S(1)} collective-permute-done((f32[2,256,512]{2,1,0:T(8,128)S(1)}, f32[2,256,512]{2,1,0:T(8,128)S(1)}, u32[]{:S(2)}, u32[]{:S(2)}) %collective-permute-start.18) | collective-permute-done | bytes 1048608 | tf_op jit(solution)/shard_map/ppermute | solution.py:28
  172.0 1.1 shard_map.69
  (24 shorter events, 3.7 us)
Async XLA Ops:
  0.0 7.6 %copy-start.3 = (f32[2,512,512]{2,1,0:T(8,128)S(1)}, f32[2,512,512]{2,1,0:T(8,128)}, u32[]{:S(2)}) copy-start(f32[2,512,512]{2,1,0:T(8,128)} %param.5) | copy-start | bytes 6291460
  0.0 12.2 %copy-start.2 = (s32[1,1,1,2]{3,2,1,0:T(1,128)S(1)}, s32[1,1,1,2]{3,2,1,0:T(1,128)}, u32[]{:S(2)}) copy-start(s32[1,1,1,2]{3,2,1,0:T(1,128)} %param.8) | copy-start | bytes 28
  1.4 29.7 %collective-permute-start.5 = (f32[2,256,512]{2,1,0:T(8,128)S(1)}, f32[2,256,512]{2,1,0:T(8,128)S(1)}, u32[]{:S(2)}, u32[]{:S(2)}) collective-permute-start(f32[2,256,512]{2,1,0:T(8,128)S(1)} %slice.11.refs_3_.refs_1_), channel_id=1, source_target_pairs={{8,0},{16,8},{24,16},{32,24},{40,32},{48,40},{56,48},{64,56},{72,6... | collective-permute-start | bytes 3145736 | tf_op jit(solution)/shard_map/ppermute | solution.py:28
  7.7 12.5 %collective-permute-start.2 = (f32[2,128,512]{2,1,0:T(8,128)S(1)}, f32[2,128,512]{2,1,0:T(8,128)S(1)}, u32[]{:S(2)}, u32[]{:S(2)}) collective-permute-start(f32[2,128,512]{2,1,0:T(8,128)S(1)} %get-tuple-element.65.refs_3_), channel_id=1, source_target_pairs={{1,0},{2,1},{3,2},{4,3},{5,4},{6,5},{7,6},{9,8},{10,9},{11,10},{12... | collective-permute-start | bytes 1572872 | tf_op jit(solution)/shard_map/ppermute | solution.py:28
  9.6 12.3 %collective-permute-start.1 = (f32[2,128,512]{2,1,0:T(8,128)S(1)}, f32[2,128,512]{2,1,0:T(8,128)S(1)}, u32[]{:S(2)}, u32[]{:S(2)}) collective-permute-start(f32[2,128,512]{2,1,0:T(8,128)S(1)} %get-tuple-element.66.refs_2_), channel_id=1, source_target_pairs={{1,0},{2,1},{3,2},{4,3},{5,4},{6,5},{7,6},{9,8},{10,9},{11,10},{12... | collective-permute-start | bytes 1572872 | tf_op jit(solution)/shard_map/ppermute | solution.py:28
  12.2 7.9 %collective-permute-start.3 = (f32[2,8,512]{2,1,0:T(8,128)S(1)}, f32[2,8,512]{2,1,0:T(8,128)S(1)}, u32[]{:S(2)}, u32[]{:S(2)}) collective-permute-start(f32[2,8,512]{2,1,0:T(8,128)S(1)} %broadcast_in_dim.2.refs_0_.refs_1_), channel_id=1, source_target_pairs={{0,8},{8,16},{16,24},{24,32},{32,40},{40,48},{48,56},{56,64},{64,7... | collective-permute-start | bytes 98312 | tf_op jit(solution)/shard_map/ppermute | solution.py:28
  22.0 18.8 %copy-start.1 = (f32[2,512,512]{2,1,0:T(8,128)S(1)}, f32[2,512,512]{2,1,0:T(8,128)}, u32[]{:S(2)}) copy-start(f32[2,512,512]{2,1,0:T(8,128)} %refs_3_.1) | copy-start | bytes 6291460
  22.0 31.1 %collective-permute-start.4 = (f32[2,264,512]{2,1,0:T(8,128)S(1)}, f32[2,264,512]{2,1,0:T(8,128)S(1)}, u32[]{:S(2)}, u32[]{:S(2)}) collective-permute-start(f32[2,264,512]{2,1,0:T(8,128)S(1)} %shard_map.56.refs_0_), channel_id=1, source_target_pairs={{8,0},{16,8},{24,16},{32,24},{40,32},{48,40},{56,48},{64,56},{72,6... | collective-permute-start | bytes 3244040 | tf_op jit(solution)/shard_map/ppermute | solution.py:28
  24.5 5.4 %collective-permute-start = (f32[2,8,512]{2,1,0:T(8,128)S(1)}, f32[2,8,512]{2,1,0:T(8,128)S(1)}, u32[]{:S(2)}, u32[]{:S(2)}) collective-permute-start(f32[2,8,512]{2,1,0:T(8,128)S(1)} %broadcast_in_dim.2.refs_0_.refs_1_), channel_id=1, source_target_pairs={{0,1},{1,2},{2,3},{3,4},{4,5},{5,6},{6,7},{8,9},{9,10},{10,11},{11... | collective-permute-start | bytes 98312 | tf_op jit(solution)/shard_map/ppermute | solution.py:28
  31.2 14.9 %collective-permute-start.7 = (f32[2,136,512]{2,1,0:T(8,128)S(1)}, f32[2,136,512]{2,1,0:T(8,128)S(1)}, u32[]{:S(2)}, u32[]{:S(2)}) collective-permute-start(f32[2,136,512]{2,1,0:T(8,128)S(1)} %get-tuple-element.37), channel_id=1, source_target_pairs={{1,0},{2,1},{3,2},{4,3},{5,4},{6,5},{7,6},{9,8},{10,9},{11,10},{12... | collective-permute-start | bytes 1671176 | tf_op jit(solution)/shard_map/ppermute | solution.py:28
  33.2 13.0 %collective-permute-start.6 = (f32[2,128,512]{2,1,0:T(8,128)S(1)}, f32[2,128,512]{2,1,0:T(8,128)S(1)}, u32[]{:S(2)}, u32[]{:S(2)}) collective-permute-start(f32[2,128,512]{2,1,0:T(8,128)S(1)} %get-tuple-element.36), channel_id=1, source_target_pairs={{1,0},{2,1},{3,2},{4,3},{5,4},{6,5},{7,6},{9,8},{10,9},{11,10},{12... | collective-permute-start | bytes 1572872 | tf_op jit(solution)/shard_map/ppermute | solution.py:28
  46.2 7.0 %copy-start = (f32[1,1,1,512,512]{4,3,2,1,0:T(8,128)S(1)}, f32[1,1,1,512,512]{4,3,2,1,0:T(8,128)}, u32[]{:S(2)}) copy-start(f32[1,1,1,512,512]{4,3,2,1,0:T(8,128)} %param.7) | copy-start | bytes 3145732
  56.6 37.3 %collective-permute-start.13 = (f32[2,264,512]{2,1,0:T(8,128)S(1)}, f32[2,264,512]{2,1,0:T(8,128)S(1)}, u32[]{:S(2)}, u32[]{:S(2)}) collective-permute-start(f32[2,264,512]{2,1,0:T(8,128)S(1)} %get-tuple-element.52.refs_6_.refs_15_), channel_id=1, source_target_pairs={{8,0},{16,8},{24,16},{32,24},{40,32},{48,40},{56,48},{64,56},{72,6... | collective-permute-start | bytes 3244040 | tf_op jit(solution)/shard_map/ppermute | solution.py:28
  63.1 30.8 %collective-permute-start.12 = (f32[2,264,512]{2,1,0:T(8,128)S(1)}, f32[2,264,512]{2,1,0:T(8,128)S(1)}, u32[]{:S(2)}, u32[]{:S(2)}) collective-permute-start(f32[2,264,512]{2,1,0:T(8,128)S(1)} %get-tuple-element.52.refs_6_.refs_15_), channel_id=1, source_target_pairs={{0,8},{8,16},{16,24},{24,32},{32,40},{40,48},{48,56},{56,64},{64,7... | collective-permute-start | bytes 3244040 | tf_op jit(solution)/shard_map/ppermute | solution.py:28
  66.1 14.2 %collective-permute-start.9 = (f32[2,256,512]{2,1,0:T(8,128)S(1)}, f32[2,256,512]{2,1,0:T(8,128)S(1)}, u32[]{:S(2)}, u32[]{:S(2)}) collective-permute-start(f32[2,256,512]{2,1,0:T(8,128)S(1)} %shard_map.60.refs_5_.refs_3_), channel_id=1, source_target_pairs={{1,0},{2,1},{3,2},{4,3},{5,4},{6,5},{7,6},{9,8},{10,9},{11,10},{12... | collective-permute-start | bytes 3145736 | tf_op jit(solution)/shard_map/ppermute | solution.py:28
  68.0 16.1 %collective-permute-start.8 = (f32[2,256,512]{2,1,0:T(8,128)S(1)}, f32[2,256,512]{2,1,0:T(8,128)S(1)}, u32[]{:S(2)}, u32[]{:S(2)}) collective-permute-start(f32[2,256,512]{2,1,0:T(8,128)S(1)} %shard_map.60.refs_5_.refs_3_), channel_id=1, source_target_pairs={{0,1},{1,2},{2,3},{3,4},{4,5},{5,6},{6,7},{8,9},{9,10},{10,11},{11... | collective-permute-start | bytes 3145736 | tf_op jit(solution)/shard_map/ppermute | solution.py:28
  85.9 29.5 %collective-permute-start.10 = (f32[2,264,512]{2,1,0:T(8,128)S(1)}, f32[2,264,512]{2,1,0:T(8,128)S(1)}, u32[]{:S(2)}, u32[]{:S(2)}) collective-permute-start(f32[2,264,512]{2,1,0:T(8,128)S(1)} %get-tuple-element.49), channel_id=1, source_target_pairs={{0,8},{8,16},{16,24},{24,32},{32,40},{40,48},{48,56},{56,64},{64,7... | collective-permute-start | bytes 3244040 | tf_op jit(solution)/shard_map/ppermute | solution.py:28
  87.8 28.1 %collective-permute-start.11 = (f32[2,264,512]{2,1,0:T(8,128)S(1)}, f32[2,264,512]{2,1,0:T(8,128)S(1)}, u32[]{:S(2)}, u32[]{:S(2)}) collective-permute-start(f32[2,264,512]{2,1,0:T(8,128)S(1)} %get-tuple-element.50.refs_0_), channel_id=1, source_target_pairs={{8,0},{16,8},{24,16},{32,24},{40,32},{48,40},{56,48},{64,56},{72,6... | collective-permute-start | bytes 3244040 | tf_op jit(solution)/shard_map/ppermute | solution.py:28
  96.0 16.1 %collective-permute-start.14 = (f32[2,256,512]{2,1,0:T(8,128)S(1)}, f32[2,256,512]{2,1,0:T(8,128)S(1)}, u32[]{:S(2)}, u32[]{:S(2)}) collective-permute-start(f32[2,256,512]{2,1,0:T(8,128)S(1)} %get-tuple-element.54), channel_id=1, source_target_pairs={{0,1},{1,2},{2,3},{3,4},{4,5},{5,6},{6,7},{8,9},{9,10},{10,11},{11... | collective-permute-start | bytes 3145736 | tf_op jit(solution)/shard_map/ppermute | solution.py:28
  97.9 15.9 %collective-permute-start.15 = (f32[2,256,512]{2,1,0:T(8,128)S(1)}, f32[2,256,512]{2,1,0:T(8,128)S(1)}, u32[]{:S(2)}, u32[]{:S(2)}) collective-permute-start(f32[2,256,512]{2,1,0:T(8,128)S(1)} %get-tuple-element.55), channel_id=1, source_target_pairs={{1,0},{2,1},{3,2},{4,3},{5,4},{6,5},{7,6},{9,8},{10,9},{11,10},{12... | collective-permute-start | bytes 3145736 | tf_op jit(solution)/shard_map/ppermute | solution.py:28
  119.5 30.4 %collective-permute-start.19 = (f32[2,256,512]{2,1,0:T(8,128)S(1)}, f32[2,256,512]{2,1,0:T(8,128)S(1)}, u32[]{:S(2)}, u32[]{:S(2)}) collective-permute-start(f32[2,256,512]{2,1,0:T(8,128)S(1)} %get-tuple-element.61.refs_4_), channel_id=1, source_target_pairs={{0,8},{8,16},{16,24},{24,32},{32,40},{40,48},{48,56},{56,64},{64,7... | collective-permute-start | bytes 3145736 | tf_op jit(solution)/shard_map/ppermute | solution.py:28
  122.3 10.5 %collective-permute-start.16 = (f32[2,128,512]{2,1,0:T(8,128)S(1)}, f32[2,128,512]{2,1,0:T(8,128)S(1)}, u32[]{:S(2)}, u32[]{:S(2)}) collective-permute-start(f32[2,128,512]{2,1,0:T(8,128)S(1)} %get-tuple-element.57.refs_4_), channel_id=1, source_target_pairs={{0,1},{1,2},{2,3},{3,4},{4,5},{5,6},{6,7},{8,9},{9,10},{10,11},{11... | collective-permute-start | bytes 1572872 | tf_op jit(solution)/shard_map/ppermute | solution.py:28
  125.2 13.2 %collective-permute-start.17 = (f32[2,128,512]{2,1,0:T(8,128)S(1)}, f32[2,128,512]{2,1,0:T(8,128)S(1)}, u32[]{:S(2)}, u32[]{:S(2)}) collective-permute-start(f32[2,128,512]{2,1,0:T(8,128)S(1)} %get-tuple-element.58.refs_5_), channel_id=1, source_target_pairs={{0,1},{1,2},{2,3},{3,4},{4,5},{5,6},{6,7},{8,9},{9,10},{10,11},{11... | collective-permute-start | bytes 1572872 | tf_op jit(solution)/shard_map/ppermute | solution.py:28
  139.0 33.0 %collective-permute-start.18 = (f32[2,256,512]{2,1,0:T(8,128)S(1)}, f32[2,256,512]{2,1,0:T(8,128)S(1)}, u32[]{:S(2)}, u32[]{:S(2)}) collective-permute-start(f32[2,256,512]{2,1,0:T(8,128)S(1)} %get-tuple-element.60.refs_0_), channel_id=1, source_target_pairs={{0,8},{8,16},{16,24},{24,32},{32,40},{40,48},{48,56},{56,64},{64,7... | collective-permute-start | bytes 3145736 | tf_op jit(solution)/shard_map/ppermute | solution.py:28
  150.4 10.5 %collective-permute-start.20 = (f32[2,128,512]{2,1,0:T(8,128)S(1)}, f32[2,128,512]{2,1,0:T(8,128)S(1)}, u32[]{:S(2)}, u32[]{:S(2)}) collective-permute-start(f32[2,128,512]{2,1,0:T(8,128)S(1)} %get-tuple-element.63), channel_id=1, source_target_pairs={{0,1},{1,2},{2,3},{3,4},{4,5},{5,6},{6,7},{8,9},{9,10},{10,11},{11... | collective-permute-start | bytes 1572872 | tf_op jit(solution)/shard_map/ppermute | solution.py:28
  152.3 14.2 %collective-permute-start.21 = (f32[2,128,512]{2,1,0:T(8,128)S(1)}, f32[2,128,512]{2,1,0:T(8,128)S(1)}, u32[]{:S(2)}, u32[]{:S(2)}) collective-permute-start(f32[2,128,512]{2,1,0:T(8,128)S(1)} %get-tuple-element.64), channel_id=1, source_target_pairs={{0,1},{1,2},{2,3},{3,4},{4,5},{5,6},{6,7},{8,9},{9,10},{10,11},{11... | collective-permute-start | bytes 1572872 | tf_op jit(solution)/shard_map/ppermute | solution.py:28

commit v5 on v4

--- a/solution.py
+++ b/solution.py
@@ -154,7 +154,7 @@
 
 def finish(acc, byt_tail, half, amp, live, bxt, left, stacked):
     w = amp.shape[0]
-    block = 128
+    block = 256
     alive = (live[0, 0] > 0).astype(F32)
     for first in range(0, w, block):
         rows = slice(first, first + block)
@@ -171,13 +171,15 @@
 
 def back(first, by, stacked, pupil, out, extra):
     w = stacked.shape[1]
-    for row, rows in split(first, w):
-        size = rows.stop - rows.start
-        back_r = dot(by[row : row + size, :], stacked[...])
-        back_i = dot(by[w + row : w + row + size, :], stacked[...])
-        pr, pi = pupil[0, row : row + size, :], pupil[1, row : row + size, :]
-        grad_r = back_r * pr + back_i * pi
-        grad_i = back_i * pr - back_r * pi
+    h = w // 2
+    back_r = dot(by[first : first + h, :], stacked[...])
+    back_i = dot(by[w + first : w + first + h, :], stacked[...])
+    for row, rows in split(first, w):
+        across = slice(row, row + rows.stop - rows.start)
+        pr, pi = pupil[0, across, :], pupil[1, across, :]
+        br, bi = back_r[rows, :], back_i[rows, :]
+        grad_r = br * pr + bi * pi
+        grad_i = bi * pr - br * pi
         if extra is not None:
             grad_r = grad_r + part(extra, 0, rows, w)
             grad_i = grad_i + part(extra, 1, rows, w)
@@ -273,7 +275,7 @@
 
 
 def between_kernel(
-    first, head, me, minus, plus, target_minus, target_plus, mine, got_minus, got_plus, to_minus, to_plus, own
+    first, head, me, minus, plus, target_minus, target_plus, mine, got_minus, got_plus, to_minus, to_plus
 ):
     w = me.shape[2]
     for row, rows in split(first, w):
@@ -286,13 +288,22 @@
 
         minus_m = [a & ~b for a, b in zip(seen(ways[0](target_minus)), (s, s_minus, s_plus))]
         plus_m = [a & b for a, b in zip(seen(ways[0](target_plus)), (s, s_minus, s_plus))]
-        _, own_minus, own_plus = seen(f)
-        own_minus, own_plus = own_minus & (s == s_minus), own_plus & (s == s_plus)
         for plane in range(2):
             values = [part(x, plane, rows, w) for x in (mine, got_minus, got_plus)]
             for out, masks in ((to_minus, minus_m), (to_plus, plus_m)):
                 terms = [jnp.where(m, v, 0.0) for m, v in zip(masks, values)]
                 put(out, plane, rows, terms[0] + terms[1] + terms[2])
+
+
+def own_kernel(first, head, me, minus, plus, mine, got_minus, got_plus, own):
+    w = me.shape[2]
+    for row, rows in split(first, w):
+        ways = ways_of(head, rows, w, row)
+        f, f_minus, f_plus = (ways[0](x) for x in (me, minus, plus))
+        s, s_minus, s_plus = (ways[1](x) for x in (me, minus, plus))
+        own_minus, own_plus = ~f & f_minus & (s == s_minus), f & ~f_plus & (s == s_plus)
+        for plane in range(2):
+            values = [part(x, plane, rows, w) for x in (mine, got_minus, got_plus)]
             others = jnp.where(own_minus, values[1], 0.0) + jnp.where(own_plus, values[2], 0.0)
             put(own, plane, rows, values[0] + others)
 
@@ -406,17 +417,29 @@
     got_above, got_under = shifted(head_grad, "row", 1), shifted(head_grad, "row", -1)
     (tail_grad,) = call(functools.partial(rest_first, h), [[half]], (by, stacked, rolled))
     got_left, got_right = each(tail_grad, "col", 1), each(tail_grad, "col", -1)
-    to_up, to_down, tail_own = call(
+    to_up, to_down = call(
         functools.partial(between_kernel, h, False),
-        [block(h + PAD)] * 2 + [half],
+        [block(h + PAD), block(h + PAD)],
         (me, left_of, right_of, above, under, tail_grad, got_left, got_right),
     )
+    (tail_own,) = call(
+        functools.partial(own_kernel, h, False),
+        [half],
+        (me, left_of, right_of, tail_grad, got_left, got_right),
+        after=(to_up,),
+    )
     tail_sums = (tail_own, shifted(to_down, "row", 1), shifted(to_up, "row", -1))
-    to_left, to_right, head_own = call(
+    to_left, to_right = call(
         functools.partial(between_kernel, 0, True),
-        [[half], [half], half],
+        [[half], [half]],
         (me, above, under, left_of, right_of, head_grad, got_above, got_under),
         after=(to_up,),
+    )
+    (head_own,) = call(
+        functools.partial(own_kernel, 0, True),
+        [half],
+        (me, above, under, head_grad, got_above, got_under),
+        after=(to_left[0],),
     )
     head_sums = (head_own, each(to_right, "col", 1), each(to_left, "col", -1))
 

time: 174 us -> 173 us (level)
    pallas_call x13 -> x15, Pallas kernels: 22.3 us -> 22.1 us  [call(): pl.pallas_call(body, out_shape=out_flat, in_specs=[ANY] * skip + [SMEM] *...]
  transfers between devices with their start and end apart: 22 -> 22, of which waited for: 16 -> 17; matrix products, arithmetic and copies ran while one was open for 3% -> 3% of each run, Pallas kernels for 9% -> 9%
where the time goes in v5:
time: 173 us
  waiting for transfers between devices  78.9 us (46%)
  starting transfers between devices  62.3 us (36%)
  Pallas kernels  24.2 us (14%)
  other arithmetic  4.4 us (3%)
    ppermute x22, waiting for transfers between devices, shifted(): lax.ppermute(value, axis, [(source, source + steps) for source in range(l...  78.9 us
    ppermute x22, starting transfers between devices, shifted(): lax.ppermute(value, axis, [(source, source + steps) for source in range(l...  62.3 us
    pallas_call x15, Pallas kernels, call(): pl.pallas_call(body, out_shape=out_flat, in_specs=[ANY] * skip + [SMEM] *...  22.1 us
    convert_element_type x1, other arithmetic, dft_tables(): (jnp.sin(angle) * scale).astype(jnp.bfloat16)  4.39 us
  transfers between devices with their start and end apart: 22, of which 17 were waited for; matrix products, arithmetic and copies ran while one was open for 3% of the time, Pallas kernels for 9%

profile of v5, /device:TPU:28, one launch (start us, length us, event | category | flops | bytes accessed | tf_op | source)
XLA Modules:
  0.0 172.6 jit_solution(14359532038015991435)
XLA Ops:
  0.0 1.4 slice.11.refs_3_.refs_1_
  1.4 6.1 %collective-permute-start.5 = (f32[2,256,512]{2,1,0:T(8,128)S(1)}, f32[2,256,512]{2,1,0:T(8,128)S(1)}, u32[]{:S(2)}, u32[]{:S(2)}) collective-permute-start(f32[2,256,512]{2,1,0:T(8,128)S(1)} %slice.11.refs_3_.refs_1_), channel_id=1, source_target_pairs={{8,0},{16,8},{24,16},{32,24},{40,32},{48,40},{56,48},{64,56},{72,6... | collective-permute-start | bytes 3145736 | tf_op jit(solution)/shard_map/ppermute | solution.py:28
  7.7 1.9 %collective-permute-start.2 = (f32[2,128,512]{2,1,0:T(8,128)S(1)}, f32[2,128,512]{2,1,0:T(8,128)S(1)}, u32[]{:S(2)}, u32[]{:S(2)}) collective-permute-start(f32[2,128,512]{2,1,0:T(8,128)S(1)} %get-tuple-element.61.refs_3_), channel_id=1, source_target_pairs={{1,0},{2,1},{3,2},{4,3},{5,4},{6,5},{7,6},{9,8},{10,9},{11,10},{12... | collective-permute-start | bytes 1572872 | tf_op jit(solution)/shard_map/ppermute | solution.py:28
  9.6 2.5 %collective-permute-start.1 = (f32[2,128,512]{2,1,0:T(8,128)S(1)}, f32[2,128,512]{2,1,0:T(8,128)S(1)}, u32[]{:S(2)}, u32[]{:S(2)}) collective-permute-start(f32[2,128,512]{2,1,0:T(8,128)S(1)} %get-tuple-element.62.refs_2_), channel_id=1, source_target_pairs={{1,0},{2,1},{3,2},{4,3},{5,4},{6,5},{7,6},{9,8},{10,9},{11,10},{12... | collective-permute-start | bytes 1572872 | tf_op jit(solution)/shard_map/ppermute | solution.py:28
  12.2 1.9 %collective-permute-start.3 = (f32[2,8,512]{2,1,0:T(8,128)S(1)}, f32[2,8,512]{2,1,0:T(8,128)S(1)}, u32[]{:S(2)}, u32[]{:S(2)}) collective-permute-start(f32[2,8,512]{2,1,0:T(8,128)S(1)} %broadcast_in_dim.2.refs_0_.refs_1_), channel_id=1, source_target_pairs={{0,8},{8,16},{16,24},{24,32},{32,40},{40,48},{48,56},{56,64},{64,7... | collective-permute-start | bytes 98312 | tf_op jit(solution)/shard_map/ppermute | solution.py:28
  14.2 6.0 %collective-permute-done.3.refs_1_.refs_3_.refs_2_ = f32[2,8,512]{2,1,0:T(8,128)S(1)} collective-permute-done((f32[2,8,512]{2,1,0:T(8,128)S(1)}, f32[2,8,512]{2,1,0:T(8,128)S(1)}, u32[]{:S(2)}, u32[]{:S(2)}) %collective-permute-start.3) | collective-permute-done | bytes 32800 | tf_op jit(solution)/shard_map/ppermute | solution.py:28
  20.2 1.7 %collective-permute-done.1.refs_4_ = f32[2,128,512]{2,1,0:T(8,128)S(1)} collective-permute-done((f32[2,128,512]{2,1,0:T(8,128)S(1)}, f32[2,128,512]{2,1,0:T(8,128)S(1)}, u32[]{:S(2)}, u32[]{:S(2)}) %collective-permute-start.1) | collective-permute-done | bytes 524320 | tf_op jit(solution)/shard_map/ppermute | solution.py:28
  22.0 2.4 %collective-permute-start.4 = (f32[2,264,512]{2,1,0:T(8,128)S(1)}, f32[2,264,512]{2,1,0:T(8,128)S(1)}, u32[]{:S(2)}, u32[]{:S(2)}) collective-permute-start(f32[2,264,512]{2,1,0:T(8,128)S(1)} %shard_map.56.refs_0_), channel_id=1, source_target_pairs={{8,0},{16,8},{24,16},{32,24},{40,32},{48,40},{56,48},{64,56},{72,6... | collective-permute-start | bytes 3244040 | tf_op jit(solution)/shard_map/ppermute | solution.py:28
  24.5 3.4 %collective-permute-start = (f32[2,8,512]{2,1,0:T(8,128)S(1)}, f32[2,8,512]{2,1,0:T(8,128)S(1)}, u32[]{:S(2)}, u32[]{:S(2)}) collective-permute-start(f32[2,8,512]{2,1,0:T(8,128)S(1)} %broadcast_in_dim.2.refs_0_.refs_1_), channel_id=1, source_target_pairs={{0,1},{1,2},{2,3},{3,4},{4,5},{5,6},{6,7},{8,9},{9,10},{10,11},{11... | collective-permute-start | bytes 98312 | tf_op jit(solution)/shard_map/ppermute | solution.py:28
  27.9 2.0 %collective-permute-done.refs_2_.refs_1_.refs_4_ = f32[2,8,512]{2,1,0:T(8,128)S(1)} collective-permute-done((f32[2,8,512]{2,1,0:T(8,128)S(1)}, f32[2,8,512]{2,1,0:T(8,128)S(1)}, u32[]{:S(2)}, u32[]{:S(2)}) %collective-permute-start) | collective-permute-done | bytes 32800 | tf_op jit(solution)/shard_map/ppermute | solution.py:28
  29.9 1.2 collective-permute-done.5.refs_4_.refs_2_
  31.2 1.9 %collective-permute-start.7 = (f32[2,136,512]{2,1,0:T(8,128)S(1)}, f32[2,136,512]{2,1,0:T(8,128)S(1)}, u32[]{:S(2)}, u32[]{:S(2)}) collective-permute-start(f32[2,136,512]{2,1,0:T(8,128)S(1)} %get-tuple-element.35), channel_id=1, source_target_pairs={{1,0},{2,1},{3,2},{4,3},{5,4},{6,5},{7,6},{9,8},{10,9},{11,10},{12... | collective-permute-start | bytes 1671176 | tf_op jit(solution)/shard_map/ppermute | solution.py:28
  33.2 2.5 %collective-permute-start.6 = (f32[2,128,512]{2,1,0:T(8,128)S(1)}, f32[2,128,512]{2,1,0:T(8,128)S(1)}, u32[]{:S(2)}, u32[]{:S(2)}) collective-permute-start(f32[2,128,512]{2,1,0:T(8,128)S(1)} %get-tuple-element.34), channel_id=1, source_target_pairs={{1,0},{2,1},{3,2},{4,3},{5,4},{6,5},{7,6},{9,8},{10,9},{11,10},{12... | collective-permute-start | bytes 1572872 | tf_op jit(solution)/shard_map/ppermute | solution.py:28
  36.4 4.4 %multiply_convert_fusion = (bf16[512,512]{1,0:T(8,128)(2,1)S(1)}, bf16[512,512]{1,0:T(8,128)(2,1)S(1)}) fusion(), kind=kLoop, calls=%fused_computation.6 | loop fusion | flops 4718592 | bytes 1048576 | tf_op jit(solution)/shard_map/convert_element_type | solution.py:38
  40.8 5.4 %shard_map.55 = (bf16[1024,1024]{1,0:T(8,128)(2,1)S(1)}, bf16[1024,1024]{1,0:T(8,128)(2,1)S(1)}, bf16[1024,1024]{1,0:T(8,128)(2,1)S(1)}, bf16[1024,512]{1,0:T(8,...) custom-call(s32[1,2]{1,0:T(1,128)S(1)} %bitcast.6, ...), custom_call_target="tpu_custom_call" | custom-call | tf_op jit(solution)/shard_map/pallas_call | solution.py:54
  46.2 1.5 shard_map.58
  47.7 5.4 %collective-permute-done.4.refs_6_ = f32[2,264,512]{2,1,0:T(8,128)S(1)} collective-permute-done((f32[2,264,512]{2,1,0:T(8,128)S(1)}, f32[2,264,512]{2,1,0:T(8,128)S(1)}, u32[]{:S(2)}, u32[]{:S(2)}) %collective-permute-start.4) | collective-permute-done | bytes 1081376 | tf_op jit(solution)/shard_map/ppermute | solution.py:28
  53.2 3.4 %shard_map.59 = (f32[2,256,512]{2,1,0:T(8,128)S(1)}, f32[2,8,512]{2,1,0:T(8,128)S(1)}, bf16[1024,512]{1,0:T(8,128)(2,1)S(1)}, f32[2,264,512]{2,1,0:T(8,128)S(1)}) custom-call(s32[1,1]{1,0:T(1,128)S(6)} %copy.8.refs_0_, f32[2,8,512]{2,1,0:T(8,128)S(1)} %broadcast_in_dim.2.refs_0_.refs_1_, f32[2,128,512]{2,1,0:T(8,128)S(1)} %get-tuple-element.62.refs_2_, ...), custom_call_target="tpu_custom_call" | custom-call | tf_op jit(solution)/shard_map/pallas_call | solution.py:54
  56.6 6.5 %collective-permute-start.13 = (f32[2,264,512]{2,1,0:T(8,128)S(1)}, f32[2,264,512]{2,1,0:T(8,128)S(1)}, u32[]{:S(2)}, u32[]{:S(2)}) collective-permute-start(f32[2,264,512]{2,1,0:T(8,128)S(1)} %get-tuple-element.49.refs_6_.refs_4_.refs_15_), channel_id=1, source_target_pairs={{8,0},{16,8},{24,16},{32,24},{40,32},{48,40},{56,48},{64,56},{72,6... | collective-permute-start | bytes 3244040 | tf_op jit(solution)/shard_map/ppermute | solution.py:28
  63.1 1.9 %collective-permute-start.12 = (f32[2,264,512]{2,1,0:T(8,128)S(1)}, f32[2,264,512]{2,1,0:T(8,128)S(1)}, u32[]{:S(2)}, u32[]{:S(2)}) collective-permute-start(f32[2,264,512]{2,1,0:T(8,128)S(1)} %get-tuple-element.49.refs_6_.refs_4_.refs_15_), channel_id=1, source_target_pairs={{0,8},{8,16},{16,24},{24,32},{32,40},{40,48},{48,56},{56,64},{64,7... | collective-permute-start | bytes 3244040 | tf_op jit(solution)/shard_map/ppermute | solution.py:28
  65.8 2.1 %collective-permute-start.9 = (f32[2,256,512]{2,1,0:T(8,128)S(1)}, f32[2,256,512]{2,1,0:T(8,128)S(1)}, u32[]{:S(2)}, u32[]{:S(2)}) collective-permute-start(f32[2,256,512]{2,1,0:T(8,128)S(1)} %shard_map.60.refs_5_.refs_4_.refs_3_), channel_id=1, source_target_pairs={{1,0},{2,1},{3,2},{4,3},{5,4},{6,5},{7,6},{9,8},{10,9},{11,10},{12... | collective-permute-start | bytes 3145736 | tf_op jit(solution)/shard_map/ppermute | solution.py:28
  67.9 2.4 %collective-permute-start.8 = (f32[2,256,512]{2,1,0:T(8,128)S(1)}, f32[2,256,512]{2,1,0:T(8,128)S(1)}, u32[]{:S(2)}, u32[]{:S(2)}) collective-permute-start(f32[2,256,512]{2,1,0:T(8,128)S(1)} %shard_map.60.refs_5_.refs_4_.refs_3_), channel_id=1, source_target_pairs={{0,1},{1,2},{2,3},{3,4},{4,5},{5,6},{6,7},{8,9},{9,10},{10,11},{11... | collective-permute-start | bytes 3145736 | tf_op jit(solution)/shard_map/ppermute | solution.py:28
  70.3 9.7 %collective-permute-done.9.refs_7_.refs_6_ = f32[2,256,512]{2,1,0:T(8,128)S(1)} collective-permute-done((f32[2,256,512]{2,1,0:T(8,128)S(1)}, f32[2,256,512]{2,1,0:T(8,128)S(1)}, u32[]{:S(2)}, u32[]{:S(2)}) %collective-permute-start.9) | collective-permute-done | bytes 1048608 | tf_op jit(solution)/shard_map/ppermute | solution.py:28
  80.0 4.0 %collective-permute-done.8.refs_6_.refs_5_ = f32[2,256,512]{2,1,0:T(8,128)S(1)} collective-permute-done((f32[2,256,512]{2,1,0:T(8,128)S(1)}, f32[2,256,512]{2,1,0:T(8,128)S(1)}, u32[]{:S(2)}, u32[]{:S(2)}) %collective-permute-start.8) | collective-permute-done | bytes 1048608 | tf_op jit(solution)/shard_map/ppermute | solution.py:28
  84.0 1.2 shard_map.61
  85.2 1.9 %collective-permute-start.10 = (f32[2,264,512]{2,1,0:T(8,128)S(1)}, f32[2,264,512]{2,1,0:T(8,128)S(1)}, u32[]{:S(2)}, u32[]{:S(2)}) collective-permute-start(f32[2,264,512]{2,1,0:T(8,128)S(1)} %get-tuple-element.47), channel_id=1, source_target_pairs={{0,8},{8,16},{16,24},{24,32},{32,40},{40,48},{48,56},{56,64},{64,7... | collective-permute-start | bytes 3244040 | tf_op jit(solution)/shard_map/ppermute | solution.py:28
  87.2 6.0 %collective-permute-start.11 = (f32[2,264,512]{2,1,0:T(8,128)S(1)}, f32[2,264,512]{2,1,0:T(8,128)S(1)}, u32[]{:S(2)}, u32[]{:S(2)}) collective-permute-start(f32[2,264,512]{2,1,0:T(8,128)S(1)} %get-tuple-element.46.refs_0_), channel_id=1, source_target_pairs={{8,0},{16,8},{24,16},{32,24},{40,32},{48,40},{56,48},{64,56},{72,6... | collective-permute-start | bytes 3244040 | tf_op jit(solution)/shard_map/ppermute | solution.py:28
  93.2 1.5 shard_map.63
  94.8 1.9 %collective-permute-start.14 = (f32[2,256,512]{2,1,0:T(8,128)S(1)}, f32[2,256,512]{2,1,0:T(8,128)S(1)}, u32[]{:S(2)}, u32[]{:S(2)}) collective-permute-start(f32[2,256,512]{2,1,0:T(8,128)S(1)} %get-tuple-element.51), channel_id=1, source_target_pairs={{0,1},{1,2},{2,3},{3,4},{4,5},{5,6},{6,7},{8,9},{9,10},{10,11},{11... | collective-permute-start | bytes 3145736 | tf_op jit(solution)/shard_map/ppermute | solution.py:28
  96.7 3.6 %collective-permute-start.15 = (f32[2,256,512]{2,1,0:T(8,128)S(1)}, f32[2,256,512]{2,1,0:T(8,128)S(1)}, u32[]{:S(2)}, u32[]{:S(2)}) collective-permute-start(f32[2,256,512]{2,1,0:T(8,128)S(1)} %get-tuple-element.50.refs_0_), channel_id=1, source_target_pairs={{1,0},{2,1},{3,2},{4,3},{5,4},{6,5},{7,6},{9,8},{10,9},{11,10},{12... | collective-permute-start | bytes 3145736 | tf_op jit(solution)/shard_map/ppermute | solution.py:28
  101.4 9.4 %collective-permute-done.14.refs_5_ = f32[2,256,512]{2,1,0:T(8,128)S(1)} collective-permute-done((f32[2,256,512]{2,1,0:T(8,128)S(1)}, f32[2,256,512]{2,1,0:T(8,128)S(1)}, u32[]{:S(2)}, u32[]{:S(2)}) %collective-permute-start.14) | collective-permute-done | bytes 1048608 | tf_op jit(solution)/shard_map/ppermute | solution.py:28
  110.9 1.8 %collective-permute-done.15.refs_6_ = f32[2,256,512]{2,1,0:T(8,128)S(1)} collective-permute-done((f32[2,256,512]{2,1,0:T(8,128)S(1)}, f32[2,256,512]{2,1,0:T(8,128)S(1)}, u32[]{:S(2)}, u32[]{:S(2)}) %collective-permute-start.15) | collective-permute-done | bytes 1048608 | tf_op jit(solution)/shard_map/ppermute | solution.py:28
  112.6 1.5 shard_map.65.refs_8_
  115.3 3.5 %shard_map.66 = (bf16[1024,512]{1,0:T(8,128)(2,1)S(1)}, f32[2,256,512]{2,1,0:T(8,128)S(1)}) custom-call(s32[1,1]{1,0:T(1,128)S(6)} %copy.8.refs_0_, f32[2,8,512]{2,1,0:T(8,128)S(1)} %broadcast_in_dim.2.refs_0_.refs_1_, f32[2,8,512]{2,1,0:T(8,128)S(1)} %get-tuple-element.42.refs_4_.refs_3_.refs_1_.refs_2_, ...), custom_call_target="tpu_custom_call" | custom-call | tf_op jit(solution)/shard_map/pallas_call | solution.py:54
  118.8 1.9 %collective-permute-start.19 = (f32[2,256,512]{2,1,0:T(8,128)S(1)}, f32[2,256,512]{2,1,0:T(8,128)S(1)}, u32[]{:S(2)}, u32[]{:S(2)}) collective-permute-start(f32[2,256,512]{2,1,0:T(8,128)S(1)} %get-tuple-element.57.refs_4_), channel_id=1, source_target_pairs={{0,8},{8,16},{16,24},{24,32},{32,40},{40,48},{48,56},{56,64},{64,7... | collective-permute-start | bytes 3145736 | tf_op jit(solution)/shard_map/ppermute | solution.py:28
  121.5 3.0 %collective-permute-start.16 = (f32[2,128,512]{2,1,0:T(8,128)S(1)}, f32[2,128,512]{2,1,0:T(8,128)S(1)}, u32[]{:S(2)}, u32[]{:S(2)}) collective-permute-start(f32[2,128,512]{2,1,0:T(8,128)S(1)} %get-tuple-element.53.refs_4_), channel_id=1, source_target_pairs={{0,1},{1,2},{2,3},{3,4},{4,5},{5,6},{6,7},{8,9},{9,10},{10,11},{11... | collective-permute-start | bytes 1572872 | tf_op jit(solution)/shard_map/ppermute | solution.py:28
  124.5 1.9 %collective-permute-start.17 = (f32[2,128,512]{2,1,0:T(8,128)S(1)}, f32[2,128,512]{2,1,0:T(8,128)S(1)}, u32[]{:S(2)}, u32[]{:S(2)}) collective-permute-start(f32[2,128,512]{2,1,0:T(8,128)S(1)} %get-tuple-element.54.refs_5_), channel_id=1, source_target_pairs={{0,1},{1,2},{2,3},{3,4},{4,5},{5,6},{6,7},{8,9},{9,10},{10,11},{11... | collective-permute-start | bytes 1572872 | tf_op jit(solution)/shard_map/ppermute | solution.py:28
  126.4 5.6 %collective-permute-done.16.refs_6_ = f32[2,128,512]{2,1,0:T(8,128)S(1)} collective-permute-done((f32[2,128,512]{2,1,0:T(8,128)S(1)}, f32[2,128,512]{2,1,0:T(8,128)S(1)}, u32[]{:S(2)}, u32[]{:S(2)}) %collective-permute-start.16) | collective-permute-done | bytes 524320 | tf_op jit(solution)/shard_map/ppermute | solution.py:28
  132.0 5.6 %collective-permute-done.17.refs_7_ = f32[2,128,512]{2,1,0:T(8,128)S(1)} collective-permute-done((f32[2,128,512]{2,1,0:T(8,128)S(1)}, f32[2,128,512]{2,1,0:T(8,128)S(1)}, u32[]{:S(2)}, u32[]{:S(2)}) %collective-permute-start.17) | collective-permute-done | bytes 524320 | tf_op jit(solution)/shard_map/ppermute | solution.py:28
  138.3 1.9 %collective-permute-start.18 = (f32[2,256,512]{2,1,0:T(8,128)S(1)}, f32[2,256,512]{2,1,0:T(8,128)S(1)}, u32[]{:S(2)}, u32[]{:S(2)}) collective-permute-start(f32[2,256,512]{2,1,0:T(8,128)S(1)} %get-tuple-element.56.refs_0_), channel_id=1, source_target_pairs={{0,8},{8,16},{16,24},{24,32},{32,40},{40,48},{48,56},{56,64},{64,7... | collective-permute-start | bytes 3145736 | tf_op jit(solution)/shard_map/ppermute | solution.py:28
  140.2 9.0 %collective-permute-done.19.refs_5_ = f32[2,256,512]{2,1,0:T(8,128)S(1)} collective-permute-done((f32[2,256,512]{2,1,0:T(8,128)S(1)}, f32[2,256,512]{2,1,0:T(8,128)S(1)}, u32[]{:S(2)}, u32[]{:S(2)}) %collective-permute-start.19) | collective-permute-done | bytes 1048608 | tf_op jit(solution)/shard_map/ppermute | solution.py:28
  149.7 1.9 %collective-permute-start.20 = (f32[2,128,512]{2,1,0:T(8,128)S(1)}, f32[2,128,512]{2,1,0:T(8,128)S(1)}, u32[]{:S(2)}, u32[]{:S(2)}) collective-permute-start(f32[2,128,512]{2,1,0:T(8,128)S(1)} %get-tuple-element.59), channel_id=1, source_target_pairs={{0,1},{1,2},{2,3},{3,4},{4,5},{5,6},{6,7},{8,9},{9,10},{10,11},{11... | collective-permute-start | bytes 1572872 | tf_op jit(solution)/shard_map/ppermute | solution.py:28
  151.6 2.4 %collective-permute-start.21 = (f32[2,128,512]{2,1,0:T(8,128)S(1)}, f32[2,128,512]{2,1,0:T(8,128)S(1)}, u32[]{:S(2)}, u32[]{:S(2)}) collective-permute-start(f32[2,128,512]{2,1,0:T(8,128)S(1)} %get-tuple-element.60), channel_id=1, source_target_pairs={{0,1},{1,2},{2,3},{3,4},{4,5},{5,6},{6,7},{8,9},{9,10},{10,11},{11... | collective-permute-start | bytes 1572872 | tf_op jit(solution)/shard_map/ppermute | solution.py:28
  154.1 6.1 %collective-permute-done.20.refs_0_ = f32[2,128,512]{2,1,0:T(8,128)S(1)} collective-permute-done((f32[2,128,512]{2,1,0:T(8,128)S(1)}, f32[2,128,512]{2,1,0:T(8,128)S(1)}, u32[]{:S(2)}, u32[]{:S(2)}) %collective-permute-start.20) | collective-permute-done | bytes 524320 | tf_op jit(solution)/shard_map/ppermute | solution.py:28
  160.2 5.6 %collective-permute-done.21.refs_1_ = f32[2,128,512]{2,1,0:T(8,128)S(1)} collective-permute-done((f32[2,128,512]{2,1,0:T(8,128)S(1)}, f32[2,128,512]{2,1,0:T(8,128)S(1)}, u32[]{:S(2)}, u32[]{:S(2)}) %collective-permute-start.21) | collective-permute-done | bytes 524320 | tf_op jit(solution)/shard_map/ppermute | solution.py:28
  165.8 1.0 shard_map.70.refs_1_
  166.8 4.5 %collective-permute-done.18.refs_0_ = f32[2,256,512]{2,1,0:T(8,128)S(1)} collective-permute-done((f32[2,256,512]{2,1,0:T(8,128)S(1)}, f32[2,256,512]{2,1,0:T(8,128)S(1)}, u32[]{:S(2)}, u32[]{:S(2)}) %collective-permute-start.18) | collective-permute-done | bytes 1048608 | tf_op jit(solution)/shard_map/ppermute | solution.py:28
  171.4 1.1 shard_map.71
  (26 shorter events, 5.3 us)
Async XLA Ops:
  0.0 7.6 %copy-start.3 = (f32[2,512,512]{2,1,0:T(8,128)S(1)}, f32[2,512,512]{2,1,0:T(8,128)}, u32[]{:S(2)}) copy-start(f32[2,512,512]{2,1,0:T(8,128)} %param.5) | copy-start | bytes 6291460
  0.0 12.2 %copy-start.2 = (s32[1,1,1,2]{3,2,1,0:T(1,128)S(1)}, s32[1,1,1,2]{3,2,1,0:T(1,128)}, u32[]{:S(2)}) copy-start(s32[1,1,1,2]{3,2,1,0:T(1,128)} %param.8) | copy-start | bytes 28
  1.4 29.7 %collective-permute-start.5 = (f32[2,256,512]{2,1,0:T(8,128)S(1)}, f32[2,256,512]{2,1,0:T(8,128)S(1)}, u32[]{:S(2)}, u32[]{:S(2)}) collective-permute-start(f32[2,256,512]{2,1,0:T(8,128)S(1)} %slice.11.refs_3_.refs_1_), channel_id=1, source_target_pairs={{8,0},{16,8},{24,16},{32,24},{40,32},{48,40},{56,48},{64,56},{72,6... | collective-permute-start | bytes 3145736 | tf_op jit(solution)/shard_map/ppermute | solution.py:28
  7.7 12.5 %collective-permute-start.2 = (f32[2,128,512]{2,1,0:T(8,128)S(1)}, f32[2,128,512]{2,1,0:T(8,128)S(1)}, u32[]{:S(2)}, u32[]{:S(2)}) collective-permute-start(f32[2,128,512]{2,1,0:T(8,128)S(1)} %get-tuple-element.61.refs_3_), channel_id=1, source_target_pairs={{1,0},{2,1},{3,2},{4,3},{5,4},{6,5},{7,6},{9,8},{10,9},{11,10},{12... | collective-permute-start | bytes 1572872 | tf_op jit(solution)/shard_map/ppermute | solution.py:28
  9.6 12.3 %collective-permute-start.1 = (f32[2,128,512]{2,1,0:T(8,128)S(1)}, f32[2,128,512]{2,1,0:T(8,128)S(1)}, u32[]{:S(2)}, u32[]{:S(2)}) collective-permute-start(f32[2,128,512]{2,1,0:T(8,128)S(1)} %get-tuple-element.62.refs_2_), channel_id=1, source_target_pairs={{1,0},{2,1},{3,2},{4,3},{5,4},{6,5},{7,6},{9,8},{10,9},{11,10},{12... | collective-permute-start | bytes 1572872 | tf_op jit(solution)/shard_map/ppermute | solution.py:28
  12.2 7.9 %collective-permute-start.3 = (f32[2,8,512]{2,1,0:T(8,128)S(1)}, f32[2,8,512]{2,1,0:T(8,128)S(1)}, u32[]{:S(2)}, u32[]{:S(2)}) collective-permute-start(f32[2,8,512]{2,1,0:T(8,128)S(1)} %broadcast_in_dim.2.refs_0_.refs_1_), channel_id=1, source_target_pairs={{0,8},{8,16},{16,24},{24,32},{32,40},{40,48},{48,56},{56,64},{64,7... | collective-permute-start | bytes 98312 | tf_op jit(solution)/shard_map/ppermute | solution.py:28
  22.0 18.8 %copy-start.1 = (f32[2,512,512]{2,1,0:T(8,128)S(1)}, f32[2,512,512]{2,1,0:T(8,128)}, u32[]{:S(2)}) copy-start(f32[2,512,512]{2,1,0:T(8,128)} %refs_3_.1) | copy-start | bytes 6291460
  22.0 31.1 %collective-permute-start.4 = (f32[2,264,512]{2,1,0:T(8,128)S(1)}, f32[2,264,512]{2,1,0:T(8,128)S(1)}, u32[]{:S(2)}, u32[]{:S(2)}) collective-permute-start(f32[2,264,512]{2,1,0:T(8,128)S(1)} %shard_map.56.refs_0_), channel_id=1, source_target_pairs={{8,0},{16,8},{24,16},{32,24},{40,32},{48,40},{56,48},{64,56},{72,6... | collective-permute-start | bytes 3244040 | tf_op jit(solution)/shard_map/ppermute | solution.py:28
  24.5 5.4 %collective-permute-start = (f32[2,8,512]{2,1,0:T(8,128)S(1)}, f32[2,8,512]{2,1,0:T(8,128)S(1)}, u32[]{:S(2)}, u32[]{:S(2)}) collective-permute-start(f32[2,8,512]{2,1,0:T(8,128)S(1)} %broadcast_in_dim.2.refs_0_.refs_1_), channel_id=1, source_target_pairs={{0,1},{1,2},{2,3},{3,4},{4,5},{5,6},{6,7},{8,9},{9,10},{10,11},{11... | collective-permute-start | bytes 98312 | tf_op jit(solution)/shard_map/ppermute | solution.py:28
  31.2 14.9 %collective-permute-start.7 = (f32[2,136,512]{2,1,0:T(8,128)S(1)}, f32[2,136,512]{2,1,0:T(8,128)S(1)}, u32[]{:S(2)}, u32[]{:S(2)}) collective-permute-start(f32[2,136,512]{2,1,0:T(8,128)S(1)} %get-tuple-element.35), channel_id=1, source_target_pairs={{1,0},{2,1},{3,2},{4,3},{5,4},{6,5},{7,6},{9,8},{10,9},{11,10},{12... | collective-permute-start | bytes 1671176 | tf_op jit(solution)/shard_map/ppermute | solution.py:28
  33.2 13.0 %collective-permute-start.6 = (f32[2,128,512]{2,1,0:T(8,128)S(1)}, f32[2,128,512]{2,1,0:T(8,128)S(1)}, u32[]{:S(2)}, u32[]{:S(2)}) collective-permute-start(f32[2,128,512]{2,1,0:T(8,128)S(1)} %get-tuple-element.34), channel_id=1, source_target_pairs={{1,0},{2,1},{3,2},{4,3},{5,4},{6,5},{7,6},{9,8},{10,9},{11,10},{12... | collective-permute-start | bytes 1572872 | tf_op jit(solution)/shard_map/ppermute | solution.py:28
  46.2 7.0 %copy-start = (f32[1,1,1,512,512]{4,3,2,1,0:T(8,128)S(1)}, f32[1,1,1,512,512]{4,3,2,1,0:T(8,128)}, u32[]{:S(2)}) copy-start(f32[1,1,1,512,512]{4,3,2,1,0:T(8,128)} %param.7) | copy-start | bytes 3145732
  56.6 36.6 %collective-permute-start.13 = (f32[2,264,512]{2,1,0:T(8,128)S(1)}, f32[2,264,512]{2,1,0:T(8,128)S(1)}, u32[]{:S(2)}, u32[]{:S(2)}) collective-permute-start(f32[2,264,512]{2,1,0:T(8,128)S(1)} %get-tuple-element.49.refs_6_.refs_4_.refs_15_), channel_id=1, source_target_pairs={{8,0},{16,8},{24,16},{32,24},{40,32},{48,40},{56,48},{64,56},{72,6... | collective-permute-start | bytes 3244040 | tf_op jit(solution)/shard_map/ppermute | solution.py:28
  63.1 30.1 %collective-permute-start.12 = (f32[2,264,512]{2,1,0:T(8,128)S(1)}, f32[2,264,512]{2,1,0:T(8,128)S(1)}, u32[]{:S(2)}, u32[]{:S(2)}) collective-permute-start(f32[2,264,512]{2,1,0:T(8,128)S(1)} %get-tuple-element.49.refs_6_.refs_4_.refs_15_), channel_id=1, source_target_pairs={{0,8},{8,16},{16,24},{24,32},{32,40},{40,48},{48,56},{56,64},{64,7... | collective-permute-start | bytes 3244040 | tf_op jit(solution)/shard_map/ppermute | solution.py:28
  65.8 14.2 %collective-permute-start.9 = (f32[2,256,512]{2,1,0:T(8,128)S(1)}, f32[2,256,512]{2,1,0:T(8,128)S(1)}, u32[]{:S(2)}, u32[]{:S(2)}) collective-permute-start(f32[2,256,512]{2,1,0:T(8,128)S(1)} %shard_map.60.refs_5_.refs_4_.refs_3_), channel_id=1, source_target_pairs={{1,0},{2,1},{3,2},{4,3},{5,4},{6,5},{7,6},{9,8},{10,9},{11,10},{12... | collective-permute-start | bytes 3145736 | tf_op jit(solution)/shard_map/ppermute | solution.py:28
  67.9 16.1 %collective-permute-start.8 = (f32[2,256,512]{2,1,0:T(8,128)S(1)}, f32[2,256,512]{2,1,0:T(8,128)S(1)}, u32[]{:S(2)}, u32[]{:S(2)}) collective-permute-start(f32[2,256,512]{2,1,0:T(8,128)S(1)} %shard_map.60.refs_5_.refs_4_.refs_3_), channel_id=1, source_target_pairs={{0,1},{1,2},{2,3},{3,4},{4,5},{5,6},{6,7},{8,9},{9,10},{10,11},{11... | collective-permute-start | bytes 3145736 | tf_op jit(solution)/shard_map/ppermute | solution.py:28
  85.2 29.5 %collective-permute-start.10 = (f32[2,264,512]{2,1,0:T(8,128)S(1)}, f32[2,264,512]{2,1,0:T(8,128)S(1)}, u32[]{:S(2)}, u32[]{:S(2)}) collective-permute-start(f32[2,264,512]{2,1,0:T(8,128)S(1)} %get-tuple-element.47), channel_id=1, source_target_pairs={{0,8},{8,16},{16,24},{24,32},{32,40},{40,48},{48,56},{56,64},{64,7... | collective-permute-start | bytes 3244040 | tf_op jit(solution)/shard_map/ppermute | solution.py:28
  87.2 28.1 %collective-permute-start.11 = (f32[2,264,512]{2,1,0:T(8,128)S(1)}, f32[2,264,512]{2,1,0:T(8,128)S(1)}, u32[]{:S(2)}, u32[]{:S(2)}) collective-permute-start(f32[2,264,512]{2,1,0:T(8,128)S(1)} %get-tuple-element.46.refs_0_), channel_id=1, source_target_pairs={{8,0},{16,8},{24,16},{32,24},{40,32},{48,40},{56,48},{64,56},{72,6... | collective-permute-start | bytes 3244040 | tf_op jit(solution)/shard_map/ppermute | solution.py:28
  94.8 16.1 %collective-permute-start.14 = (f32[2,256,512]{2,1,0:T(8,128)S(1)}, f32[2,256,512]{2,1,0:T(8,128)S(1)}, u32[]{:S(2)}, u32[]{:S(2)}) collective-permute-start(f32[2,256,512]{2,1,0:T(8,128)S(1)} %get-tuple-element.51), channel_id=1, source_target_pairs={{0,1},{1,2},{2,3},{3,4},{4,5},{5,6},{6,7},{8,9},{9,10},{10,11},{11... | collective-permute-start | bytes 3145736 | tf_op jit(solution)/shard_map/ppermute | solution.py:28
  96.7 15.9 %collective-permute-start.15 = (f32[2,256,512]{2,1,0:T(8,128)S(1)}, f32[2,256,512]{2,1,0:T(8,128)S(1)}, u32[]{:S(2)}, u32[]{:S(2)}) collective-permute-start(f32[2,256,512]{2,1,0:T(8,128)S(1)} %get-tuple-element.50.refs_0_), channel_id=1, source_target_pairs={{1,0},{2,1},{3,2},{4,3},{5,4},{6,5},{7,6},{9,8},{10,9},{11,10},{12... | collective-permute-start | bytes 3145736 | tf_op jit(solution)/shard_map/ppermute | solution.py:28
  118.8 30.4 %collective-permute-start.19 = (f32[2,256,512]{2,1,0:T(8,128)S(1)}, f32[2,256,512]{2,1,0:T(8,128)S(1)}, u32[]{:S(2)}, u32[]{:S(2)}) collective-permute-start(f32[2,256,512]{2,1,0:T(8,128)S(1)} %get-tuple-element.57.refs_4_), channel_id=1, source_target_pairs={{0,8},{8,16},{16,24},{24,32},{32,40},{40,48},{48,56},{56,64},{64,7... | collective-permute-start | bytes 3145736 | tf_op jit(solution)/shard_map/ppermute | solution.py:28
  121.5 10.5 %collective-permute-start.16 = (f32[2,128,512]{2,1,0:T(8,128)S(1)}, f32[2,128,512]{2,1,0:T(8,128)S(1)}, u32[]{:S(2)}, u32[]{:S(2)}) collective-permute-start(f32[2,128,512]{2,1,0:T(8,128)S(1)} %get-tuple-element.53.refs_4_), channel_id=1, source_target_pairs={{0,1},{1,2},{2,3},{3,4},{4,5},{5,6},{6,7},{8,9},{9,10},{10,11},{11... | collective-permute-start | bytes 1572872 | tf_op jit(solution)/shard_map/ppermute | solution.py:28
  124.5 13.1 %collective-permute-start.17 = (f32[2,128,512]{2,1,0:T(8,128)S(1)}, f32[2,128,512]{2,1,0:T(8,128)S(1)}, u32[]{:S(2)}, u32[]{:S(2)}) collective-permute-start(f32[2,128,512]{2,1,0:T(8,128)S(1)} %get-tuple-element.54.refs_5_), channel_id=1, source_target_pairs={{0,1},{1,2},{2,3},{3,4},{4,5},{5,6},{6,7},{8,9},{9,10},{10,11},{11... | collective-permute-start | bytes 1572872 | tf_op jit(solution)/shard_map/ppermute | solution.py:28
  138.3 33.1 %collective-permute-start.18 = (f32[2,256,512]{2,1,0:T(8,128)S(1)}, f32[2,256,512]{2,1,0:T(8,128)S(1)}, u32[]{:S(2)}, u32[]{:S(2)}) collective-permute-start(f32[2,256,512]{2,1,0:T(8,128)S(1)} %get-tuple-element.56.refs_0_), channel_id=1, source_target_pairs={{0,8},{8,16},{16,24},{24,32},{32,40},{40,48},{48,56},{56,64},{64,7... | collective-permute-start | bytes 3145736 | tf_op jit(solution)/shard_map/ppermute | solution.py:28
  149.7 10.5 %collective-permute-start.20 = (f32[2,128,512]{2,1,0:T(8,128)S(1)}, f32[2,128,512]{2,1,0:T(8,128)S(1)}, u32[]{:S(2)}, u32[]{:S(2)}) collective-permute-start(f32[2,128,512]{2,1,0:T(8,128)S(1)} %get-tuple-element.59), channel_id=1, source_target_pairs={{0,1},{1,2},{2,3},{3,4},{4,5},{5,6},{6,7},{8,9},{9,10},{10,11},{11... | collective-permute-start | bytes 1572872 | tf_op jit(solution)/shard_map/ppermute | solution.py:28
  151.6 14.2 %collective-permute-start.21 = (f32[2,128,512]{2,1,0:T(8,128)S(1)}, f32[2,128,512]{2,1,0:T(8,128)S(1)}, u32[]{:S(2)}, u32[]{:S(2)}) collective-permute-start(f32[2,128,512]{2,1,0:T(8,128)S(1)} %get-tuple-element.60), channel_id=1, source_target_pairs={{0,1},{1,2},{2,3},{3,4},{4,5},{5,6},{6,7},{8,9},{9,10},{10,11},{11... | collective-permute-start | bytes 1572872 | tf_op jit(solution)/shard_map/ppermute | solution.py:28

commit v6 on v5

--- a/solution.py
+++ b/solution.py
@@ -19,6 +19,7 @@
 
 EXTRA = 8
 BLOCK = 128
+ODD = 1024
 PAD = 8
 
 
@@ -26,6 +27,11 @@
     count = lax.axis_size(axis)
     leading, last = (max(0, -steps), min(count, count - steps))
     return lax.ppermute(value, axis, [(source, source + steps) for source in range(leading, last)])
+
+
+def swapped(value, axis, odd):
+    lower = range(1 if odd else 0, lax.axis_size(axis) - 1, 2)
+    return lax.ppermute(value, axis, [(a, a + 1) for a in lower] + [(a + 1, a) for a in lower])
 
 
 def dft_tables(width):
@@ -93,7 +99,7 @@
 
 
 def low(i, place):
-    return i + 1 < place[0, :1, :].astype(jnp.int32)
+    return i + 1 < (place[0, :1, :].astype(jnp.int32) & (ODD - 1))
 
 
 def far(j, place):
@@ -104,6 +110,10 @@
     i, j = indices(rows, width, first)
     pair = (functools.partial(low, i), functools.partial(far, j))
     return pair if head else pair[::-1]
+
+
+def odd_row(place):
+    return place[0, :1, :] >= ODD
 
 
 def absent(place):
@@ -205,6 +215,7 @@
 
 
 def updated(head, place, edge_row, edge_col, kept, own, minus, plus):
+    odd = odd_row(place)
     w = kept.shape[2]
 
     def window(row, rows):
@@ -214,7 +225,10 @@
         second = b if head else a
         values = []
         for plane in range(2):
-            near = jnp.where(second, part(plus, plane, rows, w), part(minus, plane, rows, w))
+            low_side, high_side = part(minus, plane, rows, w), part(plus, plane, rows, w)
+            if not head:
+                low_side, high_side = pick(odd, low_side, high_side), pick(odd, high_side, low_side)
+            near = jnp.where(second, high_side, low_side)
             value = kept[plane, rows, :] - STEP * (own[plane, rows, :] + near)
             values.append(jnp.where(outside, 0.0, value))
         return values
@@ -274,10 +288,15 @@
     end[:, end.shape[1] - EXTRA :, :] = me[...]
 
 
+def pick(odd, when_odd, when_even):
+    return jnp.where(odd, when_odd, when_even)
+
+
 def between_kernel(
     first, head, me, minus, plus, target_minus, target_plus, mine, got_minus, got_plus, to_minus, to_plus
 ):
     w = me.shape[2]
+    odd = odd_row(me)
     for row, rows in split(first, w):
         ways = ways_of(head, rows, w, row)
         f, f_minus, f_plus = (ways[0](x) for x in (me, minus, plus))
@@ -290,13 +309,21 @@
         plus_m = [a & b for a, b in zip(seen(ways[0](target_plus)), (s, s_minus, s_plus))]
         for plane in range(2):
             values = [part(x, plane, rows, w) for x in (mine, got_minus, got_plus)]
-            for out, masks in ((to_minus, minus_m), (to_plus, plus_m)):
+            if head:
+                values[1:] = pick(odd, values[1], values[2]), pick(odd, values[2], values[1])
+            sums = []
+            for masks in (minus_m, plus_m):
                 terms = [jnp.where(m, v, 0.0) for m, v in zip(masks, values)]
-                put(out, plane, rows, terms[0] + terms[1] + terms[2])
+                sums.append(terms[0] + terms[1] + terms[2])
+            if not head:
+                sums = pick(odd, sums[0], sums[1]), pick(odd, sums[1], sums[0])
+            put(to_minus, plane, rows, sums[0])
+            put(to_plus, plane, rows, sums[1])
 
 
 def own_kernel(first, head, me, minus, plus, mine, got_minus, got_plus, own):
     w = me.shape[2]
+    odd = odd_row(me)
     for row, rows in split(first, w):
         ways = ways_of(head, rows, w, row)
         f, f_minus, f_plus = (ways[0](x) for x in (me, minus, plus))
@@ -304,6 +331,8 @@
         own_minus, own_plus = ~f & f_minus & (s == s_minus), f & ~f_plus & (s == s_plus)
         for plane in range(2):
             values = [part(x, plane, rows, w) for x in (mine, got_minus, got_plus)]
+            if head:
+                values[1:] = pick(odd, values[1], values[2]), pick(odd, values[2], values[1])
             others = jnp.where(own_minus, values[1], 0.0) + jnp.where(own_plus, values[2], 0.0)
             put(own, plane, rows, values[0] + others)
 
@@ -366,7 +395,9 @@
 
     half, whole, spot = block(h), block(w), block(EXTRA)
     pieces = [block(h // 2)] * 2
-    me = jnp.broadcast_to((offset[0] + 1).astype(F32)[:, None, None], (2, EXTRA, w))
+    odd = lax.axis_index("row") % 2 * ODD
+    spots = offset[0] + 1 + jnp.stack([odd, jnp.zeros_like(odd)])
+    me = jnp.broadcast_to(spots.astype(F32)[:, None, None], (2, EXTRA, w))
     head = spectrum[:, :h]
     tail = [spectrum[:, h : h + h // 2], spectrum[:, h + h // 2 :]]
 
@@ -414,10 +445,10 @@
         scalars=(counts,),
     )
 
-    got_above, got_under = shifted(head_grad, "row", 1), shifted(head_grad, "row", -1)
+    got_pairs = [swapped(head_grad, "row", False), swapped(head_grad, "row", True)]
     (tail_grad,) = call(functools.partial(rest_first, h), [[half]], (by, stacked, rolled))
     got_left, got_right = each(tail_grad, "col", 1), each(tail_grad, "col", -1)
-    to_up, to_down = call(
+    to_even, to_odd = call(
         functools.partial(between_kernel, h, False),
         [block(h + PAD), block(h + PAD)],
         (me, left_of, right_of, above, under, tail_grad, got_left, got_right),
@@ -426,19 +457,19 @@
         functools.partial(own_kernel, h, False),
         [half],
         (me, left_of, right_of, tail_grad, got_left, got_right),
-        after=(to_up,),
-    )
-    tail_sums = (tail_own, shifted(to_down, "row", 1), shifted(to_up, "row", -1))
+        after=(to_even,),
+    )
+    tail_sums = (tail_own, swapped(to_even, "row", False), swapped(to_odd, "row", True))
     to_left, to_right = call(
         functools.partial(between_kernel, 0, True),
         [[half], [half]],
-        (me, above, under, left_of, right_of, head_grad, got_above, got_under),
-        after=(to_up,),
+        (me, above, under, left_of, right_of, head_grad, *got_pairs),
+        after=(to_even,),
     )
     (head_own,) = call(
         functools.partial(own_kernel, 0, True),
         [half],
-        (me, above, under, head_grad, got_above, got_under),
+        (me, above, under, head_grad, *got_pairs),
         after=(to_left[0],),
     )
     head_sums = (head_own, each(to_right, "col", 1), each(to_left, "col", -1))

time: 173 us -> 171 us (0.988)
  starting transfers between devices: 62.3 us -> 57.8 us
  Pallas kernels: 24.2 us -> 26.7 us
    ppermute x22 -> x18, starting transfers between devices: 62.3 us -> 47.2 us  [shifted(): lax.ppermute(value, axis, [(source, source + steps) for source in range(l...]
    ppermute x0 -> x4, starting transfers between devices: none -> 10.6 us  [swapped(): lax.ppermute(value, axis, [(a, a + 1) for a in lower] + [(a + 1, a) for a...]
    ppermute x22 -> x18, waiting for transfers between devices: 78.9 us -> 74.9 us  [shifted(): lax.ppermute(value, axis, [(source, source + steps) for source in range(l...]
    ppermute x0 -> x4, waiting for transfers between devices: none -> 3.58 us  [swapped(): lax.ppermute(value, axis, [(a, a + 1) for a in lower] + [(a + 1, a) for a...]
    pallas_call x15, Pallas kernels: 22.1 us -> 24.5 us  [call(): pl.pallas_call(body, out_shape=out_flat, in_specs=[ANY] * skip + [SMEM] *...]
  transfers between devices with their start and end apart: 22 -> 22, of which waited for: 17 -> 16; matrix products, arithmetic and copies ran while one was open for 3% -> 3% of each run, Pallas kernels for 9% -> 10%
where the time goes in v6:
time: 171 us; the launch traced here: 170 us
  waiting for transfers between devices  78.5 us (46%)
  starting transfers between devices  57.8 us (34%)
  Pallas kernels  26.7 us (16%)
  other arithmetic  4.47 us (3%)
    ppermute x18, waiting for transfers between devices, shifted(): lax.ppermute(value, axis, [(source, source + steps) for source in range(l...  74.9 us
    ppermute x18, starting transfers between devices, shifted(): lax.ppermute(value, axis, [(source, source + steps) for source in range(l...  47.2 us
    pallas_call x15, Pallas kernels, call(): pl.pallas_call(body, out_shape=out_flat, in_specs=[ANY] * skip + [SMEM] *...  24.5 us
    ppermute x4, starting transfers between devices, swapped(): lax.ppermute(value, axis, [(a, a + 1) for a in lower] + [(a + 1, a) for a...  10.6 us
    convert_element_type x1, other arithmetic, dft_tables(): (jnp.sin(angle) * scale).astype(jnp.bfloat16)  4.39 us
    ppermute x4, waiting for transfers between devices, swapped(): lax.ppermute(value, axis, [(a, a + 1) for a in lower] + [(a + 1, a) for a...  3.58 us
  transfers between devices with their start and end apart: 22, of which 16 were waited for; matrix products, arithmetic and copies ran while one was open for 3% of the time, Pallas kernels for 10%

profile of v6, /device:TPU:28, one launch (start us, length us, event | category | flops | bytes accessed | tf_op | source)
XLA Modules:
  0.0 170.2 jit_solution(10896651719645332067)
XLA Ops:
  0.0 1.4 slice.11.refs_3_.refs_1_
  1.4 6.1 %collective-permute-start.5 = (f32[2,256,512]{2,1,0:T(8,128)S(1)}, f32[2,256,512]{2,1,0:T(8,128)S(1)}, u32[]{:S(2)}, u32[]{:S(2)}) collective-permute-start(f32[2,256,512]{2,1,0:T(8,128)S(1)} %slice.11.refs_3_.refs_1_), channel_id=1, source_target_pairs={{8,0},{16,8},{24,16},{32,24},{40,32},{48,40},{56,48},{64,56},{72,6... | collective-permute-start | bytes 3145736 | tf_op jit(solution)/shard_map/ppermute | solution.py:29
  7.7 1.9 %collective-permute-start.2 = (f32[2,128,512]{2,1,0:T(8,128)S(1)}, f32[2,128,512]{2,1,0:T(8,128)}, u32[]{:S(2)}, u32[]{:S(2)}) collective-permute-start(f32[2,128,512]{2,1,0:T(8,128)S(1)} %get-tuple-element.61.refs_3_), channel_id=1, source_target_pairs={{1,0},{2,1},{3,2},{4,3},{5,4},{6,5},{7,6},{9,8},{10,9},{11,10},{12... | collective-permute-start | bytes 1572872 | tf_op jit(solution)/shard_map/ppermute | solution.py:29
  9.6 2.5 %collective-permute-start.1 = (f32[2,128,512]{2,1,0:T(8,128)S(1)}, f32[2,128,512]{2,1,0:T(8,128)}, u32[]{:S(2)}, u32[]{:S(2)}) collective-permute-start(f32[2,128,512]{2,1,0:T(8,128)S(1)} %get-tuple-element.62.refs_2_), channel_id=1, source_target_pairs={{1,0},{2,1},{3,2},{4,3},{5,4},{6,5},{7,6},{9,8},{10,9},{11,10},{12... | collective-permute-start | bytes 1572872 | tf_op jit(solution)/shard_map/ppermute | solution.py:29
  12.3 1.9 %collective-permute-start.3 = (f32[2,8,512]{2,1,0:T(8,128)S(1)}, f32[2,8,512]{2,1,0:T(8,128)S(1)}, u32[]{:S(2)}, u32[]{:S(2)}) collective-permute-start(f32[2,8,512]{2,1,0:T(8,128)S(1)} %broadcast_in_dim.2.refs_0_.refs_1_), channel_id=1, source_target_pairs={{0,8},{8,16},{16,24},{24,32},{32,40},{40,48},{48,56},{56,64},{64,7... | collective-permute-start | bytes 98312 | tf_op jit(solution)/shard_map/ppermute | solution.py:29
  14.2 6.0 %collective-permute-done.3.refs_1_.refs_3_.refs_2_ = f32[2,8,512]{2,1,0:T(8,128)S(1)} collective-permute-done((f32[2,8,512]{2,1,0:T(8,128)S(1)}, f32[2,8,512]{2,1,0:T(8,128)S(1)}, u32[]{:S(2)}, u32[]{:S(2)}) %collective-permute-start.3) | collective-permute-done | bytes 32800 | tf_op jit(solution)/shard_map/ppermute | solution.py:29
  20.2 1.7 collective-permute-done.1.refs_4_
  21.9 1.3 shard_map.56.refs_0_
  23.2 2.4 %collective-permute-start.4 = (f32[2,264,512]{2,1,0:T(8,128)S(1)}, f32[2,264,512]{2,1,0:T(8,128)S(1)}, u32[]{:S(2)}, u32[]{:S(2)}) collective-permute-start(f32[2,264,512]{2,1,0:T(8,128)S(1)} %shard_map.56.refs_0_), channel_id=1, source_target_pairs={{8,0},{16,8},{24,16},{32,24},{40,32},{48,40},{56,48},{64,56},{72,6... | collective-permute-start | bytes 3244040 | tf_op jit(solution)/shard_map/ppermute | solution.py:29
  25.7 3.4 %collective-permute-start = (f32[2,8,512]{2,1,0:T(8,128)S(1)}, f32[2,8,512]{2,1,0:T(8,128)S(1)}, u32[]{:S(2)}, u32[]{:S(2)}) collective-permute-start(f32[2,8,512]{2,1,0:T(8,128)S(1)} %broadcast_in_dim.2.refs_0_.refs_1_), channel_id=1, source_target_pairs={{0,1},{1,2},{2,3},{3,4},{4,5},{5,6},{6,7},{8,9},{9,10},{10,11},{11... | collective-permute-start | bytes 98312 | tf_op jit(solution)/shard_map/ppermute | solution.py:29
  29.1 2.0 %collective-permute-done.refs_2_.refs_1_.refs_4_ = f32[2,8,512]{2,1,0:T(8,128)S(1)} collective-permute-done((f32[2,8,512]{2,1,0:T(8,128)S(1)}, f32[2,8,512]{2,1,0:T(8,128)S(1)}, u32[]{:S(2)}, u32[]{:S(2)}) %collective-permute-start) | collective-permute-done | bytes 32800 | tf_op jit(solution)/shard_map/ppermute | solution.py:29
  31.2 1.9 %collective-permute-start.7 = (f32[2,136,512]{2,1,0:T(8,128)S(1)}, f32[2,136,512]{2,1,0:T(8,128)S(1)}, u32[]{:S(2)}, u32[]{:S(2)}) collective-permute-start(f32[2,136,512]{2,1,0:T(8,128)S(1)} %get-tuple-element.35), channel_id=1, source_target_pairs={{1,0},{2,1},{3,2},{4,3},{5,4},{6,5},{7,6},{9,8},{10,9},{11,10},{12... | collective-permute-start | bytes 1671176 | tf_op jit(solution)/shard_map/ppermute | solution.py:29
  33.2 2.5 %collective-permute-start.6 = (f32[2,128,512]{2,1,0:T(8,128)S(1)}, f32[2,128,512]{2,1,0:T(8,128)S(1)}, u32[]{:S(2)}, u32[]{:S(2)}) collective-permute-start(f32[2,128,512]{2,1,0:T(8,128)S(1)} %get-tuple-element.34), channel_id=1, source_target_pairs={{1,0},{2,1},{3,2},{4,3},{5,4},{6,5},{7,6},{9,8},{10,9},{11,10},{12... | collective-permute-start | bytes 1572872 | tf_op jit(solution)/shard_map/ppermute | solution.py:29
  36.4 4.4 %multiply_convert_fusion = (bf16[512,512]{1,0:T(8,128)(2,1)S(1)}, bf16[512,512]{1,0:T(8,128)(2,1)S(1)}) fusion(), kind=kLoop, calls=%fused_computation.6 | loop fusion | flops 4718592 | bytes 1048576 | tf_op jit(solution)/shard_map/convert_element_type | solution.py:44
  40.8 5.4 %shard_map.55 = (bf16[1024,1024]{1,0:T(8,128)(2,1)S(1)}, bf16[1024,1024]{1,0:T(8,128)(2,1)S(1)}, bf16[1024,1024]{1,0:T(8,128)(2,1)S(1)}, bf16[1024,512]{1,0:T(8,...) custom-call(s32[1,2]{1,0:T(1,128)S(1)} %bitcast.7, ...), custom_call_target="tpu_custom_call" | custom-call | tf_op jit(solution)/shard_map/pallas_call | solution.py:60
  46.2 1.5 shard_map.58
  47.7 5.4 %collective-permute-done.4.refs_6_ = f32[2,264,512]{2,1,0:T(8,128)S(1)} collective-permute-done((f32[2,264,512]{2,1,0:T(8,128)S(1)}, f32[2,264,512]{2,1,0:T(8,128)S(1)}, u32[]{:S(2)}, u32[]{:S(2)}) %collective-permute-start.4) | collective-permute-done | bytes 1081376 | tf_op jit(solution)/shard_map/ppermute | solution.py:29
  53.2 4.6 %shard_map.59 = (f32[2,256,512]{2,1,0:T(8,128)S(1)}, f32[2,8,512]{2,1,0:T(8,128)S(1)}, bf16[1024,512]{1,0:T(8,128)(2,1)S(1)}, f32[2,264,512]{2,1,0:T(8,128)S(1)}) custom-call(s32[1,1]{1,0:T(1,128)S(6)} %copy.8.refs_0_, f32[2,8,512]{2,1,0:T(8,128)S(1)} %broadcast_in_dim.2.refs_0_.refs_1_, f32[2,128,512]{2,1,0:T(8,128)S(1)} %get-tuple-element.62.refs_2_, ...), custom_call_target="tpu_custom_call" | custom-call | tf_op jit(solution)/shard_map/pallas_call | solution.py:60
  57.8 6.5 %collective-permute-start.13 = (f32[2,264,512]{2,1,0:T(8,128)S(1)}, f32[2,264,512]{2,1,0:T(8,128)S(1)}, u32[]{:S(2)}, u32[]{:S(2)}) collective-permute-start(f32[2,264,512]{2,1,0:T(8,128)S(1)} %get-tuple-element.49.refs_6_.refs_4_.refs_15_), channel_id=1, source_target_pairs={{8,16},{24,32},{40,48},{56,64},{72,80},{88,96},{104,112},{16,8},{3... | collective-permute-start | bytes 3244040 | tf_op jit(solution)/shard_map/ppermute | solution.py:34
  65.1 2.1 %collective-permute-start.9 = (f32[2,256,512]{2,1,0:T(8,128)S(1)}, f32[2,256,512]{2,1,0:T(8,128)S(1)}, u32[]{:S(2)}, u32[]{:S(2)}) collective-permute-start(f32[2,256,512]{2,1,0:T(8,128)S(1)} %shard_map.60.refs_5_.refs_4_.refs_3_), channel_id=1, source_target_pairs={{1,0},{2,1},{3,2},{4,3},{5,4},{6,5},{7,6},{9,8},{10,9},{11,10},{12... | collective-permute-start | bytes 3145736 | tf_op jit(solution)/shard_map/ppermute | solution.py:29
  67.2 2.4 %collective-permute-start.8 = (f32[2,256,512]{2,1,0:T(8,128)S(1)}, f32[2,256,512]{2,1,0:T(8,128)S(1)}, u32[]{:S(2)}, u32[]{:S(2)}) collective-permute-start(f32[2,256,512]{2,1,0:T(8,128)S(1)} %shard_map.60.refs_5_.refs_4_.refs_3_), channel_id=1, source_target_pairs={{0,1},{1,2},{2,3},{3,4},{4,5},{5,6},{6,7},{8,9},{9,10},{10,11},{11... | collective-permute-start | bytes 3145736 | tf_op jit(solution)/shard_map/ppermute | solution.py:29
  69.6 9.7 %collective-permute-done.9.refs_7_.refs_6_ = f32[2,256,512]{2,1,0:T(8,128)S(1)} collective-permute-done((f32[2,256,512]{2,1,0:T(8,128)S(1)}, f32[2,256,512]{2,1,0:T(8,128)S(1)}, u32[]{:S(2)}, u32[]{:S(2)}) %collective-permute-start.9) | collective-permute-done | bytes 1048608 | tf_op jit(solution)/shard_map/ppermute | solution.py:29
  79.3 4.0 %collective-permute-done.8.refs_6_.refs_5_ = f32[2,256,512]{2,1,0:T(8,128)S(1)} collective-permute-done((f32[2,256,512]{2,1,0:T(8,128)S(1)}, f32[2,256,512]{2,1,0:T(8,128)S(1)}, u32[]{:S(2)}, u32[]{:S(2)}) %collective-permute-start.8) | collective-permute-done | bytes 1048608 | tf_op jit(solution)/shard_map/ppermute | solution.py:29
  83.3 1.2 shard_map.61
  84.6 1.9 %collective-permute-start.11 = (f32[2,264,512]{2,1,0:T(8,128)S(1)}, f32[2,264,512]{2,1,0:T(8,128)S(1)}, u32[]{:S(2)}, u32[]{:S(2)}) collective-permute-start(f32[2,264,512]{2,1,0:T(8,128)S(1)} %get-tuple-element.47), channel_id=1, source_target_pairs={{8,16},{24,32},{40,48},{56,64},{72,80},{88,96},{104,112},{16,8},{3... | collective-permute-start | bytes 3244040 | tf_op jit(solution)/shard_map/ppermute | solution.py:34
  86.5 2.1 %collective-permute-start.10 = (f32[2,264,512]{2,1,0:T(8,128)S(1)}, f32[2,264,512]{2,1,0:T(8,128)S(1)}, u32[]{:S(2)}, u32[]{:S(2)}) collective-permute-start(f32[2,264,512]{2,1,0:T(8,128)S(1)} %get-tuple-element.46.refs_0_), channel_id=1, source_target_pairs={{0,8},{16,24},{32,40},{48,56},{64,72},{80,88},{96,104},{112,120},{... | collective-permute-start | bytes 3244040 | tf_op jit(solution)/shard_map/ppermute | solution.py:34
  89.2 1.6 shard_map.63
  90.9 1.9 %collective-permute-start.14 = (f32[2,256,512]{2,1,0:T(8,128)S(1)}, f32[2,256,512]{2,1,0:T(8,128)S(1)}, u32[]{:S(2)}, u32[]{:S(2)}) collective-permute-start(f32[2,256,512]{2,1,0:T(8,128)S(1)} %get-tuple-element.51), channel_id=1, source_target_pairs={{0,1},{1,2},{2,3},{3,4},{4,5},{5,6},{6,7},{8,9},{9,10},{10,11},{11... | collective-permute-start | bytes 3145736 | tf_op jit(solution)/shard_map/ppermute | solution.py:29
  92.8 3.6 %collective-permute-start.15 = (f32[2,256,512]{2,1,0:T(8,128)S(1)}, f32[2,256,512]{2,1,0:T(8,128)S(1)}, u32[]{:S(2)}, u32[]{:S(2)}) collective-permute-start(f32[2,256,512]{2,1,0:T(8,128)S(1)} %get-tuple-element.50.refs_0_), channel_id=1, source_target_pairs={{1,0},{2,1},{3,2},{4,3},{5,4},{6,5},{7,6},{9,8},{10,9},{11,10},{12... | collective-permute-start | bytes 3145736 | tf_op jit(solution)/shard_map/ppermute | solution.py:29
  97.6 9.4 %collective-permute-done.14.refs_5_ = f32[2,256,512]{2,1,0:T(8,128)S(1)} collective-permute-done((f32[2,256,512]{2,1,0:T(8,128)S(1)}, f32[2,256,512]{2,1,0:T(8,128)S(1)}, u32[]{:S(2)}, u32[]{:S(2)}) %collective-permute-start.14) | collective-permute-done | bytes 1048608 | tf_op jit(solution)/shard_map/ppermute | solution.py:29
  107.0 1.8 %collective-permute-done.15.refs_6_ = f32[2,256,512]{2,1,0:T(8,128)S(1)} collective-permute-done((f32[2,256,512]{2,1,0:T(8,128)S(1)}, f32[2,256,512]{2,1,0:T(8,128)S(1)}, u32[]{:S(2)}, u32[]{:S(2)}) %collective-permute-start.15) | collective-permute-done | bytes 1048608 | tf_op jit(solution)/shard_map/ppermute | solution.py:29
  108.7 1.5 shard_map.65.refs_8_
  110.2 2.9 %collective-permute-done.11.refs_7_ = f32[2,264,512]{2,1,0:T(8,128)S(1)} collective-permute-done((f32[2,264,512]{2,1,0:T(8,128)S(1)}, f32[2,264,512]{2,1,0:T(8,128)S(1)}, u32[]{:S(2)}, u32[]{:S(2)}) %collective-permute-start.11) | collective-permute-done | bytes 1081376 | tf_op jit(solution)/shard_map/ppermute | solution.py:34
  113.2 3.5 %shard_map.66 = (bf16[1024,512]{1,0:T(8,128)(2,1)S(1)}, f32[2,256,512]{2,1,0:T(8,128)S(1)}) custom-call(s32[1,1]{1,0:T(1,128)S(6)} %copy.8.refs_0_, f32[2,8,512]{2,1,0:T(8,128)S(1)} %broadcast_in_dim.2.refs_0_.refs_1_, f32[2,8,512]{2,1,0:T(8,128)S(1)} %get-tuple-element.42.refs_4_.refs_3_.refs_1_.refs_2_, ...), custom_call_target="tpu_custom_call" | custom-call | tf_op jit(solution)/shard_map/pallas_call | solution.py:60
  116.6 1.9 %collective-permute-start.19 = (f32[2,256,512]{2,1,0:T(8,128)S(1)}, f32[2,256,512]{2,1,0:T(8,128)S(1)}, u32[]{:S(2)}, u32[]{:S(2)}) collective-permute-start(f32[2,256,512]{2,1,0:T(8,128)S(1)} %get-tuple-element.57.refs_4_), channel_id=1, source_target_pairs={{0,8},{8,16},{16,24},{24,32},{32,40},{40,48},{48,56},{56,64},{64,7... | collective-permute-start | bytes 3145736 | tf_op jit(solution)/shard_map/ppermute | solution.py:29
  119.4 2.7 %collective-permute-start.16 = (f32[2,128,512]{2,1,0:T(8,128)S(1)}, f32[2,128,512]{2,1,0:T(8,128)S(1)}, u32[]{:S(2)}, u32[]{:S(2)}) collective-permute-start(f32[2,128,512]{2,1,0:T(8,128)S(1)} %get-tuple-element.53.refs_4_), channel_id=1, source_target_pairs={{0,1},{1,2},{2,3},{3,4},{4,5},{5,6},{6,7},{8,9},{9,10},{10,11},{11... | collective-permute-start | bytes 1572872 | tf_op jit(solution)/shard_map/ppermute | solution.py:29
  122.1 1.9 %collective-permute-start.17 = (f32[2,128,512]{2,1,0:T(8,128)S(1)}, f32[2,128,512]{2,1,0:T(8,128)S(1)}, u32[]{:S(2)}, u32[]{:S(2)}) collective-permute-start(f32[2,128,512]{2,1,0:T(8,128)S(1)} %get-tuple-element.54.refs_5_), channel_id=1, source_target_pairs={{0,1},{1,2},{2,3},{3,4},{4,5},{5,6},{6,7},{8,9},{9,10},{10,11},{11... | collective-permute-start | bytes 1572872 | tf_op jit(solution)/shard_map/ppermute | solution.py:29
  124.0 5.9 %collective-permute-done.16.refs_6_ = f32[2,128,512]{2,1,0:T(8,128)S(1)} collective-permute-done((f32[2,128,512]{2,1,0:T(8,128)S(1)}, f32[2,128,512]{2,1,0:T(8,128)S(1)}, u32[]{:S(2)}, u32[]{:S(2)}) %collective-permute-start.16) | collective-permute-done | bytes 524320 | tf_op jit(solution)/shard_map/ppermute | solution.py:29
  129.9 5.6 %collective-permute-done.17.refs_7_ = f32[2,128,512]{2,1,0:T(8,128)S(1)} collective-permute-done((f32[2,128,512]{2,1,0:T(8,128)S(1)}, f32[2,128,512]{2,1,0:T(8,128)S(1)}, u32[]{:S(2)}, u32[]{:S(2)}) %collective-permute-start.17) | collective-permute-done | bytes 524320 | tf_op jit(solution)/shard_map/ppermute | solution.py:29
  136.1 3.6 %collective-permute-start.18 = (f32[2,256,512]{2,1,0:T(8,128)S(1)}, f32[2,256,512]{2,1,0:T(8,128)S(1)}, u32[]{:S(2)}, u32[]{:S(2)}) collective-permute-start(f32[2,256,512]{2,1,0:T(8,128)S(1)} %get-tuple-element.56.refs_0_), channel_id=1, source_target_pairs={{0,8},{8,16},{16,24},{24,32},{32,40},{40,48},{48,56},{56,64},{64,7... | collective-permute-start | bytes 3145736 | tf_op jit(solution)/shard_map/ppermute | solution.py:29
  139.8 6.9 %collective-permute-done.19.refs_5_ = f32[2,256,512]{2,1,0:T(8,128)S(1)} collective-permute-done((f32[2,256,512]{2,1,0:T(8,128)S(1)}, f32[2,256,512]{2,1,0:T(8,128)S(1)}, u32[]{:S(2)}, u32[]{:S(2)}) %collective-permute-start.19) | collective-permute-done | bytes 1048608 | tf_op jit(solution)/shard_map/ppermute | solution.py:29
  147.2 1.9 %collective-permute-start.20 = (f32[2,128,512]{2,1,0:T(8,128)S(1)}, f32[2,128,512]{2,1,0:T(8,128)S(1)}, u32[]{:S(2)}, u32[]{:S(2)}) collective-permute-start(f32[2,128,512]{2,1,0:T(8,128)S(1)} %get-tuple-element.59), channel_id=1, source_target_pairs={{0,1},{1,2},{2,3},{3,4},{4,5},{5,6},{6,7},{8,9},{9,10},{10,11},{11... | collective-permute-start | bytes 1572872 | tf_op jit(solution)/shard_map/ppermute | solution.py:29
  149.1 2.3 %collective-permute-start.21 = (f32[2,128,512]{2,1,0:T(8,128)S(1)}, f32[2,128,512]{2,1,0:T(8,128)S(1)}, u32[]{:S(2)}, u32[]{:S(2)}) collective-permute-start(f32[2,128,512]{2,1,0:T(8,128)S(1)} %get-tuple-element.60), channel_id=1, source_target_pairs={{0,1},{1,2},{2,3},{3,4},{4,5},{5,6},{6,7},{8,9},{9,10},{10,11},{11... | collective-permute-start | bytes 1572872 | tf_op jit(solution)/shard_map/ppermute | solution.py:29
  151.4 6.3 %collective-permute-done.20.refs_0_ = f32[2,128,512]{2,1,0:T(8,128)S(1)} collective-permute-done((f32[2,128,512]{2,1,0:T(8,128)S(1)}, f32[2,128,512]{2,1,0:T(8,128)S(1)}, u32[]{:S(2)}, u32[]{:S(2)}) %collective-permute-start.20) | collective-permute-done | bytes 524320 | tf_op jit(solution)/shard_map/ppermute | solution.py:29
  157.7 5.6 %collective-permute-done.21.refs_1_ = f32[2,128,512]{2,1,0:T(8,128)S(1)} collective-permute-done((f32[2,128,512]{2,1,0:T(8,128)S(1)}, f32[2,128,512]{2,1,0:T(8,128)S(1)}, u32[]{:S(2)}, u32[]{:S(2)}) %collective-permute-start.21) | collective-permute-done | bytes 524320 | tf_op jit(solution)/shard_map/ppermute | solution.py:29
  163.3 1.0 shard_map.70.refs_1_
  164.3 4.6 %collective-permute-done.18.refs_0_ = f32[2,256,512]{2,1,0:T(8,128)S(1)} collective-permute-done((f32[2,256,512]{2,1,0:T(8,128)S(1)}, f32[2,256,512]{2,1,0:T(8,128)S(1)}, u32[]{:S(2)}, u32[]{:S(2)}) %collective-permute-start.18) | collective-permute-done | bytes 1048608 | tf_op jit(solution)/shard_map/ppermute | solution.py:29
  168.9 1.1 shard_map.71
  (26 shorter events, 4.9 us)
Async XLA Ops:
  0.0 7.6 %copy-start.3 = (f32[2,512,512]{2,1,0:T(8,128)S(1)}, f32[2,512,512]{2,1,0:T(8,128)}, u32[]{:S(2)}) copy-start(f32[2,512,512]{2,1,0:T(8,128)} %param.5) | copy-start | bytes 6291460
  0.0 12.2 %copy-start.2 = (s32[1,1,1,2]{3,2,1,0:T(1,128)S(1)}, s32[1,1,1,2]{3,2,1,0:T(1,128)}, u32[]{:S(2)}) copy-start(s32[1,1,1,2]{3,2,1,0:T(1,128)} %param.8) | copy-start | bytes 28
  1.4 29.7 %collective-permute-start.5 = (f32[2,256,512]{2,1,0:T(8,128)S(1)}, f32[2,256,512]{2,1,0:T(8,128)S(1)}, u32[]{:S(2)}, u32[]{:S(2)}) collective-permute-start(f32[2,256,512]{2,1,0:T(8,128)S(1)} %slice.11.refs_3_.refs_1_), channel_id=1, source_target_pairs={{8,0},{16,8},{24,16},{32,24},{40,32},{48,40},{56,48},{64,56},{72,6... | collective-permute-start | bytes 3145736 | tf_op jit(solution)/shard_map/ppermute | solution.py:29
  7.7 12.6 %collective-permute-start.2 = (f32[2,128,512]{2,1,0:T(8,128)S(1)}, f32[2,128,512]{2,1,0:T(8,128)}, u32[]{:S(2)}, u32[]{:S(2)}) collective-permute-start(f32[2,128,512]{2,1,0:T(8,128)S(1)} %get-tuple-element.61.refs_3_), channel_id=1, source_target_pairs={{1,0},{2,1},{3,2},{4,3},{5,4},{6,5},{7,6},{9,8},{10,9},{11,10},{12... | collective-permute-start | bytes 1572872 | tf_op jit(solution)/shard_map/ppermute | solution.py:29
  9.6 12.3 %collective-permute-start.1 = (f32[2,128,512]{2,1,0:T(8,128)S(1)}, f32[2,128,512]{2,1,0:T(8,128)}, u32[]{:S(2)}, u32[]{:S(2)}) collective-permute-start(f32[2,128,512]{2,1,0:T(8,128)S(1)} %get-tuple-element.62.refs_2_), channel_id=1, source_target_pairs={{1,0},{2,1},{3,2},{4,3},{5,4},{6,5},{7,6},{9,8},{10,9},{11,10},{12... | collective-permute-start | bytes 1572872 | tf_op jit(solution)/shard_map/ppermute | solution.py:29
  12.3 7.9 %collective-permute-start.3 = (f32[2,8,512]{2,1,0:T(8,128)S(1)}, f32[2,8,512]{2,1,0:T(8,128)S(1)}, u32[]{:S(2)}, u32[]{:S(2)}) collective-permute-start(f32[2,8,512]{2,1,0:T(8,128)S(1)} %broadcast_in_dim.2.refs_0_.refs_1_), channel_id=1, source_target_pairs={{0,8},{8,16},{16,24},{24,32},{32,40},{40,48},{48,56},{56,64},{64,7... | collective-permute-start | bytes 98312 | tf_op jit(solution)/shard_map/ppermute | solution.py:29
  23.2 17.6 %copy-start.1 = (f32[2,512,512]{2,1,0:T(8,128)S(1)}, f32[2,512,512]{2,1,0:T(8,128)}, u32[]{:S(2)}) copy-start(f32[2,512,512]{2,1,0:T(8,128)} %refs_3_.1) | copy-start | bytes 6291460
  23.2 29.9 %collective-permute-start.4 = (f32[2,264,512]{2,1,0:T(8,128)S(1)}, f32[2,264,512]{2,1,0:T(8,128)S(1)}, u32[]{:S(2)}, u32[]{:S(2)}) collective-permute-start(f32[2,264,512]{2,1,0:T(8,128)S(1)} %shard_map.56.refs_0_), channel_id=1, source_target_pairs={{8,0},{16,8},{24,16},{32,24},{40,32},{48,40},{56,48},{64,56},{72,6... | collective-permute-start | bytes 3244040 | tf_op jit(solution)/shard_map/ppermute | solution.py:29
  25.7 5.4 %collective-permute-start = (f32[2,8,512]{2,1,0:T(8,128)S(1)}, f32[2,8,512]{2,1,0:T(8,128)S(1)}, u32[]{:S(2)}, u32[]{:S(2)}) collective-permute-start(f32[2,8,512]{2,1,0:T(8,128)S(1)} %broadcast_in_dim.2.refs_0_.refs_1_), channel_id=1, source_target_pairs={{0,1},{1,2},{2,3},{3,4},{4,5},{5,6},{6,7},{8,9},{9,10},{10,11},{11... | collective-permute-start | bytes 98312 | tf_op jit(solution)/shard_map/ppermute | solution.py:29
  31.2 14.9 %collective-permute-start.7 = (f32[2,136,512]{2,1,0:T(8,128)S(1)}, f32[2,136,512]{2,1,0:T(8,128)S(1)}, u32[]{:S(2)}, u32[]{:S(2)}) collective-permute-start(f32[2,136,512]{2,1,0:T(8,128)S(1)} %get-tuple-element.35), channel_id=1, source_target_pairs={{1,0},{2,1},{3,2},{4,3},{5,4},{6,5},{7,6},{9,8},{10,9},{11,10},{12... | collective-permute-start | bytes 1671176 | tf_op jit(solution)/shard_map/ppermute | solution.py:29
  33.2 13.0 %collective-permute-start.6 = (f32[2,128,512]{2,1,0:T(8,128)S(1)}, f32[2,128,512]{2,1,0:T(8,128)S(1)}, u32[]{:S(2)}, u32[]{:S(2)}) collective-permute-start(f32[2,128,512]{2,1,0:T(8,128)S(1)} %get-tuple-element.34), channel_id=1, source_target_pairs={{1,0},{2,1},{3,2},{4,3},{5,4},{6,5},{7,6},{9,8},{10,9},{11,10},{12... | collective-permute-start | bytes 1572872 | tf_op jit(solution)/shard_map/ppermute | solution.py:29
  46.2 7.0 %copy-start = (f32[1,1,1,512,512]{4,3,2,1,0:T(8,128)S(1)}, f32[1,1,1,512,512]{4,3,2,1,0:T(8,128)}, u32[]{:S(2)}) copy-start(f32[1,1,1,512,512]{4,3,2,1,0:T(8,128)} %param.7) | copy-start | bytes 3145732
  57.8 30.8 %collective-permute-start.13 = (f32[2,264,512]{2,1,0:T(8,128)S(1)}, f32[2,264,512]{2,1,0:T(8,128)S(1)}, u32[]{:S(2)}, u32[]{:S(2)}) collective-permute-start(f32[2,264,512]{2,1,0:T(8,128)S(1)} %get-tuple-element.49.refs_6_.refs_4_.refs_15_), channel_id=1, source_target_pairs={{8,16},{24,32},{40,48},{56,64},{72,80},{88,96},{104,112},{16,8},{3... | collective-permute-start | bytes 3244040 | tf_op jit(solution)/shard_map/ppermute | solution.py:34
  64.3 25.0 %collective-permute-start.12 = (f32[2,264,512]{2,1,0:T(8,128)S(1)}, f32[2,264,512]{2,1,0:T(8,128)S(1)}, u32[]{:S(2)}, u32[]{:S(2)}) collective-permute-start(f32[2,264,512]{2,1,0:T(8,128)S(1)} %get-tuple-element.49.refs_6_.refs_4_.refs_15_), channel_id=1, source_target_pairs={{0,8},{16,24},{32,40},{48,56},{64,72},{80,88},{96,104},{112,120},{... | collective-permute-start | bytes 3244040 | tf_op jit(solution)/shard_map/ppermute | solution.py:34
  65.1 14.2 %collective-permute-start.9 = (f32[2,256,512]{2,1,0:T(8,128)S(1)}, f32[2,256,512]{2,1,0:T(8,128)S(1)}, u32[]{:S(2)}, u32[]{:S(2)}) collective-permute-start(f32[2,256,512]{2,1,0:T(8,128)S(1)} %shard_map.60.refs_5_.refs_4_.refs_3_), channel_id=1, source_target_pairs={{1,0},{2,1},{3,2},{4,3},{5,4},{6,5},{7,6},{9,8},{10,9},{11,10},{12... | collective-permute-start | bytes 3145736 | tf_op jit(solution)/shard_map/ppermute | solution.py:29
  67.2 16.1 %collective-permute-start.8 = (f32[2,256,512]{2,1,0:T(8,128)S(1)}, f32[2,256,512]{2,1,0:T(8,128)S(1)}, u32[]{:S(2)}, u32[]{:S(2)}) collective-permute-start(f32[2,256,512]{2,1,0:T(8,128)S(1)} %shard_map.60.refs_5_.refs_4_.refs_3_), channel_id=1, source_target_pairs={{0,1},{1,2},{2,3},{3,4},{4,5},{5,6},{6,7},{8,9},{9,10},{10,11},{11... | collective-permute-start | bytes 3145736 | tf_op jit(solution)/shard_map/ppermute | solution.py:29
  84.6 28.6 %collective-permute-start.11 = (f32[2,264,512]{2,1,0:T(8,128)S(1)}, f32[2,264,512]{2,1,0:T(8,128)S(1)}, u32[]{:S(2)}, u32[]{:S(2)}) collective-permute-start(f32[2,264,512]{2,1,0:T(8,128)S(1)} %get-tuple-element.47), channel_id=1, source_target_pairs={{8,16},{24,32},{40,48},{56,64},{72,80},{88,96},{104,112},{16,8},{3... | collective-permute-start | bytes 3244040 | tf_op jit(solution)/shard_map/ppermute | solution.py:34
  86.5 26.7 %collective-permute-start.10 = (f32[2,264,512]{2,1,0:T(8,128)S(1)}, f32[2,264,512]{2,1,0:T(8,128)S(1)}, u32[]{:S(2)}, u32[]{:S(2)}) collective-permute-start(f32[2,264,512]{2,1,0:T(8,128)S(1)} %get-tuple-element.46.refs_0_), channel_id=1, source_target_pairs={{0,8},{16,24},{32,40},{48,56},{64,72},{80,88},{96,104},{112,120},{... | collective-permute-start | bytes 3244040 | tf_op jit(solution)/shard_map/ppermute | solution.py:34
  90.9 16.1 %collective-permute-start.14 = (f32[2,256,512]{2,1,0:T(8,128)S(1)}, f32[2,256,512]{2,1,0:T(8,128)S(1)}, u32[]{:S(2)}, u32[]{:S(2)}) collective-permute-start(f32[2,256,512]{2,1,0:T(8,128)S(1)} %get-tuple-element.51), channel_id=1, source_target_pairs={{0,1},{1,2},{2,3},{3,4},{4,5},{5,6},{6,7},{8,9},{9,10},{10,11},{11... | collective-permute-start | bytes 3145736 | tf_op jit(solution)/shard_map/ppermute | solution.py:29
  92.8 15.9 %collective-permute-start.15 = (f32[2,256,512]{2,1,0:T(8,128)S(1)}, f32[2,256,512]{2,1,0:T(8,128)S(1)}, u32[]{:S(2)}, u32[]{:S(2)}) collective-permute-start(f32[2,256,512]{2,1,0:T(8,128)S(1)} %get-tuple-element.50.refs_0_), channel_id=1, source_target_pairs={{1,0},{2,1},{3,2},{4,3},{5,4},{6,5},{7,6},{9,8},{10,9},{11,10},{12... | collective-permute-start | bytes 3145736 | tf_op jit(solution)/shard_map/ppermute | solution.py:29
  116.6 30.0 %collective-permute-start.19 = (f32[2,256,512]{2,1,0:T(8,128)S(1)}, f32[2,256,512]{2,1,0:T(8,128)S(1)}, u32[]{:S(2)}, u32[]{:S(2)}) collective-permute-start(f32[2,256,512]{2,1,0:T(8,128)S(1)} %get-tuple-element.57.refs_4_), channel_id=1, source_target_pairs={{0,8},{8,16},{16,24},{24,32},{32,40},{40,48},{48,56},{56,64},{64,7... | collective-permute-start | bytes 3145736 | tf_op jit(solution)/shard_map/ppermute | solution.py:29
  119.4 10.5 %collective-permute-start.16 = (f32[2,128,512]{2,1,0:T(8,128)S(1)}, f32[2,128,512]{2,1,0:T(8,128)S(1)}, u32[]{:S(2)}, u32[]{:S(2)}) collective-permute-start(f32[2,128,512]{2,1,0:T(8,128)S(1)} %get-tuple-element.53.refs_4_), channel_id=1, source_target_pairs={{0,1},{1,2},{2,3},{3,4},{4,5},{5,6},{6,7},{8,9},{9,10},{10,11},{11... | collective-permute-start | bytes 1572872 | tf_op jit(solution)/shard_map/ppermute | solution.py:29
  122.1 13.4 %collective-permute-start.17 = (f32[2,128,512]{2,1,0:T(8,128)S(1)}, f32[2,128,512]{2,1,0:T(8,128)S(1)}, u32[]{:S(2)}, u32[]{:S(2)}) collective-permute-start(f32[2,128,512]{2,1,0:T(8,128)S(1)} %get-tuple-element.54.refs_5_), channel_id=1, source_target_pairs={{0,1},{1,2},{2,3},{3,4},{4,5},{5,6},{6,7},{8,9},{9,10},{10,11},{11... | collective-permute-start | bytes 1572872 | tf_op jit(solution)/shard_map/ppermute | solution.py:29
  136.1 32.8 %collective-permute-start.18 = (f32[2,256,512]{2,1,0:T(8,128)S(1)}, f32[2,256,512]{2,1,0:T(8,128)S(1)}, u32[]{:S(2)}, u32[]{:S(2)}) collective-permute-start(f32[2,256,512]{2,1,0:T(8,128)S(1)} %get-tuple-element.56.refs_0_), channel_id=1, source_target_pairs={{0,8},{8,16},{16,24},{24,32},{32,40},{40,48},{48,56},{56,64},{64,7... | collective-permute-start | bytes 3145736 | tf_op jit(solution)/shard_map/ppermute | solution.py:29
  147.2 10.5 %collective-permute-start.20 = (f32[2,128,512]{2,1,0:T(8,128)S(1)}, f32[2,128,512]{2,1,0:T(8,128)S(1)}, u32[]{:S(2)}, u32[]{:S(2)}) collective-permute-start(f32[2,128,512]{2,1,0:T(8,128)S(1)} %get-tuple-element.59), channel_id=1, source_target_pairs={{0,1},{1,2},{2,3},{3,4},{4,5},{5,6},{6,7},{8,9},{9,10},{10,11},{11... | collective-permute-start | bytes 1572872 | tf_op jit(solution)/shard_map/ppermute | solution.py:29
  149.1 14.2 %collective-permute-start.21 = (f32[2,128,512]{2,1,0:T(8,128)S(1)}, f32[2,128,512]{2,1,0:T(8,128)S(1)}, u32[]{:S(2)}, u32[]{:S(2)}) collective-permute-start(f32[2,128,512]{2,1,0:T(8,128)S(1)} %get-tuple-element.60), channel_id=1, source_target_pairs={{0,1},{1,2},{2,3},{3,4},{4,5},{5,6},{6,7},{8,9},{9,10},{10,11},{11... | collective-permute-start | bytes 1572872 | tf_op jit(solution)/shard_map/ppermute | solution.py:29

commit v7 on v6

--- a/solution.py
+++ b/solution.py
@@ -118,6 +118,12 @@
 
 def absent(place):
     return place[0, :1, :] == 0.0
+
+
+def place_kernel(offset, out):
+    odd = lax.rem(lax.axis_index("row"), 2) * ODD
+    for plane, add in ((0, odd), (1, 0)):
+        out[plane] = jnp.full(out.shape[1:], offset[0, plane] + 1 + add, jnp.int32).astype(F32)
 
 
 def prepare_kernel(offset, cos_ref, sin_ref, pupil_ref, bx, bxt, by, byt_head, byt_tail, pupil_out):
@@ -395,9 +401,7 @@
 
     half, whole, spot = block(h), block(w), block(EXTRA)
     pieces = [block(h // 2)] * 2
-    odd = lax.axis_index("row") % 2 * ODD
-    spots = offset[0] + 1 + jnp.stack([odd, jnp.zeros_like(odd)])
-    me = jnp.broadcast_to(spots.astype(F32)[:, None, None], (2, EXTRA, w))
+    (me,) = call(place_kernel, [spot], (), scalars=(offset,))
     head = spectrum[:, :h]
     tail = [spectrum[:, h : h + h // 2], spectrum[:, h + h // 2 :]]
 

time: 171 us -> 170 us (level)
  Pallas kernels: 26.7 us -> 24.8 us
    pallas_call x15 -> x16, Pallas kernels: 24.5 us -> 22.7 us  [call(): pl.pallas_call(body, out_shape=out_flat, in_specs=[ANY] * skip + [SMEM] *...]
  transfers between devices with their start and end apart: 22 -> 22, of which waited for: 16 -> 17; matrix products, arithmetic and copies ran while one was open for 3% -> 3% of each run, Pallas kernels for 10% -> 10%
where the time goes in v7:
time: 170 us; the launch traced here: 169 us
  waiting for transfers between devices  79.4 us (47%)
  starting transfers between devices  57.6 us (34%)
  Pallas kernels  24.8 us (15%)
  other arithmetic  4.39 us (3%)
    ppermute x18, waiting for transfers between devices, shifted(): lax.ppermute(value, axis, [(source, source + steps) for source in range(l...  75.9 us
    ppermute x18, starting transfers between devices, shifted(): lax.ppermute(value, axis, [(source, source + steps) for source in range(l...  47 us
    pallas_call x16, Pallas kernels, call(): pl.pallas_call(body, out_shape=out_flat, in_specs=[ANY] * skip + [SMEM] *...  22.7 us
    ppermute x4, starting transfers between devices, swapped(): lax.ppermute(value, axis, [(a, a + 1) for a in lower] + [(a + 1, a) for a...  10.6 us
    convert_element_type x1, other arithmetic, dft_tables(): (jnp.sin(angle) * scale).astype(jnp.bfloat16)  4.39 us
    ppermute x4, waiting for transfers between devices, swapped(): lax.ppermute(value, axis, [(a, a + 1) for a in lower] + [(a + 1, a) for a...  3.58 us
  transfers between devices with their start and end apart: 22, of which 17 were waited for; matrix products, arithmetic and copies ran while one was open for 3% of the time, Pallas kernels for 10%

profile of v7, /device:TPU:28, one launch (start us, length us, event | category | flops | bytes accessed | tf_op | source)
XLA Modules:
  0.0 169.0 jit_solution(11100476540975918287)
XLA Ops:
  0.0 1.4 slice.11.refs_3_.refs_1_
  1.4 6.1 %collective-permute-start.5 = (f32[2,256,512]{2,1,0:T(8,128)S(1)}, f32[2,256,512]{2,1,0:T(8,128)S(1)}, u32[]{:S(2)}, u32[]{:S(2)}) collective-permute-start(f32[2,256,512]{2,1,0:T(8,128)S(1)} %slice.11.refs_3_.refs_1_), channel_id=1, source_target_pairs={{8,0},{16,8},{24,16},{32,24},{40,32},{48,40},{56,48},{64,56},{72,6... | collective-permute-start | bytes 3145736 | tf_op jit(solution)/shard_map/ppermute | solution.py:29
  7.7 1.9 %collective-permute-start.2 = (f32[2,128,512]{2,1,0:T(8,128)S(1)}, f32[2,128,512]{2,1,0:T(8,128)S(1)}, u32[]{:S(2)}, u32[]{:S(2)}) collective-permute-start(f32[2,128,512]{2,1,0:T(8,128)S(1)} %get-tuple-element.61.refs_3_), channel_id=1, source_target_pairs={{1,0},{2,1},{3,2},{4,3},{5,4},{6,5},{7,6},{9,8},{10,9},{11,10},{12... | collective-permute-start | bytes 1572872 | tf_op jit(solution)/shard_map/ppermute | solution.py:29
  9.6 2.5 %collective-permute-start.1 = (f32[2,128,512]{2,1,0:T(8,128)S(1)}, f32[2,128,512]{2,1,0:T(8,128)S(1)}, u32[]{:S(2)}, u32[]{:S(2)}) collective-permute-start(f32[2,128,512]{2,1,0:T(8,128)S(1)} %get-tuple-element.62.refs_2_), channel_id=1, source_target_pairs={{1,0},{2,1},{3,2},{4,3},{5,4},{6,5},{7,6},{9,8},{10,9},{11,10},{12... | collective-permute-start | bytes 1572872 | tf_op jit(solution)/shard_map/ppermute | solution.py:29
  12.7 1.9 %collective-permute-start.3 = (f32[2,8,512]{2,1,0:T(8,128)S(1)}, f32[2,8,512]{2,1,0:T(8,128)S(1)}, u32[]{:S(2)}, u32[]{:S(2)}) collective-permute-start(f32[2,8,512]{2,1,0:T(8,128)S(1)} %shard_map.55.refs_0_.refs_1_), channel_id=1, source_target_pairs={{0,8},{8,16},{16,24},{24,32},{32,40},{40,48},{48,56},{56,64},{64,7... | collective-permute-start | bytes 98312 | tf_op jit(solution)/shard_map/ppermute | solution.py:29
  14.7 6.0 %collective-permute-done.3.refs_1_.refs_3_.refs_2_ = f32[2,8,512]{2,1,0:T(8,128)S(1)} collective-permute-done((f32[2,8,512]{2,1,0:T(8,128)S(1)}, f32[2,8,512]{2,1,0:T(8,128)S(1)}, u32[]{:S(2)}, u32[]{:S(2)}) %collective-permute-start.3) | collective-permute-done | bytes 32800 | tf_op jit(solution)/shard_map/ppermute | solution.py:29
  20.6 1.2 collective-permute-done.1.refs_4_
  22.0 2.4 %collective-permute-start.4 = (f32[2,264,512]{2,1,0:T(8,128)S(1)}, f32[2,264,512]{2,1,0:T(8,128)S(1)}, u32[]{:S(2)}, u32[]{:S(2)}) collective-permute-start(f32[2,264,512]{2,1,0:T(8,128)S(1)} %shard_map.57.refs_0_), channel_id=1, source_target_pairs={{8,0},{16,8},{24,16},{32,24},{40,32},{48,40},{56,48},{64,56},{72,6... | collective-permute-start | bytes 3244040 | tf_op jit(solution)/shard_map/ppermute | solution.py:29
  24.5 3.4 %collective-permute-start = (f32[2,8,512]{2,1,0:T(8,128)S(1)}, f32[2,8,512]{2,1,0:T(8,128)S(1)}, u32[]{:S(2)}, u32[]{:S(2)}) collective-permute-start(f32[2,8,512]{2,1,0:T(8,128)S(1)} %shard_map.55.refs_0_.refs_1_), channel_id=1, source_target_pairs={{0,1},{1,2},{2,3},{3,4},{4,5},{5,6},{6,7},{8,9},{9,10},{10,11},{11... | collective-permute-start | bytes 98312 | tf_op jit(solution)/shard_map/ppermute | solution.py:29
  27.9 2.0 %collective-permute-done.refs_2_.refs_1_.refs_4_ = f32[2,8,512]{2,1,0:T(8,128)S(1)} collective-permute-done((f32[2,8,512]{2,1,0:T(8,128)S(1)}, f32[2,8,512]{2,1,0:T(8,128)S(1)}, u32[]{:S(2)}, u32[]{:S(2)}) %collective-permute-start) | collective-permute-done | bytes 32800 | tf_op jit(solution)/shard_map/ppermute | solution.py:29
  29.9 1.2 collective-permute-done.5.refs_4_.refs_2_
  31.2 1.9 %collective-permute-start.7 = (f32[2,136,512]{2,1,0:T(8,128)S(1)}, f32[2,136,512]{2,1,0:T(8,128)S(1)}, u32[]{:S(2)}, u32[]{:S(2)}) collective-permute-start(f32[2,136,512]{2,1,0:T(8,128)S(1)} %get-tuple-element.35), channel_id=1, source_target_pairs={{1,0},{2,1},{3,2},{4,3},{5,4},{6,5},{7,6},{9,8},{10,9},{11,10},{12... | collective-permute-start | bytes 1671176 | tf_op jit(solution)/shard_map/ppermute | solution.py:29
  33.2 2.5 %collective-permute-start.6 = (f32[2,128,512]{2,1,0:T(8,128)S(1)}, f32[2,128,512]{2,1,0:T(8,128)S(1)}, u32[]{:S(2)}, u32[]{:S(2)}) collective-permute-start(f32[2,128,512]{2,1,0:T(8,128)S(1)} %get-tuple-element.34), channel_id=1, source_target_pairs={{1,0},{2,1},{3,2},{4,3},{5,4},{6,5},{7,6},{9,8},{10,9},{11,10},{12... | collective-permute-start | bytes 1572872 | tf_op jit(solution)/shard_map/ppermute | solution.py:29
  36.4 4.4 %multiply_convert_fusion = (bf16[512,512]{1,0:T(8,128)(2,1)S(1)}, bf16[512,512]{1,0:T(8,128)(2,1)S(1)}) fusion(), kind=kLoop, calls=%fused_computation.6 | loop fusion | flops 4718592 | bytes 1048576 | tf_op jit(solution)/shard_map/convert_element_type | solution.py:44
  40.8 5.4 %shard_map.56 = (bf16[1024,1024]{1,0:T(8,128)(2,1)S(1)}, bf16[1024,1024]{1,0:T(8,128)(2,1)S(1)}, bf16[1024,1024]{1,0:T(8,128)(2,1)S(1)}, bf16[1024,512]{1,0:T(8,...) custom-call(s32[1,2]{1,0:T(1,128)S(1)} %bitcast.5, ...), custom_call_target="tpu_custom_call" | custom-call | tf_op jit(solution)/shard_map/pallas_call | solution.py:60
  46.2 1.5 shard_map.59
  47.7 5.4 %collective-permute-done.4.refs_6_ = f32[2,264,512]{2,1,0:T(8,128)S(1)} collective-permute-done((f32[2,264,512]{2,1,0:T(8,128)S(1)}, f32[2,264,512]{2,1,0:T(8,128)S(1)}, u32[]{:S(2)}, u32[]{:S(2)}) %collective-permute-start.4) | collective-permute-done | bytes 1081376 | tf_op jit(solution)/shard_map/ppermute | solution.py:29
  53.2 3.4 %shard_map.60 = (f32[2,256,512]{2,1,0:T(8,128)S(1)}, f32[2,8,512]{2,1,0:T(8,128)S(1)}, bf16[1024,512]{1,0:T(8,128)(2,1)S(1)}, f32[2,264,512]{2,1,0:T(8,128)S(1)}) custom-call(s32[1,1]{1,0:T(1,128)S(6)} %copy.8.refs_0_, f32[2,8,512]{2,1,0:T(8,128)S(1)} %shard_map.55.refs_0_.refs_1_, f32[2,128,512]{2,1,0:T(8,128)S(1)} %get-tuple-element.62.refs_2_, ...), custom_call_target="tpu_custom_call" | custom-call | tf_op jit(solution)/shard_map/pallas_call | solution.py:60
  56.5 6.5 %collective-permute-start.13 = (f32[2,264,512]{2,1,0:T(8,128)S(1)}, f32[2,264,512]{2,1,0:T(8,128)S(1)}, u32[]{:S(2)}, u32[]{:S(2)}) collective-permute-start(f32[2,264,512]{2,1,0:T(8,128)S(1)} %get-tuple-element.49.refs_6_.refs_4_.refs_15_), channel_id=1, source_target_pairs={{8,16},{24,32},{40,48},{56,64},{72,80},{88,96},{104,112},{16,8},{3... | collective-permute-start | bytes 3244040 | tf_op jit(solution)/shard_map/ppermute | solution.py:34
  63.9 2.1 %collective-permute-start.9 = (f32[2,256,512]{2,1,0:T(8,128)S(1)}, f32[2,256,512]{2,1,0:T(8,128)S(1)}, u32[]{:S(2)}, u32[]{:S(2)}) collective-permute-start(f32[2,256,512]{2,1,0:T(8,128)S(1)} %shard_map.61.refs_5_.refs_4_.refs_3_), channel_id=1, source_target_pairs={{1,0},{2,1},{3,2},{4,3},{5,4},{6,5},{7,6},{9,8},{10,9},{11,10},{12... | collective-permute-start | bytes 3145736 | tf_op jit(solution)/shard_map/ppermute | solution.py:29
  66.0 2.2 %collective-permute-start.8 = (f32[2,256,512]{2,1,0:T(8,128)S(1)}, f32[2,256,512]{2,1,0:T(8,128)S(1)}, u32[]{:S(2)}, u32[]{:S(2)}) collective-permute-start(f32[2,256,512]{2,1,0:T(8,128)S(1)} %shard_map.61.refs_5_.refs_4_.refs_3_), channel_id=1, source_target_pairs={{0,1},{1,2},{2,3},{3,4},{4,5},{5,6},{6,7},{8,9},{9,10},{10,11},{11... | collective-permute-start | bytes 3145736 | tf_op jit(solution)/shard_map/ppermute | solution.py:29
  68.3 10.1 %collective-permute-done.9.refs_7_.refs_6_ = f32[2,256,512]{2,1,0:T(8,128)S(1)} collective-permute-done((f32[2,256,512]{2,1,0:T(8,128)S(1)}, f32[2,256,512]{2,1,0:T(8,128)S(1)}, u32[]{:S(2)}, u32[]{:S(2)}) %collective-permute-start.9) | collective-permute-done | bytes 1048608 | tf_op jit(solution)/shard_map/ppermute | solution.py:29
  78.3 3.8 %collective-permute-done.8.refs_6_.refs_5_ = f32[2,256,512]{2,1,0:T(8,128)S(1)} collective-permute-done((f32[2,256,512]{2,1,0:T(8,128)S(1)}, f32[2,256,512]{2,1,0:T(8,128)S(1)}, u32[]{:S(2)}, u32[]{:S(2)}) %collective-permute-start.8) | collective-permute-done | bytes 1048608 | tf_op jit(solution)/shard_map/ppermute | solution.py:29
  82.1 1.2 shard_map.62
  83.4 1.9 %collective-permute-start.11 = (f32[2,264,512]{2,1,0:T(8,128)S(1)}, f32[2,264,512]{2,1,0:T(8,128)S(1)}, u32[]{:S(2)}, u32[]{:S(2)}) collective-permute-start(f32[2,264,512]{2,1,0:T(8,128)S(1)} %get-tuple-element.47), channel_id=1, source_target_pairs={{8,16},{24,32},{40,48},{56,64},{72,80},{88,96},{104,112},{16,8},{3... | collective-permute-start | bytes 3244040 | tf_op jit(solution)/shard_map/ppermute | solution.py:34
  85.3 2.1 %collective-permute-start.10 = (f32[2,264,512]{2,1,0:T(8,128)S(1)}, f32[2,264,512]{2,1,0:T(8,128)S(1)}, u32[]{:S(2)}, u32[]{:S(2)}) collective-permute-start(f32[2,264,512]{2,1,0:T(8,128)S(1)} %get-tuple-element.46.refs_0_), channel_id=1, source_target_pairs={{0,8},{16,24},{32,40},{48,56},{64,72},{80,88},{96,104},{112,120},{... | collective-permute-start | bytes 3244040 | tf_op jit(solution)/shard_map/ppermute | solution.py:34
  88.0 1.6 shard_map.64
  89.7 1.9 %collective-permute-start.14 = (f32[2,256,512]{2,1,0:T(8,128)S(1)}, f32[2,256,512]{2,1,0:T(8,128)S(1)}, u32[]{:S(2)}, u32[]{:S(2)}) collective-permute-start(f32[2,256,512]{2,1,0:T(8,128)S(1)} %get-tuple-element.51), channel_id=1, source_target_pairs={{0,1},{1,2},{2,3},{3,4},{4,5},{5,6},{6,7},{8,9},{9,10},{10,11},{11... | collective-permute-start | bytes 3145736 | tf_op jit(solution)/shard_map/ppermute | solution.py:29
  91.6 3.6 %collective-permute-start.15 = (f32[2,256,512]{2,1,0:T(8,128)S(1)}, f32[2,256,512]{2,1,0:T(8,128)S(1)}, u32[]{:S(2)}, u32[]{:S(2)}) collective-permute-start(f32[2,256,512]{2,1,0:T(8,128)S(1)} %get-tuple-element.50.refs_0_), channel_id=1, source_target_pairs={{1,0},{2,1},{3,2},{4,3},{5,4},{6,5},{7,6},{9,8},{10,9},{11,10},{12... | collective-permute-start | bytes 3145736 | tf_op jit(solution)/shard_map/ppermute | solution.py:29
  96.4 9.4 %collective-permute-done.14.refs_5_ = f32[2,256,512]{2,1,0:T(8,128)S(1)} collective-permute-done((f32[2,256,512]{2,1,0:T(8,128)S(1)}, f32[2,256,512]{2,1,0:T(8,128)S(1)}, u32[]{:S(2)}, u32[]{:S(2)}) %collective-permute-start.14) | collective-permute-done | bytes 1048608 | tf_op jit(solution)/shard_map/ppermute | solution.py:29
  105.8 1.8 %collective-permute-done.15.refs_6_ = f32[2,256,512]{2,1,0:T(8,128)S(1)} collective-permute-done((f32[2,256,512]{2,1,0:T(8,128)S(1)}, f32[2,256,512]{2,1,0:T(8,128)S(1)}, u32[]{:S(2)}, u32[]{:S(2)}) %collective-permute-start.15) | collective-permute-done | bytes 1048608 | tf_op jit(solution)/shard_map/ppermute | solution.py:29
  107.5 1.5 shard_map.66.refs_8_
  109.0 2.9 %collective-permute-done.11.refs_7_ = f32[2,264,512]{2,1,0:T(8,128)S(1)} collective-permute-done((f32[2,264,512]{2,1,0:T(8,128)S(1)}, f32[2,264,512]{2,1,0:T(8,128)S(1)}, u32[]{:S(2)}, u32[]{:S(2)}) %collective-permute-start.11) | collective-permute-done | bytes 1081376 | tf_op jit(solution)/shard_map/ppermute | solution.py:34
  112.0 3.5 %shard_map.67 = (bf16[1024,512]{1,0:T(8,128)(2,1)S(1)}, f32[2,256,512]{2,1,0:T(8,128)S(1)}) custom-call(s32[1,1]{1,0:T(1,128)S(6)} %copy.8.refs_0_, f32[2,8,512]{2,1,0:T(8,128)S(1)} %shard_map.55.refs_0_.refs_1_, f32[2,8,512]{2,1,0:T(8,128)S(1)} %get-tuple-element.42.refs_4_.refs_3_.refs_1_.refs_2_, ...), custom_call_target="tpu_custom_call" | custom-call | tf_op jit(solution)/shard_map/pallas_call | solution.py:60
  115.4 1.9 %collective-permute-start.19 = (f32[2,256,512]{2,1,0:T(8,128)S(1)}, f32[2,256,512]{2,1,0:T(8,128)S(1)}, u32[]{:S(2)}, u32[]{:S(2)}) collective-permute-start(f32[2,256,512]{2,1,0:T(8,128)S(1)} %get-tuple-element.57.refs_4_), channel_id=1, source_target_pairs={{0,8},{8,16},{16,24},{24,32},{32,40},{40,48},{48,56},{56,64},{64,7... | collective-permute-start | bytes 3145736 | tf_op jit(solution)/shard_map/ppermute | solution.py:29
  118.2 2.7 %collective-permute-start.16 = (f32[2,128,512]{2,1,0:T(8,128)S(1)}, f32[2,128,512]{2,1,0:T(8,128)S(1)}, u32[]{:S(2)}, u32[]{:S(2)}) collective-permute-start(f32[2,128,512]{2,1,0:T(8,128)S(1)} %get-tuple-element.53.refs_4_), channel_id=1, source_target_pairs={{0,1},{1,2},{2,3},{3,4},{4,5},{5,6},{6,7},{8,9},{9,10},{10,11},{11... | collective-permute-start | bytes 1572872 | tf_op jit(solution)/shard_map/ppermute | solution.py:29
  120.9 1.9 %collective-permute-start.17 = (f32[2,128,512]{2,1,0:T(8,128)S(1)}, f32[2,128,512]{2,1,0:T(8,128)S(1)}, u32[]{:S(2)}, u32[]{:S(2)}) collective-permute-start(f32[2,128,512]{2,1,0:T(8,128)S(1)} %get-tuple-element.54.refs_5_), channel_id=1, source_target_pairs={{0,1},{1,2},{2,3},{3,4},{4,5},{5,6},{6,7},{8,9},{9,10},{10,11},{11... | collective-permute-start | bytes 1572872 | tf_op jit(solution)/shard_map/ppermute | solution.py:29
  122.8 5.9 %collective-permute-done.16.refs_6_ = f32[2,128,512]{2,1,0:T(8,128)S(1)} collective-permute-done((f32[2,128,512]{2,1,0:T(8,128)S(1)}, f32[2,128,512]{2,1,0:T(8,128)S(1)}, u32[]{:S(2)}, u32[]{:S(2)}) %collective-permute-start.16) | collective-permute-done | bytes 524320 | tf_op jit(solution)/shard_map/ppermute | solution.py:29
  128.7 5.6 %collective-permute-done.17.refs_7_ = f32[2,128,512]{2,1,0:T(8,128)S(1)} collective-permute-done((f32[2,128,512]{2,1,0:T(8,128)S(1)}, f32[2,128,512]{2,1,0:T(8,128)S(1)}, u32[]{:S(2)}, u32[]{:S(2)}) %collective-permute-start.17) | collective-permute-done | bytes 524320 | tf_op jit(solution)/shard_map/ppermute | solution.py:29
  134.9 3.6 %collective-permute-start.18 = (f32[2,256,512]{2,1,0:T(8,128)S(1)}, f32[2,256,512]{2,1,0:T(8,128)S(1)}, u32[]{:S(2)}, u32[]{:S(2)}) collective-permute-start(f32[2,256,512]{2,1,0:T(8,128)S(1)} %get-tuple-element.56.refs_0_), channel_id=1, source_target_pairs={{0,8},{8,16},{16,24},{24,32},{32,40},{40,48},{48,56},{56,64},{64,7... | collective-permute-start | bytes 3145736 | tf_op jit(solution)/shard_map/ppermute | solution.py:29
  138.6 6.9 %collective-permute-done.19.refs_5_ = f32[2,256,512]{2,1,0:T(8,128)S(1)} collective-permute-done((f32[2,256,512]{2,1,0:T(8,128)S(1)}, f32[2,256,512]{2,1,0:T(8,128)S(1)}, u32[]{:S(2)}, u32[]{:S(2)}) %collective-permute-start.19) | collective-permute-done | bytes 1048608 | tf_op jit(solution)/shard_map/ppermute | solution.py:29
  146.0 1.9 %collective-permute-start.20 = (f32[2,128,512]{2,1,0:T(8,128)S(1)}, f32[2,128,512]{2,1,0:T(8,128)S(1)}, u32[]{:S(2)}, u32[]{:S(2)}) collective-permute-start(f32[2,128,512]{2,1,0:T(8,128)S(1)} %get-tuple-element.59), channel_id=1, source_target_pairs={{0,1},{1,2},{2,3},{3,4},{4,5},{5,6},{6,7},{8,9},{9,10},{10,11},{11... | collective-permute-start | bytes 1572872 | tf_op jit(solution)/shard_map/ppermute | solution.py:29
  147.9 2.3 %collective-permute-start.21 = (f32[2,128,512]{2,1,0:T(8,128)S(1)}, f32[2,128,512]{2,1,0:T(8,128)S(1)}, u32[]{:S(2)}, u32[]{:S(2)}) collective-permute-start(f32[2,128,512]{2,1,0:T(8,128)S(1)} %get-tuple-element.60), channel_id=1, source_target_pairs={{0,1},{1,2},{2,3},{3,4},{4,5},{5,6},{6,7},{8,9},{9,10},{10,11},{11... | collective-permute-start | bytes 1572872 | tf_op jit(solution)/shard_map/ppermute | solution.py:29
  150.2 6.3 %collective-permute-done.20.refs_0_ = f32[2,128,512]{2,1,0:T(8,128)S(1)} collective-permute-done((f32[2,128,512]{2,1,0:T(8,128)S(1)}, f32[2,128,512]{2,1,0:T(8,128)S(1)}, u32[]{:S(2)}, u32[]{:S(2)}) %collective-permute-start.20) | collective-permute-done | bytes 524320 | tf_op jit(solution)/shard_map/ppermute | solution.py:29
  156.5 5.6 %collective-permute-done.21.refs_1_ = f32[2,128,512]{2,1,0:T(8,128)S(1)} collective-permute-done((f32[2,128,512]{2,1,0:T(8,128)S(1)}, f32[2,128,512]{2,1,0:T(8,128)S(1)}, u32[]{:S(2)}, u32[]{:S(2)}) %collective-permute-start.21) | collective-permute-done | bytes 524320 | tf_op jit(solution)/shard_map/ppermute | solution.py:29
  162.1 1.0 shard_map.71.refs_1_
  163.1 4.6 %collective-permute-done.18.refs_0_ = f32[2,256,512]{2,1,0:T(8,128)S(1)} collective-permute-done((f32[2,256,512]{2,1,0:T(8,128)S(1)}, f32[2,256,512]{2,1,0:T(8,128)S(1)}, u32[]{:S(2)}, u32[]{:S(2)}) %collective-permute-start.18) | collective-permute-done | bytes 1048608 | tf_op jit(solution)/shard_map/ppermute | solution.py:29
  167.7 1.1 shard_map.72
  (25 shorter events, 5.4 us)
Async XLA Ops:
  0.0 7.6 %copy-start.3 = (f32[2,512,512]{2,1,0:T(8,128)S(1)}, f32[2,512,512]{2,1,0:T(8,128)}, u32[]{:S(2)}) copy-start(f32[2,512,512]{2,1,0:T(8,128)} %param.5) | copy-start | bytes 6291460
  0.0 12.2 %copy-start.2 = (s32[1,1,1,2]{3,2,1,0:T(1,128)S(1)}, s32[1,1,1,2]{3,2,1,0:T(1,128)}, u32[]{:S(2)}) copy-start(s32[1,1,1,2]{3,2,1,0:T(1,128)} %param.8) | copy-start | bytes 28
  1.4 29.7 %collective-permute-start.5 = (f32[2,256,512]{2,1,0:T(8,128)S(1)}, f32[2,256,512]{2,1,0:T(8,128)S(1)}, u32[]{:S(2)}, u32[]{:S(2)}) collective-permute-start(f32[2,256,512]{2,1,0:T(8,128)S(1)} %slice.11.refs_3_.refs_1_), channel_id=1, source_target_pairs={{8,0},{16,8},{24,16},{32,24},{40,32},{48,40},{56,48},{64,56},{72,6... | collective-permute-start | bytes 3145736 | tf_op jit(solution)/shard_map/ppermute | solution.py:29
  7.7 13.0 %collective-permute-start.2 = (f32[2,128,512]{2,1,0:T(8,128)S(1)}, f32[2,128,512]{2,1,0:T(8,128)S(1)}, u32[]{:S(2)}, u32[]{:S(2)}) collective-permute-start(f32[2,128,512]{2,1,0:T(8,128)S(1)} %get-tuple-element.61.refs_3_), channel_id=1, source_target_pairs={{1,0},{2,1},{3,2},{4,3},{5,4},{6,5},{7,6},{9,8},{10,9},{11,10},{12... | collective-permute-start | bytes 1572872 | tf_op jit(solution)/shard_map/ppermute | solution.py:29
  9.6 12.3 %collective-permute-start.1 = (f32[2,128,512]{2,1,0:T(8,128)S(1)}, f32[2,128,512]{2,1,0:T(8,128)S(1)}, u32[]{:S(2)}, u32[]{:S(2)}) collective-permute-start(f32[2,128,512]{2,1,0:T(8,128)S(1)} %get-tuple-element.62.refs_2_), channel_id=1, source_target_pairs={{1,0},{2,1},{3,2},{4,3},{5,4},{6,5},{7,6},{9,8},{10,9},{11,10},{12... | collective-permute-start | bytes 1572872 | tf_op jit(solution)/shard_map/ppermute | solution.py:29
  12.7 7.9 %collective-permute-start.3 = (f32[2,8,512]{2,1,0:T(8,128)S(1)}, f32[2,8,512]{2,1,0:T(8,128)S(1)}, u32[]{:S(2)}, u32[]{:S(2)}) collective-permute-start(f32[2,8,512]{2,1,0:T(8,128)S(1)} %shard_map.55.refs_0_.refs_1_), channel_id=1, source_target_pairs={{0,8},{8,16},{16,24},{24,32},{32,40},{40,48},{48,56},{56,64},{64,7... | collective-permute-start | bytes 98312 | tf_op jit(solution)/shard_map/ppermute | solution.py:29
  22.0 18.8 %copy-start.1 = (f32[2,512,512]{2,1,0:T(8,128)S(1)}, f32[2,512,512]{2,1,0:T(8,128)}, u32[]{:S(2)}) copy-start(f32[2,512,512]{2,1,0:T(8,128)} %refs_3_.1) | copy-start | bytes 6291460
  22.0 31.1 %collective-permute-start.4 = (f32[2,264,512]{2,1,0:T(8,128)S(1)}, f32[2,264,512]{2,1,0:T(8,128)S(1)}, u32[]{:S(2)}, u32[]{:S(2)}) collective-permute-start(f32[2,264,512]{2,1,0:T(8,128)S(1)} %shard_map.57.refs_0_), channel_id=1, source_target_pairs={{8,0},{16,8},{24,16},{32,24},{40,32},{48,40},{56,48},{64,56},{72,6... | collective-permute-start | bytes 3244040 | tf_op jit(solution)/shard_map/ppermute | solution.py:29
  24.5 5.4 %collective-permute-start = (f32[2,8,512]{2,1,0:T(8,128)S(1)}, f32[2,8,512]{2,1,0:T(8,128)S(1)}, u32[]{:S(2)}, u32[]{:S(2)}) collective-permute-start(f32[2,8,512]{2,1,0:T(8,128)S(1)} %shard_map.55.refs_0_.refs_1_), channel_id=1, source_target_pairs={{0,1},{1,2},{2,3},{3,4},{4,5},{5,6},{6,7},{8,9},{9,10},{10,11},{11... | collective-permute-start | bytes 98312 | tf_op jit(solution)/shard_map/ppermute | solution.py:29
  31.2 14.9 %collective-permute-start.7 = (f32[2,136,512]{2,1,0:T(8,128)S(1)}, f32[2,136,512]{2,1,0:T(8,128)S(1)}, u32[]{:S(2)}, u32[]{:S(2)}) collective-permute-start(f32[2,136,512]{2,1,0:T(8,128)S(1)} %get-tuple-element.35), channel_id=1, source_target_pairs={{1,0},{2,1},{3,2},{4,3},{5,4},{6,5},{7,6},{9,8},{10,9},{11,10},{12... | collective-permute-start | bytes 1671176 | tf_op jit(solution)/shard_map/ppermute | solution.py:29
  33.2 13.0 %collective-permute-start.6 = (f32[2,128,512]{2,1,0:T(8,128)S(1)}, f32[2,128,512]{2,1,0:T(8,128)S(1)}, u32[]{:S(2)}, u32[]{:S(2)}) collective-permute-start(f32[2,128,512]{2,1,0:T(8,128)S(1)} %get-tuple-element.34), channel_id=1, source_target_pairs={{1,0},{2,1},{3,2},{4,3},{5,4},{6,5},{7,6},{9,8},{10,9},{11,10},{12... | collective-permute-start | bytes 1572872 | tf_op jit(solution)/shard_map/ppermute | solution.py:29
  46.2 7.0 %copy-start = (f32[1,1,1,512,512]{4,3,2,1,0:T(8,128)S(1)}, f32[1,1,1,512,512]{4,3,2,1,0:T(8,128)}, u32[]{:S(2)}) copy-start(f32[1,1,1,512,512]{4,3,2,1,0:T(8,128)} %param.7) | copy-start | bytes 3145732
  56.5 30.8 %collective-permute-start.13 = (f32[2,264,512]{2,1,0:T(8,128)S(1)}, f32[2,264,512]{2,1,0:T(8,128)S(1)}, u32[]{:S(2)}, u32[]{:S(2)}) collective-permute-start(f32[2,264,512]{2,1,0:T(8,128)S(1)} %get-tuple-element.49.refs_6_.refs_4_.refs_15_), channel_id=1, source_target_pairs={{8,16},{24,32},{40,48},{56,64},{72,80},{88,96},{104,112},{16,8},{3... | collective-permute-start | bytes 3244040 | tf_op jit(solution)/shard_map/ppermute | solution.py:34
  63.1 25.0 %collective-permute-start.12 = (f32[2,264,512]{2,1,0:T(8,128)S(1)}, f32[2,264,512]{2,1,0:T(8,128)S(1)}, u32[]{:S(2)}, u32[]{:S(2)}) collective-permute-start(f32[2,264,512]{2,1,0:T(8,128)S(1)} %get-tuple-element.49.refs_6_.refs_4_.refs_15_), channel_id=1, source_target_pairs={{0,8},{16,24},{32,40},{48,56},{64,72},{80,88},{96,104},{112,120},{... | collective-permute-start | bytes 3244040 | tf_op jit(solution)/shard_map/ppermute | solution.py:34
  63.9 14.4 %collective-permute-start.9 = (f32[2,256,512]{2,1,0:T(8,128)S(1)}, f32[2,256,512]{2,1,0:T(8,128)S(1)}, u32[]{:S(2)}, u32[]{:S(2)}) collective-permute-start(f32[2,256,512]{2,1,0:T(8,128)S(1)} %shard_map.61.refs_5_.refs_4_.refs_3_), channel_id=1, source_target_pairs={{1,0},{2,1},{3,2},{4,3},{5,4},{6,5},{7,6},{9,8},{10,9},{11,10},{12... | collective-permute-start | bytes 3145736 | tf_op jit(solution)/shard_map/ppermute | solution.py:29
  66.0 16.1 %collective-permute-start.8 = (f32[2,256,512]{2,1,0:T(8,128)S(1)}, f32[2,256,512]{2,1,0:T(8,128)S(1)}, u32[]{:S(2)}, u32[]{:S(2)}) collective-permute-start(f32[2,256,512]{2,1,0:T(8,128)S(1)} %shard_map.61.refs_5_.refs_4_.refs_3_), channel_id=1, source_target_pairs={{0,1},{1,2},{2,3},{3,4},{4,5},{5,6},{6,7},{8,9},{9,10},{10,11},{11... | collective-permute-start | bytes 3145736 | tf_op jit(solution)/shard_map/ppermute | solution.py:29
  83.4 28.6 %collective-permute-start.11 = (f32[2,264,512]{2,1,0:T(8,128)S(1)}, f32[2,264,512]{2,1,0:T(8,128)S(1)}, u32[]{:S(2)}, u32[]{:S(2)}) collective-permute-start(f32[2,264,512]{2,1,0:T(8,128)S(1)} %get-tuple-element.47), channel_id=1, source_target_pairs={{8,16},{24,32},{40,48},{56,64},{72,80},{88,96},{104,112},{16,8},{3... | collective-permute-start | bytes 3244040 | tf_op jit(solution)/shard_map/ppermute | solution.py:34
  85.3 26.7 %collective-permute-start.10 = (f32[2,264,512]{2,1,0:T(8,128)S(1)}, f32[2,264,512]{2,1,0:T(8,128)S(1)}, u32[]{:S(2)}, u32[]{:S(2)}) collective-permute-start(f32[2,264,512]{2,1,0:T(8,128)S(1)} %get-tuple-element.46.refs_0_), channel_id=1, source_target_pairs={{0,8},{16,24},{32,40},{48,56},{64,72},{80,88},{96,104},{112,120},{... | collective-permute-start | bytes 3244040 | tf_op jit(solution)/shard_map/ppermute | solution.py:34
  89.7 16.1 %collective-permute-start.14 = (f32[2,256,512]{2,1,0:T(8,128)S(1)}, f32[2,256,512]{2,1,0:T(8,128)S(1)}, u32[]{:S(2)}, u32[]{:S(2)}) collective-permute-start(f32[2,256,512]{2,1,0:T(8,128)S(1)} %get-tuple-element.51), channel_id=1, source_target_pairs={{0,1},{1,2},{2,3},{3,4},{4,5},{5,6},{6,7},{8,9},{9,10},{10,11},{11... | collective-permute-start | bytes 3145736 | tf_op jit(solution)/shard_map/ppermute | solution.py:29
  91.6 15.9 %collective-permute-start.15 = (f32[2,256,512]{2,1,0:T(8,128)S(1)}, f32[2,256,512]{2,1,0:T(8,128)S(1)}, u32[]{:S(2)}, u32[]{:S(2)}) collective-permute-start(f32[2,256,512]{2,1,0:T(8,128)S(1)} %get-tuple-element.50.refs_0_), channel_id=1, source_target_pairs={{1,0},{2,1},{3,2},{4,3},{5,4},{6,5},{7,6},{9,8},{10,9},{11,10},{12... | collective-permute-start | bytes 3145736 | tf_op jit(solution)/shard_map/ppermute | solution.py:29
  115.4 30.0 %collective-permute-start.19 = (f32[2,256,512]{2,1,0:T(8,128)S(1)}, f32[2,256,512]{2,1,0:T(8,128)S(1)}, u32[]{:S(2)}, u32[]{:S(2)}) collective-permute-start(f32[2,256,512]{2,1,0:T(8,128)S(1)} %get-tuple-element.57.refs_4_), channel_id=1, source_target_pairs={{0,8},{8,16},{16,24},{24,32},{32,40},{40,48},{48,56},{56,64},{64,7... | collective-permute-start | bytes 3145736 | tf_op jit(solution)/shard_map/ppermute | solution.py:29
  118.2 10.5 %collective-permute-start.16 = (f32[2,128,512]{2,1,0:T(8,128)S(1)}, f32[2,128,512]{2,1,0:T(8,128)S(1)}, u32[]{:S(2)}, u32[]{:S(2)}) collective-permute-start(f32[2,128,512]{2,1,0:T(8,128)S(1)} %get-tuple-element.53.refs_4_), channel_id=1, source_target_pairs={{0,1},{1,2},{2,3},{3,4},{4,5},{5,6},{6,7},{8,9},{9,10},{10,11},{11... | collective-permute-start | bytes 1572872 | tf_op jit(solution)/shard_map/ppermute | solution.py:29
  120.9 13.4 %collective-permute-start.17 = (f32[2,128,512]{2,1,0:T(8,128)S(1)}, f32[2,128,512]{2,1,0:T(8,128)S(1)}, u32[]{:S(2)}, u32[]{:S(2)}) collective-permute-start(f32[2,128,512]{2,1,0:T(8,128)S(1)} %get-tuple-element.54.refs_5_), channel_id=1, source_target_pairs={{0,1},{1,2},{2,3},{3,4},{4,5},{5,6},{6,7},{8,9},{9,10},{10,11},{11... | collective-permute-start | bytes 1572872 | tf_op jit(solution)/shard_map/ppermute | solution.py:29
  134.9 32.8 %collective-permute-start.18 = (f32[2,256,512]{2,1,0:T(8,128)S(1)}, f32[2,256,512]{2,1,0:T(8,128)S(1)}, u32[]{:S(2)}, u32[]{:S(2)}) collective-permute-start(f32[2,256,512]{2,1,0:T(8,128)S(1)} %get-tuple-element.56.refs_0_), channel_id=1, source_target_pairs={{0,8},{8,16},{16,24},{24,32},{32,40},{40,48},{48,56},{56,64},{64,7... | collective-permute-start | bytes 3145736 | tf_op jit(solution)/shard_map/ppermute | solution.py:29
  146.0 10.5 %collective-permute-start.20 = (f32[2,128,512]{2,1,0:T(8,128)S(1)}, f32[2,128,512]{2,1,0:T(8,128)S(1)}, u32[]{:S(2)}, u32[]{:S(2)}) collective-permute-start(f32[2,128,512]{2,1,0:T(8,128)S(1)} %get-tuple-element.59), channel_id=1, source_target_pairs={{0,1},{1,2},{2,3},{3,4},{4,5},{5,6},{6,7},{8,9},{9,10},{10,11},{11... | collective-permute-start | bytes 1572872 | tf_op jit(solution)/shard_map/ppermute | solution.py:29
  147.9 14.2 %collective-permute-start.21 = (f32[2,128,512]{2,1,0:T(8,128)S(1)}, f32[2,128,512]{2,1,0:T(8,128)S(1)}, u32[]{:S(2)}, u32[]{:S(2)}) collective-permute-start(f32[2,128,512]{2,1,0:T(8,128)S(1)} %get-tuple-element.60), channel_id=1, source_target_pairs={{0,1},{1,2},{2,3},{3,4},{4,5},{5,6},{6,7},{8,9},{9,10},{10,11},{11... | collective-permute-start | bytes 1572872 | tf_op jit(solution)/shard_map/ppermute | solution.py:29

commit v8 on v7

--- a/solution.py
+++ b/solution.py
@@ -19,6 +19,7 @@
 
 EXTRA = 8
 BLOCK = 128
+STORES = 4
 ODD = 1024
 PAD = 8
 
@@ -298,11 +299,10 @@
     return jnp.where(odd, when_odd, when_even)
 
 
-def between_kernel(
+def between(
     first, head, me, minus, plus, target_minus, target_plus, mine, got_minus, got_plus, to_minus, to_plus
 ):
     w = me.shape[2]
-    odd = odd_row(me)
     for row, rows in split(first, w):
         ways = ways_of(head, rows, w, row)
         f, f_minus, f_plus = (ways[0](x) for x in (me, minus, plus))
@@ -315,16 +315,34 @@
         plus_m = [a & b for a, b in zip(seen(ways[0](target_plus)), (s, s_minus, s_plus))]
         for plane in range(2):
             values = [part(x, plane, rows, w) for x in (mine, got_minus, got_plus)]
-            if head:
-                values[1:] = pick(odd, values[1], values[2]), pick(odd, values[2], values[1])
             sums = []
             for masks in (minus_m, plus_m):
                 terms = [jnp.where(m, v, 0.0) for m, v in zip(masks, values)]
                 sums.append(terms[0] + terms[1] + terms[2])
-            if not head:
-                sums = pick(odd, sums[0], sums[1]), pick(odd, sums[1], sums[0])
             put(to_minus, plane, rows, sums[0])
             put(to_plus, plane, rows, sums[1])
+
+
+def by_parity(when_odd, when_even):
+    odd = lax.rem(lax.axis_index("row"), 2) == 1
+    pl.when(odd)(when_odd)
+    pl.when(jnp.logical_not(odd))(when_even)
+
+
+def between_kernel(
+    first, head, me, minus, plus, target_minus, target_plus, mine, got_one, got_two, to_one, to_two
+):
+    places = (me, minus, plus, target_minus, target_plus, mine)
+    if head:
+        by_parity(
+            lambda: between(first, head, *places, got_one, got_two, to_one, to_two),
+            lambda: between(first, head, *places, got_two, got_one, to_one, to_two),
+        )
+    else:
+        by_parity(
+            lambda: between(first, head, *places, got_one, got_two, to_one, to_two),
+            lambda: between(first, head, *places, got_one, got_two, to_two, to_one),
+        )
 
 
 def own_kernel(first, head, me, minus, plus, mine, got_minus, got_plus, own):
@@ -365,17 +383,17 @@
     def kernel(base, *refs):
         pieces = refs[: len(got)]
         out, value, sems = refs[-3:]
-        copies, row = [], 0
-        for k, piece in enumerate(pieces):
-            size = min(piece.shape[1], h - row)
-            rows = slice(row, row + size)
-            value[:, rows, :] = base[:, rows, :] - STEP * piece[:, :size, :]
+        copies = []
+        for k in range(STORES):
+            size = h // STORES
+            rows = slice(k * size, (k + 1) * size)
+            for plane in range(2):
+                value[plane, rows, :] = base[plane, rows, :] - STEP * part(list(pieces), plane, rows, w)
             copy = pltpu.make_async_copy(
-                value.at[:, pl.ds(row, size), :], out.at[:, pl.ds(first + row, size), :], sems.at[k]
+                value.at[:, pl.ds(k * size, size), :], out.at[:, pl.ds(first + k * size, size), :], sems.at[k]
             )
             copy.start()
             copies.append(copy)
-            row += size
         for copy in copies:
             copy.wait()
 
@@ -384,7 +402,7 @@
         out_shape=whole,
         in_specs=[VMEM] * (1 + len(got)) + [ANY] * len(held),
         out_specs=ANY,
-        scratch_shapes=[pltpu.VMEM((2, h, w), F32), pltpu.SemaphoreType.DMA((len(got),))],
+        scratch_shapes=[pltpu.VMEM((2, h, w), F32), pltpu.SemaphoreType.DMA((STORES,))],
         input_output_aliases={1 + len(got): 0} if held else {},
         compiler_params=pltpu.CompilerParams(vmem_limit_bytes=LIMIT),
     )(base, *got, *held)

time: 170 us -> 169 us (level)
  no operation moved by 1% of the time
where the time goes in v8:
time: 169 us
  waiting for transfers between devices  79.4 us (47%)
  starting transfers between devices  57.7 us (34%)
  Pallas kernels  24.7 us (15%)
  other arithmetic  4.39 us (3%)
    ppermute x18, waiting for transfers between devices, shifted(): lax.ppermute(value, axis, [(source, source + steps) for source in range(l...  75.8 us
    ppermute x18, starting transfers between devices, shifted(): lax.ppermute(value, axis, [(source, source + steps) for source in range(l...  47.1 us
    pallas_call x16, Pallas kernels, call(): pl.pallas_call(body, out_shape=out_flat, in_specs=[ANY] * skip + [SMEM] *...  22.6 us
    ppermute x4, starting transfers between devices, swapped(): lax.ppermute(value, axis, [(a, a + 1) for a in lower] + [(a + 1, a) for a...  10.6 us
    convert_element_type x1, other arithmetic, dft_tables(): (jnp.sin(angle) * scale).astype(jnp.bfloat16)  4.39 us
    ppermute x4, waiting for transfers between devices, swapped(): lax.ppermute(value, axis, [(a, a + 1) for a in lower] + [(a + 1, a) for a...  3.67 us
  transfers between devices with their start and end apart: 22, of which 17 were waited for; matrix products, arithmetic and copies ran while one was open for 3% of the time, Pallas kernels for 10%

profile of v8, /device:TPU:28, one launch (start us, length us, event | category | flops | bytes accessed | tf_op | source)
XLA Modules:
  0.0 168.8 jit_solution(12064670155228149129)
XLA Ops:
  0.0 1.4 slice.11.refs_3_.refs_1_
  1.4 6.1 %collective-permute-start.5 = (f32[2,256,512]{2,1,0:T(8,128)S(1)}, f32[2,256,512]{2,1,0:T(8,128)S(1)}, u32[]{:S(2)}, u32[]{:S(2)}) collective-permute-start(f32[2,256,512]{2,1,0:T(8,128)S(1)} %slice.11.refs_3_.refs_1_), channel_id=1, source_target_pairs={{8,0},{16,8},{24,16},{32,24},{40,32},{48,40},{56,48},{64,56},{72,6... | collective-permute-start | bytes 3145736 | tf_op jit(solution)/shard_map/ppermute | solution.py:30
  7.7 1.9 %collective-permute-start.2 = (f32[2,128,512]{2,1,0:T(8,128)S(1)}, f32[2,128,512]{2,1,0:T(8,128)S(1)}, u32[]{:S(2)}, u32[]{:S(2)}) collective-permute-start(f32[2,128,512]{2,1,0:T(8,128)S(1)} %get-tuple-element.61.refs_3_), channel_id=1, source_target_pairs={{1,0},{2,1},{3,2},{4,3},{5,4},{6,5},{7,6},{9,8},{10,9},{11,10},{12... | collective-permute-start | bytes 1572872 | tf_op jit(solution)/shard_map/ppermute | solution.py:30
  9.6 2.5 %collective-permute-start.1 = (f32[2,128,512]{2,1,0:T(8,128)S(1)}, f32[2,128,512]{2,1,0:T(8,128)S(1)}, u32[]{:S(2)}, u32[]{:S(2)}) collective-permute-start(f32[2,128,512]{2,1,0:T(8,128)S(1)} %get-tuple-element.62.refs_2_), channel_id=1, source_target_pairs={{1,0},{2,1},{3,2},{4,3},{5,4},{6,5},{7,6},{9,8},{10,9},{11,10},{12... | collective-permute-start | bytes 1572872 | tf_op jit(solution)/shard_map/ppermute | solution.py:30
  12.7 1.9 %collective-permute-start.3 = (f32[2,8,512]{2,1,0:T(8,128)S(1)}, f32[2,8,512]{2,1,0:T(8,128)S(1)}, u32[]{:S(2)}, u32[]{:S(2)}) collective-permute-start(f32[2,8,512]{2,1,0:T(8,128)S(1)} %shard_map.55.refs_0_.refs_1_), channel_id=1, source_target_pairs={{0,8},{8,16},{16,24},{24,32},{32,40},{40,48},{48,56},{56,64},{64,7... | collective-permute-start | bytes 98312 | tf_op jit(solution)/shard_map/ppermute | solution.py:30
  14.7 6.0 %collective-permute-done.3.refs_1_.refs_3_.refs_2_ = f32[2,8,512]{2,1,0:T(8,128)S(1)} collective-permute-done((f32[2,8,512]{2,1,0:T(8,128)S(1)}, f32[2,8,512]{2,1,0:T(8,128)S(1)}, u32[]{:S(2)}, u32[]{:S(2)}) %collective-permute-start.3) | collective-permute-done | bytes 32800 | tf_op jit(solution)/shard_map/ppermute | solution.py:30
  20.6 1.2 collective-permute-done.1.refs_4_
  22.0 2.4 %collective-permute-start.4 = (f32[2,264,512]{2,1,0:T(8,128)S(1)}, f32[2,264,512]{2,1,0:T(8,128)S(1)}, u32[]{:S(2)}, u32[]{:S(2)}) collective-permute-start(f32[2,264,512]{2,1,0:T(8,128)S(1)} %shard_map.57.refs_0_), channel_id=1, source_target_pairs={{8,0},{16,8},{24,16},{32,24},{40,32},{48,40},{56,48},{64,56},{72,6... | collective-permute-start | bytes 3244040 | tf_op jit(solution)/shard_map/ppermute | solution.py:30
  24.5 3.4 %collective-permute-start = (f32[2,8,512]{2,1,0:T(8,128)S(1)}, f32[2,8,512]{2,1,0:T(8,128)S(1)}, u32[]{:S(2)}, u32[]{:S(2)}) collective-permute-start(f32[2,8,512]{2,1,0:T(8,128)S(1)} %shard_map.55.refs_0_.refs_1_), channel_id=1, source_target_pairs={{0,1},{1,2},{2,3},{3,4},{4,5},{5,6},{6,7},{8,9},{9,10},{10,11},{11... | collective-permute-start | bytes 98312 | tf_op jit(solution)/shard_map/ppermute | solution.py:30
  27.9 2.0 %collective-permute-done.refs_2_.refs_1_.refs_4_ = f32[2,8,512]{2,1,0:T(8,128)S(1)} collective-permute-done((f32[2,8,512]{2,1,0:T(8,128)S(1)}, f32[2,8,512]{2,1,0:T(8,128)S(1)}, u32[]{:S(2)}, u32[]{:S(2)}) %collective-permute-start) | collective-permute-done | bytes 32800 | tf_op jit(solution)/shard_map/ppermute | solution.py:30
  29.9 1.2 collective-permute-done.5.refs_4_.refs_2_
  31.2 1.9 %collective-permute-start.7 = (f32[2,136,512]{2,1,0:T(8,128)S(1)}, f32[2,136,512]{2,1,0:T(8,128)S(1)}, u32[]{:S(2)}, u32[]{:S(2)}) collective-permute-start(f32[2,136,512]{2,1,0:T(8,128)S(1)} %get-tuple-element.35), channel_id=1, source_target_pairs={{1,0},{2,1},{3,2},{4,3},{5,4},{6,5},{7,6},{9,8},{10,9},{11,10},{12... | collective-permute-start | bytes 1671176 | tf_op jit(solution)/shard_map/ppermute | solution.py:30
  33.2 2.5 %collective-permute-start.6 = (f32[2,128,512]{2,1,0:T(8,128)S(1)}, f32[2,128,512]{2,1,0:T(8,128)S(1)}, u32[]{:S(2)}, u32[]{:S(2)}) collective-permute-start(f32[2,128,512]{2,1,0:T(8,128)S(1)} %get-tuple-element.34), channel_id=1, source_target_pairs={{1,0},{2,1},{3,2},{4,3},{5,4},{6,5},{7,6},{9,8},{10,9},{11,10},{12... | collective-permute-start | bytes 1572872 | tf_op jit(solution)/shard_map/ppermute | solution.py:30
  36.4 4.4 %multiply_convert_fusion = (bf16[512,512]{1,0:T(8,128)(2,1)S(1)}, bf16[512,512]{1,0:T(8,128)(2,1)S(1)}) fusion(), kind=kLoop, calls=%fused_computation.6 | loop fusion | flops 4718592 | bytes 1048576 | tf_op jit(solution)/shard_map/convert_element_type | solution.py:45
  40.8 5.4 %shard_map.56 = (bf16[1024,1024]{1,0:T(8,128)(2,1)S(1)}, bf16[1024,1024]{1,0:T(8,128)(2,1)S(1)}, bf16[1024,1024]{1,0:T(8,128)(2,1)S(1)}, bf16[1024,512]{1,0:T(8,...) custom-call(s32[1,2]{1,0:T(1,128)S(1)} %bitcast.5, ...), custom_call_target="tpu_custom_call" | custom-call | tf_op jit(solution)/shard_map/pallas_call | solution.py:61
  46.2 1.5 shard_map.59
  47.7 5.4 %collective-permute-done.4.refs_6_ = f32[2,264,512]{2,1,0:T(8,128)S(1)} collective-permute-done((f32[2,264,512]{2,1,0:T(8,128)S(1)}, f32[2,264,512]{2,1,0:T(8,128)S(1)}, u32[]{:S(2)}, u32[]{:S(2)}) %collective-permute-start.4) | collective-permute-done | bytes 1081376 | tf_op jit(solution)/shard_map/ppermute | solution.py:30
  53.2 3.4 %shard_map.60 = (f32[2,256,512]{2,1,0:T(8,128)S(1)}, f32[2,8,512]{2,1,0:T(8,128)S(1)}, bf16[1024,512]{1,0:T(8,128)(2,1)S(1)}, f32[2,264,512]{2,1,0:T(8,128)S(1)}) custom-call(s32[1,1]{1,0:T(1,128)S(6)} %copy.8.refs_0_, f32[2,8,512]{2,1,0:T(8,128)S(1)} %shard_map.55.refs_0_.refs_1_, f32[2,128,512]{2,1,0:T(8,128)S(1)} %get-tuple-element.62.refs_2_, ...), custom_call_target="tpu_custom_call" | custom-call | tf_op jit(solution)/shard_map/pallas_call | solution.py:61
  56.5 6.5 %collective-permute-start.13 = (f32[2,264,512]{2,1,0:T(8,128)S(1)}, f32[2,264,512]{2,1,0:T(8,128)S(1)}, u32[]{:S(2)}, u32[]{:S(2)}) collective-permute-start(f32[2,264,512]{2,1,0:T(8,128)S(1)} %get-tuple-element.49.refs_6_.refs_4_.refs_15_), channel_id=1, source_target_pairs={{8,16},{24,32},{40,48},{56,64},{72,80},{88,96},{104,112},{16,8},{3... | collective-permute-start | bytes 3244040 | tf_op jit(solution)/shard_map/ppermute | solution.py:35
  63.9 2.1 %collective-permute-start.9 = (f32[2,256,512]{2,1,0:T(8,128)S(1)}, f32[2,256,512]{2,1,0:T(8,128)S(1)}, u32[]{:S(2)}, u32[]{:S(2)}) collective-permute-start(f32[2,256,512]{2,1,0:T(8,128)S(1)} %shard_map.61.refs_5_.refs_4_.refs_3_), channel_id=1, source_target_pairs={{1,0},{2,1},{3,2},{4,3},{5,4},{6,5},{7,6},{9,8},{10,9},{11,10},{12... | collective-permute-start | bytes 3145736 | tf_op jit(solution)/shard_map/ppermute | solution.py:30
  66.0 2.2 %collective-permute-start.8 = (f32[2,256,512]{2,1,0:T(8,128)S(1)}, f32[2,256,512]{2,1,0:T(8,128)S(1)}, u32[]{:S(2)}, u32[]{:S(2)}) collective-permute-start(f32[2,256,512]{2,1,0:T(8,128)S(1)} %shard_map.61.refs_5_.refs_4_.refs_3_), channel_id=1, source_target_pairs={{0,1},{1,2},{2,3},{3,4},{4,5},{5,6},{6,7},{8,9},{9,10},{10,11},{11... | collective-permute-start | bytes 3145736 | tf_op jit(solution)/shard_map/ppermute | solution.py:30
  68.3 10.1 %collective-permute-done.9.refs_7_.refs_6_ = f32[2,256,512]{2,1,0:T(8,128)S(1)} collective-permute-done((f32[2,256,512]{2,1,0:T(8,128)S(1)}, f32[2,256,512]{2,1,0:T(8,128)S(1)}, u32[]{:S(2)}, u32[]{:S(2)}) %collective-permute-start.9) | collective-permute-done | bytes 1048608 | tf_op jit(solution)/shard_map/ppermute | solution.py:30
  78.3 3.8 %collective-permute-done.8.refs_6_.refs_5_ = f32[2,256,512]{2,1,0:T(8,128)S(1)} collective-permute-done((f32[2,256,512]{2,1,0:T(8,128)S(1)}, f32[2,256,512]{2,1,0:T(8,128)S(1)}, u32[]{:S(2)}, u32[]{:S(2)}) %collective-permute-start.8) | collective-permute-done | bytes 1048608 | tf_op jit(solution)/shard_map/ppermute | solution.py:30
  82.1 1.2 shard_map.62
  83.4 1.9 %collective-permute-start.11 = (f32[2,264,512]{2,1,0:T(8,128)S(1)}, f32[2,264,512]{2,1,0:T(8,128)S(1)}, u32[]{:S(2)}, u32[]{:S(2)}) collective-permute-start(f32[2,264,512]{2,1,0:T(8,128)S(1)} %get-tuple-element.47), channel_id=1, source_target_pairs={{8,16},{24,32},{40,48},{56,64},{72,80},{88,96},{104,112},{16,8},{3... | collective-permute-start | bytes 3244040 | tf_op jit(solution)/shard_map/ppermute | solution.py:35
  85.3 2.1 %collective-permute-start.10 = (f32[2,264,512]{2,1,0:T(8,128)S(1)}, f32[2,264,512]{2,1,0:T(8,128)S(1)}, u32[]{:S(2)}, u32[]{:S(2)}) collective-permute-start(f32[2,264,512]{2,1,0:T(8,128)S(1)} %get-tuple-element.46.refs_0_), channel_id=1, source_target_pairs={{0,8},{16,24},{32,40},{48,56},{64,72},{80,88},{96,104},{112,120},{... | collective-permute-start | bytes 3244040 | tf_op jit(solution)/shard_map/ppermute | solution.py:35
  88.0 1.5 shard_map.64
  89.6 1.9 %collective-permute-start.14 = (f32[2,256,512]{2,1,0:T(8,128)S(1)}, f32[2,256,512]{2,1,0:T(8,128)S(1)}, u32[]{:S(2)}, u32[]{:S(2)}) collective-permute-start(f32[2,256,512]{2,1,0:T(8,128)S(1)} %get-tuple-element.51), channel_id=1, source_target_pairs={{0,1},{1,2},{2,3},{3,4},{4,5},{5,6},{6,7},{8,9},{9,10},{10,11},{11... | collective-permute-start | bytes 3145736 | tf_op jit(solution)/shard_map/ppermute | solution.py:30
  91.5 3.9 %collective-permute-start.15 = (f32[2,256,512]{2,1,0:T(8,128)S(1)}, f32[2,256,512]{2,1,0:T(8,128)S(1)}, u32[]{:S(2)}, u32[]{:S(2)}) collective-permute-start(f32[2,256,512]{2,1,0:T(8,128)S(1)} %get-tuple-element.50.refs_0_), channel_id=1, source_target_pairs={{1,0},{2,1},{3,2},{4,3},{5,4},{6,5},{7,6},{9,8},{10,9},{11,10},{12... | collective-permute-start | bytes 3145736 | tf_op jit(solution)/shard_map/ppermute | solution.py:30
  96.5 9.2 %collective-permute-done.14.refs_5_ = f32[2,256,512]{2,1,0:T(8,128)S(1)} collective-permute-done((f32[2,256,512]{2,1,0:T(8,128)S(1)}, f32[2,256,512]{2,1,0:T(8,128)S(1)}, u32[]{:S(2)}, u32[]{:S(2)}) %collective-permute-start.14) | collective-permute-done | bytes 1048608 | tf_op jit(solution)/shard_map/ppermute | solution.py:30
  105.7 1.8 %collective-permute-done.15.refs_6_ = f32[2,256,512]{2,1,0:T(8,128)S(1)} collective-permute-done((f32[2,256,512]{2,1,0:T(8,128)S(1)}, f32[2,256,512]{2,1,0:T(8,128)S(1)}, u32[]{:S(2)}, u32[]{:S(2)}) %collective-permute-start.15) | collective-permute-done | bytes 1048608 | tf_op jit(solution)/shard_map/ppermute | solution.py:30
  107.4 1.5 shard_map.66.refs_8_
  108.9 3.0 %collective-permute-done.11.refs_7_ = f32[2,264,512]{2,1,0:T(8,128)S(1)} collective-permute-done((f32[2,264,512]{2,1,0:T(8,128)S(1)}, f32[2,264,512]{2,1,0:T(8,128)S(1)}, u32[]{:S(2)}, u32[]{:S(2)}) %collective-permute-start.11) | collective-permute-done | bytes 1081376 | tf_op jit(solution)/shard_map/ppermute | solution.py:35
  112.0 3.5 %shard_map.67 = (bf16[1024,512]{1,0:T(8,128)(2,1)S(1)}, f32[2,256,512]{2,1,0:T(8,128)S(1)}) custom-call(s32[1,1]{1,0:T(1,128)S(6)} %copy.8.refs_0_, f32[2,8,512]{2,1,0:T(8,128)S(1)} %shard_map.55.refs_0_.refs_1_, f32[2,8,512]{2,1,0:T(8,128)S(1)} %get-tuple-element.42.refs_4_.refs_3_.refs_1_.refs_2_, ...), custom_call_target="tpu_custom_call" | custom-call | tf_op jit(solution)/shard_map/pallas_call | solution.py:61
  115.4 1.9 %collective-permute-start.19 = (f32[2,256,512]{2,1,0:T(8,128)S(1)}, f32[2,256,512]{2,1,0:T(8,128)S(1)}, u32[]{:S(2)}, u32[]{:S(2)}) collective-permute-start(f32[2,256,512]{2,1,0:T(8,128)S(1)} %get-tuple-element.57.refs_4_), channel_id=1, source_target_pairs={{0,8},{8,16},{16,24},{24,32},{32,40},{40,48},{48,56},{56,64},{64,7... | collective-permute-start | bytes 3145736 | tf_op jit(solution)/shard_map/ppermute | solution.py:30
  118.2 2.6 %collective-permute-start.16 = (f32[2,128,512]{2,1,0:T(8,128)S(1)}, f32[2,128,512]{2,1,0:T(8,128)S(1)}, u32[]{:S(2)}, u32[]{:S(2)}) collective-permute-start(f32[2,128,512]{2,1,0:T(8,128)S(1)} %get-tuple-element.53.refs_4_), channel_id=1, source_target_pairs={{0,1},{1,2},{2,3},{3,4},{4,5},{5,6},{6,7},{8,9},{9,10},{10,11},{11... | collective-permute-start | bytes 1572872 | tf_op jit(solution)/shard_map/ppermute | solution.py:30
  120.8 1.9 %collective-permute-start.17 = (f32[2,128,512]{2,1,0:T(8,128)S(1)}, f32[2,128,512]{2,1,0:T(8,128)S(1)}, u32[]{:S(2)}, u32[]{:S(2)}) collective-permute-start(f32[2,128,512]{2,1,0:T(8,128)S(1)} %get-tuple-element.54.refs_5_), channel_id=1, source_target_pairs={{0,1},{1,2},{2,3},{3,4},{4,5},{5,6},{6,7},{8,9},{9,10},{10,11},{11... | collective-permute-start | bytes 1572872 | tf_op jit(solution)/shard_map/ppermute | solution.py:30
  122.7 6.0 %collective-permute-done.16.refs_6_ = f32[2,128,512]{2,1,0:T(8,128)S(1)} collective-permute-done((f32[2,128,512]{2,1,0:T(8,128)S(1)}, f32[2,128,512]{2,1,0:T(8,128)S(1)}, u32[]{:S(2)}, u32[]{:S(2)}) %collective-permute-start.16) | collective-permute-done | bytes 524320 | tf_op jit(solution)/shard_map/ppermute | solution.py:30
  128.7 5.6 %collective-permute-done.17.refs_7_ = f32[2,128,512]{2,1,0:T(8,128)S(1)} collective-permute-done((f32[2,128,512]{2,1,0:T(8,128)S(1)}, f32[2,128,512]{2,1,0:T(8,128)S(1)}, u32[]{:S(2)}, u32[]{:S(2)}) %collective-permute-start.17) | collective-permute-done | bytes 524320 | tf_op jit(solution)/shard_map/ppermute | solution.py:30
  134.9 3.6 %collective-permute-start.18 = (f32[2,256,512]{2,1,0:T(8,128)S(1)}, f32[2,256,512]{2,1,0:T(8,128)S(1)}, u32[]{:S(2)}, u32[]{:S(2)}) collective-permute-start(f32[2,256,512]{2,1,0:T(8,128)S(1)} %get-tuple-element.56.refs_0_), channel_id=1, source_target_pairs={{0,8},{8,16},{16,24},{24,32},{32,40},{40,48},{48,56},{56,64},{64,7... | collective-permute-start | bytes 3145736 | tf_op jit(solution)/shard_map/ppermute | solution.py:30
  138.6 6.9 %collective-permute-done.19.refs_5_ = f32[2,256,512]{2,1,0:T(8,128)S(1)} collective-permute-done((f32[2,256,512]{2,1,0:T(8,128)S(1)}, f32[2,256,512]{2,1,0:T(8,128)S(1)}, u32[]{:S(2)}, u32[]{:S(2)}) %collective-permute-start.19) | collective-permute-done | bytes 1048608 | tf_op jit(solution)/shard_map/ppermute | solution.py:30
  146.0 1.9 %collective-permute-start.20 = (f32[2,128,512]{2,1,0:T(8,128)S(1)}, f32[2,128,512]{2,1,0:T(8,128)S(1)}, u32[]{:S(2)}, u32[]{:S(2)}) collective-permute-start(f32[2,128,512]{2,1,0:T(8,128)S(1)} %get-tuple-element.59), channel_id=1, source_target_pairs={{0,1},{1,2},{2,3},{3,4},{4,5},{5,6},{6,7},{8,9},{9,10},{10,11},{11... | collective-permute-start | bytes 1572872 | tf_op jit(solution)/shard_map/ppermute | solution.py:30
  147.9 2.2 %collective-permute-start.21 = (f32[2,128,512]{2,1,0:T(8,128)S(1)}, f32[2,128,512]{2,1,0:T(8,128)S(1)}, u32[]{:S(2)}, u32[]{:S(2)}) collective-permute-start(f32[2,128,512]{2,1,0:T(8,128)S(1)} %get-tuple-element.60), channel_id=1, source_target_pairs={{0,1},{1,2},{2,3},{3,4},{4,5},{5,6},{6,7},{8,9},{9,10},{10,11},{11... | collective-permute-start | bytes 1572872 | tf_op jit(solution)/shard_map/ppermute | solution.py:30
  150.1 6.4 %collective-permute-done.20.refs_0_ = f32[2,128,512]{2,1,0:T(8,128)S(1)} collective-permute-done((f32[2,128,512]{2,1,0:T(8,128)S(1)}, f32[2,128,512]{2,1,0:T(8,128)S(1)}, u32[]{:S(2)}, u32[]{:S(2)}) %collective-permute-start.20) | collective-permute-done | bytes 524320 | tf_op jit(solution)/shard_map/ppermute | solution.py:30
  156.5 5.6 %collective-permute-done.21.refs_1_ = f32[2,128,512]{2,1,0:T(8,128)S(1)} collective-permute-done((f32[2,128,512]{2,1,0:T(8,128)S(1)}, f32[2,128,512]{2,1,0:T(8,128)S(1)}, u32[]{:S(2)}, u32[]{:S(2)}) %collective-permute-start.21) | collective-permute-done | bytes 524320 | tf_op jit(solution)/shard_map/ppermute | solution.py:30
  162.1 1.0 shard_map.71.refs_1_
  163.1 4.5 %collective-permute-done.18.refs_0_ = f32[2,256,512]{2,1,0:T(8,128)S(1)} collective-permute-done((f32[2,256,512]{2,1,0:T(8,128)S(1)}, f32[2,256,512]{2,1,0:T(8,128)S(1)}, u32[]{:S(2)}, u32[]{:S(2)}) %collective-permute-start.18) | collective-permute-done | bytes 1048608 | tf_op jit(solution)/shard_map/ppermute | solution.py:30
  167.6 1.0 shard_map.72
  (25 shorter events, 5.4 us)
Async XLA Ops:
  0.0 7.6 %copy-start.3 = (f32[2,512,512]{2,1,0:T(8,128)S(1)}, f32[2,512,512]{2,1,0:T(8,128)}, u32[]{:S(2)}) copy-start(f32[2,512,512]{2,1,0:T(8,128)} %param.5) | copy-start | bytes 6291460
  0.0 12.2 %copy-start.2 = (s32[1,1,1,2]{3,2,1,0:T(1,128)S(1)}, s32[1,1,1,2]{3,2,1,0:T(1,128)}, u32[]{:S(2)}) copy-start(s32[1,1,1,2]{3,2,1,0:T(1,128)} %param.8) | copy-start | bytes 28
  1.4 29.7 %collective-permute-start.5 = (f32[2,256,512]{2,1,0:T(8,128)S(1)}, f32[2,256,512]{2,1,0:T(8,128)S(1)}, u32[]{:S(2)}, u32[]{:S(2)}) collective-permute-start(f32[2,256,512]{2,1,0:T(8,128)S(1)} %slice.11.refs_3_.refs_1_), channel_id=1, source_target_pairs={{8,0},{16,8},{24,16},{32,24},{40,32},{48,40},{56,48},{64,56},{72,6... | collective-permute-start | bytes 3145736 | tf_op jit(solution)/shard_map/ppermute | solution.py:30
  7.7 13.0 %collective-permute-start.2 = (f32[2,128,512]{2,1,0:T(8,128)S(1)}, f32[2,128,512]{2,1,0:T(8,128)S(1)}, u32[]{:S(2)}, u32[]{:S(2)}) collective-permute-start(f32[2,128,512]{2,1,0:T(8,128)S(1)} %get-tuple-element.61.refs_3_), channel_id=1, source_target_pairs={{1,0},{2,1},{3,2},{4,3},{5,4},{6,5},{7,6},{9,8},{10,9},{11,10},{12... | collective-permute-start | bytes 1572872 | tf_op jit(solution)/shard_map/ppermute | solution.py:30
  9.6 12.3 %collective-permute-start.1 = (f32[2,128,512]{2,1,0:T(8,128)S(1)}, f32[2,128,512]{2,1,0:T(8,128)S(1)}, u32[]{:S(2)}, u32[]{:S(2)}) collective-permute-start(f32[2,128,512]{2,1,0:T(8,128)S(1)} %get-tuple-element.62.refs_2_), channel_id=1, source_target_pairs={{1,0},{2,1},{3,2},{4,3},{5,4},{6,5},{7,6},{9,8},{10,9},{11,10},{12... | collective-permute-start | bytes 1572872 | tf_op jit(solution)/shard_map/ppermute | solution.py:30
  12.7 7.9 %collective-permute-start.3 = (f32[2,8,512]{2,1,0:T(8,128)S(1)}, f32[2,8,512]{2,1,0:T(8,128)S(1)}, u32[]{:S(2)}, u32[]{:S(2)}) collective-permute-start(f32[2,8,512]{2,1,0:T(8,128)S(1)} %shard_map.55.refs_0_.refs_1_), channel_id=1, source_target_pairs={{0,8},{8,16},{16,24},{24,32},{32,40},{40,48},{48,56},{56,64},{64,7... | collective-permute-start | bytes 98312 | tf_op jit(solution)/shard_map/ppermute | solution.py:30
  22.0 18.8 %copy-start.1 = (f32[2,512,512]{2,1,0:T(8,128)S(1)}, f32[2,512,512]{2,1,0:T(8,128)}, u32[]{:S(2)}) copy-start(f32[2,512,512]{2,1,0:T(8,128)} %refs_3_.1) | copy-start | bytes 6291460
  22.0 31.1 %collective-permute-start.4 = (f32[2,264,512]{2,1,0:T(8,128)S(1)}, f32[2,264,512]{2,1,0:T(8,128)S(1)}, u32[]{:S(2)}, u32[]{:S(2)}) collective-permute-start(f32[2,264,512]{2,1,0:T(8,128)S(1)} %shard_map.57.refs_0_), channel_id=1, source_target_pairs={{8,0},{16,8},{24,16},{32,24},{40,32},{48,40},{56,48},{64,56},{72,6... | collective-permute-start | bytes 3244040 | tf_op jit(solution)/shard_map/ppermute | solution.py:30
  24.5 5.4 %collective-permute-start = (f32[2,8,512]{2,1,0:T(8,128)S(1)}, f32[2,8,512]{2,1,0:T(8,128)S(1)}, u32[]{:S(2)}, u32[]{:S(2)}) collective-permute-start(f32[2,8,512]{2,1,0:T(8,128)S(1)} %shard_map.55.refs_0_.refs_1_), channel_id=1, source_target_pairs={{0,1},{1,2},{2,3},{3,4},{4,5},{5,6},{6,7},{8,9},{9,10},{10,11},{11... | collective-permute-start | bytes 98312 | tf_op jit(solution)/shard_map/ppermute | solution.py:30
  31.2 14.9 %collective-permute-start.7 = (f32[2,136,512]{2,1,0:T(8,128)S(1)}, f32[2,136,512]{2,1,0:T(8,128)S(1)}, u32[]{:S(2)}, u32[]{:S(2)}) collective-permute-start(f32[2,136,512]{2,1,0:T(8,128)S(1)} %get-tuple-element.35), channel_id=1, source_target_pairs={{1,0},{2,1},{3,2},{4,3},{5,4},{6,5},{7,6},{9,8},{10,9},{11,10},{12... | collective-permute-start | bytes 1671176 | tf_op jit(solution)/shard_map/ppermute | solution.py:30
  33.2 13.0 %collective-permute-start.6 = (f32[2,128,512]{2,1,0:T(8,128)S(1)}, f32[2,128,512]{2,1,0:T(8,128)S(1)}, u32[]{:S(2)}, u32[]{:S(2)}) collective-permute-start(f32[2,128,512]{2,1,0:T(8,128)S(1)} %get-tuple-element.34), channel_id=1, source_target_pairs={{1,0},{2,1},{3,2},{4,3},{5,4},{6,5},{7,6},{9,8},{10,9},{11,10},{12... | collective-permute-start | bytes 1572872 | tf_op jit(solution)/shard_map/ppermute | solution.py:30
  46.2 7.0 %copy-start = (f32[1,1,1,512,512]{4,3,2,1,0:T(8,128)S(1)}, f32[1,1,1,512,512]{4,3,2,1,0:T(8,128)}, u32[]{:S(2)}) copy-start(f32[1,1,1,512,512]{4,3,2,1,0:T(8,128)} %param.7) | copy-start | bytes 3145732
  56.5 30.9 %collective-permute-start.13 = (f32[2,264,512]{2,1,0:T(8,128)S(1)}, f32[2,264,512]{2,1,0:T(8,128)S(1)}, u32[]{:S(2)}, u32[]{:S(2)}) collective-permute-start(f32[2,264,512]{2,1,0:T(8,128)S(1)} %get-tuple-element.49.refs_6_.refs_4_.refs_15_), channel_id=1, source_target_pairs={{8,16},{24,32},{40,48},{56,64},{72,80},{88,96},{104,112},{16,8},{3... | collective-permute-start | bytes 3244040 | tf_op jit(solution)/shard_map/ppermute | solution.py:35
  63.1 25.0 %collective-permute-start.12 = (f32[2,264,512]{2,1,0:T(8,128)S(1)}, f32[2,264,512]{2,1,0:T(8,128)S(1)}, u32[]{:S(2)}, u32[]{:S(2)}) collective-permute-start(f32[2,264,512]{2,1,0:T(8,128)S(1)} %get-tuple-element.49.refs_6_.refs_4_.refs_15_), channel_id=1, source_target_pairs={{0,8},{16,24},{32,40},{48,56},{64,72},{80,88},{96,104},{112,120},{... | collective-permute-start | bytes 3244040 | tf_op jit(solution)/shard_map/ppermute | solution.py:35
  63.9 14.4 %collective-permute-start.9 = (f32[2,256,512]{2,1,0:T(8,128)S(1)}, f32[2,256,512]{2,1,0:T(8,128)S(1)}, u32[]{:S(2)}, u32[]{:S(2)}) collective-permute-start(f32[2,256,512]{2,1,0:T(8,128)S(1)} %shard_map.61.refs_5_.refs_4_.refs_3_), channel_id=1, source_target_pairs={{1,0},{2,1},{3,2},{4,3},{5,4},{6,5},{7,6},{9,8},{10,9},{11,10},{12... | collective-permute-start | bytes 3145736 | tf_op jit(solution)/shard_map/ppermute | solution.py:30
  66.0 16.1 %collective-permute-start.8 = (f32[2,256,512]{2,1,0:T(8,128)S(1)}, f32[2,256,512]{2,1,0:T(8,128)S(1)}, u32[]{:S(2)}, u32[]{:S(2)}) collective-permute-start(f32[2,256,512]{2,1,0:T(8,128)S(1)} %shard_map.61.refs_5_.refs_4_.refs_3_), channel_id=1, source_target_pairs={{0,1},{1,2},{2,3},{3,4},{4,5},{5,6},{6,7},{8,9},{9,10},{10,11},{11... | collective-permute-start | bytes 3145736 | tf_op jit(solution)/shard_map/ppermute | solution.py:30
  83.4 28.6 %collective-permute-start.11 = (f32[2,264,512]{2,1,0:T(8,128)S(1)}, f32[2,264,512]{2,1,0:T(8,128)S(1)}, u32[]{:S(2)}, u32[]{:S(2)}) collective-permute-start(f32[2,264,512]{2,1,0:T(8,128)S(1)} %get-tuple-element.47), channel_id=1, source_target_pairs={{8,16},{24,32},{40,48},{56,64},{72,80},{88,96},{104,112},{16,8},{3... | collective-permute-start | bytes 3244040 | tf_op jit(solution)/shard_map/ppermute | solution.py:35
  85.3 26.7 %collective-permute-start.10 = (f32[2,264,512]{2,1,0:T(8,128)S(1)}, f32[2,264,512]{2,1,0:T(8,128)S(1)}, u32[]{:S(2)}, u32[]{:S(2)}) collective-permute-start(f32[2,264,512]{2,1,0:T(8,128)S(1)} %get-tuple-element.46.refs_0_), channel_id=1, source_target_pairs={{0,8},{16,24},{32,40},{48,56},{64,72},{80,88},{96,104},{112,120},{... | collective-permute-start | bytes 3244040 | tf_op jit(solution)/shard_map/ppermute | solution.py:35
  89.6 16.1 %collective-permute-start.14 = (f32[2,256,512]{2,1,0:T(8,128)S(1)}, f32[2,256,512]{2,1,0:T(8,128)S(1)}, u32[]{:S(2)}, u32[]{:S(2)}) collective-permute-start(f32[2,256,512]{2,1,0:T(8,128)S(1)} %get-tuple-element.51), channel_id=1, source_target_pairs={{0,1},{1,2},{2,3},{3,4},{4,5},{5,6},{6,7},{8,9},{9,10},{10,11},{11... | collective-permute-start | bytes 3145736 | tf_op jit(solution)/shard_map/ppermute | solution.py:30
  91.5 15.9 %collective-permute-start.15 = (f32[2,256,512]{2,1,0:T(8,128)S(1)}, f32[2,256,512]{2,1,0:T(8,128)S(1)}, u32[]{:S(2)}, u32[]{:S(2)}) collective-permute-start(f32[2,256,512]{2,1,0:T(8,128)S(1)} %get-tuple-element.50.refs_0_), channel_id=1, source_target_pairs={{1,0},{2,1},{3,2},{4,3},{5,4},{6,5},{7,6},{9,8},{10,9},{11,10},{12... | collective-permute-start | bytes 3145736 | tf_op jit(solution)/shard_map/ppermute | solution.py:30
  115.4 30.0 %collective-permute-start.19 = (f32[2,256,512]{2,1,0:T(8,128)S(1)}, f32[2,256,512]{2,1,0:T(8,128)S(1)}, u32[]{:S(2)}, u32[]{:S(2)}) collective-permute-start(f32[2,256,512]{2,1,0:T(8,128)S(1)} %get-tuple-element.57.refs_4_), channel_id=1, source_target_pairs={{0,8},{8,16},{16,24},{24,32},{32,40},{40,48},{48,56},{56,64},{64,7... | collective-permute-start | bytes 3145736 | tf_op jit(solution)/shard_map/ppermute | solution.py:30
  118.2 10.5 %collective-permute-start.16 = (f32[2,128,512]{2,1,0:T(8,128)S(1)}, f32[2,128,512]{2,1,0:T(8,128)S(1)}, u32[]{:S(2)}, u32[]{:S(2)}) collective-permute-start(f32[2,128,512]{2,1,0:T(8,128)S(1)} %get-tuple-element.53.refs_4_), channel_id=1, source_target_pairs={{0,1},{1,2},{2,3},{3,4},{4,5},{5,6},{6,7},{8,9},{9,10},{10,11},{11... | collective-permute-start | bytes 1572872 | tf_op jit(solution)/shard_map/ppermute | solution.py:30
  120.8 13.5 %collective-permute-start.17 = (f32[2,128,512]{2,1,0:T(8,128)S(1)}, f32[2,128,512]{2,1,0:T(8,128)S(1)}, u32[]{:S(2)}, u32[]{:S(2)}) collective-permute-start(f32[2,128,512]{2,1,0:T(8,128)S(1)} %get-tuple-element.54.refs_5_), channel_id=1, source_target_pairs={{0,1},{1,2},{2,3},{3,4},{4,5},{5,6},{6,7},{8,9},{9,10},{10,11},{11... | collective-permute-start | bytes 1572872 | tf_op jit(solution)/shard_map/ppermute | solution.py:30
  134.9 32.7 %collective-permute-start.18 = (f32[2,256,512]{2,1,0:T(8,128)S(1)}, f32[2,256,512]{2,1,0:T(8,128)S(1)}, u32[]{:S(2)}, u32[]{:S(2)}) collective-permute-start(f32[2,256,512]{2,1,0:T(8,128)S(1)} %get-tuple-element.56.refs_0_), channel_id=1, source_target_pairs={{0,8},{8,16},{16,24},{24,32},{32,40},{40,48},{48,56},{56,64},{64,7... | collective-permute-start | bytes 3145736 | tf_op jit(solution)/shard_map/ppermute | solution.py:30
  146.0 10.5 %collective-permute-start.20 = (f32[2,128,512]{2,1,0:T(8,128)S(1)}, f32[2,128,512]{2,1,0:T(8,128)S(1)}, u32[]{:S(2)}, u32[]{:S(2)}) collective-permute-start(f32[2,128,512]{2,1,0:T(8,128)S(1)} %get-tuple-element.59), channel_id=1, source_target_pairs={{0,1},{1,2},{2,3},{3,4},{4,5},{5,6},{6,7},{8,9},{9,10},{10,11},{11... | collective-permute-start | bytes 1572872 | tf_op jit(solution)/shard_map/ppermute | solution.py:30
  147.9 14.2 %collective-permute-start.21 = (f32[2,128,512]{2,1,0:T(8,128)S(1)}, f32[2,128,512]{2,1,0:T(8,128)S(1)}, u32[]{:S(2)}, u32[]{:S(2)}) collective-permute-start(f32[2,128,512]{2,1,0:T(8,128)S(1)} %get-tuple-element.60), channel_id=1, source_target_pairs={{0,1},{1,2},{2,3},{3,4},{4,5},{5,6},{6,7},{8,9},{9,10},{10,11},{11... | collective-permute-start | bytes 1572872 | tf_op jit(solution)/shard_map/ppermute | solution.py:30

commit v9 on v8

--- a/solution.py
+++ b/solution.py
@@ -516,12 +516,12 @@
     )
     tail_left = each(tail_total, "col", 1)
     tail_down, tail_base = call(
-        functools.partial(final_kernel, h, False), [half, half], (me, left_of, tail, tail_total, tail_left)
+        functools.partial(final_kernel, h, False), [block(h + PAD), half], (me, left_of, tail, tail_total, tail_left)
     )
     tail_got = shifted(tail_down, "row", 1)
     head_right, head_base = call(
         functools.partial(final_kernel, 0, True),
-        [pieces, half],
+        [[half], half],
         (me, above, head, head_total, head_above),
         after=(tail_down,),
     )

time: 169 us -> 170 us (level)
  waiting for transfers between devices: 79.4 us -> 82.3 us
  starting transfers between devices: 57.7 us -> 55.5 us
    ppermute x18 -> x17, waiting for transfers between devices: 75.8 us -> 78.6 us  [shifted(): lax.ppermute(value, axis, [(source, source + steps) for source in range(l...]
    ppermute x18 -> x17, starting transfers between devices: 47.1 us -> 44.9 us  [shifted(): lax.ppermute(value, axis, [(source, source + steps) for source in range(l...]
  transfers between devices with their start and end apart: 22 -> 21, of which waited for: 17 -> 16; matrix products, arithmetic and copies ran while one was open for 3% -> 3% of each run, Pallas kernels for 10% -> 10%
where the time goes in v9:
time: 170 us
  waiting for transfers between devices  82.3 us (48%)
  starting transfers between devices  55.5 us (33%)
  Pallas kernels  24.7 us (15%)
  other arithmetic  4.39 us (3%)
    ppermute x17, waiting for transfers between devices, shifted(): lax.ppermute(value, axis, [(source, source + steps) for source in range(l...  78.6 us
    ppermute x17, starting transfers between devices, shifted(): lax.ppermute(value, axis, [(source, source + steps) for source in range(l...  44.9 us
    pallas_call x16, Pallas kernels, call(): pl.pallas_call(body, out_shape=out_flat, in_specs=[ANY] * skip + [SMEM] *...  22.6 us
    ppermute x4, starting transfers between devices, swapped(): lax.ppermute(value, axis, [(a, a + 1) for a in lower] + [(a + 1, a) for a...  10.6 us
    convert_element_type x1, other arithmetic, dft_tables(): (jnp.sin(angle) * scale).astype(jnp.bfloat16)  4.39 us
    ppermute x4, waiting for transfers between devices, swapped(): lax.ppermute(value, axis, [(a, a + 1) for a in lower] + [(a + 1, a) for a...  3.67 us
  transfers between devices with their start and end apart: 21, of which 16 were waited for; matrix products, arithmetic and copies ran while one was open for 3% of the time, Pallas kernels for 10%

profile of v9, /device:TPU:28, one launch (start us, length us, event | category | flops | bytes accessed | tf_op | source)
XLA Modules:
  0.0 169.5 jit_solution(16219402790364288849)
XLA Ops:
  0.0 1.4 slice.11.refs_3_.refs_1_
  1.4 6.1 %collective-permute-start.5 = (f32[2,256,512]{2,1,0:T(8,128)S(1)}, f32[2,256,512]{2,1,0:T(8,128)S(1)}, u32[]{:S(2)}, u32[]{:S(2)}) collective-permute-start(f32[2,256,512]{2,1,0:T(8,128)S(1)} %slice.11.refs_3_.refs_1_), channel_id=1, source_target_pairs={{8,0},{16,8},{24,16},{32,24},{40,32},{48,40},{56,48},{64,56},{72,6... | collective-permute-start | bytes 3145736 | tf_op jit(solution)/shard_map/ppermute | solution.py:30
  7.7 1.9 %collective-permute-start.2 = (f32[2,128,512]{2,1,0:T(8,128)S(1)}, f32[2,128,512]{2,1,0:T(8,128)S(1)}, u32[]{:S(2)}, u32[]{:S(2)}) collective-permute-start(f32[2,128,512]{2,1,0:T(8,128)S(1)} %get-tuple-element.59.refs_3_), channel_id=1, source_target_pairs={{1,0},{2,1},{3,2},{4,3},{5,4},{6,5},{7,6},{9,8},{10,9},{11,10},{12... | collective-permute-start | bytes 1572872 | tf_op jit(solution)/shard_map/ppermute | solution.py:30
  9.6 2.5 %collective-permute-start.1 = (f32[2,128,512]{2,1,0:T(8,128)S(1)}, f32[2,128,512]{2,1,0:T(8,128)S(1)}, u32[]{:S(2)}, u32[]{:S(2)}) collective-permute-start(f32[2,128,512]{2,1,0:T(8,128)S(1)} %get-tuple-element.60.refs_2_), channel_id=1, source_target_pairs={{1,0},{2,1},{3,2},{4,3},{5,4},{6,5},{7,6},{9,8},{10,9},{11,10},{12... | collective-permute-start | bytes 1572872 | tf_op jit(solution)/shard_map/ppermute | solution.py:30
  12.7 1.9 %collective-permute-start.3 = (f32[2,8,512]{2,1,0:T(8,128)S(1)}, f32[2,8,512]{2,1,0:T(8,128)S(1)}, u32[]{:S(2)}, u32[]{:S(2)}) collective-permute-start(f32[2,8,512]{2,1,0:T(8,128)S(1)} %shard_map.55.refs_0_.refs_1_), channel_id=1, source_target_pairs={{0,8},{8,16},{16,24},{24,32},{32,40},{40,48},{48,56},{56,64},{64,7... | collective-permute-start | bytes 98312 | tf_op jit(solution)/shard_map/ppermute | solution.py:30
  14.7 6.0 %collective-permute-done.3.refs_1_.refs_3_.refs_2_ = f32[2,8,512]{2,1,0:T(8,128)S(1)} collective-permute-done((f32[2,8,512]{2,1,0:T(8,128)S(1)}, f32[2,8,512]{2,1,0:T(8,128)S(1)}, u32[]{:S(2)}, u32[]{:S(2)}) %collective-permute-start.3) | collective-permute-done | bytes 32800 | tf_op jit(solution)/shard_map/ppermute | solution.py:30
  20.6 1.2 collective-permute-done.1.refs_4_
  22.0 2.4 %collective-permute-start.4 = (f32[2,264,512]{2,1,0:T(8,128)S(1)}, f32[2,264,512]{2,1,0:T(8,128)S(1)}, u32[]{:S(2)}, u32[]{:S(2)}) collective-permute-start(f32[2,264,512]{2,1,0:T(8,128)S(1)} %shard_map.57.refs_0_), channel_id=1, source_target_pairs={{8,0},{16,8},{24,16},{32,24},{40,32},{48,40},{56,48},{64,56},{72,6... | collective-permute-start | bytes 3244040 | tf_op jit(solution)/shard_map/ppermute | solution.py:30
  24.5 3.4 %collective-permute-start = (f32[2,8,512]{2,1,0:T(8,128)S(1)}, f32[2,8,512]{2,1,0:T(8,128)S(1)}, u32[]{:S(2)}, u32[]{:S(2)}) collective-permute-start(f32[2,8,512]{2,1,0:T(8,128)S(1)} %shard_map.55.refs_0_.refs_1_), channel_id=1, source_target_pairs={{0,1},{1,2},{2,3},{3,4},{4,5},{5,6},{6,7},{8,9},{9,10},{10,11},{11... | collective-permute-start | bytes 98312 | tf_op jit(solution)/shard_map/ppermute | solution.py:30
  27.9 2.0 %collective-permute-done.refs_2_.refs_1_.refs_4_ = f32[2,8,512]{2,1,0:T(8,128)S(1)} collective-permute-done((f32[2,8,512]{2,1,0:T(8,128)S(1)}, f32[2,8,512]{2,1,0:T(8,128)S(1)}, u32[]{:S(2)}, u32[]{:S(2)}) %collective-permute-start) | collective-permute-done | bytes 32800 | tf_op jit(solution)/shard_map/ppermute | solution.py:30
  29.9 1.2 collective-permute-done.5.refs_4_.refs_2_
  31.2 1.9 %collective-permute-start.7 = (f32[2,136,512]{2,1,0:T(8,128)S(1)}, f32[2,136,512]{2,1,0:T(8,128)S(1)}, u32[]{:S(2)}, u32[]{:S(2)}) collective-permute-start(f32[2,136,512]{2,1,0:T(8,128)S(1)} %get-tuple-element.34), channel_id=1, source_target_pairs={{1,0},{2,1},{3,2},{4,3},{5,4},{6,5},{7,6},{9,8},{10,9},{11,10},{12... | collective-permute-start | bytes 1671176 | tf_op jit(solution)/shard_map/ppermute | solution.py:30
  33.2 2.5 %collective-permute-start.6 = (f32[2,128,512]{2,1,0:T(8,128)S(1)}, f32[2,128,512]{2,1,0:T(8,128)S(1)}, u32[]{:S(2)}, u32[]{:S(2)}) collective-permute-start(f32[2,128,512]{2,1,0:T(8,128)S(1)} %get-tuple-element.33), channel_id=1, source_target_pairs={{1,0},{2,1},{3,2},{4,3},{5,4},{6,5},{7,6},{9,8},{10,9},{11,10},{12... | collective-permute-start | bytes 1572872 | tf_op jit(solution)/shard_map/ppermute | solution.py:30
  36.4 4.4 %multiply_convert_fusion = (bf16[512,512]{1,0:T(8,128)(2,1)S(1)}, bf16[512,512]{1,0:T(8,128)(2,1)S(1)}) fusion(), kind=kLoop, calls=%fused_computation.6 | loop fusion | flops 4718592 | bytes 1048576 | tf_op jit(solution)/shard_map/convert_element_type | solution.py:45
  40.8 5.4 %shard_map.56 = (bf16[1024,1024]{1,0:T(8,128)(2,1)S(1)}, bf16[1024,1024]{1,0:T(8,128)(2,1)S(1)}, bf16[1024,1024]{1,0:T(8,128)(2,1)S(1)}, bf16[1024,512]{1,0:T(8,...) custom-call(s32[1,2]{1,0:T(1,128)S(1)} %bitcast.5, ...), custom_call_target="tpu_custom_call" | custom-call | tf_op jit(solution)/shard_map/pallas_call | solution.py:61
  46.2 1.5 shard_map.59
  47.7 5.4 %collective-permute-done.4.refs_6_ = f32[2,264,512]{2,1,0:T(8,128)S(1)} collective-permute-done((f32[2,264,512]{2,1,0:T(8,128)S(1)}, f32[2,264,512]{2,1,0:T(8,128)S(1)}, u32[]{:S(2)}, u32[]{:S(2)}) %collective-permute-start.4) | collective-permute-done | bytes 1081376 | tf_op jit(solution)/shard_map/ppermute | solution.py:30
  53.2 3.4 %shard_map.60 = (f32[2,256,512]{2,1,0:T(8,128)S(1)}, f32[2,8,512]{2,1,0:T(8,128)S(1)}, bf16[1024,512]{1,0:T(8,128)(2,1)S(1)}, f32[2,264,512]{2,1,0:T(8,128)S(1)}) custom-call(s32[1,1]{1,0:T(1,128)S(6)} %copy.8.refs_0_, f32[2,8,512]{2,1,0:T(8,128)S(1)} %shard_map.55.refs_0_.refs_1_, f32[2,128,512]{2,1,0:T(8,128)S(1)} %get-tuple-element.60.refs_2_, ...), custom_call_target="tpu_custom_call" | custom-call | tf_op jit(solution)/shard_map/pallas_call | solution.py:61
  56.5 6.5 %collective-permute-start.13 = (f32[2,264,512]{2,1,0:T(8,128)S(1)}, f32[2,264,512]{2,1,0:T(8,128)S(1)}, u32[]{:S(2)}, u32[]{:S(2)}) collective-permute-start(f32[2,264,512]{2,1,0:T(8,128)S(1)} %get-tuple-element.48.refs_6_.refs_4_.refs_15_), channel_id=1, source_target_pairs={{8,16},{24,32},{40,48},{56,64},{72,80},{88,96},{104,112},{16,8},{3... | collective-permute-start | bytes 3244040 | tf_op jit(solution)/shard_map/ppermute | solution.py:35
  63.1 0.8 shard_map.61.refs_5_.refs_4_.refs_3_
  63.9 2.1 %collective-permute-start.9 = (f32[2,256,512]{2,1,0:T(8,128)S(1)}, f32[2,256,512]{2,1,0:T(8,128)S(1)}, u32[]{:S(2)}, u32[]{:S(2)}) collective-permute-start(f32[2,256,512]{2,1,0:T(8,128)S(1)} %shard_map.61.refs_5_.refs_4_.refs_3_), channel_id=1, source_target_pairs={{1,0},{2,1},{3,2},{4,3},{5,4},{6,5},{7,6},{9,8},{10,9},{11,10},{12... | collective-permute-start | bytes 3145736 | tf_op jit(solution)/shard_map/ppermute | solution.py:30
  66.0 2.2 %collective-permute-start.8 = (f32[2,256,512]{2,1,0:T(8,128)S(1)}, f32[2,256,512]{2,1,0:T(8,128)S(1)}, u32[]{:S(2)}, u32[]{:S(2)}) collective-permute-start(f32[2,256,512]{2,1,0:T(8,128)S(1)} %shard_map.61.refs_5_.refs_4_.refs_3_), channel_id=1, source_target_pairs={{0,1},{1,2},{2,3},{3,4},{4,5},{5,6},{6,7},{8,9},{9,10},{10,11},{11... | collective-permute-start | bytes 3145736 | tf_op jit(solution)/shard_map/ppermute | solution.py:30
  68.3 10.1 %collective-permute-done.9.refs_7_.refs_6_ = f32[2,256,512]{2,1,0:T(8,128)S(1)} collective-permute-done((f32[2,256,512]{2,1,0:T(8,128)S(1)}, f32[2,256,512]{2,1,0:T(8,128)S(1)}, u32[]{:S(2)}, u32[]{:S(2)}) %collective-permute-start.9) | collective-permute-done | bytes 1048608 | tf_op jit(solution)/shard_map/ppermute | solution.py:30
  78.3 3.8 %collective-permute-done.8.refs_6_.refs_5_ = f32[2,256,512]{2,1,0:T(8,128)S(1)} collective-permute-done((f32[2,256,512]{2,1,0:T(8,128)S(1)}, f32[2,256,512]{2,1,0:T(8,128)S(1)}, u32[]{:S(2)}, u32[]{:S(2)}) %collective-permute-start.8) | collective-permute-done | bytes 1048608 | tf_op jit(solution)/shard_map/ppermute | solution.py:30
  82.1 1.2 shard_map.62
  83.4 1.9 %collective-permute-start.11 = (f32[2,264,512]{2,1,0:T(8,128)S(1)}, f32[2,264,512]{2,1,0:T(8,128)S(1)}, u32[]{:S(2)}, u32[]{:S(2)}) collective-permute-start(f32[2,264,512]{2,1,0:T(8,128)S(1)} %get-tuple-element.46), channel_id=1, source_target_pairs={{8,16},{24,32},{40,48},{56,64},{72,80},{88,96},{104,112},{16,8},{3... | collective-permute-start | bytes 3244040 | tf_op jit(solution)/shard_map/ppermute | solution.py:35
  85.3 2.1 %collective-permute-start.10 = (f32[2,264,512]{2,1,0:T(8,128)S(1)}, f32[2,264,512]{2,1,0:T(8,128)S(1)}, u32[]{:S(2)}, u32[]{:S(2)}) collective-permute-start(f32[2,264,512]{2,1,0:T(8,128)S(1)} %get-tuple-element.45.refs_0_), channel_id=1, source_target_pairs={{0,8},{16,24},{32,40},{48,56},{64,72},{80,88},{96,104},{112,120},{... | collective-permute-start | bytes 3244040 | tf_op jit(solution)/shard_map/ppermute | solution.py:35
  88.0 1.5 shard_map.64
  89.6 1.9 %collective-permute-start.14 = (f32[2,256,512]{2,1,0:T(8,128)S(1)}, f32[2,256,512]{2,1,0:T(8,128)S(1)}, u32[]{:S(2)}, u32[]{:S(2)}) collective-permute-start(f32[2,256,512]{2,1,0:T(8,128)S(1)} %get-tuple-element.50), channel_id=1, source_target_pairs={{0,1},{1,2},{2,3},{3,4},{4,5},{5,6},{6,7},{8,9},{9,10},{10,11},{11... | collective-permute-start | bytes 3145736 | tf_op jit(solution)/shard_map/ppermute | solution.py:30
  91.5 3.9 %collective-permute-start.15 = (f32[2,256,512]{2,1,0:T(8,128)S(1)}, f32[2,256,512]{2,1,0:T(8,128)S(1)}, u32[]{:S(2)}, u32[]{:S(2)}) collective-permute-start(f32[2,256,512]{2,1,0:T(8,128)S(1)} %get-tuple-element.49.refs_0_), channel_id=1, source_target_pairs={{1,0},{2,1},{3,2},{4,3},{5,4},{6,5},{7,6},{9,8},{10,9},{11,10},{12... | collective-permute-start | bytes 3145736 | tf_op jit(solution)/shard_map/ppermute | solution.py:30
  96.5 9.2 %collective-permute-done.14.refs_5_ = f32[2,256,512]{2,1,0:T(8,128)S(1)} collective-permute-done((f32[2,256,512]{2,1,0:T(8,128)S(1)}, f32[2,256,512]{2,1,0:T(8,128)S(1)}, u32[]{:S(2)}, u32[]{:S(2)}) %collective-permute-start.14) | collective-permute-done | bytes 1048608 | tf_op jit(solution)/shard_map/ppermute | solution.py:30
  105.7 1.8 %collective-permute-done.15.refs_6_ = f32[2,256,512]{2,1,0:T(8,128)S(1)} collective-permute-done((f32[2,256,512]{2,1,0:T(8,128)S(1)}, f32[2,256,512]{2,1,0:T(8,128)S(1)}, u32[]{:S(2)}, u32[]{:S(2)}) %collective-permute-start.15) | collective-permute-done | bytes 1048608 | tf_op jit(solution)/shard_map/ppermute | solution.py:30
  107.4 1.5 shard_map.66.refs_8_
  108.9 3.0 %collective-permute-done.11.refs_7_ = f32[2,264,512]{2,1,0:T(8,128)S(1)} collective-permute-done((f32[2,264,512]{2,1,0:T(8,128)S(1)}, f32[2,264,512]{2,1,0:T(8,128)S(1)}, u32[]{:S(2)}, u32[]{:S(2)}) %collective-permute-start.11) | collective-permute-done | bytes 1081376 | tf_op jit(solution)/shard_map/ppermute | solution.py:35
  112.0 3.5 %shard_map.67 = (bf16[1024,512]{1,0:T(8,128)(2,1)S(1)}, f32[2,256,512]{2,1,0:T(8,128)S(1)}) custom-call(s32[1,1]{1,0:T(1,128)S(6)} %copy.8.refs_0_, f32[2,8,512]{2,1,0:T(8,128)S(1)} %shard_map.55.refs_0_.refs_1_, f32[2,8,512]{2,1,0:T(8,128)S(1)} %get-tuple-element.41.refs_4_.refs_3_.refs_1_.refs_2_, ...), custom_call_target="tpu_custom_call" | custom-call | tf_op jit(solution)/shard_map/pallas_call | solution.py:61
  115.4 1.9 %collective-permute-start.19 = (f32[2,256,512]{2,1,0:T(8,128)S(1)}, f32[2,256,512]{2,1,0:T(8,128)S(1)}, u32[]{:S(2)}, u32[]{:S(2)}) collective-permute-start(f32[2,256,512]{2,1,0:T(8,128)S(1)} %get-tuple-element.56.refs_4_), channel_id=1, source_target_pairs={{0,8},{8,16},{16,24},{24,32},{32,40},{40,48},{48,56},{56,64},{64,7... | collective-permute-start | bytes 3145736 | tf_op jit(solution)/shard_map/ppermute | solution.py:30
  117.4 0.8 shard_map.68
  118.2 2.6 %collective-permute-start.16 = (f32[2,128,512]{2,1,0:T(8,128)S(1)}, f32[2,128,512]{2,1,0:T(8,128)S(1)}, u32[]{:S(2)}, u32[]{:S(2)}) collective-permute-start(f32[2,128,512]{2,1,0:T(8,128)S(1)} %get-tuple-element.52.refs_4_), channel_id=1, source_target_pairs={{0,1},{1,2},{2,3},{3,4},{4,5},{5,6},{6,7},{8,9},{9,10},{10,11},{11... | collective-permute-start | bytes 1572872 | tf_op jit(solution)/shard_map/ppermute | solution.py:30
  120.8 1.9 %collective-permute-start.17 = (f32[2,128,512]{2,1,0:T(8,128)S(1)}, f32[2,128,512]{2,1,0:T(8,128)S(1)}, u32[]{:S(2)}, u32[]{:S(2)}) collective-permute-start(f32[2,128,512]{2,1,0:T(8,128)S(1)} %get-tuple-element.53.refs_5_), channel_id=1, source_target_pairs={{0,1},{1,2},{2,3},{3,4},{4,5},{5,6},{6,7},{8,9},{9,10},{10,11},{11... | collective-permute-start | bytes 1572872 | tf_op jit(solution)/shard_map/ppermute | solution.py:30
  122.7 6.0 %collective-permute-done.16.refs_6_ = f32[2,128,512]{2,1,0:T(8,128)S(1)} collective-permute-done((f32[2,128,512]{2,1,0:T(8,128)S(1)}, f32[2,128,512]{2,1,0:T(8,128)S(1)}, u32[]{:S(2)}, u32[]{:S(2)}) %collective-permute-start.16) | collective-permute-done | bytes 524320 | tf_op jit(solution)/shard_map/ppermute | solution.py:30
  128.7 5.6 %collective-permute-done.17.refs_7_ = f32[2,128,512]{2,1,0:T(8,128)S(1)} collective-permute-done((f32[2,128,512]{2,1,0:T(8,128)S(1)}, f32[2,128,512]{2,1,0:T(8,128)S(1)}, u32[]{:S(2)}, u32[]{:S(2)}) %collective-permute-start.17) | collective-permute-done | bytes 524320 | tf_op jit(solution)/shard_map/ppermute | solution.py:30
  134.9 3.6 %collective-permute-start.18 = (f32[2,264,512]{2,1,0:T(8,128)S(1)}, f32[2,264,512]{2,1,0:T(8,128)S(1)}, u32[]{:S(2)}, u32[]{:S(2)}) collective-permute-start(f32[2,264,512]{2,1,0:T(8,128)S(1)} %get-tuple-element.55.refs_0_), channel_id=1, source_target_pairs={{0,8},{8,16},{16,24},{24,32},{32,40},{40,48},{48,56},{56,64},{64,7... | collective-permute-start | bytes 3244040 | tf_op jit(solution)/shard_map/ppermute | solution.py:30
  138.6 6.9 %collective-permute-done.19.refs_5_ = f32[2,256,512]{2,1,0:T(8,128)S(1)} collective-permute-done((f32[2,256,512]{2,1,0:T(8,128)S(1)}, f32[2,256,512]{2,1,0:T(8,128)S(1)}, u32[]{:S(2)}, u32[]{:S(2)}) %collective-permute-start.19) | collective-permute-done | bytes 1048608 | tf_op jit(solution)/shard_map/ppermute | solution.py:30
  146.0 1.9 %collective-permute-start.20 = (f32[2,256,512]{2,1,0:T(8,128)S(1)}, f32[2,256,512]{2,1,0:T(8,128)S(1)}, u32[]{:S(2)}, u32[]{:S(2)}) collective-permute-start(f32[2,256,512]{2,1,0:T(8,128)S(1)} %get-tuple-element.58), channel_id=1, source_target_pairs={{0,1},{1,2},{2,3},{3,4},{4,5},{5,6},{6,7},{8,9},{9,10},{10,11},{11... | collective-permute-start | bytes 3145736 | tf_op jit(solution)/shard_map/ppermute | solution.py:30
  147.9 14.2 %collective-permute-done.20.refs_0_ = f32[2,256,512]{2,1,0:T(8,128)S(1)} collective-permute-done((f32[2,256,512]{2,1,0:T(8,128)S(1)}, f32[2,256,512]{2,1,0:T(8,128)S(1)}, u32[]{:S(2)}, u32[]{:S(2)}) %collective-permute-start.20) | collective-permute-done | bytes 1048608 | tf_op jit(solution)/shard_map/ppermute | solution.py:30
  162.1 1.0 shard_map.71.refs_1_
  163.1 5.2 %collective-permute-done.18.refs_0_ = f32[2,264,512]{2,1,0:T(8,128)S(1)} collective-permute-done((f32[2,264,512]{2,1,0:T(8,128)S(1)}, f32[2,264,512]{2,1,0:T(8,128)S(1)}, u32[]{:S(2)}, u32[]{:S(2)}) %collective-permute-start.18) | collective-permute-done | bytes 1081376 | tf_op jit(solution)/shard_map/ppermute | solution.py:30
  168.3 1.0 shard_map.72
  (23 shorter events, 3.8 us)
Async XLA Ops:
  0.0 7.6 %copy-start.3 = (f32[2,512,512]{2,1,0:T(8,128)S(1)}, f32[2,512,512]{2,1,0:T(8,128)}, u32[]{:S(2)}) copy-start(f32[2,512,512]{2,1,0:T(8,128)} %param.5) | copy-start | bytes 6291460
  0.0 12.2 %copy-start.2 = (s32[1,1,1,2]{3,2,1,0:T(1,128)S(1)}, s32[1,1,1,2]{3,2,1,0:T(1,128)}, u32[]{:S(2)}) copy-start(s32[1,1,1,2]{3,2,1,0:T(1,128)} %param.8) | copy-start | bytes 28
  1.4 29.7 %collective-permute-start.5 = (f32[2,256,512]{2,1,0:T(8,128)S(1)}, f32[2,256,512]{2,1,0:T(8,128)S(1)}, u32[]{:S(2)}, u32[]{:S(2)}) collective-permute-start(f32[2,256,512]{2,1,0:T(8,128)S(1)} %slice.11.refs_3_.refs_1_), channel_id=1, source_target_pairs={{8,0},{16,8},{24,16},{32,24},{40,32},{48,40},{56,48},{64,56},{72,6... | collective-permute-start | bytes 3145736 | tf_op jit(solution)/shard_map/ppermute | solution.py:30
  7.7 13.0 %collective-permute-start.2 = (f32[2,128,512]{2,1,0:T(8,128)S(1)}, f32[2,128,512]{2,1,0:T(8,128)S(1)}, u32[]{:S(2)}, u32[]{:S(2)}) collective-permute-start(f32[2,128,512]{2,1,0:T(8,128)S(1)} %get-tuple-element.59.refs_3_), channel_id=1, source_target_pairs={{1,0},{2,1},{3,2},{4,3},{5,4},{6,5},{7,6},{9,8},{10,9},{11,10},{12... | collective-permute-start | bytes 1572872 | tf_op jit(solution)/shard_map/ppermute | solution.py:30
  9.6 12.3 %collective-permute-start.1 = (f32[2,128,512]{2,1,0:T(8,128)S(1)}, f32[2,128,512]{2,1,0:T(8,128)S(1)}, u32[]{:S(2)}, u32[]{:S(2)}) collective-permute-start(f32[2,128,512]{2,1,0:T(8,128)S(1)} %get-tuple-element.60.refs_2_), channel_id=1, source_target_pairs={{1,0},{2,1},{3,2},{4,3},{5,4},{6,5},{7,6},{9,8},{10,9},{11,10},{12... | collective-permute-start | bytes 1572872 | tf_op jit(solution)/shard_map/ppermute | solution.py:30
  12.7 7.9 %collective-permute-start.3 = (f32[2,8,512]{2,1,0:T(8,128)S(1)}, f32[2,8,512]{2,1,0:T(8,128)S(1)}, u32[]{:S(2)}, u32[]{:S(2)}) collective-permute-start(f32[2,8,512]{2,1,0:T(8,128)S(1)} %shard_map.55.refs_0_.refs_1_), channel_id=1, source_target_pairs={{0,8},{8,16},{16,24},{24,32},{32,40},{40,48},{48,56},{56,64},{64,7... | collective-permute-start | bytes 98312 | tf_op jit(solution)/shard_map/ppermute | solution.py:30
  22.0 18.8 %copy-start.1 = (f32[2,512,512]{2,1,0:T(8,128)S(1)}, f32[2,512,512]{2,1,0:T(8,128)}, u32[]{:S(2)}) copy-start(f32[2,512,512]{2,1,0:T(8,128)} %refs_3_.1) | copy-start | bytes 6291460
  22.0 31.1 %collective-permute-start.4 = (f32[2,264,512]{2,1,0:T(8,128)S(1)}, f32[2,264,512]{2,1,0:T(8,128)S(1)}, u32[]{:S(2)}, u32[]{:S(2)}) collective-permute-start(f32[2,264,512]{2,1,0:T(8,128)S(1)} %shard_map.57.refs_0_), channel_id=1, source_target_pairs={{8,0},{16,8},{24,16},{32,24},{40,32},{48,40},{56,48},{64,56},{72,6... | collective-permute-start | bytes 3244040 | tf_op jit(solution)/shard_map/ppermute | solution.py:30
  24.5 5.4 %collective-permute-start = (f32[2,8,512]{2,1,0:T(8,128)S(1)}, f32[2,8,512]{2,1,0:T(8,128)S(1)}, u32[]{:S(2)}, u32[]{:S(2)}) collective-permute-start(f32[2,8,512]{2,1,0:T(8,128)S(1)} %shard_map.55.refs_0_.refs_1_), channel_id=1, source_target_pairs={{0,1},{1,2},{2,3},{3,4},{4,5},{5,6},{6,7},{8,9},{9,10},{10,11},{11... | collective-permute-start | bytes 98312 | tf_op jit(solution)/shard_map/ppermute | solution.py:30
  31.2 14.9 %collective-permute-start.7 = (f32[2,136,512]{2,1,0:T(8,128)S(1)}, f32[2,136,512]{2,1,0:T(8,128)S(1)}, u32[]{:S(2)}, u32[]{:S(2)}) collective-permute-start(f32[2,136,512]{2,1,0:T(8,128)S(1)} %get-tuple-element.34), channel_id=1, source_target_pairs={{1,0},{2,1},{3,2},{4,3},{5,4},{6,5},{7,6},{9,8},{10,9},{11,10},{12... | collective-permute-start | bytes 1671176 | tf_op jit(solution)/shard_map/ppermute | solution.py:30
  33.2 13.0 %collective-permute-start.6 = (f32[2,128,512]{2,1,0:T(8,128)S(1)}, f32[2,128,512]{2,1,0:T(8,128)S(1)}, u32[]{:S(2)}, u32[]{:S(2)}) collective-permute-start(f32[2,128,512]{2,1,0:T(8,128)S(1)} %get-tuple-element.33), channel_id=1, source_target_pairs={{1,0},{2,1},{3,2},{4,3},{5,4},{6,5},{7,6},{9,8},{10,9},{11,10},{12... | collective-permute-start | bytes 1572872 | tf_op jit(solution)/shard_map/ppermute | solution.py:30
  46.2 7.0 %copy-start = (f32[1,1,1,512,512]{4,3,2,1,0:T(8,128)S(1)}, f32[1,1,1,512,512]{4,3,2,1,0:T(8,128)}, u32[]{:S(2)}) copy-start(f32[1,1,1,512,512]{4,3,2,1,0:T(8,128)} %param.7) | copy-start | bytes 3145732
  56.5 30.9 %collective-permute-start.13 = (f32[2,264,512]{2,1,0:T(8,128)S(1)}, f32[2,264,512]{2,1,0:T(8,128)S(1)}, u32[]{:S(2)}, u32[]{:S(2)}) collective-permute-start(f32[2,264,512]{2,1,0:T(8,128)S(1)} %get-tuple-element.48.refs_6_.refs_4_.refs_15_), channel_id=1, source_target_pairs={{8,16},{24,32},{40,48},{56,64},{72,80},{88,96},{104,112},{16,8},{3... | collective-permute-start | bytes 3244040 | tf_op jit(solution)/shard_map/ppermute | solution.py:35
  63.1 25.0 %collective-permute-start.12 = (f32[2,264,512]{2,1,0:T(8,128)S(1)}, f32[2,264,512]{2,1,0:T(8,128)S(1)}, u32[]{:S(2)}, u32[]{:S(2)}) collective-permute-start(f32[2,264,512]{2,1,0:T(8,128)S(1)} %get-tuple-element.48.refs_6_.refs_4_.refs_15_), channel_id=1, source_target_pairs={{0,8},{16,24},{32,40},{48,56},{64,72},{80,88},{96,104},{112,120},{... | collective-permute-start | bytes 3244040 | tf_op jit(solution)/shard_map/ppermute | solution.py:35
  63.9 14.4 %collective-permute-start.9 = (f32[2,256,512]{2,1,0:T(8,128)S(1)}, f32[2,256,512]{2,1,0:T(8,128)S(1)}, u32[]{:S(2)}, u32[]{:S(2)}) collective-permute-start(f32[2,256,512]{2,1,0:T(8,128)S(1)} %shard_map.61.refs_5_.refs_4_.refs_3_), channel_id=1, source_target_pairs={{1,0},{2,1},{3,2},{4,3},{5,4},{6,5},{7,6},{9,8},{10,9},{11,10},{12... | collective-permute-start | bytes 3145736 | tf_op jit(solution)/shard_map/ppermute | solution.py:30
  66.0 16.1 %collective-permute-start.8 = (f32[2,256,512]{2,1,0:T(8,128)S(1)}, f32[2,256,512]{2,1,0:T(8,128)S(1)}, u32[]{:S(2)}, u32[]{:S(2)}) collective-permute-start(f32[2,256,512]{2,1,0:T(8,128)S(1)} %shard_map.61.refs_5_.refs_4_.refs_3_), channel_id=1, source_target_pairs={{0,1},{1,2},{2,3},{3,4},{4,5},{5,6},{6,7},{8,9},{9,10},{10,11},{11... | collective-permute-start | bytes 3145736 | tf_op jit(solution)/shard_map/ppermute | solution.py:30
  83.4 28.6 %collective-permute-start.11 = (f32[2,264,512]{2,1,0:T(8,128)S(1)}, f32[2,264,512]{2,1,0:T(8,128)S(1)}, u32[]{:S(2)}, u32[]{:S(2)}) collective-permute-start(f32[2,264,512]{2,1,0:T(8,128)S(1)} %get-tuple-element.46), channel_id=1, source_target_pairs={{8,16},{24,32},{40,48},{56,64},{72,80},{88,96},{104,112},{16,8},{3... | collective-permute-start | bytes 3244040 | tf_op jit(solution)/shard_map/ppermute | solution.py:35
  85.3 26.7 %collective-permute-start.10 = (f32[2,264,512]{2,1,0:T(8,128)S(1)}, f32[2,264,512]{2,1,0:T(8,128)S(1)}, u32[]{:S(2)}, u32[]{:S(2)}) collective-permute-start(f32[2,264,512]{2,1,0:T(8,128)S(1)} %get-tuple-element.45.refs_0_), channel_id=1, source_target_pairs={{0,8},{16,24},{32,40},{48,56},{64,72},{80,88},{96,104},{112,120},{... | collective-permute-start | bytes 3244040 | tf_op jit(solution)/shard_map/ppermute | solution.py:35
  89.6 16.1 %collective-permute-start.14 = (f32[2,256,512]{2,1,0:T(8,128)S(1)}, f32[2,256,512]{2,1,0:T(8,128)S(1)}, u32[]{:S(2)}, u32[]{:S(2)}) collective-permute-start(f32[2,256,512]{2,1,0:T(8,128)S(1)} %get-tuple-element.50), channel_id=1, source_target_pairs={{0,1},{1,2},{2,3},{3,4},{4,5},{5,6},{6,7},{8,9},{9,10},{10,11},{11... | collective-permute-start | bytes 3145736 | tf_op jit(solution)/shard_map/ppermute | solution.py:30
  91.5 15.9 %collective-permute-start.15 = (f32[2,256,512]{2,1,0:T(8,128)S(1)}, f32[2,256,512]{2,1,0:T(8,128)S(1)}, u32[]{:S(2)}, u32[]{:S(2)}) collective-permute-start(f32[2,256,512]{2,1,0:T(8,128)S(1)} %get-tuple-element.49.refs_0_), channel_id=1, source_target_pairs={{1,0},{2,1},{3,2},{4,3},{5,4},{6,5},{7,6},{9,8},{10,9},{11,10},{12... | collective-permute-start | bytes 3145736 | tf_op jit(solution)/shard_map/ppermute | solution.py:30
  115.4 30.0 %collective-permute-start.19 = (f32[2,256,512]{2,1,0:T(8,128)S(1)}, f32[2,256,512]{2,1,0:T(8,128)S(1)}, u32[]{:S(2)}, u32[]{:S(2)}) collective-permute-start(f32[2,256,512]{2,1,0:T(8,128)S(1)} %get-tuple-element.56.refs_4_), channel_id=1, source_target_pairs={{0,8},{8,16},{16,24},{24,32},{32,40},{40,48},{48,56},{56,64},{64,7... | collective-permute-start | bytes 3145736 | tf_op jit(solution)/shard_map/ppermute | solution.py:30
  118.2 10.5 %collective-permute-start.16 = (f32[2,128,512]{2,1,0:T(8,128)S(1)}, f32[2,128,512]{2,1,0:T(8,128)S(1)}, u32[]{:S(2)}, u32[]{:S(2)}) collective-permute-start(f32[2,128,512]{2,1,0:T(8,128)S(1)} %get-tuple-element.52.refs_4_), channel_id=1, source_target_pairs={{0,1},{1,2},{2,3},{3,4},{4,5},{5,6},{6,7},{8,9},{9,10},{10,11},{11... | collective-permute-start | bytes 1572872 | tf_op jit(solution)/shard_map/ppermute | solution.py:30
  120.8 13.5 %collective-permute-start.17 = (f32[2,128,512]{2,1,0:T(8,128)S(1)}, f32[2,128,512]{2,1,0:T(8,128)S(1)}, u32[]{:S(2)}, u32[]{:S(2)}) collective-permute-start(f32[2,128,512]{2,1,0:T(8,128)S(1)} %get-tuple-element.53.refs_5_), channel_id=1, source_target_pairs={{0,1},{1,2},{2,3},{3,4},{4,5},{5,6},{6,7},{8,9},{9,10},{10,11},{11... | collective-permute-start | bytes 1572872 | tf_op jit(solution)/shard_map/ppermute | solution.py:30
  134.9 33.4 %collective-permute-start.18 = (f32[2,264,512]{2,1,0:T(8,128)S(1)}, f32[2,264,512]{2,1,0:T(8,128)S(1)}, u32[]{:S(2)}, u32[]{:S(2)}) collective-permute-start(f32[2,264,512]{2,1,0:T(8,128)S(1)} %get-tuple-element.55.refs_0_), channel_id=1, source_target_pairs={{0,8},{8,16},{16,24},{24,32},{32,40},{40,48},{48,56},{56,64},{64,7... | collective-permute-start | bytes 3244040 | tf_op jit(solution)/shard_map/ppermute | solution.py:30
  146.0 16.1 %collective-permute-start.20 = (f32[2,256,512]{2,1,0:T(8,128)S(1)}, f32[2,256,512]{2,1,0:T(8,128)S(1)}, u32[]{:S(2)}, u32[]{:S(2)}) collective-permute-start(f32[2,256,512]{2,1,0:T(8,128)S(1)} %get-tuple-element.58), channel_id=1, source_target_pairs={{0,1},{1,2},{2,3},{3,4},{4,5},{5,6},{6,7},{8,9},{9,10},{10,11},{11... | collective-permute-start | bytes 3145736 | tf_op jit(solution)/shard_map/ppermute | solution.py:30
